TPU v7x, 512 devices: a whole 4x4x16 slice. The times are simulated.
512 devices in a mesh: ctx: 16 (over z_lo, core), head: 8 (over x, z_hi), dp: 4 (over y).
Axes of the slice: x: 4, y: 4, z: 16 (z_hi: 2, z_lo: 8; z = z_hi * 8 + z_lo), core: 2. Of those that a mesh axis runs over, the one named last changes fastest.
Arguments:
- queries: bfloat16 [8192, 4096], P(('dp', 'ctx'), 'head'), parts along dimension 0, may hold values from -6 to 6
- key_rows: bfloat16 [8192, 4096], P(('dp', 'ctx'), 'head'), parts along dimension 0, may hold values from -6 to 6
- value_rows: bfloat16 [8192, 4096], P(('dp', 'ctx'), 'head'), parts along dimension 0, may hold values from -6 to 6
- gate_values: bfloat16 [8192, 4096], P(('dp', 'ctx'), 'head'), parts along dimension 0, may hold values from -6 to 6
- cotangent: bfloat16 [8192, 4096], P(('dp', 'ctx'), 'head'), parts along dimension 0, may hold values from -6 to 6
- decay_rates: float32 [16, 4096], P(None, 'head'), may hold values from 0 to 1, as said below
- residues: float32 [16, 4096], P(None, 'head'), may hold values from -4 to 4
- skip_gain: float32 [4096], P('head'), may hold values from -6 to 6
Outputs:
- queries_adjoint: bfloat16 [8192, 4096], P(('dp', 'ctx'), 'head'), parts along dimension 0
- keys_adjoint: bfloat16 [8192, 4096], P(('dp', 'ctx'), 'head'), parts along dimension 0
- values_adjoint: bfloat16 [8192, 4096], P(('dp', 'ctx'), 'head'), parts along dimension 0
- gate_adjoint: bfloat16 [8192, 4096], P(('dp', 'ctx'), 'head'), parts along dimension 0
- residues_adjoint: float32 [64, 4096], P('dp', 'head'), parts along dimension 0
There are 4 independent parts, one for each index of `dp`. A program takes and returns all parts, laid end to end along the dimension named above; an argument that names none is the same for every part. Nothing has to cross between parts.
Inputs may be any that keep to these rules, and one draw needn't show every extreme that they name: `decay_rates`: every rate lies between 0.6 / 2048 and 1/16 per position.
All inputs are finite; a program needn't handle non-finite values.
Results may differ from a plain program's by a relative error of at most 0.0094.
Values may be sent and summed in bfloat16 or wider, within the bound.
No kernel may reach another device: no remote copies, remote signals or barrier semaphores. Data moves between devices by JAX's collectives and lax.ppermute only.
A program may use at most 64 MiB of HBM per device.

v0:
```python
import math

import jax
import jax.numpy as jnp
from jax import lax
from jax.sharding import PartitionSpec as P

HEAD = 128
WIN = 4


def passed_along(array, axis, by):
    length = lax.axis_size(axis)
    return lax.ppermute(array, axis, [(i, (i + by) % length) for i in range(length)])


def window_mask(row_count):
    row_ids = jnp.arange(row_count)[:, None, None]
    lag_ids = jnp.arange(WIN + 1)[None, :, None]
    column_ids = jnp.arange(row_count)[None, None, :]
    return ((lag_ids > 0) | (column_ids <= row_ids)) & ((lag_ids < WIN) | (column_ids > row_ids))


def local(queries, key_rows, value_rows, gate_values, cotangent, decay_rates, residues, skip_gain):
    members = lax.axis_size("ctx")
    tok_rows, channels = queries.shape
    local_heads = channels // HEAD
    scale_factor = 1.0 / math.sqrt(HEAD)
    weights = jnp.sqrt(-jnp.expm1(-2.0 * decay_rates))
    mixing = residues * weights
    loop_gap = -jnp.expm1(-decay_rates * (tok_rows * members))
    device_decay = jnp.exp(-decay_rates * tok_rows)
    piece_rows = min(128, tok_rows)
    pieces = tok_rows // piece_rows
    offsets = jnp.arange(piece_rows, dtype=jnp.float32)[:, None, None]
    piece_index = jnp.arange(pieces, dtype=jnp.float32)[:, None, None]
    start_weights = jnp.exp(-decay_rates[None] * offsets)
    growth = jnp.exp(decay_rates[None] * offsets)
    delta_rows = cotangent.astype(jnp.float32) * gate_values.astype(jnp.float32)
    blocks_delta = delta_rows.reshape(pieces, piece_rows, channels)
    piece_starts = jnp.einsum(
        "qpc,mqc->mpc", start_weights, blocks_delta, precision=lax.Precision.HIGHEST
    )
    head_state = jnp.sum(
        jnp.exp(-decay_rates[None] * (piece_index * piece_rows)) * piece_starts, axis=0
    )

    def backward_turn(turn_index, moving):
        return passed_along(device_decay * moving + head_state, "ctx", -1)

    incoming = lax.fori_loop(0, members, backward_turn, jnp.zeros_like(head_state)) / loop_gap

    def backward_step(carried, segment):
        local_part = growth * lax.cumsum(start_weights * segment[:, None, :], axis=0, reverse=True)
        states = local_part + jnp.exp(-decay_rates[None] * (piece_rows - offsets)) * carried[None]
        mixture = jnp.sum(mixing[None] * states, axis=1) + skip_gain[None] * segment
        return (states[0], mixture)

    unused_state, adjoint_rows = lax.scan(backward_step, incoming, blocks_delta, reverse=True)
    attended_adjoint = adjoint_rows.reshape(tok_rows, channels).astype(jnp.bfloat16)
    key_value = jnp.stack([key_rows, value_rows])
    window = [key_value]
    moving = key_value
    for lag_index in range(WIN):
        moving = passed_along(moving, "ctx", 1)
        window.append(moving)
    stacked = jnp.stack(window)
    key_window = stacked[:, 0]
    value_window = stacked[:, 1]
    allowed = window_mask(tok_rows)
    attended_parts = []
    query_adjoints = []
    key_partials = []
    value_partials = []
    for head_index in range(local_heads):
        first = head_index * HEAD
        query_head = queries[:, first : first + HEAD]
        key_head = key_window[:, :, first : first + HEAD]
        value_head = value_window[:, :, first : first + HEAD]
        adjoint_head = attended_adjoint[:, first : first + HEAD]
        scores = (
            jnp.einsum("re,kse->rks", query_head, key_head, preferred_element_type=jnp.float32)
            * scale_factor
        )
        masked = jnp.where(allowed, scores, -jnp.inf)
        row_top = jnp.max(masked, axis=(1, 2), keepdims=True)
        raised = jnp.exp(masked - row_top)
        probability = raised / jnp.sum(raised, axis=(1, 2), keepdims=True)
        rounded_prob = probability.astype(jnp.bfloat16)
        attended_parts.append(
            jnp.einsum(
                "rks,kse->re", rounded_prob, value_head, preferred_element_type=jnp.float32
            ).astype(jnp.bfloat16)
        )
        weight_adjoint = jnp.einsum(
            "re,kse->rks", adjoint_head, value_head, preferred_element_type=jnp.float32
        )
        inner_sum = jnp.sum(probability * weight_adjoint, axis=(1, 2), keepdims=True)
        score_adjoint = (probability * (weight_adjoint - inner_sum) * scale_factor).astype(
            jnp.bfloat16
        )
        query_adjoints.append(
            jnp.einsum(
                "rks,kse->re", score_adjoint, key_head, preferred_element_type=jnp.float32
            ).astype(jnp.bfloat16)
        )
        key_partials.append(
            jnp.einsum(
                "rks,re->kse", score_adjoint, query_head, preferred_element_type=jnp.float32
            ).astype(jnp.bfloat16)
        )
        value_partials.append(
            jnp.einsum(
                "rks,re->kse", rounded_prob, adjoint_head, preferred_element_type=jnp.float32
            ).astype(jnp.bfloat16)
        )
    attended = jnp.concatenate(attended_parts, axis=1)
    queries_adjoint = jnp.concatenate(query_adjoints, axis=1)
    partials = jnp.stack(
        [jnp.concatenate(key_partials, axis=2), jnp.concatenate(value_partials, axis=2)], axis=1
    )
    collected = partials[0].astype(jnp.float32)
    for lag_index in range(1, WIN + 1):
        collected = collected + passed_along(partials[lag_index], "ctx", -lag_index).astype(
            jnp.float32
        )
    keys_adjoint = collected[0].astype(jnp.bfloat16)
    values_adjoint = collected[1].astype(jnp.bfloat16)
    signal = attended.astype(jnp.float32)
    blocks_signal = signal.reshape(pieces, piece_rows, channels)
    end_weights = jnp.exp(-decay_rates[None] * (piece_rows - 1.0 - offsets))
    piece_ends = jnp.einsum(
        "qpc,mqc->mpc", end_weights, blocks_signal, precision=lax.Precision.HIGHEST
    )
    tail_state = jnp.sum(
        jnp.exp(-decay_rates[None] * ((pieces - 1.0 - piece_index) * piece_rows)) * piece_ends,
        axis=0,
    )

    def forward_turn(turn_index, moving):
        return passed_along(device_decay * moving + tail_state, "ctx", 1)

    arriving = lax.fori_loop(0, members, forward_turn, jnp.zeros_like(tail_state)) / loop_gap
    entering = jnp.exp(-decay_rates[None] * (offsets + 1.0))

    def forward_step(carried, step_item):
        segment, matched = step_item
        local_part = start_weights * jnp.cumsum(growth * segment[:, None, :], axis=0)
        states = local_part + entering * carried[None]
        mixture = jnp.sum(mixing[None] * states, axis=1) + skip_gain[None] * segment
        product = jnp.sum(weights[None] * matched[:, None, :] * states, axis=0)
        return (states[-1], (mixture, product))

    closing, (mixed_rows, products) = lax.scan(
        forward_step, arriving, (blocks_signal, blocks_delta)
    )
    gate_adjoint = (cotangent.astype(jnp.float32) * mixed_rows.reshape(tok_rows, channels)).astype(
        jnp.bfloat16
    )
    residues_adjoint = lax.psum(jnp.sum(products, axis=0), "ctx")
    return (queries_adjoint, keys_adjoint, values_adjoint, gate_adjoint, residues_adjoint)


def solution(mesh):
    in_specs = (
        P(("dp", "ctx"), "head"),
        P(("dp", "ctx"), "head"),
        P(("dp", "ctx"), "head"),
        P(("dp", "ctx"), "head"),
        P(("dp", "ctx"), "head"),
        P(None, "head"),
        P(None, "head"),
        P("head"),
    )
    out_specs = (
        P(("dp", "ctx"), "head"),
        P(("dp", "ctx"), "head"),
        P(("dp", "ctx"), "head"),
        P(("dp", "ctx"), "head"),
        P("dp", "head"),
    )
    return jax.shard_map(local, mesh=mesh, in_specs=in_specs, out_specs=out_specs, check_vma=False)
```

profile of v0, /device:TPU:1, one launch (start us, length us, event | category | flops | bytes accessed | tf_op | source)
XLA Modules:
  0.0 583.1 jit_solution(3463437683806566200)
XLA Ops:
  8.5 11.1 %fusion.2 = f32[128,16,512]{2,1,0:T(8,128)} fusion(f32[128,512]{1,0:T(8,128)S(1)} %get-tuple-element.151, f32[16,512]{1,0:T(8,128)S(1)} %get-tuple-element.163), kind=kOutput, calls=%fused_computation.10 | output fusion | flops 135266304 | bytes 4489216 | tf_op jit(solution)/shard_map/while/body/eval_jaxpr/reduce_window_sum | solution.py:54
  29.7 10.9 %collective-permute-done.4 = bf16[2,128,512]{2,1,0:T(8,128)(2,1)S(1)} collective-permute-done((bf16[2,128,512]{2,1,0:T(8,128)(2,1)S(1)}, bf16[2,128,512]{2,1,0:T(8,128)(2,1)S(1)}, u32[]{:S(2)}, u32[]{:S(2)}) %collective-permute-start.4) | collective-permute-done | bytes 262176 | tf_op jit(solution)/shard_map/ppermute | solution.py:14
  42.8 12.1 %collective-permute-done.5 = bf16[2,128,512]{2,1,0:T(8,128)(2,1)S(1)} collective-permute-done((bf16[2,128,512]{2,1,0:T(8,128)(2,1)S(1)}, bf16[2,128,512]{2,1,0:T(8,128)(2,1)S(1)}, u32[]{:S(2)}, u32[]{:S(2)}) %collective-permute-start.5) | collective-permute-done | bytes 262176 | tf_op jit(solution)/shard_map/ppermute | solution.py:14
  60.8 184.1 %while.4 = (s32[]{:T(128)}, f32[16,512]{1,0:T(8,128)S(1)}, f32[16,512]{1,0:T(8,128)S(1)}, f32[16,512]{1,0:T(8,128)S(1)}, s32[]{:T(128)}) while((s32[]{:T(128)}, f32[16,512]{1,0:T(8,128)S(1)}, f32[16,512]{1,0:T(8,128)S(1)}, f32[16,512]{1,0:T(8,128)S(1)}, s32[]{:T(128)}) %tuple.67), condition=%wide.region_4.0_spmd, body=%wide.region_3.4_spmd.sunk | while | flops 16386 | bytes 262245 | solution.py:51
  60.8 13.8 %collective-permute-start = (f32[16,512]{1,0:T(8,128)S(1)}, f32[16,512]{1,0:T(8,128)S(1)}, u32[]{:S(2)}, u32[]{:S(2)}) collective-permute-start(f32[16,512]{1,0:T(8,128)S(1)} %multiply_add_fusion.5), channel_id=1, source_target_pairs={{0,480},{32,0},{64,32},{96,64},{128,96},{160,128},{192,160},{224,1... | collective-permute-start | bytes 98312 | tf_op jit(solution)/shard_map/while/body/eval_jaxpr/ppermute | solution.py:14
  90.8 11.0 %collective-permute-start = (f32[16,512]{1,0:T(8,128)S(1)}, f32[16,512]{1,0:T(8,128)S(1)}, u32[]{:S(2)}, u32[]{:S(2)}) collective-permute-start(f32[16,512]{1,0:T(8,128)S(1)} %multiply_add_fusion.5), channel_id=1, source_target_pairs={{0,480},{32,0},{64,32},{96,64},{128,96},{160,128},{192,160},{224,1... | collective-permute-start | bytes 98312 | tf_op jit(solution)/shard_map/while/body/eval_jaxpr/ppermute | solution.py:14
  102.6 11.0 %collective-permute-start = (f32[16,512]{1,0:T(8,128)S(1)}, f32[16,512]{1,0:T(8,128)S(1)}, u32[]{:S(2)}, u32[]{:S(2)}) collective-permute-start(f32[16,512]{1,0:T(8,128)S(1)} %multiply_add_fusion.5), channel_id=1, source_target_pairs={{0,480},{32,0},{64,32},{96,64},{128,96},{160,128},{192,160},{224,1... | collective-permute-start | bytes 98312 | tf_op jit(solution)/shard_map/while/body/eval_jaxpr/ppermute | solution.py:14
  114.5 11.0 %collective-permute-start = (f32[16,512]{1,0:T(8,128)S(1)}, f32[16,512]{1,0:T(8,128)S(1)}, u32[]{:S(2)}, u32[]{:S(2)}) collective-permute-start(f32[16,512]{1,0:T(8,128)S(1)} %multiply_add_fusion.5), channel_id=1, source_target_pairs={{0,480},{32,0},{64,32},{96,64},{128,96},{160,128},{192,160},{224,1... | collective-permute-start | bytes 98312 | tf_op jit(solution)/shard_map/while/body/eval_jaxpr/ppermute | solution.py:14
  126.3 11.0 %collective-permute-start = (f32[16,512]{1,0:T(8,128)S(1)}, f32[16,512]{1,0:T(8,128)S(1)}, u32[]{:S(2)}, u32[]{:S(2)}) collective-permute-start(f32[16,512]{1,0:T(8,128)S(1)} %multiply_add_fusion.5), channel_id=1, source_target_pairs={{0,480},{32,0},{64,32},{96,64},{128,96},{160,128},{192,160},{224,1... | collective-permute-start | bytes 98312 | tf_op jit(solution)/shard_map/while/body/eval_jaxpr/ppermute | solution.py:14
  138.2 11.0 %collective-permute-start = (f32[16,512]{1,0:T(8,128)S(1)}, f32[16,512]{1,0:T(8,128)S(1)}, u32[]{:S(2)}, u32[]{:S(2)}) collective-permute-start(f32[16,512]{1,0:T(8,128)S(1)} %multiply_add_fusion.5), channel_id=1, source_target_pairs={{0,480},{32,0},{64,32},{96,64},{128,96},{160,128},{192,160},{224,1... | collective-permute-start | bytes 98312 | tf_op jit(solution)/shard_map/while/body/eval_jaxpr/ppermute | solution.py:14
  150.0 11.0 %collective-permute-start = (f32[16,512]{1,0:T(8,128)S(1)}, f32[16,512]{1,0:T(8,128)S(1)}, u32[]{:S(2)}, u32[]{:S(2)}) collective-permute-start(f32[16,512]{1,0:T(8,128)S(1)} %multiply_add_fusion.5), channel_id=1, source_target_pairs={{0,480},{32,0},{64,32},{96,64},{128,96},{160,128},{192,160},{224,1... | collective-permute-start | bytes 98312 | tf_op jit(solution)/shard_map/while/body/eval_jaxpr/ppermute | solution.py:14
  161.9 11.0 %collective-permute-start = (f32[16,512]{1,0:T(8,128)S(1)}, f32[16,512]{1,0:T(8,128)S(1)}, u32[]{:S(2)}, u32[]{:S(2)}) collective-permute-start(f32[16,512]{1,0:T(8,128)S(1)} %multiply_add_fusion.5), channel_id=1, source_target_pairs={{0,480},{32,0},{64,32},{96,64},{128,96},{160,128},{192,160},{224,1... | collective-permute-start | bytes 98312 | tf_op jit(solution)/shard_map/while/body/eval_jaxpr/ppermute | solution.py:14
  173.7 11.0 %collective-permute-start = (f32[16,512]{1,0:T(8,128)S(1)}, f32[16,512]{1,0:T(8,128)S(1)}, u32[]{:S(2)}, u32[]{:S(2)}) collective-permute-start(f32[16,512]{1,0:T(8,128)S(1)} %multiply_add_fusion.5), channel_id=1, source_target_pairs={{0,480},{32,0},{64,32},{96,64},{128,96},{160,128},{192,160},{224,1... | collective-permute-start | bytes 98312 | tf_op jit(solution)/shard_map/while/body/eval_jaxpr/ppermute | solution.py:14
  185.6 11.0 %collective-permute-start = (f32[16,512]{1,0:T(8,128)S(1)}, f32[16,512]{1,0:T(8,128)S(1)}, u32[]{:S(2)}, u32[]{:S(2)}) collective-permute-start(f32[16,512]{1,0:T(8,128)S(1)} %multiply_add_fusion.5), channel_id=1, source_target_pairs={{0,480},{32,0},{64,32},{96,64},{128,96},{160,128},{192,160},{224,1... | collective-permute-start | bytes 98312 | tf_op jit(solution)/shard_map/while/body/eval_jaxpr/ppermute | solution.py:14
  197.4 11.0 %collective-permute-start = (f32[16,512]{1,0:T(8,128)S(1)}, f32[16,512]{1,0:T(8,128)S(1)}, u32[]{:S(2)}, u32[]{:S(2)}) collective-permute-start(f32[16,512]{1,0:T(8,128)S(1)} %multiply_add_fusion.5), channel_id=1, source_target_pairs={{0,480},{32,0},{64,32},{96,64},{128,96},{160,128},{192,160},{224,1... | collective-permute-start | bytes 98312 | tf_op jit(solution)/shard_map/while/body/eval_jaxpr/ppermute | solution.py:14
  209.3 11.0 %collective-permute-start = (f32[16,512]{1,0:T(8,128)S(1)}, f32[16,512]{1,0:T(8,128)S(1)}, u32[]{:S(2)}, u32[]{:S(2)}) collective-permute-start(f32[16,512]{1,0:T(8,128)S(1)} %multiply_add_fusion.5), channel_id=1, source_target_pairs={{0,480},{32,0},{64,32},{96,64},{128,96},{160,128},{192,160},{224,1... | collective-permute-start | bytes 98312 | tf_op jit(solution)/shard_map/while/body/eval_jaxpr/ppermute | solution.py:14
  221.1 11.0 %collective-permute-start = (f32[16,512]{1,0:T(8,128)S(1)}, f32[16,512]{1,0:T(8,128)S(1)}, u32[]{:S(2)}, u32[]{:S(2)}) collective-permute-start(f32[16,512]{1,0:T(8,128)S(1)} %multiply_add_fusion.5), channel_id=1, source_target_pairs={{0,480},{32,0},{64,32},{96,64},{128,96},{160,128},{192,160},{224,1... | collective-permute-start | bytes 98312 | tf_op jit(solution)/shard_map/while/body/eval_jaxpr/ppermute | solution.py:14
  233.0 11.0 %collective-permute-start = (f32[16,512]{1,0:T(8,128)S(1)}, f32[16,512]{1,0:T(8,128)S(1)}, u32[]{:S(2)}, u32[]{:S(2)}) collective-permute-start(f32[16,512]{1,0:T(8,128)S(1)} %multiply_add_fusion.5), channel_id=1, source_target_pairs={{0,480},{32,0},{64,32},{96,64},{128,96},{160,128},{192,160},{224,1... | collective-permute-start | bytes 98312 | tf_op jit(solution)/shard_map/while/body/eval_jaxpr/ppermute | solution.py:14
  244.8 189.6 %while.5 = (s32[]{:T(128)}, f32[16,512]{1,0:T(8,128)S(1)}, f32[16,512]{1,0:T(8,128)S(1)}, f32[16,512]{1,0:T(8,128)S(1)}, s32[]{:T(128)}) while((s32[]{:T(128)}, f32[16,512]{1,0:T(8,128)S(1)}, f32[16,512]{1,0:T(8,128)S(1)}, f32[16,512]{1,0:T(8,128)S(1)}, s32[]{:T(128)}) %tuple.73), condition=%wide.region_18.19_spmd, body=%wide.region_17.18_spmd.sunk | while | flops 16386 | bytes 262245 | solution.py:143
  258.5 9.9 %collective-permute-done.1 = f32[16,512]{1,0:T(8,128)S(1)} collective-permute-done((f32[16,512]{1,0:T(8,128)S(1)}, f32[16,512]{1,0:T(8,128)S(1)}, u32[]{:S(2)}, u32[]{:S(2)}) %collective-permute-start.1) | collective-permute-done | bytes 32800 | tf_op jit(solution)/shard_map/while/body/eval_jaxpr/ppermute | solution.py:14
  270.3 9.9 %collective-permute-done.1 = f32[16,512]{1,0:T(8,128)S(1)} collective-permute-done((f32[16,512]{1,0:T(8,128)S(1)}, f32[16,512]{1,0:T(8,128)S(1)}, u32[]{:S(2)}, u32[]{:S(2)}) %collective-permute-start.1) | collective-permute-done | bytes 32800 | tf_op jit(solution)/shard_map/while/body/eval_jaxpr/ppermute | solution.py:14
  282.2 9.9 %collective-permute-done.1 = f32[16,512]{1,0:T(8,128)S(1)} collective-permute-done((f32[16,512]{1,0:T(8,128)S(1)}, f32[16,512]{1,0:T(8,128)S(1)}, u32[]{:S(2)}, u32[]{:S(2)}) %collective-permute-start.1) | collective-permute-done | bytes 32800 | tf_op jit(solution)/shard_map/while/body/eval_jaxpr/ppermute | solution.py:14
  294.0 9.9 %collective-permute-done.1 = f32[16,512]{1,0:T(8,128)S(1)} collective-permute-done((f32[16,512]{1,0:T(8,128)S(1)}, f32[16,512]{1,0:T(8,128)S(1)}, u32[]{:S(2)}, u32[]{:S(2)}) %collective-permute-start.1) | collective-permute-done | bytes 32800 | tf_op jit(solution)/shard_map/while/body/eval_jaxpr/ppermute | solution.py:14
  317.7 9.9 %collective-permute-done.1 = f32[16,512]{1,0:T(8,128)S(1)} collective-permute-done((f32[16,512]{1,0:T(8,128)S(1)}, f32[16,512]{1,0:T(8,128)S(1)}, u32[]{:S(2)}, u32[]{:S(2)}) %collective-permute-start.1) | collective-permute-done | bytes 32800 | tf_op jit(solution)/shard_map/while/body/eval_jaxpr/ppermute | solution.py:14
  329.6 9.9 %collective-permute-done.1 = f32[16,512]{1,0:T(8,128)S(1)} collective-permute-done((f32[16,512]{1,0:T(8,128)S(1)}, f32[16,512]{1,0:T(8,128)S(1)}, u32[]{:S(2)}, u32[]{:S(2)}) %collective-permute-start.1) | collective-permute-done | bytes 32800 | tf_op jit(solution)/shard_map/while/body/eval_jaxpr/ppermute | solution.py:14
  353.3 9.9 %collective-permute-done.1 = f32[16,512]{1,0:T(8,128)S(1)} collective-permute-done((f32[16,512]{1,0:T(8,128)S(1)}, f32[16,512]{1,0:T(8,128)S(1)}, u32[]{:S(2)}, u32[]{:S(2)}) %collective-permute-start.1) | collective-permute-done | bytes 32800 | tf_op jit(solution)/shard_map/while/body/eval_jaxpr/ppermute | solution.py:14
  365.1 9.9 %collective-permute-done.1 = f32[16,512]{1,0:T(8,128)S(1)} collective-permute-done((f32[16,512]{1,0:T(8,128)S(1)}, f32[16,512]{1,0:T(8,128)S(1)}, u32[]{:S(2)}, u32[]{:S(2)}) %collective-permute-start.1) | collective-permute-done | bytes 32800 | tf_op jit(solution)/shard_map/while/body/eval_jaxpr/ppermute | solution.py:14
  400.7 9.9 %collective-permute-done.1 = f32[16,512]{1,0:T(8,128)S(1)} collective-permute-done((f32[16,512]{1,0:T(8,128)S(1)}, f32[16,512]{1,0:T(8,128)S(1)}, u32[]{:S(2)}, u32[]{:S(2)}) %collective-permute-start.1) | collective-permute-done | bytes 32800 | tf_op jit(solution)/shard_map/while/body/eval_jaxpr/ppermute | solution.py:14
  424.4 10.0 %collective-permute-done.1 = f32[16,512]{1,0:T(8,128)S(1)} collective-permute-done((f32[16,512]{1,0:T(8,128)S(1)}, f32[16,512]{1,0:T(8,128)S(1)}, u32[]{:S(2)}, u32[]{:S(2)}) %collective-permute-start.1) | collective-permute-done | bytes 32800 | tf_op jit(solution)/shard_map/while/body/eval_jaxpr/ppermute | solution.py:14
  434.5 29.8 %multiply_reduce_fusion.2 = (f32[16,512]{1,0:T(8,128)S(1)}, f32[128,512]{1,0:T(8,128)S(1)}, f32[128,512]{1,0:T(8,128)S(1)}) fusion(f32[16,512]{1,0:T(8,128)S(1)} %get-tuple-element.160, f32[128,512]{1,0:T(8,128)S(1)} %get-tuple-element.151, f32[16,512]{1,0:T(8,128)S(1)} %get-tuple-element.159, f32[16,512]{1,0:T(8,128)S(1)} %get-tuple-element.157, ...), kind=kOutput, calls=%fused_computation.4 | output fusion | flops 152952832 | bytes 5473280 | tf_op jit(solution)/shard_map/while/body/eval_jaxpr/jit(cumsum)/reduce_window_sum | solution.py:148
  470.4 11.2 %collective-permute-start.6 = (bf16[2,128,512]{1,2,0:T(8,128)(2,1)}, bf16[2,128,512]{1,2,0:T(8,128)(2,1)S(1)}, u32[]{:S(2)}, u32[]{:S(2)}) collective-permute-start(bf16[2,128,512]{1,2,0:T(8,128)(2,1)} %get-tuple-element.143), channel_id=1, source_target_pairs={{0,480},{32,0},{64,32},{96,64},{128,96},{160,128},{192,160},{224,1... | collective-permute-start | bytes 786440 | tf_op jit(solution)/shard_map/ppermute | solution.py:14
  488.5 91.9 %psum.7 = f32[16,512]{1,0:T(8,128)} all-reduce(f32[16,512]{1,0:T(8,128)S(1)} %get-tuple-element.122), channel_id=1, replica_groups=mesh['ctx'=16,'head'=8,'dp'=4] {'ctx'}, use_global_device_ids=true, to_apply=%region_21.22 | all-reduce | flops 8192 | bytes 65536 | tf_op jit(solution)/shard_map/psum | solution.py:160
  (182 shorter events, 158.6 us)
Async XLA Ops:
  1.7 17.9 %collective-permute-start.2 = (bf16[2,128,512]{2,1,0:T(8,128)(2,1)S(1)}, bf16[2,128,512]{2,1,0:T(8,128)(2,1)S(1)}, u32[]{:S(2)}, u32[]{:S(2)}) collective-permute-start(bf16[2,128,512]{2,1,0:T(8,128)(2,1)S(1)} %pad_maximum_fusion.1), channel_id=1, source_target_pairs={{0,32},{32,64},{64,96},{96,128},{128,160},{160,192},{192,224},{224... | collective-permute-start | bytes 786440 | tf_op jit(solution)/shard_map/ppermute | solution.py:14
  26.4 14.3 %collective-permute-start.4 = (bf16[2,128,512]{2,1,0:T(8,128)(2,1)S(1)}, bf16[2,128,512]{2,1,0:T(8,128)(2,1)S(1)}, u32[]{:S(2)}, u32[]{:S(2)}) collective-permute-start(bf16[2,128,512]{2,1,0:T(8,128)(2,1)S(1)} %collective-permute-done.3), channel_id=1, source_target_pairs={{0,32},{32,64},{64,96},{96,128},{128,160},{160,192},{192,224},{224... | collective-permute-start | bytes 786440 | tf_op jit(solution)/shard_map/ppermute | solution.py:14
  40.7 14.3 %collective-permute-start.5 = (bf16[2,128,512]{2,1,0:T(8,128)(2,1)S(1)}, bf16[2,128,512]{2,1,0:T(8,128)(2,1)S(1)}, u32[]{:S(2)}, u32[]{:S(2)}) collective-permute-start(bf16[2,128,512]{2,1,0:T(8,128)(2,1)S(1)} %collective-permute-done.4), channel_id=1, source_target_pairs={{0,32},{32,64},{64,96},{96,128},{128,160},{160,192},{192,224},{224... | collective-permute-start | bytes 786440 | tf_op jit(solution)/shard_map/ppermute | solution.py:14
  60.8 14.6 %collective-permute-start = (f32[16,512]{1,0:T(8,128)S(1)}, f32[16,512]{1,0:T(8,128)S(1)}, u32[]{:S(2)}, u32[]{:S(2)}) collective-permute-start(f32[16,512]{1,0:T(8,128)S(1)} %multiply_add_fusion.5), channel_id=1, source_target_pairs={{0,480},{32,0},{64,32},{96,64},{128,96},{160,128},{192,160},{224,1... | collective-permute-start | bytes 98312 | tf_op jit(solution)/shard_map/while/body/eval_jaxpr/ppermute | solution.py:14
  90.8 11.8 %collective-permute-start = (f32[16,512]{1,0:T(8,128)S(1)}, f32[16,512]{1,0:T(8,128)S(1)}, u32[]{:S(2)}, u32[]{:S(2)}) collective-permute-start(f32[16,512]{1,0:T(8,128)S(1)} %multiply_add_fusion.5), channel_id=1, source_target_pairs={{0,480},{32,0},{64,32},{96,64},{128,96},{160,128},{192,160},{224,1... | collective-permute-start | bytes 98312 | tf_op jit(solution)/shard_map/while/body/eval_jaxpr/ppermute | solution.py:14
  102.6 11.8 %collective-permute-start = (f32[16,512]{1,0:T(8,128)S(1)}, f32[16,512]{1,0:T(8,128)S(1)}, u32[]{:S(2)}, u32[]{:S(2)}) collective-permute-start(f32[16,512]{1,0:T(8,128)S(1)} %multiply_add_fusion.5), channel_id=1, source_target_pairs={{0,480},{32,0},{64,32},{96,64},{128,96},{160,128},{192,160},{224,1... | collective-permute-start | bytes 98312 | tf_op jit(solution)/shard_map/while/body/eval_jaxpr/ppermute | solution.py:14
  114.5 11.8 %collective-permute-start = (f32[16,512]{1,0:T(8,128)S(1)}, f32[16,512]{1,0:T(8,128)S(1)}, u32[]{:S(2)}, u32[]{:S(2)}) collective-permute-start(f32[16,512]{1,0:T(8,128)S(1)} %multiply_add_fusion.5), channel_id=1, source_target_pairs={{0,480},{32,0},{64,32},{96,64},{128,96},{160,128},{192,160},{224,1... | collective-permute-start | bytes 98312 | tf_op jit(solution)/shard_map/while/body/eval_jaxpr/ppermute | solution.py:14
  126.3 11.8 %collective-permute-start = (f32[16,512]{1,0:T(8,128)S(1)}, f32[16,512]{1,0:T(8,128)S(1)}, u32[]{:S(2)}, u32[]{:S(2)}) collective-permute-start(f32[16,512]{1,0:T(8,128)S(1)} %multiply_add_fusion.5), channel_id=1, source_target_pairs={{0,480},{32,0},{64,32},{96,64},{128,96},{160,128},{192,160},{224,1... | collective-permute-start | bytes 98312 | tf_op jit(solution)/shard_map/while/body/eval_jaxpr/ppermute | solution.py:14
  138.2 11.8 %collective-permute-start = (f32[16,512]{1,0:T(8,128)S(1)}, f32[16,512]{1,0:T(8,128)S(1)}, u32[]{:S(2)}, u32[]{:S(2)}) collective-permute-start(f32[16,512]{1,0:T(8,128)S(1)} %multiply_add_fusion.5), channel_id=1, source_target_pairs={{0,480},{32,0},{64,32},{96,64},{128,96},{160,128},{192,160},{224,1... | collective-permute-start | bytes 98312 | tf_op jit(solution)/shard_map/while/body/eval_jaxpr/ppermute | solution.py:14
  150.0 11.8 %collective-permute-start = (f32[16,512]{1,0:T(8,128)S(1)}, f32[16,512]{1,0:T(8,128)S(1)}, u32[]{:S(2)}, u32[]{:S(2)}) collective-permute-start(f32[16,512]{1,0:T(8,128)S(1)} %multiply_add_fusion.5), channel_id=1, source_target_pairs={{0,480},{32,0},{64,32},{96,64},{128,96},{160,128},{192,160},{224,1... | collective-permute-start | bytes 98312 | tf_op jit(solution)/shard_map/while/body/eval_jaxpr/ppermute | solution.py:14
  161.9 11.8 %collective-permute-start = (f32[16,512]{1,0:T(8,128)S(1)}, f32[16,512]{1,0:T(8,128)S(1)}, u32[]{:S(2)}, u32[]{:S(2)}) collective-permute-start(f32[16,512]{1,0:T(8,128)S(1)} %multiply_add_fusion.5), channel_id=1, source_target_pairs={{0,480},{32,0},{64,32},{96,64},{128,96},{160,128},{192,160},{224,1... | collective-permute-start | bytes 98312 | tf_op jit(solution)/shard_map/while/body/eval_jaxpr/ppermute | solution.py:14
  173.7 11.8 %collective-permute-start = (f32[16,512]{1,0:T(8,128)S(1)}, f32[16,512]{1,0:T(8,128)S(1)}, u32[]{:S(2)}, u32[]{:S(2)}) collective-permute-start(f32[16,512]{1,0:T(8,128)S(1)} %multiply_add_fusion.5), channel_id=1, source_target_pairs={{0,480},{32,0},{64,32},{96,64},{128,96},{160,128},{192,160},{224,1... | collective-permute-start | bytes 98312 | tf_op jit(solution)/shard_map/while/body/eval_jaxpr/ppermute | solution.py:14
  185.6 11.8 %collective-permute-start = (f32[16,512]{1,0:T(8,128)S(1)}, f32[16,512]{1,0:T(8,128)S(1)}, u32[]{:S(2)}, u32[]{:S(2)}) collective-permute-start(f32[16,512]{1,0:T(8,128)S(1)} %multiply_add_fusion.5), channel_id=1, source_target_pairs={{0,480},{32,0},{64,32},{96,64},{128,96},{160,128},{192,160},{224,1... | collective-permute-start | bytes 98312 | tf_op jit(solution)/shard_map/while/body/eval_jaxpr/ppermute | solution.py:14
  197.4 11.8 %collective-permute-start = (f32[16,512]{1,0:T(8,128)S(1)}, f32[16,512]{1,0:T(8,128)S(1)}, u32[]{:S(2)}, u32[]{:S(2)}) collective-permute-start(f32[16,512]{1,0:T(8,128)S(1)} %multiply_add_fusion.5), channel_id=1, source_target_pairs={{0,480},{32,0},{64,32},{96,64},{128,96},{160,128},{192,160},{224,1... | collective-permute-start | bytes 98312 | tf_op jit(solution)/shard_map/while/body/eval_jaxpr/ppermute | solution.py:14
  209.3 11.8 %collective-permute-start = (f32[16,512]{1,0:T(8,128)S(1)}, f32[16,512]{1,0:T(8,128)S(1)}, u32[]{:S(2)}, u32[]{:S(2)}) collective-permute-start(f32[16,512]{1,0:T(8,128)S(1)} %multiply_add_fusion.5), channel_id=1, source_target_pairs={{0,480},{32,0},{64,32},{96,64},{128,96},{160,128},{192,160},{224,1... | collective-permute-start | bytes 98312 | tf_op jit(solution)/shard_map/while/body/eval_jaxpr/ppermute | solution.py:14
  221.1 11.8 %collective-permute-start = (f32[16,512]{1,0:T(8,128)S(1)}, f32[16,512]{1,0:T(8,128)S(1)}, u32[]{:S(2)}, u32[]{:S(2)}) collective-permute-start(f32[16,512]{1,0:T(8,128)S(1)} %multiply_add_fusion.5), channel_id=1, source_target_pairs={{0,480},{32,0},{64,32},{96,64},{128,96},{160,128},{192,160},{224,1... | collective-permute-start | bytes 98312 | tf_op jit(solution)/shard_map/while/body/eval_jaxpr/ppermute | solution.py:14
  233.0 11.8 %collective-permute-start = (f32[16,512]{1,0:T(8,128)S(1)}, f32[16,512]{1,0:T(8,128)S(1)}, u32[]{:S(2)}, u32[]{:S(2)}) collective-permute-start(f32[16,512]{1,0:T(8,128)S(1)} %multiply_add_fusion.5), channel_id=1, source_target_pairs={{0,480},{32,0},{64,32},{96,64},{128,96},{160,128},{192,160},{224,1... | collective-permute-start | bytes 98312 | tf_op jit(solution)/shard_map/while/body/eval_jaxpr/ppermute | solution.py:14
  256.5 11.8 %collective-permute-start.1 = (f32[16,512]{1,0:T(8,128)S(1)}, f32[16,512]{1,0:T(8,128)S(1)}, u32[]{:S(2)}, u32[]{:S(2)}) collective-permute-start(f32[16,512]{1,0:T(8,128)S(1)} %multiply_add_fusion.6), channel_id=1, source_target_pairs={{0,32},{32,64},{64,96},{96,128},{128,160},{160,192},{192,224},{224... | collective-permute-start | bytes 98312 | tf_op jit(solution)/shard_map/while/body/eval_jaxpr/ppermute | solution.py:14
  280.2 11.8 %collective-permute-start.1 = (f32[16,512]{1,0:T(8,128)S(1)}, f32[16,512]{1,0:T(8,128)S(1)}, u32[]{:S(2)}, u32[]{:S(2)}) collective-permute-start(f32[16,512]{1,0:T(8,128)S(1)} %multiply_add_fusion.6), channel_id=1, source_target_pairs={{0,32},{32,64},{64,96},{96,128},{128,160},{160,192},{192,224},{224... | collective-permute-start | bytes 98312 | tf_op jit(solution)/shard_map/while/body/eval_jaxpr/ppermute | solution.py:14
  292.1 11.8 %collective-permute-start.1 = (f32[16,512]{1,0:T(8,128)S(1)}, f32[16,512]{1,0:T(8,128)S(1)}, u32[]{:S(2)}, u32[]{:S(2)}) collective-permute-start(f32[16,512]{1,0:T(8,128)S(1)} %multiply_add_fusion.6), channel_id=1, source_target_pairs={{0,32},{32,64},{64,96},{96,128},{128,160},{160,192},{192,224},{224... | collective-permute-start | bytes 98312 | tf_op jit(solution)/shard_map/while/body/eval_jaxpr/ppermute | solution.py:14
  315.8 11.8 %collective-permute-start.1 = (f32[16,512]{1,0:T(8,128)S(1)}, f32[16,512]{1,0:T(8,128)S(1)}, u32[]{:S(2)}, u32[]{:S(2)}) collective-permute-start(f32[16,512]{1,0:T(8,128)S(1)} %multiply_add_fusion.6), channel_id=1, source_target_pairs={{0,32},{32,64},{64,96},{96,128},{128,160},{160,192},{192,224},{224... | collective-permute-start | bytes 98312 | tf_op jit(solution)/shard_map/while/body/eval_jaxpr/ppermute | solution.py:14
  327.6 11.8 %collective-permute-start.1 = (f32[16,512]{1,0:T(8,128)S(1)}, f32[16,512]{1,0:T(8,128)S(1)}, u32[]{:S(2)}, u32[]{:S(2)}) collective-permute-start(f32[16,512]{1,0:T(8,128)S(1)} %multiply_add_fusion.6), channel_id=1, source_target_pairs={{0,32},{32,64},{64,96},{96,128},{128,160},{160,192},{192,224},{224... | collective-permute-start | bytes 98312 | tf_op jit(solution)/shard_map/while/body/eval_jaxpr/ppermute | solution.py:14
  339.5 11.8 %collective-permute-start.1 = (f32[16,512]{1,0:T(8,128)S(1)}, f32[16,512]{1,0:T(8,128)S(1)}, u32[]{:S(2)}, u32[]{:S(2)}) collective-permute-start(f32[16,512]{1,0:T(8,128)S(1)} %multiply_add_fusion.6), channel_id=1, source_target_pairs={{0,32},{32,64},{64,96},{96,128},{128,160},{160,192},{192,224},{224... | collective-permute-start | bytes 98312 | tf_op jit(solution)/shard_map/while/body/eval_jaxpr/ppermute | solution.py:14
  351.3 11.8 %collective-permute-start.1 = (f32[16,512]{1,0:T(8,128)S(1)}, f32[16,512]{1,0:T(8,128)S(1)}, u32[]{:S(2)}, u32[]{:S(2)}) collective-permute-start(f32[16,512]{1,0:T(8,128)S(1)} %multiply_add_fusion.6), channel_id=1, source_target_pairs={{0,32},{32,64},{64,96},{96,128},{128,160},{160,192},{192,224},{224... | collective-permute-start | bytes 98312 | tf_op jit(solution)/shard_map/while/body/eval_jaxpr/ppermute | solution.py:14
  363.2 11.8 %collective-permute-start.1 = (f32[16,512]{1,0:T(8,128)S(1)}, f32[16,512]{1,0:T(8,128)S(1)}, u32[]{:S(2)}, u32[]{:S(2)}) collective-permute-start(f32[16,512]{1,0:T(8,128)S(1)} %multiply_add_fusion.6), channel_id=1, source_target_pairs={{0,32},{32,64},{64,96},{96,128},{128,160},{160,192},{192,224},{224... | collective-permute-start | bytes 98312 | tf_op jit(solution)/shard_map/while/body/eval_jaxpr/ppermute | solution.py:14
  375.0 11.8 %collective-permute-start.1 = (f32[16,512]{1,0:T(8,128)S(1)}, f32[16,512]{1,0:T(8,128)S(1)}, u32[]{:S(2)}, u32[]{:S(2)}) collective-permute-start(f32[16,512]{1,0:T(8,128)S(1)} %multiply_add_fusion.6), channel_id=1, source_target_pairs={{0,32},{32,64},{64,96},{96,128},{128,160},{160,192},{192,224},{224... | collective-permute-start | bytes 98312 | tf_op jit(solution)/shard_map/while/body/eval_jaxpr/ppermute | solution.py:14
  398.7 11.8 %collective-permute-start.1 = (f32[16,512]{1,0:T(8,128)S(1)}, f32[16,512]{1,0:T(8,128)S(1)}, u32[]{:S(2)}, u32[]{:S(2)}) collective-permute-start(f32[16,512]{1,0:T(8,128)S(1)} %multiply_add_fusion.6), channel_id=1, source_target_pairs={{0,32},{32,64},{64,96},{96,128},{128,160},{160,192},{192,224},{224... | collective-permute-start | bytes 98312 | tf_op jit(solution)/shard_map/while/body/eval_jaxpr/ppermute | solution.py:14
  422.4 11.9 %collective-permute-start.1 = (f32[16,512]{1,0:T(8,128)S(1)}, f32[16,512]{1,0:T(8,128)S(1)}, u32[]{:S(2)}, u32[]{:S(2)}) collective-permute-start(f32[16,512]{1,0:T(8,128)S(1)} %multiply_add_fusion.6), channel_id=1, source_target_pairs={{0,32},{32,64},{64,96},{96,128},{128,160},{160,192},{192,224},{224... | collective-permute-start | bytes 98312 | tf_op jit(solution)/shard_map/while/body/eval_jaxpr/ppermute | solution.py:14
  470.4 110.0 %collective-permute-start.6 = (bf16[2,128,512]{1,2,0:T(8,128)(2,1)}, bf16[2,128,512]{1,2,0:T(8,128)(2,1)S(1)}, u32[]{:S(2)}, u32[]{:S(2)}) collective-permute-start(bf16[2,128,512]{1,2,0:T(8,128)(2,1)} %get-tuple-element.143), channel_id=1, source_target_pairs={{0,480},{32,0},{64,32},{96,64},{128,96},{160,128},{192,160},{224,1... | collective-permute-start | bytes 786440 | tf_op jit(solution)/shard_map/ppermute | solution.py:14
  481.7 98.8 %collective-permute-start.7 = (bf16[2,128,512]{1,2,0:T(8,128)(2,1)}, bf16[2,128,512]{1,2,0:T(8,128)(2,1)S(1)}, u32[]{:S(2)}, u32[]{:S(2)}) collective-permute-start(bf16[2,128,512]{1,2,0:T(8,128)(2,1)} %get-tuple-element.144), channel_id=1, source_target_pairs={{0,448},{32,480},{64,0},{96,32},{128,64},{160,96},{192,128},{224,1... | collective-permute-start | bytes 786440 | tf_op jit(solution)/shard_map/ppermute | solution.py:14
  483.6 96.9 %collective-permute-start.9 = (bf16[2,128,512]{1,2,0:T(8,128)(2,1)S(1)}, bf16[2,128,512]{1,2,0:T(8,128)(2,1)S(1)}, u32[]{:S(2)}, u32[]{:S(2)}) collective-permute-start(bf16[2,128,512]{1,2,0:T(8,128)(2,1)S(1)} %get-tuple-element.145), channel_id=1, source_target_pairs={{0,384},{32,416},{64,448},{96,480},{128,0},{160,32},{192,64},{224,... | collective-permute-start | bytes 786440 | tf_op jit(solution)/shard_map/ppermute | solution.py:14
  485.5 94.9 %collective-permute-start.8 = (bf16[2,128,512]{1,2,0:T(8,128)(2,1)S(1)}, bf16[2,128,512]{1,2,0:T(8,128)(2,1)}, u32[]{:S(2)}, u32[]{:S(2)}) collective-permute-start(bf16[2,128,512]{1,2,0:T(8,128)(2,1)S(1)} %get-tuple-element.146), channel_id=1, source_target_pairs={{0,416},{32,448},{64,480},{96,0},{128,32},{160,64},{192,96},{224,1... | collective-permute-start | bytes 786440 | tf_op jit(solution)/shard_map/ppermute | solution.py:14
  (26 other events, 775.1 us)
where the time goes:
time: 589 us; the launch traced here: 583 us
  starting transfers between devices  228 us (39%)
  waiting for transfers between devices  201 us (34%)
  blocking collectives  91.9 us (16%)
  other arithmetic  51.4 us (9%)
  matrix products  6.17 us (1%)
    ppermute x40, starting transfers between devices, passed_along(): lax.ppermute(array, axis, [(i, (i + by) % length) for i in range(length)])  228 us
    ppermute x40, waiting for transfers between devices, passed_along(): lax.ppermute(array, axis, [(i, (i + by) % length) for i in range(length)])  201 us
    psum x1, blocking collectives, local(): residues_adjoint = lax.psum(jnp.sum(products, axis=0), 'ctx')  91.9 us
    another operation x1, other arithmetic, forward_step(): jnp.cumsum(growth * segment[:, None, :], axis=0)  29.8 us
  transfers between devices with their start and end apart: 40, of which 35 were waited for; matrix products, arithmetic and copies ran while one was open for 3% of the time, Pallas kernels for 0%

commit v1 on v0

v1 whole, which is shorter than its diff:
```python
import math

import jax
import jax.numpy as jnp
from jax import lax
from jax.experimental import pallas as pl
from jax.experimental.pallas import tpu as pltpu
from jax.sharding import PartitionSpec as P

HEAD = 128
WIN = 4
LANES = 128
SUBS = 8
GROUP = 8
F32 = jnp.float32
BF16 = jnp.bfloat16


def call(body, outs, scratch=(), in_specs=None, count=0, name=None):
    specs = [pl.BlockSpec(memory_space=pltpu.SMEM)]
    specs += [pl.BlockSpec(memory_space=pltpu.VMEM)] * (count - 1)
    return pl.pallas_call(
        body,
        out_shape=[jax.ShapeDtypeStruct(s, d) for s, d in outs],
        in_specs=specs,
        out_specs=[pl.BlockSpec(memory_space=pltpu.VMEM)] * len(outs),
        scratch_shapes=list(scratch),
        name=name,
    )


def halves(core, width):
    own = pl.multiple_of(core * width, LANES)
    other = pl.multiple_of((1 - core) * width, LANES)
    return own, other


def pack_body(pos, q, k, v, gate, cot, keep_kv, give_kv, give_all):
    width = q.shape[1] // 2
    own, other = halves(pos[0], width)
    keep_kv[0] = k[:, pl.ds(own, width)]
    keep_kv[1] = v[:, pl.ds(own, width)]
    k_give = k[:, pl.ds(other, width)]
    v_give = v[:, pl.ds(other, width)]
    give_kv[0] = k_give
    give_kv[1] = v_give
    give_all[0] = k_give
    give_all[1] = v_give
    give_all[2] = q[:, pl.ds(other, width)]
    give_all[3] = gate[:, pl.ds(other, width)]
    give_all[4] = cot[:, pl.ds(other, width)]


def rows3(values):
    return jnp.broadcast_to(values[:, None, :], (values.shape[0], SUBS, values.shape[1]))


def each_group(poles, width, body):
    pole_groups = poles // GROUP
    lane_groups = width // LANES

    def step(index, carry):
        lane_group = index // pole_groups
        first_lane = pl.multiple_of(lane_group * LANES, LANES)
        first_pole = pl.multiple_of((index % pole_groups) * GROUP, GROUP)
        body(first_pole, lane_group, first_lane)
        return carry

    lax.fori_loop(0, pole_groups * lane_groups, step, 0)


def head_body(pos, gate, cot, given, rates, delta, totals, slots, head_ref):
    rows, channels = gate.shape
    width = channels // 2
    poles = rates.shape[0]
    chips = slots.shape[0]
    own, other = halves(pos[0], width)
    tokens = delta.shape[1]
    steps = tokens // SUBS
    mine = pl.multiple_of(pos[0] * rows, rows)
    theirs = pl.multiple_of((1 - pos[0]) * rows, rows)
    for lane_group in range(width // LANES):
        lanes = slice(lane_group * LANES, (lane_group + 1) * LANES)
        at_own = pl.ds(own + lane_group * LANES, LANES)
        delta[lane_group, pl.ds(mine, rows), :] = gate[:, at_own].astype(F32) * cot[:, at_own].astype(F32)
        delta[lane_group, pl.ds(theirs, rows), :] = given[3, :, lanes].astype(F32) * given[
            4, :, lanes
        ].astype(F32)

    def group(first_pole, lane_group, first_lane):
        rate = rates[pl.ds(first_pole, GROUP), pl.ds(own + first_lane, LANES)]
        lam = rows3(jnp.exp(-rate))
        state = jnp.zeros((GROUP, SUBS, LANES), F32)
        for j in reversed(range(steps)):
            state = lam * state + delta[lane_group, pl.ds(j, SUBS, stride=steps), :][None]
        totals[pl.ds(first_pole, GROUP), :, pl.ds(first_lane, LANES)] = state
        block = lax.broadcasted_iota(jnp.int32, (GROUP, SUBS, LANES), 1).astype(F32)
        power = jnp.exp(-rows3(rate) * (block * steps))
        head_ref[pl.ds(first_pole, GROUP), pl.ds(first_lane, LANES)] = jnp.sum(power * state, axis=1)

    each_group(poles, width, group)
    rate = rates[:, pl.ds(own, width)]
    send_slots(slots, head_ref[...], rate, tokens, chips, lambda k: pos[1] - k)


def send_slots(slots, state, rate, tokens, chips, place):
    decay = jnp.exp(-rate * tokens)
    value = state / (1.0 - jnp.exp(-rate * (tokens * chips)))
    for k in range(1, chips + 1):
        slots[lax.rem(place(k) + 2 * chips, chips), 0 : rate.shape[0], :] = value.astype(BF16)
        if k < chips:
            value = value * decay


def block_ids(shape):
    return lax.broadcasted_iota(jnp.int32, shape, 1)


def entering_later(totals, incoming, lam_block):
    ids = block_ids(totals.shape)
    value = jnp.where(ids == SUBS - 1, rows3(incoming), pltpu.roll(totals, SUBS - 1, 1))
    power = lam_block
    for shift in (1, 2, 4):
        moved = pltpu.roll(value, SUBS - shift, 1)
        value = value + jnp.where(ids < SUBS - shift, power * moved, 0.0)
        power = power * power
    return value


def entering_earlier(totals, arriving, lam_block):
    ids = block_ids(totals.shape)
    value = jnp.where(ids == 0, rows3(arriving), pltpu.roll(totals, 1, 1))
    power = lam_block
    for shift in (1, 2, 4):
        moved = pltpu.roll(value, shift, 1)
        value = value + jnp.where(ids >= shift, power * moved, 0.0)
        power = power * power
    return value


def pole_weights(rate):
    tangent = jnp.tanh(rate)
    return jnp.sqrt(2.0 * tangent / (1.0 + tangent))


def attention_body(
    pos,
    q,
    keep_kv,
    given,
    same1,
    cross1,
    same2,
    cross2,
    delta,
    totals,
    slots_in,
    rates,
    residues,
    skip,
    dq_keep,
    dkv_keep,
    swap_out,
    out_same1,
    out_cross1,
    out_same2,
    out_cross2,
    attended,
    tail_totals,
    slots,
    qbuf,
    kbuf,
    vbuf,
    adj32,
    adj16,
    dk_acc,
    dv_acc,
    incoming_ref,
    tail_ref,
    part_ref,
    dqbuf,
):
    core = pos[0]
    rows, channels = q.shape
    width = channels // 2
    poles = rates.shape[0]
    tokens = delta.shape[1]
    steps = tokens // SUBS
    chips = slots.shape[0]
    own, other = halves(core, width)
    mine = pl.multiple_of(core * rows, rows)
    theirs = pl.multiple_of((1 - core) * rows, rows)
    scale = 1.0 / math.sqrt(HEAD)

    incoming = slots_in[0].astype(F32)
    for j in range(1, chips):
        incoming = incoming + slots_in[j].astype(F32)
    incoming_ref[...] = incoming

    for lane_group in range(width // LANES):
        gain = skip[:, pl.ds(own + lane_group * LANES, LANES)]
        for j in range(steps):
            at = pl.ds(j, SUBS, stride=steps)
            adj32[lane_group, at, :] = gain * delta[lane_group, at, :]

    def adjoint_group(first_pole, lane_group, first_lane):
        rate = rates[pl.ds(first_pole, GROUP), pl.ds(own + first_lane, LANES)]
        lam = rows3(jnp.exp(-rate))
        mixing = rows3(
            residues[pl.ds(first_pole, GROUP), pl.ds(own + first_lane, LANES)] * pole_weights(rate)
        )
        lane_at = pl.ds(first_lane, LANES)
        state = entering_later(
            totals[pl.ds(first_pole, GROUP), :, lane_at],
            incoming_ref[pl.ds(first_pole, GROUP), lane_at],
            rows3(jnp.exp(-rate * steps)),
        )
        for j in reversed(range(steps)):
            at = pl.ds(j, SUBS, stride=steps)
            state = lam * state + delta[lane_group, at, :][None]
            adj32[lane_group, at, :] = adj32[lane_group, at, :] + jnp.sum(mixing * state, axis=0)

    each_group(poles, width, adjoint_group)
    adj16[...] = adj32[...].astype(BF16)

    qbuf[pl.ds(mine, rows), :] = q[:, pl.ds(own, width)]
    qbuf[pl.ds(theirs, rows), :] = given[2]
    for slot, buf in ((0, kbuf), (1, vbuf)):
        buf[pl.ds(mine, rows), :] = same2[slot]
        buf[pl.ds(theirs, rows), :] = cross2[slot]
        buf[pl.ds(mine + tokens, rows), :] = same1[slot]
        buf[pl.ds(theirs + tokens, rows), :] = cross1[slot]
        buf[pl.ds(mine + 2 * tokens, rows), :] = keep_kv[slot]
        buf[pl.ds(theirs + 2 * tokens, rows), :] = given[slot]

    span = (WIN + 1) * rows
    key_ids = lax.broadcasted_iota(jnp.int32, (span, rows), 0)
    row_ids = lax.broadcasted_iota(jnp.int32, (span, rows), 1)
    allowed = (key_ids > row_ids) & (key_ids <= row_ids + WIN * rows)
    over_keys = (((0,), (0,)), ((), ()))
    over_head = (((1,), (1,)), ((), ()))
    for head in range(width // HEAD):
        at_head = slice(head * HEAD, (head + 1) * HEAD)
        for block in range(tokens // rows):
            at_rows = slice(block * rows, (block + 1) * rows)
            at_keys = slice(block * rows, block * rows + span)
            query = qbuf[at_rows, at_head]
            key = kbuf[at_keys, at_head]
            value = vbuf[at_keys, at_head]
            adjoint = adj16[head, at_rows, :]
            scores = lax.dot_general(key, query, over_head, preferred_element_type=F32) * scale
            scores = jnp.where(allowed, scores, -jnp.inf)
            raised = jnp.exp(scores - jnp.max(scores, axis=0, keepdims=True))
            probability = raised * (1.0 / jnp.sum(raised, axis=0, keepdims=True))
            rounded = probability.astype(BF16)
            attended[head, at_rows, :] = (
                lax.dot_general(rounded, value, over_keys, preferred_element_type=F32)
                .astype(BF16)
                .astype(F32)
            )
            weight = lax.dot_general(value, adjoint, over_head, preferred_element_type=F32)
            inner = jnp.sum(probability * weight, axis=0, keepdims=True)
            score_adjoint = (probability * (weight - inner) * scale).astype(BF16)
            dqbuf[at_rows, at_head] = lax.dot_general(
                score_adjoint, key, over_keys, preferred_element_type=F32
            ).astype(BF16)
            dk = jnp.dot(score_adjoint, query, preferred_element_type=F32)
            dv = jnp.dot(rounded, adjoint, preferred_element_type=F32)
            if block == 0:
                dk_acc[at_keys, at_head] = dk
                dv_acc[at_keys, at_head] = dv
            else:
                edge = span - rows
                first = slice(block * rows, block * rows + edge)
                last = slice(block * rows + edge, block * rows + span)
                dk_acc[first, at_head] = dk_acc[first, at_head] + dk[:edge]
                dv_acc[first, at_head] = dv_acc[first, at_head] + dv[:edge]
                dk_acc[last, at_head] = dk[edge:]
                dv_acc[last, at_head] = dv[edge:]

    for slot, acc in ((0, dk_acc), (1, dv_acc)):
        out_same2[slot] = acc[pl.ds(mine, rows), :].astype(BF16)
        out_cross2[slot] = acc[pl.ds(theirs, rows), :].astype(BF16)
        out_same1[slot] = acc[pl.ds(mine + tokens, rows), :].astype(BF16)
        out_cross1[slot] = acc[pl.ds(theirs + tokens, rows), :].astype(BF16)
        dkv_keep[slot] = acc[pl.ds(mine + 2 * tokens, rows), :]
        swap_out[slot] = acc[pl.ds(theirs + 2 * tokens, rows), :].astype(BF16)
    swap_out[2] = dqbuf[pl.ds(theirs, rows), :]
    dq_keep[...] = dqbuf[pl.ds(mine, rows), :]

    def tail_group(first_pole, lane_group, first_lane):
        rate = rates[pl.ds(first_pole, GROUP), pl.ds(own + first_lane, LANES)]
        pole_at = pl.ds(first_pole, GROUP)
        lane_at = pl.ds(first_lane, LANES)
        lam = rows3(jnp.exp(-rate))
        state = jnp.zeros((GROUP, SUBS, LANES), F32)
        matched = jnp.zeros((GROUP, SUBS, LANES), F32)
        for j in range(steps):
            at = pl.ds(j, SUBS, stride=steps)
            state = lam * state + attended[lane_group, at, :][None]
            matched = matched + delta[lane_group, at, :][None] * state
        tail_totals[pole_at, :, lane_at] = state
        lam_block = rows3(jnp.exp(-rate * steps))
        entering = entering_earlier(state, jnp.zeros((GROUP, LANES), F32), lam_block)
        full = state + lam_block * entering
        tail = full[:, SUBS - 1, :]
        matched = matched + lam * totals[pole_at, :, lane_at] * entering
        part = jnp.sum(matched, axis=1) + jnp.exp(-rate) * tail * incoming_ref[pole_at, lane_at]
        tail_ref[pole_at, lane_at] = tail
        part_ref[pole_at, lane_at] = pole_weights(rate) * part

    each_group(poles, width, tail_group)
    rate = rates[:, pl.ds(own, width)]
    send_slots(slots, tail_ref[...], rate, tokens, chips, lambda k: pos[1] + k)
    part = part_ref[...].astype(BF16)
    for j in range(chips):
        slots[j, poles : 2 * poles, :] = part


def gate_body(
    pos,
    cot,
    given,
    attended,
    tail_totals,
    slots_in,
    rates,
    residues,
    skip,
    gate_keep,
    gate_give,
    res_keep,
    mix32,
    arriving_ref,
):
    core = pos[0]
    rows, channels = cot.shape
    width = channels // 2
    poles = rates.shape[0]
    tokens = attended.shape[1]
    steps = tokens // SUBS
    chips = slots_in.shape[0]
    own, other = halves(core, width)
    mine = pl.multiple_of(core * rows, rows)
    theirs = pl.multiple_of((1 - core) * rows, rows)
    both = slots_in[0].astype(F32)
    for j in range(1, chips):
        both = both + slots_in[j].astype(F32)
    arriving_ref[...] = both[:poles]
    total = both[poles:]
    res_keep[...] = total
    high = total.astype(BF16)
    gate_give[rows : rows + poles, :] = high
    gate_give[rows + poles : rows + 2 * poles, :] = (total - high.astype(F32)).astype(BF16)
    for lane_group in range(width // LANES):
        gain = skip[:, pl.ds(own + lane_group * LANES, LANES)]
        for j in range(steps):
            at = pl.ds(j, SUBS, stride=steps)
            mix32[lane_group, at, :] = gain * attended[lane_group, at, :]

    def group(first_pole, lane_group, first_lane):
        rate = rates[pl.ds(first_pole, GROUP), pl.ds(own + first_lane, LANES)]
        lam = rows3(jnp.exp(-rate))
        mixing = rows3(
            residues[pl.ds(first_pole, GROUP), pl.ds(own + first_lane, LANES)] * pole_weights(rate)
        )
        lane_at = pl.ds(first_lane, LANES)
        pole_at = pl.ds(first_pole, GROUP)
        state = entering_earlier(
            tail_totals[pole_at, :, lane_at],
            arriving_ref[pole_at, lane_at],
            rows3(jnp.exp(-rate * steps)),
        )
        for j in range(steps):
            at = pl.ds(j, SUBS, stride=steps)
            state = lam * state + attended[lane_group, at, :][None]
            mix32[lane_group, at, :] = mix32[lane_group, at, :] + jnp.sum(mixing * state, axis=0)

    each_group(poles, width, group)
    for lane_group in range(width // LANES):
        lanes = slice(lane_group * LANES, (lane_group + 1) * LANES)
        at_own = pl.ds(own + lane_group * LANES, LANES)
        gate_keep[:, lanes] = (
            cot[:, at_own].astype(F32) * mix32[lane_group, pl.ds(mine, rows), :]
        ).astype(BF16)
        gate_give[0:rows, lanes] = (
            given[4, :, lanes].astype(F32) * mix32[lane_group, pl.ds(theirs, rows), :]
        ).astype(BF16)


def final_body(
    pos,
    dq_keep,
    dkv_keep,
    swap_in,
    same1,
    cross1,
    same2,
    cross2,
    gate_keep,
    gate_in,
    res_keep,
    dq,
    dk,
    dv,
    dgate,
    dres,
):
    rows, width = dq_keep.shape
    poles = res_keep.shape[0]
    own, other = halves(pos[0], width)
    for slot, out in ((0, dk), (1, dv)):
        out[:, pl.ds(own, width)] = (
            dkv_keep[slot] + same1[slot].astype(F32) + same2[slot].astype(F32)
        ).astype(BF16)
        out[:, pl.ds(other, width)] = (
            swap_in[slot].astype(F32) + cross1[slot].astype(F32) + cross2[slot].astype(F32)
        ).astype(BF16)
    dq[:, pl.ds(own, width)] = dq_keep[...]
    dq[:, pl.ds(other, width)] = swap_in[2]
    dgate[:, pl.ds(own, width)] = gate_keep[...]
    dgate[:, pl.ds(other, width)] = gate_in[0:rows, :]
    dres[:, pl.ds(own, width)] = res_keep[...]
    dres[:, pl.ds(other, width)] = gate_in[rows : rows + poles, :].astype(F32) + gate_in[
        rows + poles : rows + 2 * poles, :
    ].astype(F32)


def chip_shift(array, by, crossed):
    members = lax.axis_size("ctx")
    pairs = []
    for source in range(members):
        chip, core = source // 2, source % 2
        target = ((chip + by) % (members // 2)) * 2 + ((1 - core) if crossed else core)
        pairs.append((source, target))
    return lax.ppermute(array, "ctx", pairs)


def chip_exchange(slots):
    members = lax.axis_size("ctx")
    groups = [list(range(core, members, 2)) for core in range(2)]
    return lax.all_to_all(slots, "ctx", 0, 0, axis_index_groups=groups)


def local(queries, key_rows, value_rows, gate_values, cotangent, decay_rates, residues, skip_gain):
    rows, channels = queries.shape
    width = channels // 2
    poles = decay_rates.shape[0]
    chips = lax.axis_size("ctx") // 2
    tokens = 2 * rows
    place = lax.axis_index("ctx")
    pos = jnp.stack([place % 2, place // 2]).astype(jnp.int32)
    skip = skip_gain.reshape(1, channels)
    pair = (2, rows, width)
    keep_kv, give_kv, give_all = call(
        pack_body, [(pair, BF16), (pair, BF16), ((5, rows, width), BF16)], count=6, name="pack"
    )(pos, queries, key_rows, value_rows, gate_values, cotangent)
    given = chip_shift(give_all, 0, True)
    same1 = chip_shift(keep_kv, 1, False)
    cross1 = chip_shift(give_kv, 1, True)
    same2 = chip_shift(keep_kv, 2, False)
    cross2 = chip_shift(give_kv, 2, True)
    delta, totals, head_slots = call(
        head_body,
        [
            ((width // LANES, tokens, LANES), F32),
            ((poles, SUBS, width), F32),
            ((chips, poles, width), BF16),
        ],
        scratch=[pltpu.VMEM((poles, width), F32)],
        count=5,
        name="head_states",
    )(pos, gate_values, cotangent, given, decay_rates)
    head_in = chip_exchange(head_slots)
    span = (WIN + 2) * rows
    outs = call(
        attention_body,
        [
            ((rows, width), BF16),
            (pair, F32),
            ((3, rows, width), BF16),
            (pair, BF16),
            (pair, BF16),
            (pair, BF16),
            (pair, BF16),
            ((width // LANES, tokens, LANES), F32),
            ((poles, SUBS, width), F32),
            ((chips, 2 * poles, width), BF16),
        ],
        scratch=[
            pltpu.VMEM((tokens, width), BF16),
            pltpu.VMEM((span, width), BF16),
            pltpu.VMEM((span, width), BF16),
            pltpu.VMEM((width // LANES, tokens, LANES), F32),
            pltpu.VMEM((width // LANES, tokens, LANES), BF16),
            pltpu.VMEM((span, width), F32),
            pltpu.VMEM((span, width), F32),
            pltpu.VMEM((poles, width), F32),
            pltpu.VMEM((poles, width), F32),
            pltpu.VMEM((poles, width), F32),
            pltpu.VMEM((tokens, width), BF16),
        ],
        count=14,
        name="attention",
    )(
        pos,
        queries,
        keep_kv,
        given,
        same1,
        cross1,
        same2,
        cross2,
        delta,
        totals,
        head_in,
        decay_rates,
        residues,
        skip,
    )
    dq_keep, dkv_keep, swap_out, out_same1, out_cross1, out_same2, out_cross2 = outs[:7]
    attended, tail_totals, tail_slots = outs[7:]
    tail_in = chip_exchange(tail_slots)
    back_same1 = chip_shift(out_same1, -1, False)
    back_cross1 = chip_shift(out_cross1, -1, True)
    back_same2 = chip_shift(out_same2, -2, False)
    back_cross2 = chip_shift(out_cross2, -2, True)
    swap_in = chip_shift(swap_out, 0, True)
    gate_keep, gate_give, res_keep = call(
        gate_body,
        [
            ((rows, width), BF16),
            ((rows + 2 * poles, width), BF16),
            ((poles, width), F32),
        ],
        scratch=[pltpu.VMEM((width // LANES, tokens, LANES), F32), pltpu.VMEM((poles, width), F32)],
        count=9,
        name="gate",
    )(pos, cotangent, given, attended, tail_totals, tail_in, decay_rates, residues, skip)
    gate_in = chip_shift(gate_give, 0, True)
    full = (rows, channels)
    return tuple(
        call(
            final_body,
            [(full, BF16), (full, BF16), (full, BF16), (full, BF16), ((poles, channels), F32)],
            count=11,
            name="final",
        )(
            pos,
            dq_keep,
            dkv_keep,
            swap_in,
            back_same1,
            back_cross1,
            back_same2,
            back_cross2,
            gate_keep,
            gate_in,
            res_keep,
        )
    )


def solution(mesh):
    wide = P(("dp", "ctx"), "head")
    in_specs = (wide, wide, wide, wide, wide, P(None, "head"), P(None, "head"), P("head"))
    out_specs = (wide, wide, wide, wide, P("dp", "head"))
    return jax.shard_map(local, mesh=mesh, in_specs=in_specs, out_specs=out_specs, check_vma=False)
```

time: 589 us -> 99.5 us (0.17)
  waiting for transfers between devices: 201 us -> 19.8 us
  starting transfers between devices: 228 us -> 56.7 us
  blocking collectives: 91.9 us -> 0 us
  other arithmetic: 51.4 us -> 0.67 us
  Pallas kernels: 0 us -> 17.9 us
  matrix products: 6.17 us -> 0 us
    ppermute x40 -> x11, starting transfers between devices: 228 us -> 46.1 us  [chip_shift(): return lax.ppermute(array, 'ctx', pairs)]
    ppermute x40 -> x11, waiting for transfers between devices: 201 us -> 19.8 us  [chip_shift(): return lax.ppermute(array, 'ctx', pairs)]
    psum x1 -> x0, blocking collectives: 91.9 us -> none  [local(): residues_adjoint = lax.psum(jnp.sum(products, axis=0), 'ctx')]
    another operation x6 -> x1, other arithmetic: 43.2 us -> 0.67 us  [local(): pos = jnp.stack([place % 2, place // 2]).astype(jnp.int32)]
    pallas_call x0 -> x5, Pallas kernels: none -> 17.9 us  [the longest x1 7.87 us: local(): call(attention_body, [((rows, width), BF16), (pair, F32), ((3, rows, widt...]
    all_to_all x0 -> x2, starting transfers between devices: none -> 10.6 us  [chip_exchange(): return lax.all_to_all(slots, 'ctx', 0, 0, axis_index_groups=groups)]
    dot_general x24 -> x0, matrix products: 6.17 us -> none  [the longest x4 1.08 us: local(): jnp.einsum('re,kse->rks', adjoint_head, value_head, preferred_element_typ...]
  transfers between devices with their start and end apart: 40 -> 13, of which waited for: 35 -> 4; matrix products, arithmetic and copies ran while one was open for 3% -> 0% of each run, Pallas kernels for 0% -> 3%
where the time goes in v1:
time: 99.5 us; the launch traced here: 98.8 us
  starting transfers between devices  56.7 us (57%)
  waiting for transfers between devices  19.8 us (20%)
  Pallas kernels  17.9 us (18%)
  local copies, waits for them, and re-layouts  2.79 us (3%)
    ppermute x11, starting transfers between devices, chip_shift(): return lax.ppermute(array, 'ctx', pairs)  46.1 us
    ppermute x11, waiting for transfers between devices, chip_shift(): return lax.ppermute(array, 'ctx', pairs)  19.8 us
    all_to_all x2, starting transfers between devices, chip_exchange(): return lax.all_to_all(slots, 'ctx', 0, 0, axis_index_groups=groups)  10.6 us
    pallas_call x1, Pallas kernels, local(): call(attention_body, [((rows, width), BF16), (pair, F32), ((3, rows, widt...  7.87 us
    pallas_call x1, Pallas kernels, local(): call(gate_body, [((rows, width), BF16), ((rows + 2 * poles, width), BF16)...  3.27 us
    unnamed x32, local copies, waits for them, and re-layouts  2.79 us
    pallas_call x1, Pallas kernels, local(): call(head_body, [((width // LANES, tokens, LANES), F32), ((poles, SUBS, w...  2.63 us
    pallas_call x1, Pallas kernels, local(): call(final_body, [(full, BF16), (full, BF16), (full, BF16), (full, BF16),...  2.11 us
  transfers between devices with their start and end apart: 13, of which 4 were waited for; matrix products, arithmetic and copies ran while one was open for 0% of the time, Pallas kernels for 3%

profile of v1, /device:TPU:1, one launch (start us, length us, event | category | flops | bytes accessed | tf_op | source)
XLA Modules:
  0.0 98.8 jit_solution(4359008762684532534)
XLA Ops:
  0.6 0.7 pad_add_fusion.pos
  1.3 2.0 %pack.1 = (bf16[2,128,256]{2,1,0:T(8,128)(2,1)}, bf16[2,128,256]{2,1,0:T(8,128)(2,1)}, bf16[5,128,256]{2,1,0:T(8,128)(2,1)}) custom-call(s32[2]{0:T(128)} %pad_add_fusion.pos, bf16[128,512]{1,0:T(8,128)(2,1)} %q.3, bf16[128,512]{1,0:T(8,128)(2,1)} %k.1, bf16[128,512]{1,0:T(8,128)(2,1)} %v.1, bf16[128,512]{1,0:T(8,128)(2,1)} %gate.4, bf16[128,512]{1,0:T(8,128)(2,1)} %cot.5), custom_call_target="tpu_custom_call" | custom-call | tf_op jit(solution)/shard_map/pack/pallas_call | solution.py:455
  3.3 8.8 %collective-permute-start = (bf16[5,128,256]{2,1,0:T(8,128)(2,1)}, bf16[5,128,256]{2,1,0:T(8,128)(2,1)S(1)}, u32[]{:S(2)}, u32[]{:S(2)}) collective-permute-start(bf16[5,128,256]{2,1,0:T(8,128)(2,1)} %get-tuple-element.25), channel_id=1, source_target_pairs={{0,32},{32,0},{64,96},{96,64},{128,160},{160,128},{192,224},{224,1... | collective-permute-start | bytes 983048 | tf_op jit(solution)/shard_map/ppermute | solution.py:436
  12.1 1.4 %collective-permute-done.given = bf16[5,128,256]{2,1,0:T(8,128)(2,1)S(1)} collective-permute-done((bf16[5,128,256]{2,1,0:T(8,128)(2,1)}, bf16[5,128,256]{2,1,0:T(8,128)(2,1)S(1)}, u32[]{:S(2)}, u32[]{:S(2)}) %collective-permute-start) | collective-permute-done | bytes 327712 | tf_op jit(solution)/shard_map/ppermute | solution.py:436
  13.6 0.7 copy-done
  14.3 2.6 %head_states.1 = (f32[2,256,128]{2,1,0:T(8,128)}, f32[16,8,256]{2,1,0:T(8,128)}, bf16[8,16,256]{2,1,0:T(8,128)(2,1)}) custom-call(s32[2]{0:T(128)} %pad_add_fusion.pos, bf16[128,512]{1,0:T(8,128)(2,1)} %gate.4, bf16[128,512]{1,0:T(8,128)(2,1)} %cot.5, bf16[5,128,256]{2,1,0:T(8,128)(2,1)} %copy-done, f32[16,512]{1,0:T(8,128)} %rates.5), custom_call_target="tpu_custom_call" | custom-call | tf_op jit(solution)/shard_map/head_states/pallas_call | solution.py:463
  16.9 7.0 %all-to-all-start = ((bf16[8,16,256]{2,1,0:T(8,128)(2,1)}), bf16[8,16,256]{2,1,0:T(8,128)(2,1)S(1)}, u32[]{:S(2)}, u32[]{:S(2)}) async-start(bf16[8,16,256]{2,1,0:T(8,128)(2,1)} %get-tuple-element.29), calls=%async_computation | async-start | bytes 131072 | tf_op jit(solution)/shard_map/all_to_all | solution.py:442
  23.9 5.1 %collective-permute-start.4 = (bf16[2,128,256]{2,1,0:T(8,128)(2,1)S(1)}, bf16[2,128,256]{2,1,0:T(8,128)(2,1)S(1)}, u32[]{:S(2)}, u32[]{:S(2)}) collective-permute-start(bf16[2,128,256]{2,1,0:T(8,128)(2,1)S(1)} %copy-done.15), channel_id=1, source_target_pairs={{0,160},{32,128},{64,224},{96,192},{128,288},{160,256},{192,352},{... | collective-permute-start | bytes 393224 | tf_op jit(solution)/shard_map/ppermute | solution.py:436
  29.0 2.6 %collective-permute-start.2 = (bf16[2,128,256]{2,1,0:T(8,128)(2,1)S(1)}, bf16[2,128,256]{2,1,0:T(8,128)(2,1)S(1)}, u32[]{:S(2)}, u32[]{:S(2)}) collective-permute-start(bf16[2,128,256]{2,1,0:T(8,128)(2,1)S(1)} %copy-done.15), channel_id=1, source_target_pairs={{0,96},{32,64},{64,160},{96,128},{128,224},{160,192},{192,288},{22... | collective-permute-start | bytes 393224 | tf_op jit(solution)/shard_map/ppermute | solution.py:436
  31.6 5.2 %collective-permute-start.3 = (bf16[2,128,256]{2,1,0:T(8,128)(2,1)S(1)}, bf16[2,128,256]{2,1,0:T(8,128)(2,1)S(1)}, u32[]{:S(2)}, u32[]{:S(2)}) collective-permute-start(bf16[2,128,256]{2,1,0:T(8,128)(2,1)S(1)} %copy-done.5), channel_id=1, source_target_pairs={{0,128},{32,160},{64,192},{96,224},{128,256},{160,288},{192,320},{... | collective-permute-start | bytes 393224 | tf_op jit(solution)/shard_map/ppermute | solution.py:436
  36.8 3.1 %collective-permute-start.1 = (bf16[2,128,256]{2,1,0:T(8,128)(2,1)S(1)}, bf16[2,128,256]{2,1,0:T(8,128)(2,1)S(1)}, u32[]{:S(2)}, u32[]{:S(2)}) collective-permute-start(bf16[2,128,256]{2,1,0:T(8,128)(2,1)S(1)} %copy-done.5), channel_id=1, source_target_pairs={{0,64},{32,96},{64,128},{96,160},{128,192},{160,224},{192,256},{22... | collective-permute-start | bytes 393224 | tf_op jit(solution)/shard_map/ppermute | solution.py:436
  39.9 3.6 %collective-permute-done.4.cross2 = bf16[2,128,256]{2,1,0:T(8,128)(2,1)S(1)} collective-permute-done((bf16[2,128,256]{2,1,0:T(8,128)(2,1)S(1)}, bf16[2,128,256]{2,1,0:T(8,128)(2,1)S(1)}, u32[]{:S(2)}, u32[]{:S(2)}) %collective-permute-start.4) | collective-permute-done | bytes 131104 | tf_op jit(solution)/shard_map/ppermute | solution.py:436
  43.5 8.4 %collective-permute-done.3.same2 = bf16[2,128,256]{2,1,0:T(8,128)(2,1)S(1)} collective-permute-done((bf16[2,128,256]{2,1,0:T(8,128)(2,1)S(1)}, bf16[2,128,256]{2,1,0:T(8,128)(2,1)S(1)}, u32[]{:S(2)}, u32[]{:S(2)}) %collective-permute-start.3) | collective-permute-done | bytes 131104 | tf_op jit(solution)/shard_map/ppermute | solution.py:436
  51.9 0.6 copy-done.11
  52.5 0.0 copy-done.12
  52.6 0.0 copy-done.2
  52.6 7.9 %attention.1 = (bf16[128,256]{1,0:T(8,128)(2,1)}, f32[2,128,256]{2,1,0:T(8,128)}, bf16[3,128,256]{2,1,0:T(8,128)(2,1)}, bf16[2,128,256]{2,1,0:T(8,128)(2,1)}, bf...) custom-call(s32[2]{0:T(128)} %pad_add_fusion.pos, ...), custom_call_target="tpu_custom_call" | custom-call | tf_op jit(solution)/shard_map/attention/pallas_call | solution.py:476
  60.4 3.6 %all-to-all-start.1 = ((bf16[8,32,256]{2,1,0:T(8,128)(2,1)}), bf16[8,32,256]{2,1,0:T(8,128)(2,1)S(1)}, u32[]{:S(2)}, u32[]{:S(2)}) async-start(bf16[8,32,256]{2,1,0:T(8,128)(2,1)} %get-tuple-element.39), calls=%async_computation.1 | async-start | bytes 262144 | tf_op jit(solution)/shard_map/all_to_all | solution.py:442
  64.0 10.0 %collective-permute-start.6 = (bf16[2,128,256]{2,1,0:T(8,128)(2,1)}, bf16[2,128,256]{2,1,0:T(8,128)(2,1)S(1)}, u32[]{:S(2)}, u32[]{:S(2)}) collective-permute-start(bf16[2,128,256]{2,1,0:T(8,128)(2,1)} %get-tuple-element.33), channel_id=1, source_target_pairs={{0,448},{32,480},{64,0},{96,32},{128,64},{160,96},{192,128},{224,1... | collective-permute-start | bytes 393224 | tf_op jit(solution)/shard_map/ppermute | solution.py:436
  74.0 3.1 %collective-permute-start.5 = (bf16[3,128,256]{2,1,0:T(8,128)(2,1)S(1)}, bf16[3,128,256]{2,1,0:T(8,128)(2,1)S(1)}, u32[]{:S(2)}, u32[]{:S(2)}) collective-permute-start(bf16[3,128,256]{2,1,0:T(8,128)(2,1)S(1)} %copy-done.14), channel_id=1, source_target_pairs={{0,32},{32,0},{64,96},{96,64},{128,160},{160,128},{192,224},{224,1... | collective-permute-start | bytes 589832 | tf_op jit(solution)/shard_map/ppermute | solution.py:436
  77.2 2.1 %collective-permute-start.7 = (bf16[2,128,256]{2,1,0:T(8,128)(2,1)}, bf16[2,128,256]{2,1,0:T(8,128)(2,1)S(1)}, u32[]{:S(2)}, u32[]{:S(2)}) collective-permute-start(bf16[2,128,256]{2,1,0:T(8,128)(2,1)} %get-tuple-element.34), channel_id=1, source_target_pairs={{0,480},{32,448},{64,32},{96,0},{128,96},{160,64},{192,160},{224,1... | collective-permute-start | bytes 393224 | tf_op jit(solution)/shard_map/ppermute | solution.py:436
  79.3 1.9 %collective-permute-start.8 = (bf16[2,128,256]{2,1,0:T(8,128)(2,1)}, bf16[2,128,256]{2,1,0:T(8,128)(2,1)S(1)}, u32[]{:S(2)}, u32[]{:S(2)}) collective-permute-start(bf16[2,128,256]{2,1,0:T(8,128)(2,1)} %get-tuple-element.35), channel_id=1, source_target_pairs={{0,384},{32,416},{64,448},{96,480},{128,0},{160,32},{192,64},{224,... | collective-permute-start | bytes 393224 | tf_op jit(solution)/shard_map/ppermute | solution.py:436
  81.2 2.2 %collective-permute-start.9 = (bf16[2,128,256]{2,1,0:T(8,128)(2,1)}, bf16[2,128,256]{2,1,0:T(8,128)(2,1)S(1)}, u32[]{:S(2)}, u32[]{:S(2)}) collective-permute-start(bf16[2,128,256]{2,1,0:T(8,128)(2,1)} %get-tuple-element.36), channel_id=1, source_target_pairs={{0,416},{32,384},{64,480},{96,448},{128,32},{160,0},{192,96},{224,... | collective-permute-start | bytes 393224 | tf_op jit(solution)/shard_map/ppermute | solution.py:436
  83.4 0.0 copy-start.1
  83.4 0.6 copy-done.1
  84.1 3.3 %gate.5 = (bf16[128,256]{1,0:T(8,128)(2,1)}, bf16[160,256]{1,0:T(8,128)(2,1)}, f32[16,256]{1,0:T(8,128)}) custom-call(s32[2]{0:T(128)} %pad_add_fusion.pos, bf16[128,512]{1,0:T(8,128)(2,1)} %cot.5, bf16[5,128,256]{2,1,0:T(8,128)(2,1)} %copy-done, f32[2,256,128]{2,1,0:T(8,128)} %get-tuple-element.37.attended, f32[16,8,256]{2,1,0:T(8,128)} %get-tuple-element.38.tail_totals, ...), custom_call_target="tpu_custom_call" | custom-call | tf_op jit(solution)/shard_map/gate/pallas_call | solution.py:529
  87.4 2.1 %collective-permute-start.10 = (bf16[160,256]{1,0:T(8,128)(2,1)}, bf16[160,256]{1,0:T(8,128)(2,1)S(1)}, u32[]{:S(2)}, u32[]{:S(2)}) collective-permute-start(bf16[160,256]{1,0:T(8,128)(2,1)} %get-tuple-element.41), channel_id=1, source_target_pairs={{0,32},{32,0},{64,96},{96,64},{128,160},{160,128},{192,224},{224,1... | collective-permute-start | bytes 245768 | tf_op jit(solution)/shard_map/ppermute | solution.py:436
  89.5 6.4 %collective-permute-done.9.cross2 = bf16[2,128,256]{2,1,0:T(8,128)(2,1)S(1)} collective-permute-done((bf16[2,128,256]{2,1,0:T(8,128)(2,1)}, bf16[2,128,256]{2,1,0:T(8,128)(2,1)S(1)}, u32[]{:S(2)}, u32[]{:S(2)}) %collective-permute-start.9) | collective-permute-done | bytes 131104 | tf_op jit(solution)/shard_map/ppermute | solution.py:436
  96.0 0.6 copy-done.8
  96.6 0.1 copy-done.3
  96.6 0.0 copy-done.13
  96.7 2.1 %final.1 = (bf16[128,512]{1,0:T(8,128)(2,1)}, bf16[128,512]{1,0:T(8,128)(2,1)}, bf16[128,512]{1,0:T(8,128)(2,1)}, bf16[128,512]{1,0:T(8,128)(2,1)}, f32[16,512]{1,0:T(8,128)}) custom-call(s32[2]{0:T(128)} %pad_add_fusion.pos, bf16[128,256]{1,0:T(8,128)(2,1)} %get-tuple-element.30.dq_keep, f32[2,128,256]{2,1,0:T(8,128)} %get-tuple-element.31.dkv_keep, ...), custom_call_target="tpu_custom_call" | custom-call | tf_op jit(solution)/shard_map/final/pallas_call | solution.py:543
  (32 shorter events, 0.1 us)
Async XLA Ops:
  3.3 10.2 %collective-permute-start = (bf16[5,128,256]{2,1,0:T(8,128)(2,1)}, bf16[5,128,256]{2,1,0:T(8,128)(2,1)S(1)}, u32[]{:S(2)}, u32[]{:S(2)}) collective-permute-start(bf16[5,128,256]{2,1,0:T(8,128)(2,1)} %get-tuple-element.25), channel_id=1, source_target_pairs={{0,32},{32,0},{64,96},{96,64},{128,160},{160,128},{192,224},{224,1... | collective-permute-start | bytes 983048 | tf_op jit(solution)/shard_map/ppermute | solution.py:436
  13.6 0.7 copy-start
  14.3 9.6 %copy-start.15 = (bf16[2,128,256]{2,1,0:T(8,128)(2,1)S(1)}, bf16[2,128,256]{2,1,0:T(8,128)(2,1)}, u32[]{:S(2)}) copy-start(bf16[2,128,256]{2,1,0:T(8,128)(2,1)} %get-tuple-element.26) | copy-start | bytes 393220
  16.9 14.7 %copy-start.5 = (bf16[2,128,256]{2,1,0:T(8,128)(2,1)S(1)}, bf16[2,128,256]{2,1,0:T(8,128)(2,1)}, u32[]{:S(2)}) copy-start(bf16[2,128,256]{2,1,0:T(8,128)(2,1)} %get-tuple-element.24.keep_kv) | copy-start | bytes 393220
  16.9 34.9 %all-to-all-start = ((bf16[8,16,256]{2,1,0:T(8,128)(2,1)}), bf16[8,16,256]{2,1,0:T(8,128)(2,1)S(1)}, u32[]{:S(2)}, u32[]{:S(2)}) async-start(bf16[8,16,256]{2,1,0:T(8,128)(2,1)} %get-tuple-element.29), calls=%async_computation | async-start | bytes 131072 | tf_op jit(solution)/shard_map/all_to_all | solution.py:442
  23.9 19.5 %collective-permute-start.4 = (bf16[2,128,256]{2,1,0:T(8,128)(2,1)S(1)}, bf16[2,128,256]{2,1,0:T(8,128)(2,1)S(1)}, u32[]{:S(2)}, u32[]{:S(2)}) collective-permute-start(bf16[2,128,256]{2,1,0:T(8,128)(2,1)S(1)} %copy-done.15), channel_id=1, source_target_pairs={{0,160},{32,128},{64,224},{96,192},{128,288},{160,256},{192,352},{... | collective-permute-start | bytes 393224 | tf_op jit(solution)/shard_map/ppermute | solution.py:436
  29.0 14.5 %collective-permute-start.2 = (bf16[2,128,256]{2,1,0:T(8,128)(2,1)S(1)}, bf16[2,128,256]{2,1,0:T(8,128)(2,1)S(1)}, u32[]{:S(2)}, u32[]{:S(2)}) collective-permute-start(bf16[2,128,256]{2,1,0:T(8,128)(2,1)S(1)} %copy-done.15), channel_id=1, source_target_pairs={{0,96},{32,64},{64,160},{96,128},{128,224},{160,192},{192,288},{22... | collective-permute-start | bytes 393224 | tf_op jit(solution)/shard_map/ppermute | solution.py:436
  31.6 20.3 %collective-permute-start.3 = (bf16[2,128,256]{2,1,0:T(8,128)(2,1)S(1)}, bf16[2,128,256]{2,1,0:T(8,128)(2,1)S(1)}, u32[]{:S(2)}, u32[]{:S(2)}) collective-permute-start(bf16[2,128,256]{2,1,0:T(8,128)(2,1)S(1)} %copy-done.5), channel_id=1, source_target_pairs={{0,128},{32,160},{64,192},{96,224},{128,256},{160,288},{192,320},{... | collective-permute-start | bytes 393224 | tf_op jit(solution)/shard_map/ppermute | solution.py:436
  36.8 15.1 %collective-permute-start.1 = (bf16[2,128,256]{2,1,0:T(8,128)(2,1)S(1)}, bf16[2,128,256]{2,1,0:T(8,128)(2,1)S(1)}, u32[]{:S(2)}, u32[]{:S(2)}) collective-permute-start(bf16[2,128,256]{2,1,0:T(8,128)(2,1)S(1)} %copy-done.5), channel_id=1, source_target_pairs={{0,64},{32,96},{64,128},{96,160},{128,192},{160,224},{192,256},{22... | collective-permute-start | bytes 393224 | tf_op jit(solution)/shard_map/ppermute | solution.py:436
  43.5 8.4 %copy-start.9 = (bf16[2,128,256]{2,1,0:T(8,128)(2,1)}, bf16[2,128,256]{2,1,0:T(8,128)(2,1)S(1)}, u32[]{:S(2)}) copy-start(bf16[2,128,256]{2,1,0:T(8,128)(2,1)S(1)} %collective-permute-done.4.cross2) | copy-start | bytes 393220
  43.5 8.4 %copy-start.10 = (bf16[2,128,256]{2,1,0:T(8,128)(2,1)}, bf16[2,128,256]{2,1,0:T(8,128)(2,1)S(1)}, u32[]{:S(2)}) copy-start(bf16[2,128,256]{2,1,0:T(8,128)(2,1)S(1)} %collective-permute-done.2.cross1) | copy-start | bytes 393220
  51.9 0.7 copy-start.11
  51.9 0.7 copy-start.12
  51.9 0.7 copy-start.2
  60.4 13.6 %copy-start.14 = (bf16[3,128,256]{2,1,0:T(8,128)(2,1)S(1)}, bf16[3,128,256]{2,1,0:T(8,128)(2,1)}, u32[]{:S(2)}) copy-start(bf16[3,128,256]{2,1,0:T(8,128)(2,1)} %get-tuple-element.32) | copy-start | bytes 589828
  60.4 23.0 %all-to-all-start.1 = ((bf16[8,32,256]{2,1,0:T(8,128)(2,1)}), bf16[8,32,256]{2,1,0:T(8,128)(2,1)S(1)}, u32[]{:S(2)}, u32[]{:S(2)}) async-start(bf16[8,32,256]{2,1,0:T(8,128)(2,1)} %get-tuple-element.39), calls=%async_computation.1 | async-start | bytes 262144 | tf_op jit(solution)/shard_map/all_to_all | solution.py:442
  64.0 23.3 %collective-permute-start.6 = (bf16[2,128,256]{2,1,0:T(8,128)(2,1)}, bf16[2,128,256]{2,1,0:T(8,128)(2,1)S(1)}, u32[]{:S(2)}, u32[]{:S(2)}) collective-permute-start(bf16[2,128,256]{2,1,0:T(8,128)(2,1)} %get-tuple-element.33), channel_id=1, source_target_pairs={{0,448},{32,480},{64,0},{96,32},{128,64},{160,96},{192,128},{224,1... | collective-permute-start | bytes 393224 | tf_op jit(solution)/shard_map/ppermute | solution.py:436
  74.0 21.9 %collective-permute-start.5 = (bf16[3,128,256]{2,1,0:T(8,128)(2,1)S(1)}, bf16[3,128,256]{2,1,0:T(8,128)(2,1)S(1)}, u32[]{:S(2)}, u32[]{:S(2)}) collective-permute-start(bf16[3,128,256]{2,1,0:T(8,128)(2,1)S(1)} %copy-done.14), channel_id=1, source_target_pairs={{0,32},{32,0},{64,96},{96,64},{128,160},{160,128},{192,224},{224,1... | collective-permute-start | bytes 589832 | tf_op jit(solution)/shard_map/ppermute | solution.py:436
  77.2 12.3 %collective-permute-start.7 = (bf16[2,128,256]{2,1,0:T(8,128)(2,1)}, bf16[2,128,256]{2,1,0:T(8,128)(2,1)S(1)}, u32[]{:S(2)}, u32[]{:S(2)}) collective-permute-start(bf16[2,128,256]{2,1,0:T(8,128)(2,1)} %get-tuple-element.34), channel_id=1, source_target_pairs={{0,480},{32,448},{64,32},{96,0},{128,96},{160,64},{192,160},{224,1... | collective-permute-start | bytes 393224 | tf_op jit(solution)/shard_map/ppermute | solution.py:436
  79.3 10.2 %collective-permute-start.8 = (bf16[2,128,256]{2,1,0:T(8,128)(2,1)}, bf16[2,128,256]{2,1,0:T(8,128)(2,1)S(1)}, u32[]{:S(2)}, u32[]{:S(2)}) collective-permute-start(bf16[2,128,256]{2,1,0:T(8,128)(2,1)} %get-tuple-element.35), channel_id=1, source_target_pairs={{0,384},{32,416},{64,448},{96,480},{128,0},{160,32},{192,64},{224,... | collective-permute-start | bytes 393224 | tf_op jit(solution)/shard_map/ppermute | solution.py:436
  81.2 14.7 %collective-permute-start.9 = (bf16[2,128,256]{2,1,0:T(8,128)(2,1)}, bf16[2,128,256]{2,1,0:T(8,128)(2,1)S(1)}, u32[]{:S(2)}, u32[]{:S(2)}) collective-permute-start(bf16[2,128,256]{2,1,0:T(8,128)(2,1)} %get-tuple-element.36), channel_id=1, source_target_pairs={{0,416},{32,384},{64,480},{96,448},{128,32},{160,0},{192,96},{224,... | collective-permute-start | bytes 393224 | tf_op jit(solution)/shard_map/ppermute | solution.py:436
  83.4 0.7 copy-start.1
  87.4 8.6 %copy-start.4 = (bf16[2,128,256]{2,1,0:T(8,128)(2,1)}, bf16[2,128,256]{2,1,0:T(8,128)(2,1)S(1)}, u32[]{:S(2)}) copy-start(bf16[2,128,256]{2,1,0:T(8,128)(2,1)S(1)} %collective-permute-done.6.same1) | copy-start | bytes 393220
  87.4 8.6 %collective-permute-start.10 = (bf16[160,256]{1,0:T(8,128)(2,1)}, bf16[160,256]{1,0:T(8,128)(2,1)S(1)}, u32[]{:S(2)}, u32[]{:S(2)}) collective-permute-start(bf16[160,256]{1,0:T(8,128)(2,1)} %get-tuple-element.41), channel_id=1, source_target_pairs={{0,32},{32,0},{64,96},{96,64},{128,160},{160,128},{192,224},{224,1... | collective-permute-start | bytes 245768 | tf_op jit(solution)/shard_map/ppermute | solution.py:436
  89.5 6.5 %copy-start.6 = (bf16[2,128,256]{2,1,0:T(8,128)(2,1)}, bf16[2,128,256]{2,1,0:T(8,128)(2,1)S(1)}, u32[]{:S(2)}) copy-start(bf16[2,128,256]{2,1,0:T(8,128)(2,1)S(1)} %collective-permute-done.7.cross1) | copy-start | bytes 393220
  89.5 6.4 %copy-start.7 = (bf16[2,128,256]{2,1,0:T(8,128)(2,1)}, bf16[2,128,256]{2,1,0:T(8,128)(2,1)S(1)}, u32[]{:S(2)}) copy-start(bf16[2,128,256]{2,1,0:T(8,128)(2,1)S(1)} %collective-permute-done.8.same2) | copy-start | bytes 393220
  95.9 0.7 copy-start.8
  95.9 0.7 copy-start.3
  95.9 0.7 copy-start.13

commit v2 on v1

--- a/solution.py
+++ b/solution.py
@@ -16,17 +16,30 @@
 BF16 = jnp.bfloat16
 
 
-def call(body, outs, scratch=(), in_specs=None, count=0, name=None):
-    specs = [pl.BlockSpec(memory_space=pltpu.SMEM)]
-    specs += [pl.BlockSpec(memory_space=pltpu.VMEM)] * (count - 1)
-    return pl.pallas_call(
-        body,
-        out_shape=[jax.ShapeDtypeStruct(s, d) for s, d in outs],
-        in_specs=specs,
-        out_specs=[pl.BlockSpec(memory_space=pltpu.VMEM)] * len(outs),
-        scratch_shapes=list(scratch),
-        name=name,
-    )
+def call(body, outs, scratch=(), near=(), name=None):
+    def run(*args):
+        args = [
+            pltpu.with_memory_space_constraint(a, pltpu.VMEM) if n in near else a
+            for n, a in enumerate(args)
+        ]
+        return pl.pallas_call(
+            body,
+            out_shape=[
+                pltpu.VMEM(s, d) if local_out else jax.ShapeDtypeStruct(s, d) for s, d, local_out in outs
+            ],
+            in_specs=[pl.BlockSpec(memory_space=pltpu.VMEM)] * len(args),
+            out_specs=[pl.BlockSpec(memory_space=pltpu.VMEM)] * len(outs),
+            scratch_shapes=list(scratch),
+            compiler_params=pltpu.CompilerParams(vmem_limit_bytes=8 * 1024 * 1024),
+            name=name,
+        )(*args)
+
+    return run
+
+
+def place():
+    index = lax.axis_index("ctx")
+    return lax.rem(index, 2), lax.div(index, 2)
 
 
 def halves(core, width):
@@ -35,17 +48,19 @@
     return own, other
 
 
-def pack_body(pos, q, k, v, gate, cot, keep_kv, give_kv, give_all):
+def pack_kv_body(k, v, keep_kv, give_kv):
+    width = k.shape[1] // 2
+    own, other = halves(place()[0], width)
+    for slot, array in ((0, k), (1, v)):
+        keep_kv[slot] = array[:, pl.ds(own, width)]
+        give_kv[slot] = array[:, pl.ds(other, width)]
+
+
+def pack_body(give_kv, q, gate, cot, give_all):
     width = q.shape[1] // 2
-    own, other = halves(pos[0], width)
-    keep_kv[0] = k[:, pl.ds(own, width)]
-    keep_kv[1] = v[:, pl.ds(own, width)]
-    k_give = k[:, pl.ds(other, width)]
-    v_give = v[:, pl.ds(other, width)]
-    give_kv[0] = k_give
-    give_kv[1] = v_give
-    give_all[0] = k_give
-    give_all[1] = v_give
+    own, other = halves(place()[0], width)
+    give_all[0] = give_kv[0]
+    give_all[1] = give_kv[1]
     give_all[2] = q[:, pl.ds(other, width)]
     give_all[3] = gate[:, pl.ds(other, width)]
     give_all[4] = cot[:, pl.ds(other, width)]
@@ -69,16 +84,17 @@
     lax.fori_loop(0, pole_groups * lane_groups, step, 0)
 
 
-def head_body(pos, gate, cot, given, rates, delta, totals, slots, head_ref):
+def head_body(gate, cot, given, rates, delta, totals, slots, head_ref):
     rows, channels = gate.shape
     width = channels // 2
     poles = rates.shape[0]
     chips = slots.shape[0]
-    own, other = halves(pos[0], width)
+    core, chip = place()
+    own, other = halves(core, width)
     tokens = delta.shape[1]
     steps = tokens // SUBS
-    mine = pl.multiple_of(pos[0] * rows, rows)
-    theirs = pl.multiple_of((1 - pos[0]) * rows, rows)
+    mine = pl.multiple_of(core * rows, rows)
+    theirs = pl.multiple_of((1 - core) * rows, rows)
     for lane_group in range(width // LANES):
         lanes = slice(lane_group * LANES, (lane_group + 1) * LANES)
         at_own = pl.ds(own + lane_group * LANES, LANES)
@@ -100,7 +116,7 @@
 
     each_group(poles, width, group)
     rate = rates[:, pl.ds(own, width)]
-    send_slots(slots, head_ref[...], rate, tokens, chips, lambda k: pos[1] - k)
+    send_slots(slots, head_ref[...], rate, tokens, chips, lambda k: chip - k)
 
 
 def send_slots(slots, state, rate, tokens, chips, place):
@@ -143,55 +159,14 @@
     return jnp.sqrt(2.0 * tangent / (1.0 + tangent))
 
 
-def attention_body(
-    pos,
-    q,
-    keep_kv,
-    given,
-    same1,
-    cross1,
-    same2,
-    cross2,
-    delta,
-    totals,
-    slots_in,
-    rates,
-    residues,
-    skip,
-    dq_keep,
-    dkv_keep,
-    swap_out,
-    out_same1,
-    out_cross1,
-    out_same2,
-    out_cross2,
-    attended,
-    tail_totals,
-    slots,
-    qbuf,
-    kbuf,
-    vbuf,
-    adj32,
-    adj16,
-    dk_acc,
-    dv_acc,
-    incoming_ref,
-    tail_ref,
-    part_ref,
-    dqbuf,
-):
-    core = pos[0]
-    rows, channels = q.shape
-    width = channels // 2
+def adjoint_body(delta, totals, slots_in, rates, residues, skip, adj16, incoming_ref, adj32):
+    width = delta.shape[0] * LANES
     poles = rates.shape[0]
     tokens = delta.shape[1]
     steps = tokens // SUBS
-    chips = slots.shape[0]
+    chips = slots_in.shape[0]
+    core, chip = place()
     own, other = halves(core, width)
-    mine = pl.multiple_of(core * rows, rows)
-    theirs = pl.multiple_of((1 - core) * rows, rows)
-    scale = 1.0 / math.sqrt(HEAD)
-
     incoming = slots_in[0].astype(F32)
     for j in range(1, chips):
         incoming = incoming + slots_in[j].astype(F32)
@@ -222,6 +197,51 @@
 
     each_group(poles, width, adjoint_group)
     adj16[...] = adj32[...].astype(BF16)
+
+
+def attention_body(
+    q,
+    keep_kv,
+    given,
+    same1,
+    cross1,
+    same2,
+    cross2,
+    delta,
+    totals,
+    adj16,
+    incoming_ref,
+    rates,
+    dq_keep,
+    dkv_keep,
+    swap_out,
+    out_same1,
+    out_cross1,
+    out_same2,
+    out_cross2,
+    attended,
+    tail_totals,
+    slots,
+    qbuf,
+    kbuf,
+    vbuf,
+    dk_acc,
+    dv_acc,
+    tail_ref,
+    part_ref,
+    dqbuf,
+):
+    core, chip = place()
+    rows, channels = q.shape
+    width = channels // 2
+    poles = rates.shape[0]
+    tokens = delta.shape[1]
+    steps = tokens // SUBS
+    chips = slots.shape[0]
+    own, other = halves(core, width)
+    mine = pl.multiple_of(core * rows, rows)
+    theirs = pl.multiple_of((1 - core) * rows, rows)
+    scale = 1.0 / math.sqrt(HEAD)
 
     qbuf[pl.ds(mine, rows), :] = q[:, pl.ds(own, width)]
     qbuf[pl.ds(theirs, rows), :] = given[2]
@@ -311,15 +331,13 @@
 
     each_group(poles, width, tail_group)
     rate = rates[:, pl.ds(own, width)]
-    send_slots(slots, tail_ref[...], rate, tokens, chips, lambda k: pos[1] + k)
+    send_slots(slots, tail_ref[...], rate, tokens, chips, lambda k: chip + k)
     part = part_ref[...].astype(BF16)
     for j in range(chips):
         slots[j, poles : 2 * poles, :] = part
 
 
-def gate_body(
-    pos,
-    cot,
+def gate_body(cot,
     given,
     attended,
     tail_totals,
@@ -333,7 +351,7 @@
     mix32,
     arriving_ref,
 ):
-    core = pos[0]
+    core, chip = place()
     rows, channels = cot.shape
     width = channels // 2
     poles = rates.shape[0]
@@ -388,9 +406,7 @@
         ).astype(BF16)
 
 
-def final_body(
-    pos,
-    dq_keep,
+def final_body(dq_keep,
     dkv_keep,
     swap_in,
     same1,
@@ -408,7 +424,7 @@
 ):
     rows, width = dq_keep.shape
     poles = res_keep.shape[0]
-    own, other = halves(pos[0], width)
+    own, other = halves(place()[0], width)
     for slot, out in ((0, dk), (1, dv)):
         out[:, pl.ds(own, width)] = (
             dkv_keep[slot] + same1[slot].astype(F32) + same2[slot].astype(F32)
@@ -448,62 +464,65 @@
     poles = decay_rates.shape[0]
     chips = lax.axis_size("ctx") // 2
     tokens = 2 * rows
-    place = lax.axis_index("ctx")
-    pos = jnp.stack([place % 2, place // 2]).astype(jnp.int32)
     skip = skip_gain.reshape(1, channels)
+    groups = width // LANES
     pair = (2, rows, width)
-    keep_kv, give_kv, give_all = call(
-        pack_body, [(pair, BF16), (pair, BF16), ((5, rows, width), BF16)], count=6, name="pack"
-    )(pos, queries, key_rows, value_rows, gate_values, cotangent)
-    given = chip_shift(give_all, 0, True)
+    split = (groups, tokens, LANES)
+    states = (poles, SUBS, width)
+    span = (WIN + 2) * rows
+    keep_kv, give_kv = call(pack_kv_body, [(pair, BF16, True), (pair, BF16, True)], name="pack_kv")(
+        key_rows, value_rows
+    )
+    (give_all,) = call(pack_body, [((5, rows, width), BF16, True)], near=(0,), name="pack")(
+        give_kv, queries, gate_values, cotangent
+    )
+    same2 = chip_shift(keep_kv, 2, False)
+    cross2 = chip_shift(give_kv, 2, True)
     same1 = chip_shift(keep_kv, 1, False)
     cross1 = chip_shift(give_kv, 1, True)
-    same2 = chip_shift(keep_kv, 2, False)
-    cross2 = chip_shift(give_kv, 2, True)
+    given = chip_shift(give_all, 0, True)
     delta, totals, head_slots = call(
         head_body,
-        [
-            ((width // LANES, tokens, LANES), F32),
-            ((poles, SUBS, width), F32),
-            ((chips, poles, width), BF16),
-        ],
+        [(split, F32, True), (states, F32, True), ((chips, poles, width), BF16, True)],
         scratch=[pltpu.VMEM((poles, width), F32)],
-        count=5,
+        near=(2,),
         name="head_states",
-    )(pos, gate_values, cotangent, given, decay_rates)
+    )(gate_values, cotangent, given, decay_rates)
     head_in = chip_exchange(head_slots)
-    span = (WIN + 2) * rows
+    adjoint, incoming = call(
+        adjoint_body,
+        [(split, BF16, True), ((poles, width), F32, True)],
+        scratch=[pltpu.VMEM(split, F32)],
+        near=(0, 1, 2),
+        name="adjoint",
+    )(delta, totals, head_in, decay_rates, residues, skip)
     outs = call(
         attention_body,
         [
-            ((rows, width), BF16),
-            (pair, F32),
-            ((3, rows, width), BF16),
-            (pair, BF16),
-            (pair, BF16),
-            (pair, BF16),
-            (pair, BF16),
-            ((width // LANES, tokens, LANES), F32),
-            ((poles, SUBS, width), F32),
-            ((chips, 2 * poles, width), BF16),
+            ((rows, width), BF16, True),
+            (pair, F32, True),
+            ((3, rows, width), BF16, True),
+            (pair, BF16, True),
+            (pair, BF16, True),
+            (pair, BF16, True),
+            (pair, BF16, True),
+            (split, F32, True),
+            (states, F32, True),
+            ((chips, 2 * poles, width), BF16, True),
         ],
         scratch=[
             pltpu.VMEM((tokens, width), BF16),
             pltpu.VMEM((span, width), BF16),
             pltpu.VMEM((span, width), BF16),
-            pltpu.VMEM((width // LANES, tokens, LANES), F32),
-            pltpu.VMEM((width // LANES, tokens, LANES), BF16),
             pltpu.VMEM((span, width), F32),
             pltpu.VMEM((span, width), F32),
             pltpu.VMEM((poles, width), F32),
             pltpu.VMEM((poles, width), F32),
-            pltpu.VMEM((poles, width), F32),
             pltpu.VMEM((tokens, width), BF16),
         ],
-        count=14,
+        near=tuple(range(1, 11)),
         name="attention",
     )(
-        pos,
         queries,
         keep_kv,
         given,
@@ -513,40 +532,39 @@
         cross2,
         delta,
         totals,
-        head_in,
+        adjoint,
+        incoming,
         decay_rates,
-        residues,
-        skip,
     )
     dq_keep, dkv_keep, swap_out, out_same1, out_cross1, out_same2, out_cross2 = outs[:7]
     attended, tail_totals, tail_slots = outs[7:]
-    tail_in = chip_exchange(tail_slots)
+    back_same2 = chip_shift(out_same2, -2, False)
+    back_cross2 = chip_shift(out_cross2, -2, True)
     back_same1 = chip_shift(out_same1, -1, False)
     back_cross1 = chip_shift(out_cross1, -1, True)
-    back_same2 = chip_shift(out_same2, -2, False)
-    back_cross2 = chip_shift(out_cross2, -2, True)
+    tail_in = chip_exchange(tail_slots)
     swap_in = chip_shift(swap_out, 0, True)
     gate_keep, gate_give, res_keep = call(
         gate_body,
         [
-            ((rows, width), BF16),
-            ((rows + 2 * poles, width), BF16),
-            ((poles, width), F32),
+            ((rows, width), BF16, True),
+            ((rows + 2 * poles, width), BF16, True),
+            ((poles, width), F32, True),
         ],
-        scratch=[pltpu.VMEM((width // LANES, tokens, LANES), F32), pltpu.VMEM((poles, width), F32)],
-        count=9,
+        scratch=[pltpu.VMEM(split, F32), pltpu.VMEM((poles, width), F32)],
+        near=(1, 2, 3, 4),
         name="gate",
-    )(pos, cotangent, given, attended, tail_totals, tail_in, decay_rates, residues, skip)
+    )(cotangent, given, attended, tail_totals, tail_in, decay_rates, residues, skip)
     gate_in = chip_shift(gate_give, 0, True)
     full = (rows, channels)
+    wide = (full, BF16, False)
     return tuple(
         call(
             final_body,
-            [(full, BF16), (full, BF16), (full, BF16), (full, BF16), ((poles, channels), F32)],
-            count=11,
+            [wide, wide, wide, wide, ((poles, channels), F32, False)],
+            near=tuple(range(10)),
             name="final",
         )(
-            pos,
             dq_keep,
             dkv_keep,
             swap_in,

time: 99.5 us -> 90.7 us (0.912)
  Pallas kernels: 17.9 us -> 9.79 us
    pallas_call x5 -> x7, Pallas kernels: 17.9 us -> 9.79 us  [run(): pl.pallas_call(body, out_shape=[pltpu.VMEM(s, d) if local_out else jax.Sh...]
    unnamed x32 -> x18, local copies, waits for them, and re-layouts: 2.79 us -> 3.43 us
  transfers between devices with their start and end apart: 13 -> 13, of which waited for: 4 -> 5; matrix products, arithmetic and copies ran while one was open for 0% -> 0% of each run, Pallas kernels for 3% -> 3%
where the time goes in v2:
time: 90.7 us; the launch traced here: 89.9 us
  starting transfers between devices  56.2 us (62%)
  waiting for transfers between devices  19.7 us (22%)
  Pallas kernels  9.79 us (11%)
  local copies, waits for them, and re-layouts  3.43 us (4%)
    ppermute x11, starting transfers between devices, chip_shift(): return lax.ppermute(array, 'ctx', pairs)  45.8 us
    ppermute x11, waiting for transfers between devices, chip_shift(): return lax.ppermute(array, 'ctx', pairs)  19.7 us
    all_to_all x2, starting transfers between devices, chip_exchange(): return lax.all_to_all(slots, 'ctx', 0, 0, axis_index_groups=groups)  10.4 us
    pallas_call x7, Pallas kernels, run(): pl.pallas_call(body, out_shape=[pltpu.VMEM(s, d) if local_out else jax.Sh...  9.79 us
    unnamed x18, local copies, waits for them, and re-layouts  3.43 us
  transfers between devices with their start and end apart: 13, of which 5 were waited for; matrix products, arithmetic and copies ran while one was open for 0% of the time, Pallas kernels for 3%

profile of v2, /device:TPU:1, one launch (start us, length us, event | category | flops | bytes accessed | tf_op | source)
XLA Modules:
  0.0 89.9 jit_solution(9660168127084902630)
XLA Ops:
  0.7 0.9 %copy-done.6 = bf16[128,512]{1,0:T(8,128)(2,1)S(1)} copy-done((bf16[128,512]{1,0:T(8,128)(2,1)S(1)}, bf16[128,512]{1,0:T(8,128)(2,1)}, u32[]{:S(2)}) %copy-start.6) | copy-done | bytes 131096
  1.6 0.9 %copy-done.7 = bf16[128,512]{1,0:T(8,128)(2,1)S(1)} copy-done((bf16[128,512]{1,0:T(8,128)(2,1)S(1)}, bf16[128,512]{1,0:T(8,128)(2,1)}, u32[]{:S(2)}) %copy-start.7) | copy-done | bytes 131096
  2.5 0.0 copy-start.3
  2.6 0.9 copy-done.3
  3.5 8.8 %collective-permute-start = (bf16[5,128,256]{2,1,0:T(8,128)(2,1)S(1)}, bf16[5,128,256]{2,1,0:T(8,128)(2,1)S(1)}, u32[]{:S(2)}, u32[]{:S(2)}) collective-permute-start(bf16[5,128,256]{2,1,0:T(8,128)(2,1)S(1)} %pack.1), channel_id=1, source_target_pairs={{0,32},{32,0},{64,96},{96,64},{128,160},{160,128},{192,224},{224,1... | collective-permute-start | bytes 983048 | tf_op jit(solution)/shard_map/ppermute | solution.py:452
  12.3 1.2 %collective-permute-done.given = bf16[5,128,256]{2,1,0:T(8,128)(2,1)S(1)} collective-permute-done((bf16[5,128,256]{2,1,0:T(8,128)(2,1)S(1)}, bf16[5,128,256]{2,1,0:T(8,128)(2,1)S(1)}, u32[]{:S(2)}, u32[]{:S(2)}) %collective-permute-start) | collective-permute-done | bytes 327712 | tf_op jit(solution)/shard_map/ppermute | solution.py:452
  13.5 1.4 %head_states.1 = (f32[2,256,128]{2,1,0:T(8,128)S(1)}, f32[16,8,256]{2,1,0:T(8,128)S(1)}, bf16[8,16,256]{2,1,0:T(8,128)(2,1)}) custom-call(bf16[128,512]{1,0:T(8,128)(2,1)S(1)} %copy-done.2, bf16[128,512]{1,0:T(8,128)(2,1)S(1)} %copy-done, bf16[5,128,256]{2,1,0:T(8,128)(2,1)S(1)} %collective-permute-done.given, f32[16,512]{1,0:T(8,128)S(1)} %copy-done.1), custom_call_target="tpu_custom_call" | custom-call | tf_op jit(solution)/shard_map/head_states/pallas_call | solution.py:25
  14.9 7.0 %all-to-all-start = ((bf16[8,16,256]{2,1,0:T(8,128)(2,1)}), bf16[8,16,256]{2,1,0:T(8,128)(2,1)S(1)}, u32[]{:S(2)}, u32[]{:S(2)}) async-start(bf16[8,16,256]{2,1,0:T(8,128)(2,1)} %get-tuple-element.29), calls=%async_computation | async-start | bytes 131072 | tf_op jit(solution)/shard_map/all_to_all | solution.py:458
  21.9 4.3 %collective-permute-start.3 = (bf16[2,128,256]{2,1,0:T(8,128)(2,1)S(1)}, bf16[2,128,256]{2,1,0:T(8,128)(2,1)S(1)}, u32[]{:S(2)}, u32[]{:S(2)}) collective-permute-start(bf16[2,128,256]{2,1,0:T(8,128)(2,1)S(1)} %get-tuple-element.25.keep_kv), channel_id=1, source_target_pairs={{0,128},{32,160},{64,192},{96,224},{128,256},{160,288},{192,320},{... | collective-permute-start | bytes 393224 | tf_op jit(solution)/shard_map/ppermute | solution.py:452
  26.2 3.1 %collective-permute-start.1 = (bf16[2,128,256]{2,1,0:T(8,128)(2,1)S(1)}, bf16[2,128,256]{2,1,0:T(8,128)(2,1)S(1)}, u32[]{:S(2)}, u32[]{:S(2)}) collective-permute-start(bf16[2,128,256]{2,1,0:T(8,128)(2,1)S(1)} %get-tuple-element.25.keep_kv), channel_id=1, source_target_pairs={{0,64},{32,96},{64,128},{96,160},{128,192},{160,224},{192,256},{22... | collective-permute-start | bytes 393224 | tf_op jit(solution)/shard_map/ppermute | solution.py:452
  29.3 6.6 %collective-permute-start.4 = (bf16[2,128,256]{2,1,0:T(8,128)(2,1)S(1)}, bf16[2,128,256]{2,1,0:T(8,128)(2,1)S(1)}, u32[]{:S(2)}, u32[]{:S(2)}) collective-permute-start(bf16[2,128,256]{2,1,0:T(8,128)(2,1)S(1)} %get-tuple-element.26.give_kv), channel_id=1, source_target_pairs={{0,160},{32,128},{64,224},{96,192},{128,288},{160,256},{192,352},{... | collective-permute-start | bytes 393224 | tf_op jit(solution)/shard_map/ppermute | solution.py:452
  35.9 2.0 %collective-permute-start.2 = (bf16[2,128,256]{2,1,0:T(8,128)(2,1)S(1)}, bf16[2,128,256]{2,1,0:T(8,128)(2,1)S(1)}, u32[]{:S(2)}, u32[]{:S(2)}) collective-permute-start(bf16[2,128,256]{2,1,0:T(8,128)(2,1)S(1)} %get-tuple-element.26.give_kv), channel_id=1, source_target_pairs={{0,96},{32,64},{64,160},{96,128},{128,224},{160,192},{192,288},{22... | collective-permute-start | bytes 393224 | tf_op jit(solution)/shard_map/ppermute | solution.py:452
  37.9 0.0 all-to-all-done.slots_in
  37.9 0.0 copy-start.8
  37.9 0.7 copy-done.8
  38.5 1.4 %adjoint.1 = (bf16[2,256,128]{2,1,0:T(8,128)(2,1)S(1)}, f32[16,256]{1,0:T(8,128)S(1)}) custom-call(f32[2,256,128]{2,1,0:T(8,128)S(1)} %get-tuple-element.27.delta, f32[16,8,256]{2,1,0:T(8,128)S(1)} %get-tuple-element.28.totals, bf16[8,16,256]{2,1,0:T(8,128)(2,1)S(1)} %all-to-all-done.slots_in, f32[16,512]{1,0:T(8,128)S(1)} %copy-done.1, ...), custom_call_target="tpu_custom_call" | custom-call | tf_op jit(solution)/shard_map/adjoint/pallas_call | solution.py:25
  39.9 1.2 %collective-permute-done.3.same2 = bf16[2,128,256]{2,1,0:T(8,128)(2,1)S(1)} collective-permute-done((bf16[2,128,256]{2,1,0:T(8,128)(2,1)S(1)}, bf16[2,128,256]{2,1,0:T(8,128)(2,1)S(1)}, u32[]{:S(2)}, u32[]{:S(2)}) %collective-permute-start.3) | collective-permute-done | bytes 131104 | tf_op jit(solution)/shard_map/ppermute | solution.py:452
  41.2 0.0 collective-permute-done.1.same1
  41.2 8.5 %collective-permute-done.4.cross2 = bf16[2,128,256]{2,1,0:T(8,128)(2,1)S(1)} collective-permute-done((bf16[2,128,256]{2,1,0:T(8,128)(2,1)S(1)}, bf16[2,128,256]{2,1,0:T(8,128)(2,1)S(1)}, u32[]{:S(2)}, u32[]{:S(2)}) %collective-permute-start.4) | collective-permute-done | bytes 131104 | tf_op jit(solution)/shard_map/ppermute | solution.py:452
  49.6 4.8 %attention.1 = (bf16[128,256]{1,0:T(8,128)(2,1)S(1)}, f32[2,128,256]{2,1,0:T(8,128)S(1)}, bf16[3,128,256]{2,1,0:T(8,128)(2,1)S(1)}, bf16[2,128,256]{2,1,0:T(8,12...) custom-call(bf16[128,512]{1,0:T(8,128)(2,1)S(1)} %copy-done.4, ...), custom_call_target="tpu_custom_call" | custom-call | tf_op jit(solution)/shard_map/attention/pallas_call | solution.py:25
  54.4 3.4 %all-to-all-start.1 = ((bf16[8,32,256]{2,1,0:T(8,128)(2,1)}), bf16[8,32,256]{2,1,0:T(8,128)(2,1)S(1)}, u32[]{:S(2)}, u32[]{:S(2)}) async-start(bf16[8,32,256]{2,1,0:T(8,128)(2,1)} %get-tuple-element.41), calls=%async_computation.1 | async-start | bytes 262144 | tf_op jit(solution)/shard_map/all_to_all | solution.py:458
  57.8 9.9 %collective-permute-start.6 = (bf16[2,128,256]{2,1,0:T(8,128)(2,1)S(1)}, bf16[2,128,256]{2,1,0:T(8,128)(2,1)S(1)}, u32[]{:S(2)}, u32[]{:S(2)}) collective-permute-start(bf16[2,128,256]{2,1,0:T(8,128)(2,1)S(1)} %get-tuple-element.35), channel_id=1, source_target_pairs={{0,448},{32,480},{64,0},{96,32},{128,64},{160,96},{192,128},{224,1... | collective-permute-start | bytes 393224 | tf_op jit(solution)/shard_map/ppermute | solution.py:452
  67.7 2.8 %collective-permute-start.5 = (bf16[3,128,256]{2,1,0:T(8,128)(2,1)S(1)}, bf16[3,128,256]{2,1,0:T(8,128)(2,1)S(1)}, u32[]{:S(2)}, u32[]{:S(2)}) collective-permute-start(bf16[3,128,256]{2,1,0:T(8,128)(2,1)S(1)} %get-tuple-element.34), channel_id=1, source_target_pairs={{0,32},{32,0},{64,96},{96,64},{128,160},{160,128},{192,224},{224,1... | collective-permute-start | bytes 589832 | tf_op jit(solution)/shard_map/ppermute | solution.py:452
  70.5 2.1 %collective-permute-start.7 = (bf16[2,128,256]{2,1,0:T(8,128)(2,1)S(1)}, bf16[2,128,256]{2,1,0:T(8,128)(2,1)S(1)}, u32[]{:S(2)}, u32[]{:S(2)}) collective-permute-start(bf16[2,128,256]{2,1,0:T(8,128)(2,1)S(1)} %get-tuple-element.36), channel_id=1, source_target_pairs={{0,480},{32,448},{64,32},{96,0},{128,96},{160,64},{192,160},{224,1... | collective-permute-start | bytes 393224 | tf_op jit(solution)/shard_map/ppermute | solution.py:452
  72.6 1.9 %collective-permute-start.8 = (bf16[2,128,256]{2,1,0:T(8,128)(2,1)S(1)}, bf16[2,128,256]{2,1,0:T(8,128)(2,1)S(1)}, u32[]{:S(2)}, u32[]{:S(2)}) collective-permute-start(bf16[2,128,256]{2,1,0:T(8,128)(2,1)S(1)} %get-tuple-element.37), channel_id=1, source_target_pairs={{0,384},{32,416},{64,448},{96,480},{128,0},{160,32},{192,64},{224,... | collective-permute-start | bytes 393224 | tf_op jit(solution)/shard_map/ppermute | solution.py:452
  74.6 2.2 %collective-permute-start.9 = (bf16[2,128,256]{2,1,0:T(8,128)(2,1)S(1)}, bf16[2,128,256]{2,1,0:T(8,128)(2,1)S(1)}, u32[]{:S(2)}, u32[]{:S(2)}) collective-permute-start(bf16[2,128,256]{2,1,0:T(8,128)(2,1)S(1)} %get-tuple-element.38), channel_id=1, source_target_pairs={{0,416},{32,384},{64,480},{96,448},{128,32},{160,0},{192,96},{224,... | collective-permute-start | bytes 393224 | tf_op jit(solution)/shard_map/ppermute | solution.py:452
  76.8 1.4 %gate.5 = (bf16[128,256]{1,0:T(8,128)(2,1)S(1)}, bf16[160,256]{1,0:T(8,128)(2,1)S(1)}, f32[16,256]{1,0:T(8,128)S(1)}) custom-call(bf16[128,512]{1,0:T(8,128)(2,1)S(1)} %copy-done, bf16[5,128,256]{2,1,0:T(8,128)(2,1)S(1)} %collective-permute-done.given, f32[2,256,128]{2,1,0:T(8,128)S(1)} %get-tuple-element.39.attended, ...), custom_call_target="tpu_custom_call" | custom-call | tf_op jit(solution)/shard_map/gate/pallas_call | solution.py:25
  78.2 0.0 collective-permute-done.6.same1
  78.2 2.1 %collective-permute-start.10 = (bf16[160,256]{1,0:T(8,128)(2,1)S(1)}, bf16[160,256]{1,0:T(8,128)(2,1)S(1)}, u32[]{:S(2)}, u32[]{:S(2)}) collective-permute-start(bf16[160,256]{1,0:T(8,128)(2,1)S(1)} %get-tuple-element.43), channel_id=1, source_target_pairs={{0,32},{32,0},{64,96},{96,64},{128,160},{160,128},{192,224},{224,1... | collective-permute-start | bytes 245768 | tf_op jit(solution)/shard_map/ppermute | solution.py:452
  80.3 0.8 collective-permute-done.8.same2
  81.1 7.9 %collective-permute-done.9.cross2 = bf16[2,128,256]{2,1,0:T(8,128)(2,1)S(1)} collective-permute-done((bf16[2,128,256]{2,1,0:T(8,128)(2,1)S(1)}, bf16[2,128,256]{2,1,0:T(8,128)(2,1)S(1)}, u32[]{:S(2)}, u32[]{:S(2)}) %collective-permute-start.9) | collective-permute-done | bytes 131104 | tf_op jit(solution)/shard_map/ppermute | solution.py:452
  89.1 0.9 final.1
  (19 shorter events, 0.1 us)
Async XLA Ops:
  0.6 1.9 %copy-start = (bf16[128,512]{1,0:T(8,128)(2,1)S(1)}, bf16[128,512]{1,0:T(8,128)(2,1)}, u32[]{:S(2)}) copy-start(bf16[128,512]{1,0:T(8,128)(2,1)} %cot.5) | copy-start | bytes 393220
  0.6 1.9 %copy-start.2 = (bf16[128,512]{1,0:T(8,128)(2,1)S(1)}, bf16[128,512]{1,0:T(8,128)(2,1)}, u32[]{:S(2)}) copy-start(bf16[128,512]{1,0:T(8,128)(2,1)} %gate.4) | copy-start | bytes 393220
  0.7 0.9 %copy-start.6 = (bf16[128,512]{1,0:T(8,128)(2,1)S(1)}, bf16[128,512]{1,0:T(8,128)(2,1)}, u32[]{:S(2)}) copy-start(bf16[128,512]{1,0:T(8,128)(2,1)} %k.1) | copy-start | bytes 393220
  1.6 0.9 %copy-start.7 = (bf16[128,512]{1,0:T(8,128)(2,1)S(1)}, bf16[128,512]{1,0:T(8,128)(2,1)}, u32[]{:S(2)}) copy-start(bf16[128,512]{1,0:T(8,128)(2,1)} %v.1) | copy-start | bytes 393220
  2.5 0.9 %copy-start.3 = (bf16[128,512]{1,0:T(8,128)(2,1)S(1)}, bf16[128,512]{1,0:T(8,128)(2,1)}, u32[]{:S(2)}) copy-start(bf16[128,512]{1,0:T(8,128)(2,1)} %q.3) | copy-start | bytes 393220
  3.5 10.1 %copy-start.1 = (f32[16,512]{1,0:T(8,128)S(1)}, f32[16,512]{1,0:T(8,128)}, u32[]{:S(2)}) copy-start(f32[16,512]{1,0:T(8,128)} %rates.7) | copy-start | bytes 98308
  3.5 10.0 %collective-permute-start = (bf16[5,128,256]{2,1,0:T(8,128)(2,1)S(1)}, bf16[5,128,256]{2,1,0:T(8,128)(2,1)S(1)}, u32[]{:S(2)}, u32[]{:S(2)}) collective-permute-start(bf16[5,128,256]{2,1,0:T(8,128)(2,1)S(1)} %pack.1), channel_id=1, source_target_pairs={{0,32},{32,0},{64,96},{96,64},{128,160},{160,128},{192,224},{224,1... | collective-permute-start | bytes 983048 | tf_op jit(solution)/shard_map/ppermute | solution.py:452
  14.9 23.0 %copy-start.5 = (f32[16,512]{1,0:T(8,128)S(1)}, f32[16,512]{1,0:T(8,128)}, u32[]{:S(2)}) copy-start(f32[16,512]{1,0:T(8,128)} %residues.3) | copy-start | bytes 98308
  14.9 23.0 %all-to-all-start = ((bf16[8,16,256]{2,1,0:T(8,128)(2,1)}), bf16[8,16,256]{2,1,0:T(8,128)(2,1)S(1)}, u32[]{:S(2)}, u32[]{:S(2)}) async-start(bf16[8,16,256]{2,1,0:T(8,128)(2,1)} %get-tuple-element.29), calls=%async_computation | async-start | bytes 131072 | tf_op jit(solution)/shard_map/all_to_all | solution.py:458
  21.9 19.3 %collective-permute-start.3 = (bf16[2,128,256]{2,1,0:T(8,128)(2,1)S(1)}, bf16[2,128,256]{2,1,0:T(8,128)(2,1)S(1)}, u32[]{:S(2)}, u32[]{:S(2)}) collective-permute-start(bf16[2,128,256]{2,1,0:T(8,128)(2,1)S(1)} %get-tuple-element.25.keep_kv), channel_id=1, source_target_pairs={{0,128},{32,160},{64,192},{96,224},{128,256},{160,288},{192,320},{... | collective-permute-start | bytes 393224 | tf_op jit(solution)/shard_map/ppermute | solution.py:452
  26.2 15.0 %collective-permute-start.1 = (bf16[2,128,256]{2,1,0:T(8,128)(2,1)S(1)}, bf16[2,128,256]{2,1,0:T(8,128)(2,1)S(1)}, u32[]{:S(2)}, u32[]{:S(2)}) collective-permute-start(bf16[2,128,256]{2,1,0:T(8,128)(2,1)S(1)} %get-tuple-element.25.keep_kv), channel_id=1, source_target_pairs={{0,64},{32,96},{64,128},{96,160},{128,192},{160,224},{192,256},{22... | collective-permute-start | bytes 393224 | tf_op jit(solution)/shard_map/ppermute | solution.py:452
  29.3 20.4 %collective-permute-start.4 = (bf16[2,128,256]{2,1,0:T(8,128)(2,1)S(1)}, bf16[2,128,256]{2,1,0:T(8,128)(2,1)S(1)}, u32[]{:S(2)}, u32[]{:S(2)}) collective-permute-start(bf16[2,128,256]{2,1,0:T(8,128)(2,1)S(1)} %get-tuple-element.26.give_kv), channel_id=1, source_target_pairs={{0,160},{32,128},{64,224},{96,192},{128,288},{160,256},{192,352},{... | collective-permute-start | bytes 393224 | tf_op jit(solution)/shard_map/ppermute | solution.py:452
  35.9 13.8 %collective-permute-start.2 = (bf16[2,128,256]{2,1,0:T(8,128)(2,1)S(1)}, bf16[2,128,256]{2,1,0:T(8,128)(2,1)S(1)}, u32[]{:S(2)}, u32[]{:S(2)}) collective-permute-start(bf16[2,128,256]{2,1,0:T(8,128)(2,1)S(1)} %get-tuple-element.26.give_kv), channel_id=1, source_target_pairs={{0,96},{32,64},{64,160},{96,128},{128,224},{160,192},{192,288},{22... | collective-permute-start | bytes 393224 | tf_op jit(solution)/shard_map/ppermute | solution.py:452
  37.9 0.7 copy-start.8
  38.5 11.1 %copy-start.4 = (bf16[128,512]{1,0:T(8,128)(2,1)S(1)}, bf16[128,512]{1,0:T(8,128)(2,1)}, u32[]{:S(2)}) copy-start(bf16[128,512]{1,0:T(8,128)(2,1)} %q.3) | copy-start | bytes 393220
  54.4 22.4 %all-to-all-start.1 = ((bf16[8,32,256]{2,1,0:T(8,128)(2,1)}), bf16[8,32,256]{2,1,0:T(8,128)(2,1)S(1)}, u32[]{:S(2)}, u32[]{:S(2)}) async-start(bf16[8,32,256]{2,1,0:T(8,128)(2,1)} %get-tuple-element.41), calls=%async_computation.1 | async-start | bytes 262144 | tf_op jit(solution)/shard_map/all_to_all | solution.py:458
  57.8 20.4 %collective-permute-start.6 = (bf16[2,128,256]{2,1,0:T(8,128)(2,1)S(1)}, bf16[2,128,256]{2,1,0:T(8,128)(2,1)S(1)}, u32[]{:S(2)}, u32[]{:S(2)}) collective-permute-start(bf16[2,128,256]{2,1,0:T(8,128)(2,1)S(1)} %get-tuple-element.35), channel_id=1, source_target_pairs={{0,448},{32,480},{64,0},{96,32},{128,64},{160,96},{192,128},{224,1... | collective-permute-start | bytes 393224 | tf_op jit(solution)/shard_map/ppermute | solution.py:452
  67.7 21.4 %collective-permute-start.5 = (bf16[3,128,256]{2,1,0:T(8,128)(2,1)S(1)}, bf16[3,128,256]{2,1,0:T(8,128)(2,1)S(1)}, u32[]{:S(2)}, u32[]{:S(2)}) collective-permute-start(bf16[3,128,256]{2,1,0:T(8,128)(2,1)S(1)} %get-tuple-element.34), channel_id=1, source_target_pairs={{0,32},{32,0},{64,96},{96,64},{128,160},{160,128},{192,224},{224,1... | collective-permute-start | bytes 589832 | tf_op jit(solution)/shard_map/ppermute | solution.py:452
  70.5 9.8 %collective-permute-start.7 = (bf16[2,128,256]{2,1,0:T(8,128)(2,1)S(1)}, bf16[2,128,256]{2,1,0:T(8,128)(2,1)S(1)}, u32[]{:S(2)}, u32[]{:S(2)}) collective-permute-start(bf16[2,128,256]{2,1,0:T(8,128)(2,1)S(1)} %get-tuple-element.36), channel_id=1, source_target_pairs={{0,480},{32,448},{64,32},{96,0},{128,96},{160,64},{192,160},{224,1... | collective-permute-start | bytes 393224 | tf_op jit(solution)/shard_map/ppermute | solution.py:452
  72.6 8.5 %collective-permute-start.8 = (bf16[2,128,256]{2,1,0:T(8,128)(2,1)S(1)}, bf16[2,128,256]{2,1,0:T(8,128)(2,1)S(1)}, u32[]{:S(2)}, u32[]{:S(2)}) collective-permute-start(bf16[2,128,256]{2,1,0:T(8,128)(2,1)S(1)} %get-tuple-element.37), channel_id=1, source_target_pairs={{0,384},{32,416},{64,448},{96,480},{128,0},{160,32},{192,64},{224,... | collective-permute-start | bytes 393224 | tf_op jit(solution)/shard_map/ppermute | solution.py:452
  74.6 14.5 %collective-permute-start.9 = (bf16[2,128,256]{2,1,0:T(8,128)(2,1)S(1)}, bf16[2,128,256]{2,1,0:T(8,128)(2,1)S(1)}, u32[]{:S(2)}, u32[]{:S(2)}) collective-permute-start(bf16[2,128,256]{2,1,0:T(8,128)(2,1)S(1)} %get-tuple-element.38), channel_id=1, source_target_pairs={{0,416},{32,384},{64,480},{96,448},{128,32},{160,0},{192,96},{224,... | collective-permute-start | bytes 393224 | tf_op jit(solution)/shard_map/ppermute | solution.py:452
  78.2 10.9 %collective-permute-start.10 = (bf16[160,256]{1,0:T(8,128)(2,1)S(1)}, bf16[160,256]{1,0:T(8,128)(2,1)S(1)}, u32[]{:S(2)}, u32[]{:S(2)}) collective-permute-start(bf16[160,256]{1,0:T(8,128)(2,1)S(1)} %get-tuple-element.43), channel_id=1, source_target_pairs={{0,32},{32,0},{64,96},{96,64},{128,160},{160,128},{192,224},{224,1... | collective-permute-start | bytes 245768 | tf_op jit(solution)/shard_map/ppermute | solution.py:452

commit v3 on v2

v3 whole, which is shorter than its diff:
```python
import math

import jax
import jax.numpy as jnp
from jax import lax
from jax.experimental import pallas as pl
from jax.experimental.pallas import tpu as pltpu
from jax.sharding import PartitionSpec as P

HEAD = 128
WIN = 4
LANES = 128
SUBS = 8
GROUP = 8
FORWARD_COST = pl.CostEstimate(flops=10**11, transcendentals=0, bytes_accessed=10**8)
F32 = jnp.float32
BF16 = jnp.bfloat16
OVER_KEYS = (((0,), (0,)), ((), ()))
OVER_HEAD = (((1,), (1,)), ((), ()))


def call(body, outs, scratch=(), near=(), far=(), cost=None, name=None):
    def run(*args):
        args = list(args)
        specs = []
        for n in range(len(args)):
            space = pltpu.HBM if n in far else pltpu.VMEM
            specs.append(pl.BlockSpec(memory_space=space))
            if n in near or n in far:
                args[n] = pltpu.with_memory_space_constraint(args[n], space)
        return pl.pallas_call(
            body,
            out_shape=[
                pltpu.VMEM(s, d) if local_out else jax.ShapeDtypeStruct(s, d) for s, d, local_out in outs
            ],
            in_specs=specs,
            out_specs=[pl.BlockSpec(memory_space=pltpu.VMEM)] * len(outs),
            scratch_shapes=list(scratch),
            compiler_params=pltpu.CompilerParams(vmem_limit_bytes=8 * 1024 * 1024),
            cost_estimate=cost,
            name=name,
        )(*args)

    return run


def place():
    index = lax.axis_index("ctx")
    return lax.rem(index, 2), lax.div(index, 2)


def halves(core, width):
    own = pl.multiple_of(core * width, LANES)
    other = pl.multiple_of((1 - core) * width, LANES)
    return own, other


def pack_body(
    k, v, q, gate, cot, rates, residues, skip, keep_kv, give_kv, keep_rest, give_all, params, buf, small, sems
):
    width = k.shape[1] // 2
    poles = rates.shape[0]
    own, other = halves(place()[0], width)
    arrays = (k, v, q, gate, cot)
    copies = [pltpu.make_async_copy(a, buf.at[n], sems.at[n]) for n, a in enumerate(arrays)]
    for n, (array, first, count) in enumerate(
        ((rates, 0, poles), (residues, poles, poles), (skip, 2 * poles, 1))
    ):
        copies.append(
            pltpu.make_async_copy(array, small.at[pl.ds(first, count)], sems.at[len(arrays) + n])
        )
    for copy in copies:
        copy.start()
    for n in range(len(arrays)):
        copies[n].wait()
        give = buf[n, :, pl.ds(other, width)]
        keep = buf[n, :, pl.ds(own, width)]
        give_all[n] = give
        if n < 2:
            give_kv[n] = give
            keep_kv[n] = keep
        else:
            keep_rest[n - 2] = keep
    for copy in copies[len(arrays) :]:
        copy.wait()
    params[...] = small[0 : 2 * poles + 1, pl.ds(own, width)]


def rows3(values):
    return jnp.broadcast_to(values[:, None, :], (values.shape[0], SUBS, values.shape[1]))


def each_group(poles, width, body):
    pole_groups = poles // GROUP
    lane_groups = width // LANES

    def step(index, carry):
        lane_group = index // pole_groups
        first_lane = pl.multiple_of(lane_group * LANES, LANES)
        first_pole = pl.multiple_of((index % pole_groups) * GROUP, GROUP)
        body(first_pole, lane_group, first_lane)
        return carry

    lax.fori_loop(0, pole_groups * lane_groups, step, 0)


def head_body(keep_rest, given, params, delta, totals, slots, head_ref):
    rows, width = keep_rest.shape[1:]
    poles = totals.shape[0]
    chips = slots.shape[0]
    core, chip = place()
    own, other = halves(core, width)
    tokens = delta.shape[1]
    steps = tokens // SUBS
    mine = pl.multiple_of(core * rows, rows)
    theirs = pl.multiple_of((1 - core) * rows, rows)
    for lane_group in range(width // LANES):
        lanes = slice(lane_group * LANES, (lane_group + 1) * LANES)
        delta[lane_group, pl.ds(mine, rows), :] = keep_rest[1, :, lanes].astype(F32) * keep_rest[
            2, :, lanes
        ].astype(F32)
        delta[lane_group, pl.ds(theirs, rows), :] = given[3, :, lanes].astype(F32) * given[
            4, :, lanes
        ].astype(F32)

    def group(first_pole, lane_group, first_lane):
        rate = params[pl.ds(first_pole, GROUP), pl.ds(first_lane, LANES)]
        lam = rows3(jnp.exp(-rate))
        state = jnp.zeros((GROUP, SUBS, LANES), F32)
        for j in reversed(range(steps)):
            state = lam * state + delta[lane_group, pl.ds(j, SUBS, stride=steps), :][None]
        totals[pl.ds(first_pole, GROUP), :, pl.ds(first_lane, LANES)] = state
        block = lax.broadcasted_iota(jnp.int32, (GROUP, SUBS, LANES), 1).astype(F32)
        power = jnp.exp(-rows3(rate) * (block * steps))
        head_ref[pl.ds(first_pole, GROUP), pl.ds(first_lane, LANES)] = jnp.sum(power * state, axis=1)

    each_group(poles, width, group)
    head = head_ref[...].astype(BF16)
    for j in range(chips):
        slots[j] = head


def around(own, rate, tokens, order, out):
    decay = jnp.exp(-rate * tokens)
    value = own(order[-1])
    power = decay
    for n in reversed(order[:-1]):
        value = value + power * own(n)
        power = power * decay
    value = value / (1.0 - jnp.exp(-rate * (tokens * len(order))))
    for n in order:
        out[n] = value
        value = own(n) + decay * value


def block_ids(shape):
    return lax.broadcasted_iota(jnp.int32, shape, 1)


def entering_later(totals, incoming, lam_block):
    ids = block_ids(totals.shape)
    value = jnp.where(ids == SUBS - 1, rows3(incoming), pltpu.roll(totals, SUBS - 1, 1))
    power = lam_block
    for shift in (1, 2, 4):
        moved = pltpu.roll(value, SUBS - shift, 1)
        value = value + jnp.where(ids < SUBS - shift, power * moved, 0.0)
        power = power * power
    return value


def entering_earlier(totals, arriving, lam_block):
    ids = block_ids(totals.shape)
    value = jnp.where(ids == 0, rows3(arriving), pltpu.roll(totals, 1, 1))
    power = lam_block
    for shift in (1, 2, 4):
        moved = pltpu.roll(value, shift, 1)
        value = value + jnp.where(ids >= shift, power * moved, 0.0)
        power = power * power
    return value


def pole_weights(rate):
    tangent = jnp.tanh(rate)
    return jnp.sqrt(2.0 * tangent / (1.0 + tangent))


def assemble(core, keep_rest, keep_kv, given, same1, cross1, same2, cross2, qbuf, kbuf, vbuf):
    rows = keep_rest.shape[1]
    tokens = 2 * rows
    mine = pl.multiple_of(core * rows, rows)
    theirs = pl.multiple_of((1 - core) * rows, rows)
    qbuf[pl.ds(mine, rows), :] = keep_rest[0]
    qbuf[pl.ds(theirs, rows), :] = given[2]
    for slot, buf in ((0, kbuf), (1, vbuf)):
        buf[pl.ds(mine, rows), :] = same2[slot]
        buf[pl.ds(theirs, rows), :] = cross2[slot]
        buf[pl.ds(mine + tokens, rows), :] = same1[slot]
        buf[pl.ds(theirs + tokens, rows), :] = cross1[slot]
        buf[pl.ds(mine + 2 * tokens, rows), :] = keep_kv[slot]
        buf[pl.ds(theirs + 2 * tokens, rows), :] = given[slot]


def allowed_pairs(rows):
    span = (WIN + 1) * rows
    key_ids = lax.broadcasted_iota(jnp.int32, (span, rows), 0)
    row_ids = lax.broadcasted_iota(jnp.int32, (span, rows), 1)
    return (key_ids > row_ids) & (key_ids <= row_ids + WIN * rows)


def forward_body(
    keep_rest,
    keep_kv,
    given,
    same1,
    cross1,
    same2,
    cross2,
    delta,
    totals,
    params,
    stats,
    attended,
    tail_totals,
    slots,
    qbuf,
    kbuf,
    vbuf,
    tail_ref,
    part_ref,
):
    rows, width = keep_rest.shape[1:]
    poles = totals.shape[0]
    tokens = delta.shape[1]
    steps = tokens // SUBS
    chips = slots.shape[0]
    core, chip = place()
    scale = 1.0 / math.sqrt(HEAD)
    assemble(core, keep_rest, keep_kv, given, same1, cross1, same2, cross2, qbuf, kbuf, vbuf)
    span = (WIN + 1) * rows
    allowed = allowed_pairs(rows)
    for head in range(width // HEAD):
        at_head = slice(head * HEAD, (head + 1) * HEAD)
        for block in range(tokens // rows):
            at_rows = slice(block * rows, (block + 1) * rows)
            at_keys = slice(block * rows, block * rows + span)
            scores = (
                lax.dot_general(
                    kbuf[at_keys, at_head], qbuf[at_rows, at_head], OVER_HEAD, preferred_element_type=F32
                )
                * scale
            )
            scores = jnp.where(allowed, scores, -jnp.inf)
            top = jnp.max(scores, axis=0, keepdims=True)
            raised = jnp.exp(scores - top)
            share = 1.0 / jnp.sum(raised, axis=0, keepdims=True)
            probability = raised * share
            stats[head, block, 0:1, :] = top
            stats[head, block, 1:2, :] = share
            attended[head, at_rows, :] = (
                lax.dot_general(
                    probability.astype(BF16), vbuf[at_keys, at_head], OVER_KEYS, preferred_element_type=F32
                )
                .astype(BF16)
                .astype(F32)
            )

    def tail_group(first_pole, lane_group, first_lane):
        rate = params[pl.ds(first_pole, GROUP), pl.ds(first_lane, LANES)]
        pole_at = pl.ds(first_pole, GROUP)
        lane_at = pl.ds(first_lane, LANES)
        lam = rows3(jnp.exp(-rate))
        state = jnp.zeros((GROUP, SUBS, LANES), F32)
        matched = jnp.zeros((GROUP, SUBS, LANES), F32)
        for j in range(steps):
            at = pl.ds(j, SUBS, stride=steps)
            state = lam * state + attended[lane_group, at, :][None]
            matched = matched + delta[lane_group, at, :][None] * state
        tail_totals[pole_at, :, lane_at] = state
        lam_block = rows3(jnp.exp(-rate * steps))
        entering = entering_earlier(state, jnp.zeros((GROUP, LANES), F32), lam_block)
        full = state + lam_block * entering
        matched = matched + lam * totals[pole_at, :, lane_at] * entering
        tail_ref[pole_at, lane_at] = full[:, SUBS - 1, :]
        part_ref[pole_at, lane_at] = jnp.sum(matched, axis=1)

    each_group(poles, width, tail_group)
    tail = tail_ref[...].astype(BF16)
    part = part_ref[...].astype(BF16)
    for j in range(chips):
        slots[j, 0:poles, :] = tail
        slots[j, poles : 2 * poles, :] = part


def backward_body(
    keep_rest,
    keep_kv,
    given,
    same1,
    cross1,
    same2,
    cross2,
    stats,
    delta,
    totals,
    slots_in,
    params,
    dq_keep,
    dkv_keep,
    swap_out,
    out_same1,
    out_cross1,
    out_same2,
    out_cross2,
    incoming_all,
    qbuf,
    kbuf,
    vbuf,
    adj16,
    adj32,
    dk_acc,
    dv_acc,
    dqbuf,
):
    tokens, width = qbuf.shape
    rows = tokens // 2
    poles = totals.shape[0]
    steps = tokens // SUBS
    chips = slots_in.shape[0]
    core, chip = place()
    mine = pl.multiple_of(core * rows, rows)
    theirs = pl.multiple_of((1 - core) * rows, rows)
    scale = 1.0 / math.sqrt(HEAD)
    assemble(core, keep_rest, keep_kv, given, same1, cross1, same2, cross2, qbuf, kbuf, vbuf)

    around(
        lambda n: slots_in[n].astype(F32),
        params[0:poles, :],
        tokens,
        list(reversed(range(chips))),
        incoming_all,
    )
    for lane_group in range(width // LANES):
        gain = params[2 * poles : 2 * poles + 1, lane_group * LANES : (lane_group + 1) * LANES]
        adj32[lane_group] = gain * delta[lane_group]

    def adjoint_group(first_pole, lane_group, first_lane):
        rate = params[pl.ds(first_pole, GROUP), pl.ds(first_lane, LANES)]
        lam = rows3(jnp.exp(-rate))
        mixing = rows3(
            params[pl.ds(poles + first_pole, GROUP), pl.ds(first_lane, LANES)] * pole_weights(rate)
        )
        lane_at = pl.ds(first_lane, LANES)
        state = entering_later(
            totals[pl.ds(first_pole, GROUP), :, lane_at],
            incoming_all[chip, pl.ds(first_pole, GROUP), lane_at],
            rows3(jnp.exp(-rate * steps)),
        )
        for j in reversed(range(steps)):
            at = pl.ds(j, SUBS, stride=steps)
            state = lam * state + delta[lane_group, at, :][None]
            adj32[lane_group, at, :] = adj32[lane_group, at, :] + jnp.sum(mixing * state, axis=0)

    each_group(poles, width, adjoint_group)
    adj16[...] = adj32[...].astype(BF16)

    span = (WIN + 1) * rows
    allowed = allowed_pairs(rows)
    for head in range(width // HEAD):
        at_head = slice(head * HEAD, (head + 1) * HEAD)
        for block in range(tokens // rows):
            at_rows = slice(block * rows, (block + 1) * rows)
            at_keys = slice(block * rows, block * rows + span)
            query = qbuf[at_rows, at_head]
            key = kbuf[at_keys, at_head]
            value = vbuf[at_keys, at_head]
            adjoint = adj16[head, at_rows, :]
            scores = lax.dot_general(key, query, OVER_HEAD, preferred_element_type=F32) * scale
            scores = jnp.where(allowed, scores, -jnp.inf)
            probability = jnp.exp(scores - stats[head, block, 0:1, :]) * stats[head, block, 1:2, :]
            rounded = probability.astype(BF16)
            weight = lax.dot_general(value, adjoint, OVER_HEAD, preferred_element_type=F32)
            inner = jnp.sum(probability * weight, axis=0, keepdims=True)
            score_adjoint = (probability * (weight - inner) * scale).astype(BF16)
            dqbuf[at_rows, at_head] = lax.dot_general(
                score_adjoint, key, OVER_KEYS, preferred_element_type=F32
            ).astype(BF16)
            dk = jnp.dot(score_adjoint, query, preferred_element_type=F32)
            dv = jnp.dot(rounded, adjoint, preferred_element_type=F32)
            if block == 0:
                dk_acc[at_keys, at_head] = dk
                dv_acc[at_keys, at_head] = dv
            else:
                edge = span - rows
                first = slice(block * rows, block * rows + edge)
                last = slice(block * rows + edge, block * rows + span)
                dk_acc[first, at_head] = dk_acc[first, at_head] + dk[:edge]
                dv_acc[first, at_head] = dv_acc[first, at_head] + dv[:edge]
                dk_acc[last, at_head] = dk[edge:]
                dv_acc[last, at_head] = dv[edge:]

    for slot, acc in ((0, dk_acc), (1, dv_acc)):
        out_same2[slot] = acc[pl.ds(mine, rows), :].astype(BF16)
        out_cross2[slot] = acc[pl.ds(theirs, rows), :].astype(BF16)
        out_same1[slot] = acc[pl.ds(mine + tokens, rows), :].astype(BF16)
        out_cross1[slot] = acc[pl.ds(theirs + tokens, rows), :].astype(BF16)
        dkv_keep[slot] = acc[pl.ds(mine + 2 * tokens, rows), :]
        swap_out[slot] = acc[pl.ds(theirs + 2 * tokens, rows), :].astype(BF16)
    swap_out[2] = dqbuf[pl.ds(theirs, rows), :]
    dq_keep[...] = dqbuf[pl.ds(mine, rows), :]


def gate_body(
    keep_rest,
    given,
    attended,
    tail_totals,
    slots_in,
    incoming_all,
    params,
    gate_keep,
    gate_give,
    res_keep,
    mix32,
    arriving_ref,
):
    core, chip = place()
    rows, width = keep_rest.shape[1:]
    poles = tail_totals.shape[0]
    tokens = attended.shape[1]
    steps = tokens // SUBS
    chips = slots_in.shape[0]
    mine = pl.multiple_of(core * rows, rows)
    theirs = pl.multiple_of((1 - core) * rows, rows)
    rate = params[0:poles, :]
    around(
        lambda n: slots_in[n, 0:poles, :].astype(F32), rate, tokens, list(range(chips)), arriving_ref
    )
    parts = slots_in[0, poles : 2 * poles, :].astype(F32)
    crossed = slots_in[0, 0:poles, :].astype(F32) * incoming_all[0]
    for n in range(1, chips):
        parts = parts + slots_in[n, poles : 2 * poles, :].astype(F32)
        crossed = crossed + slots_in[n, 0:poles, :].astype(F32) * incoming_all[n]
    total = pole_weights(rate) * (parts + jnp.exp(-rate) * crossed)
    res_keep[...] = total
    high = total.astype(BF16)
    gate_give[rows : rows + poles, :] = high
    gate_give[rows + poles : rows + 2 * poles, :] = (total - high.astype(F32)).astype(BF16)
    for lane_group in range(width // LANES):
        gain = params[2 * poles : 2 * poles + 1, lane_group * LANES : (lane_group + 1) * LANES]
        mix32[lane_group] = gain * attended[lane_group]

    def group(first_pole, lane_group, first_lane):
        rate = params[pl.ds(first_pole, GROUP), pl.ds(first_lane, LANES)]
        lam = rows3(jnp.exp(-rate))
        mixing = rows3(
            params[pl.ds(poles + first_pole, GROUP), pl.ds(first_lane, LANES)] * pole_weights(rate)
        )
        lane_at = pl.ds(first_lane, LANES)
        pole_at = pl.ds(first_pole, GROUP)
        state = entering_earlier(
            tail_totals[pole_at, :, lane_at],
            arriving_ref[chip, pole_at, lane_at],
            rows3(jnp.exp(-rate * steps)),
        )
        for j in range(steps):
            at = pl.ds(j, SUBS, stride=steps)
            state = lam * state + attended[lane_group, at, :][None]
            mix32[lane_group, at, :] = mix32[lane_group, at, :] + jnp.sum(mixing * state, axis=0)

    each_group(poles, width, group)
    for lane_group in range(width // LANES):
        lanes = slice(lane_group * LANES, (lane_group + 1) * LANES)
        gate_keep[:, lanes] = (
            keep_rest[2, :, lanes].astype(F32) * mix32[lane_group, pl.ds(mine, rows), :]
        ).astype(BF16)
        gate_give[0:rows, lanes] = (
            given[4, :, lanes].astype(F32) * mix32[lane_group, pl.ds(theirs, rows), :]
        ).astype(BF16)


def final_body(dq_keep,
    dkv_keep,
    swap_in,
    same1,
    cross1,
    same2,
    cross2,
    gate_keep,
    gate_in,
    res_keep,
    dq,
    dk,
    dv,
    dgate,
    dres,
):
    rows, width = dq_keep.shape
    poles = res_keep.shape[0]
    own, other = halves(place()[0], width)
    for slot, out in ((0, dk), (1, dv)):
        out[:, pl.ds(own, width)] = (
            dkv_keep[slot] + same1[slot].astype(F32) + same2[slot].astype(F32)
        ).astype(BF16)
        out[:, pl.ds(other, width)] = (
            swap_in[slot].astype(F32) + cross1[slot].astype(F32) + cross2[slot].astype(F32)
        ).astype(BF16)
    dq[:, pl.ds(own, width)] = dq_keep[...]
    dq[:, pl.ds(other, width)] = swap_in[2]
    dgate[:, pl.ds(own, width)] = gate_keep[...]
    dgate[:, pl.ds(other, width)] = gate_in[0:rows, :]
    dres[:, pl.ds(own, width)] = res_keep[...]
    dres[:, pl.ds(other, width)] = gate_in[rows : rows + poles, :].astype(F32) + gate_in[
        rows + poles : rows + 2 * poles, :
    ].astype(F32)


def chip_shift(array, by, crossed):
    members = lax.axis_size("ctx")
    pairs = []
    for source in range(members):
        chip, core = source // 2, source % 2
        target = ((chip + by) % (members // 2)) * 2 + ((1 - core) if crossed else core)
        pairs.append((source, target))
    return lax.ppermute(array, "ctx", pairs)


def chip_exchange(slots):
    members = lax.axis_size("ctx")
    groups = [list(range(core, members, 2)) for core in range(2)]
    return lax.all_to_all(slots, "ctx", 0, 0, axis_index_groups=groups)


def local(queries, key_rows, value_rows, gate_values, cotangent, decay_rates, residues, skip_gain):
    rows, channels = queries.shape
    width = channels // 2
    poles = decay_rates.shape[0]
    chips = lax.axis_size("ctx") // 2
    tokens = 2 * rows
    skip = skip_gain.reshape(1, channels)
    groups = width // LANES
    pair = (2, rows, width)
    split = (groups, tokens, LANES)
    states = (poles, SUBS, width)
    span = (WIN + 2) * rows
    keep_kv, give_kv, keep_rest, give_all, params = call(
        pack_body,
        [
            (pair, BF16, True),
            (pair, BF16, True),
            ((3, rows, width), BF16, True),
            ((5, rows, width), BF16, True),
            ((2 * poles + 1, width), F32, True),
        ],
        scratch=[
            pltpu.VMEM((5, rows, channels), BF16),
            pltpu.VMEM((2 * poles + SUBS, channels), F32),
            pltpu.SemaphoreType.DMA((8,)),
        ],
        far=tuple(range(8)),
        name="pack",
    )(key_rows, value_rows, queries, gate_values, cotangent, decay_rates, residues, skip)
    same2 = chip_shift(keep_kv, 2, False)
    cross2 = chip_shift(give_kv, 2, True)
    same1 = chip_shift(keep_kv, 1, False)
    cross1 = chip_shift(give_kv, 1, True)
    given = chip_shift(give_all, 0, True)
    delta, totals, head_slots = call(
        head_body,
        [(split, F32, True), (states, F32, True), ((chips, poles, width), BF16, True)],
        scratch=[pltpu.VMEM((poles, width), F32)],
        near=(0, 1, 2),
        name="head_states",
    )(keep_rest, given, params)
    head_in = chip_exchange(head_slots)
    halo = (keep_rest, keep_kv, given, same1, cross1, same2, cross2)
    halo_buffers = [
        pltpu.VMEM((tokens, width), BF16),
        pltpu.VMEM((span, width), BF16),
        pltpu.VMEM((span, width), BF16),
    ]
    stats, attended, tail_totals, tail_slots = call(
        forward_body,
        [
            ((groups, 2, SUBS, rows), F32, True),
            (split, F32, True),
            (states, F32, True),
            ((chips, 2 * poles, width), BF16, True),
        ],
        scratch=halo_buffers + [pltpu.VMEM((poles, width), F32), pltpu.VMEM((poles, width), F32)],
        near=tuple(range(10)),
        cost=FORWARD_COST,
        name="forward",
    )(*halo, delta, totals, params)
    tail_in = chip_exchange(tail_slots)
    outs = call(
        backward_body,
        [
            ((rows, width), BF16, True),
            (pair, F32, True),
            ((3, rows, width), BF16, True),
            (pair, BF16, True),
            (pair, BF16, True),
            (pair, BF16, True),
            (pair, BF16, True),
            ((chips, poles, width), F32, True),
        ],
        scratch=halo_buffers
        + [
            pltpu.VMEM(split, BF16),
            pltpu.VMEM(split, F32),
            pltpu.VMEM((span, width), F32),
            pltpu.VMEM((span, width), F32),
            pltpu.VMEM((tokens, width), BF16),
        ],
        near=tuple(range(12)),
        name="backward",
    )(*halo, stats, delta, totals, head_in, params)
    dq_keep, dkv_keep, swap_out, out_same1, out_cross1, out_same2, out_cross2, incoming_all = outs
    back_same2 = chip_shift(out_same2, -2, False)
    back_cross2 = chip_shift(out_cross2, -2, True)
    back_same1 = chip_shift(out_same1, -1, False)
    back_cross1 = chip_shift(out_cross1, -1, True)
    swap_in = chip_shift(swap_out, 0, True)
    gate_keep, gate_give, res_keep = call(
        gate_body,
        [
            ((rows, width), BF16, True),
            ((rows + 2 * poles, width), BF16, True),
            ((poles, width), F32, True),
        ],
        scratch=[pltpu.VMEM(split, F32), pltpu.VMEM((chips, poles, width), F32)],
        near=tuple(range(7)),
        name="gate",
    )(keep_rest, given, attended, tail_totals, tail_in, incoming_all, params)
    gate_in = chip_shift(gate_give, 0, True)
    full = (rows, channels)
    wide = (full, BF16, False)
    return tuple(
        call(
            final_body,
            [wide, wide, wide, wide, ((poles, channels), F32, False)],
            near=tuple(range(10)),
            name="final",
        )(
            dq_keep,
            dkv_keep,
            swap_in,
            back_same1,
            back_cross1,
            back_same2,
            back_cross2,
            gate_keep,
            gate_in,
            res_keep,
        )
    )


def solution(mesh):
    wide = P(("dp", "ctx"), "head")
    in_specs = (wide, wide, wide, wide, wide, P(None, "head"), P(None, "head"), P("head"))
    out_specs = (wide, wide, wide, wide, P("dp", "head"))
    return jax.shard_map(local, mesh=mesh, in_specs=in_specs, out_specs=out_specs, check_vma=False)
```

time: 90.7 us -> 83.5 us (0.921)
  waiting for transfers between devices: 19.7 us -> 15.8 us
  local copies, waits for them, and re-layouts: 3.43 us -> 0 us
  Pallas kernels: 9.79 us -> 10.8 us
    ppermute x11, waiting for transfers between devices: 19.7 us -> 12.4 us  [chip_shift(): return lax.ppermute(array, 'ctx', pairs)]
    unnamed x18 -> x0, local copies, waits for them, and re-layouts: 3.43 us -> none
    all_to_all x2, waiting for transfers between devices: 0.01 us -> 3.36 us  [chip_exchange(): return lax.all_to_all(slots, 'ctx', 0, 0, axis_index_groups=groups)]
    ppermute x11, starting transfers between devices: 45.8 us -> 44.4 us  [chip_shift(): return lax.ppermute(array, 'ctx', pairs)]
    pallas_call x7 -> x6, Pallas kernels: 9.79 us -> 10.8 us  [run(): pl.pallas_call(body, out_shape=[pltpu.VMEM(s, d) if local_out else jax.Sh...]
  transfers between devices with their start and end apart: 13 -> 13, of which waited for: 5 -> 4; matrix products, arithmetic and copies ran while one was open for 0% -> 0% of each run, Pallas kernels for 3% -> 10%
where the time goes in v3:
time: 83.5 us; the launch traced here: 83 us
  starting transfers between devices  55.6 us (67%)
  waiting for transfers between devices  15.8 us (19%)
  Pallas kernels  10.8 us (13%)
    ppermute x11, starting transfers between devices, chip_shift(): return lax.ppermute(array, 'ctx', pairs)  44.4 us
    ppermute x11, waiting for transfers between devices, chip_shift(): return lax.ppermute(array, 'ctx', pairs)  12.4 us
    all_to_all x2, starting transfers between devices, chip_exchange(): return lax.all_to_all(slots, 'ctx', 0, 0, axis_index_groups=groups)  11.2 us
    pallas_call x6, Pallas kernels, run(): pl.pallas_call(body, out_shape=[pltpu.VMEM(s, d) if local_out else jax.Sh...  10.8 us
    all_to_all x2, waiting for transfers between devices, chip_exchange(): return lax.all_to_all(slots, 'ctx', 0, 0, axis_index_groups=groups)  3.36 us
  transfers between devices with their start and end apart: 13, of which 4 were waited for; matrix products, arithmetic and copies ran while one was open for 0% of the time, Pallas kernels for 10%

profile of v3, /device:TPU:1, one launch (start us, length us, event | category | flops | bytes accessed | tf_op | source)
XLA Modules:
  0.0 83.0 jit_solution(12519574282074329067)
XLA Ops:
  0.6 1.3 %pack.1 = (bf16[2,128,256]{2,1,0:T(8,128)(2,1)S(1)}, bf16[2,128,256]{2,1,0:T(8,128)(2,1)S(1)}, bf16[3,128,256]{2,1,0:T(8,128)(2,1)S(1)}, bf16[5,128,256]{2,1,0:T(8,128)(2,1)S(1)}, f32[33,256]{1,0:T(8,128)S(1)}) custom-call(bf16[128,512]{1,0:T(8,128)(2,1)} %k.1, bf16[128,512]{1,0:T(8,128)(2,1)} %v.1, bf16[128,512]{1,0:T(8,128)(2,1)} %q.1, ...), custom_call_target="tpu_custom_call" | custom-call | tf_op jit(solution)/shard_map/pack/pallas_call | solution.py:31
  1.9 8.8 %collective-permute-start = (bf16[5,128,256]{2,1,0:T(8,128)(2,1)S(1)}, bf16[5,128,256]{2,1,0:T(8,128)(2,1)S(1)}, u32[]{:S(2)}, u32[]{:S(2)}) collective-permute-start(bf16[5,128,256]{2,1,0:T(8,128)(2,1)S(1)} %get-tuple-element.30), channel_id=1, source_target_pairs={{0,32},{32,0},{64,96},{96,64},{128,160},{160,128},{192,224},{224,1... | collective-permute-start | bytes 983048 | tf_op jit(solution)/shard_map/ppermute | solution.py:524
  10.7 1.9 %collective-permute-start.4 = (bf16[2,128,256]{2,1,0:T(8,128)(2,1)S(1)}, bf16[2,128,256]{2,1,0:T(8,128)(2,1)S(1)}, u32[]{:S(2)}, u32[]{:S(2)}) collective-permute-start(bf16[2,128,256]{2,1,0:T(8,128)(2,1)S(1)} %get-tuple-element.31), channel_id=1, source_target_pairs={{0,160},{32,128},{64,224},{96,192},{128,288},{160,256},{192,352},{... | collective-permute-start | bytes 393224 | tf_op jit(solution)/shard_map/ppermute | solution.py:524
  12.6 1.9 %collective-permute-start.2 = (bf16[2,128,256]{2,1,0:T(8,128)(2,1)S(1)}, bf16[2,128,256]{2,1,0:T(8,128)(2,1)S(1)}, u32[]{:S(2)}, u32[]{:S(2)}) collective-permute-start(bf16[2,128,256]{2,1,0:T(8,128)(2,1)S(1)} %get-tuple-element.31), channel_id=1, source_target_pairs={{0,96},{32,64},{64,160},{96,128},{128,224},{160,192},{192,288},{22... | collective-permute-start | bytes 393224 | tf_op jit(solution)/shard_map/ppermute | solution.py:524
  14.5 5.6 %collective-permute-start.3 = (bf16[2,128,256]{2,1,0:T(8,128)(2,1)S(1)}, bf16[2,128,256]{2,1,0:T(8,128)(2,1)S(1)}, u32[]{:S(2)}, u32[]{:S(2)}) collective-permute-start(bf16[2,128,256]{2,1,0:T(8,128)(2,1)S(1)} %get-tuple-element.29.keep_kv), channel_id=1, source_target_pairs={{0,128},{32,160},{64,192},{96,224},{128,256},{160,288},{192,320},{... | collective-permute-start | bytes 393224 | tf_op jit(solution)/shard_map/ppermute | solution.py:524
  20.2 3.5 %collective-permute-start.1 = (bf16[2,128,256]{2,1,0:T(8,128)(2,1)S(1)}, bf16[2,128,256]{2,1,0:T(8,128)(2,1)S(1)}, u32[]{:S(2)}, u32[]{:S(2)}) collective-permute-start(bf16[2,128,256]{2,1,0:T(8,128)(2,1)S(1)} %get-tuple-element.29.keep_kv), channel_id=1, source_target_pairs={{0,64},{32,96},{64,128},{96,160},{128,192},{160,224},{192,256},{22... | collective-permute-start | bytes 393224 | tf_op jit(solution)/shard_map/ppermute | solution.py:524
  23.7 0.0 collective-permute-done.given
  23.7 1.3 %head_states.1 = (f32[2,256,128]{2,1,0:T(8,128)S(1)}, f32[16,8,256]{2,1,0:T(8,128)S(1)}, bf16[8,16,256]{2,1,0:T(8,128)(2,1)}) custom-call(bf16[3,128,256]{2,1,0:T(8,128)(2,1)S(1)} %get-tuple-element.28.keep_rest, bf16[5,128,256]{2,1,0:T(8,128)(2,1)S(1)} %collective-permute-done.given, f32[33,256]{1,0:T(8,128)S(1)} %get-tuple-element.32.params), custom_call_target="tpu_custom_call" | custom-call | tf_op jit(solution)/shard_map/head_states/pallas_call | solution.py:31
  25.1 7.7 %all-to-all-start = ((bf16[8,16,256]{2,1,0:T(8,128)(2,1)}), bf16[8,16,256]{2,1,0:T(8,128)(2,1)S(1)}, u32[]{:S(2)}, u32[]{:S(2)}) async-start(bf16[8,16,256]{2,1,0:T(8,128)(2,1)} %get-tuple-element.36), calls=%async_computation | async-start | bytes 131072 | tf_op jit(solution)/shard_map/all_to_all | solution.py:530
  32.8 0.0 collective-permute-done.4.cross2
  32.8 0.0 collective-permute-done.2.cross1
  32.8 3.4 %collective-permute-done.3.same2 = bf16[2,128,256]{2,1,0:T(8,128)(2,1)S(1)} collective-permute-done((bf16[2,128,256]{2,1,0:T(8,128)(2,1)S(1)}, bf16[2,128,256]{2,1,0:T(8,128)(2,1)S(1)}, u32[]{:S(2)}, u32[]{:S(2)}) %collective-permute-start.3) | collective-permute-done | bytes 131104 | tf_op jit(solution)/shard_map/ppermute | solution.py:524
  36.2 0.0 collective-permute-done.1.same1
  36.2 3.0 %forward.1 = (f32[2,2,8,128]{3,2,1,0:T(8,128)S(1)}, f32[2,256,128]{2,1,0:T(8,128)S(1)}, f32[16,8,256]{2,1,0:T(8,128)S(1)}, bf16[8,32,256]{2,1,0:T(8,128)(2,1)}) custom-call(bf16[3,128,256]{2,1,0:T(8,128)(2,1)S(1)} %get-tuple-element.28.keep_rest, bf16[2,128,256]{2,1,0:T(8,128)(2,1)S(1)} %get-tuple-element.29.keep_kv, ...), custom_call_target="tpu_custom_call" | custom-call | flops 99999997952 | bytes 100000000 | tf_op jit(solution)/shard_map/forward/pallas_call | solution.py:31
  39.2 3.4 %all-to-all-done.slots_in = bf16[8,16,256]{2,1,0:T(8,128)(2,1)S(1)} async-done(((bf16[8,16,256]{2,1,0:T(8,128)(2,1)}), bf16[8,16,256]{2,1,0:T(8,128)(2,1)S(1)}, u32[]{:S(2)}, u32[]{:S(2)}) %all-to-all-start) | async-done | bytes 65568 | tf_op jit(solution)/shard_map/all_to_all | solution.py:530
  42.6 3.5 %all-to-all-start.1 = ((bf16[8,32,256]{2,1,0:T(8,128)(2,1)}), bf16[8,32,256]{2,1,0:T(8,128)(2,1)S(1)}, u32[]{:S(2)}, u32[]{:S(2)}) async-start(bf16[8,32,256]{2,1,0:T(8,128)(2,1)} %get-tuple-element.46), calls=%async_computation.1 | async-start | bytes 262144 | tf_op jit(solution)/shard_map/all_to_all | solution.py:530
  46.1 3.2 %backward.1 = (bf16[128,256]{1,0:T(8,128)(2,1)S(1)}, f32[2,128,256]{2,1,0:T(8,128)S(1)}, bf16[3,128,256]{2,1,0:T(8,128)(2,1)S(1)}, bf16[2,128,256]{2,1,0:T(8,128...) custom-call(bf16[3,128,256]{2,1,0:T(8,128)(2,1)S(1)} %get-tuple-elem, ...), custom_call_target="tpu_custom_call" | custom-call | tf_op jit(solution)/shard_map/backward/pallas_call | solution.py:31
  49.3 10.0 %collective-permute-start.6 = (bf16[2,128,256]{2,1,0:T(8,128)(2,1)S(1)}, bf16[2,128,256]{2,1,0:T(8,128)(2,1)S(1)}, u32[]{:S(2)}, u32[]{:S(2)}) collective-permute-start(bf16[2,128,256]{2,1,0:T(8,128)(2,1)S(1)} %get-tuple-element.40), channel_id=1, source_target_pairs={{0,448},{32,480},{64,0},{96,32},{128,64},{160,96},{192,128},{224,1... | collective-permute-start | bytes 393224 | tf_op jit(solution)/shard_map/ppermute | solution.py:524
  59.3 4.3 %collective-permute-start.5 = (bf16[3,128,256]{2,1,0:T(8,128)(2,1)S(1)}, bf16[3,128,256]{2,1,0:T(8,128)(2,1)S(1)}, u32[]{:S(2)}, u32[]{:S(2)}) collective-permute-start(bf16[3,128,256]{2,1,0:T(8,128)(2,1)S(1)} %get-tuple-element.39), channel_id=1, source_target_pairs={{0,32},{32,0},{64,96},{96,64},{128,160},{160,128},{192,224},{224,1... | collective-permute-start | bytes 589832 | tf_op jit(solution)/shard_map/ppermute | solution.py:524
  63.6 2.1 %collective-permute-start.7 = (bf16[2,128,256]{2,1,0:T(8,128)(2,1)S(1)}, bf16[2,128,256]{2,1,0:T(8,128)(2,1)S(1)}, u32[]{:S(2)}, u32[]{:S(2)}) collective-permute-start(bf16[2,128,256]{2,1,0:T(8,128)(2,1)S(1)} %get-tuple-element.41), channel_id=1, source_target_pairs={{0,480},{32,448},{64,32},{96,0},{128,96},{160,64},{192,160},{224,1... | collective-permute-start | bytes 393224 | tf_op jit(solution)/shard_map/ppermute | solution.py:524
  65.7 1.9 %collective-permute-start.8 = (bf16[2,128,256]{2,1,0:T(8,128)(2,1)S(1)}, bf16[2,128,256]{2,1,0:T(8,128)(2,1)S(1)}, u32[]{:S(2)}, u32[]{:S(2)}) collective-permute-start(bf16[2,128,256]{2,1,0:T(8,128)(2,1)S(1)} %get-tuple-element.42), channel_id=1, source_target_pairs={{0,384},{32,416},{64,448},{96,480},{128,0},{160,32},{192,64},{224,... | collective-permute-start | bytes 393224 | tf_op jit(solution)/shard_map/ppermute | solution.py:524
  67.6 2.2 %collective-permute-start.9 = (bf16[2,128,256]{2,1,0:T(8,128)(2,1)S(1)}, bf16[2,128,256]{2,1,0:T(8,128)(2,1)S(1)}, u32[]{:S(2)}, u32[]{:S(2)}) collective-permute-start(bf16[2,128,256]{2,1,0:T(8,128)(2,1)S(1)} %get-tuple-element.43), channel_id=1, source_target_pairs={{0,416},{32,384},{64,480},{96,448},{128,32},{160,0},{192,96},{224,... | collective-permute-start | bytes 393224 | tf_op jit(solution)/shard_map/ppermute | solution.py:524
  69.8 0.0 all-to-all-done.1.slots_in
  69.8 1.2 %gate.3 = (bf16[128,256]{1,0:T(8,128)(2,1)S(1)}, bf16[160,256]{1,0:T(8,128)(2,1)S(1)}, f32[16,256]{1,0:T(8,128)S(1)}) custom-call(bf16[3,128,256]{2,1,0:T(8,128)(2,1)S(1)} %get-tuple-element.28.keep_rest, bf16[5,128,256]{2,1,0:T(8,128)(2,1)S(1)} %collective-permute-done.given, f32[2,256,128]{2,1,0:T(8,128)S(1)} %get-tuple-element.44.attended, ...), custom_call_target="tpu_custom_call" | custom-call | tf_op jit(solution)/shard_map/gate/pallas_call | solution.py:31
  71.0 0.0 collective-permute-done.6.same1
  71.0 2.1 %collective-permute-start.10 = (bf16[160,256]{1,0:T(8,128)(2,1)S(1)}, bf16[160,256]{1,0:T(8,128)(2,1)S(1)}, u32[]{:S(2)}, u32[]{:S(2)}) collective-permute-start(bf16[160,256]{1,0:T(8,128)(2,1)S(1)} %get-tuple-element.49), channel_id=1, source_target_pairs={{0,32},{32,0},{64,96},{96,64},{128,160},{160,128},{192,224},{224,1... | collective-permute-start | bytes 245768 | tf_op jit(solution)/shard_map/ppermute | solution.py:524
  73.1 0.0 collective-permute-done.7.cross1
  73.1 4.0 %collective-permute-done.8.same2 = bf16[2,128,256]{2,1,0:T(8,128)(2,1)S(1)} collective-permute-done((bf16[2,128,256]{2,1,0:T(8,128)(2,1)S(1)}, bf16[2,128,256]{2,1,0:T(8,128)(2,1)S(1)}, u32[]{:S(2)}, u32[]{:S(2)}) %collective-permute-start.8) | collective-permute-done | bytes 131104 | tf_op jit(solution)/shard_map/ppermute | solution.py:524
  77.1 4.9 %collective-permute-done.9.cross2 = bf16[2,128,256]{2,1,0:T(8,128)(2,1)S(1)} collective-permute-done((bf16[2,128,256]{2,1,0:T(8,128)(2,1)S(1)}, bf16[2,128,256]{2,1,0:T(8,128)(2,1)S(1)}, u32[]{:S(2)}, u32[]{:S(2)}) %collective-permute-start.9) | collective-permute-done | bytes 131104 | tf_op jit(solution)/shard_map/ppermute | solution.py:524
  82.1 0.0 collective-permute-done.5.swap_in
  82.1 0.0 collective-permute-done.10.gate_in
  82.1 0.9 %final.1 = (bf16[128,512]{1,0:T(8,128)(2,1)}, bf16[128,512]{1,0:T(8,128)(2,1)}, bf16[128,512]{1,0:T(8,128)(2,1)}, bf16[128,512]{1,0:T(8,128)(2,1)}, f32[16,512]{1,0:T(8,128)}) custom-call(bf16[128,256]{1,0:T(8,128)(2,1)S(1)} %get-tuple-element.37.dq_keep, f32[2,128,256]{2,1,0:T(8,128)S(1)} %get-tuple-element.38.dkv_keep, ...), custom_call_target="tpu_custom_call" | custom-call | tf_op jit(solution)/shard_map/final/pallas_call | solution.py:31
Async XLA Ops:
  1.9 21.8 %collective-permute-start = (bf16[5,128,256]{2,1,0:T(8,128)(2,1)S(1)}, bf16[5,128,256]{2,1,0:T(8,128)(2,1)S(1)}, u32[]{:S(2)}, u32[]{:S(2)}) collective-permute-start(bf16[5,128,256]{2,1,0:T(8,128)(2,1)S(1)} %get-tuple-element.30), channel_id=1, source_target_pairs={{0,32},{32,0},{64,96},{96,64},{128,160},{160,128},{192,224},{224,1... | collective-permute-start | bytes 983048 | tf_op jit(solution)/shard_map/ppermute | solution.py:524
  10.7 22.1 %collective-permute-start.4 = (bf16[2,128,256]{2,1,0:T(8,128)(2,1)S(1)}, bf16[2,128,256]{2,1,0:T(8,128)(2,1)S(1)}, u32[]{:S(2)}, u32[]{:S(2)}) collective-permute-start(bf16[2,128,256]{2,1,0:T(8,128)(2,1)S(1)} %get-tuple-element.31), channel_id=1, source_target_pairs={{0,160},{32,128},{64,224},{96,192},{128,288},{160,256},{192,352},{... | collective-permute-start | bytes 393224 | tf_op jit(solution)/shard_map/ppermute | solution.py:524
  12.6 20.2 %collective-permute-start.2 = (bf16[2,128,256]{2,1,0:T(8,128)(2,1)S(1)}, bf16[2,128,256]{2,1,0:T(8,128)(2,1)S(1)}, u32[]{:S(2)}, u32[]{:S(2)}) collective-permute-start(bf16[2,128,256]{2,1,0:T(8,128)(2,1)S(1)} %get-tuple-element.31), channel_id=1, source_target_pairs={{0,96},{32,64},{64,160},{96,128},{128,224},{160,192},{192,288},{22... | collective-permute-start | bytes 393224 | tf_op jit(solution)/shard_map/ppermute | solution.py:524
  14.5 21.7 %collective-permute-start.3 = (bf16[2,128,256]{2,1,0:T(8,128)(2,1)S(1)}, bf16[2,128,256]{2,1,0:T(8,128)(2,1)S(1)}, u32[]{:S(2)}, u32[]{:S(2)}) collective-permute-start(bf16[2,128,256]{2,1,0:T(8,128)(2,1)S(1)} %get-tuple-element.29.keep_kv), channel_id=1, source_target_pairs={{0,128},{32,160},{64,192},{96,224},{128,256},{160,288},{192,320},{... | collective-permute-start | bytes 393224 | tf_op jit(solution)/shard_map/ppermute | solution.py:524
  20.2 16.1 %collective-permute-start.1 = (bf16[2,128,256]{2,1,0:T(8,128)(2,1)S(1)}, bf16[2,128,256]{2,1,0:T(8,128)(2,1)S(1)}, u32[]{:S(2)}, u32[]{:S(2)}) collective-permute-start(bf16[2,128,256]{2,1,0:T(8,128)(2,1)S(1)} %get-tuple-element.29.keep_kv), channel_id=1, source_target_pairs={{0,64},{32,96},{64,128},{96,160},{128,192},{160,224},{192,256},{22... | collective-permute-start | bytes 393224 | tf_op jit(solution)/shard_map/ppermute | solution.py:524
  25.1 17.5 %all-to-all-start = ((bf16[8,16,256]{2,1,0:T(8,128)(2,1)}), bf16[8,16,256]{2,1,0:T(8,128)(2,1)S(1)}, u32[]{:S(2)}, u32[]{:S(2)}) async-start(bf16[8,16,256]{2,1,0:T(8,128)(2,1)} %get-tuple-element.36), calls=%async_computation | async-start | bytes 131072 | tf_op jit(solution)/shard_map/all_to_all | solution.py:530
  42.6 27.2 %all-to-all-start.1 = ((bf16[8,32,256]{2,1,0:T(8,128)(2,1)}), bf16[8,32,256]{2,1,0:T(8,128)(2,1)S(1)}, u32[]{:S(2)}, u32[]{:S(2)}) async-start(bf16[8,32,256]{2,1,0:T(8,128)(2,1)} %get-tuple-element.46), calls=%async_computation.1 | async-start | bytes 262144 | tf_op jit(solution)/shard_map/all_to_all | solution.py:530
  49.3 21.7 %collective-permute-start.6 = (bf16[2,128,256]{2,1,0:T(8,128)(2,1)S(1)}, bf16[2,128,256]{2,1,0:T(8,128)(2,1)S(1)}, u32[]{:S(2)}, u32[]{:S(2)}) collective-permute-start(bf16[2,128,256]{2,1,0:T(8,128)(2,1)S(1)} %get-tuple-element.40), channel_id=1, source_target_pairs={{0,448},{32,480},{64,0},{96,32},{128,64},{160,96},{192,128},{224,1... | collective-permute-start | bytes 393224 | tf_op jit(solution)/shard_map/ppermute | solution.py:524
  59.3 22.8 %collective-permute-start.5 = (bf16[3,128,256]{2,1,0:T(8,128)(2,1)S(1)}, bf16[3,128,256]{2,1,0:T(8,128)(2,1)S(1)}, u32[]{:S(2)}, u32[]{:S(2)}) collective-permute-start(bf16[3,128,256]{2,1,0:T(8,128)(2,1)S(1)} %get-tuple-element.39), channel_id=1, source_target_pairs={{0,32},{32,0},{64,96},{96,64},{128,160},{160,128},{192,224},{224,1... | collective-permute-start | bytes 589832 | tf_op jit(solution)/shard_map/ppermute | solution.py:524
  63.6 9.6 %collective-permute-start.7 = (bf16[2,128,256]{2,1,0:T(8,128)(2,1)S(1)}, bf16[2,128,256]{2,1,0:T(8,128)(2,1)S(1)}, u32[]{:S(2)}, u32[]{:S(2)}) collective-permute-start(bf16[2,128,256]{2,1,0:T(8,128)(2,1)S(1)} %get-tuple-element.41), channel_id=1, source_target_pairs={{0,480},{32,448},{64,32},{96,0},{128,96},{160,64},{192,160},{224,1... | collective-permute-start | bytes 393224 | tf_op jit(solution)/shard_map/ppermute | solution.py:524
  65.7 11.5 %collective-permute-start.8 = (bf16[2,128,256]{2,1,0:T(8,128)(2,1)S(1)}, bf16[2,128,256]{2,1,0:T(8,128)(2,1)S(1)}, u32[]{:S(2)}, u32[]{:S(2)}) collective-permute-start(bf16[2,128,256]{2,1,0:T(8,128)(2,1)S(1)} %get-tuple-element.42), channel_id=1, source_target_pairs={{0,384},{32,416},{64,448},{96,480},{128,0},{160,32},{192,64},{224,... | collective-permute-start | bytes 393224 | tf_op jit(solution)/shard_map/ppermute | solution.py:524
  67.6 14.5 %collective-permute-start.9 = (bf16[2,128,256]{2,1,0:T(8,128)(2,1)S(1)}, bf16[2,128,256]{2,1,0:T(8,128)(2,1)S(1)}, u32[]{:S(2)}, u32[]{:S(2)}) collective-permute-start(bf16[2,128,256]{2,1,0:T(8,128)(2,1)S(1)} %get-tuple-element.43), channel_id=1, source_target_pairs={{0,416},{32,384},{64,480},{96,448},{128,32},{160,0},{192,96},{224,... | collective-permute-start | bytes 393224 | tf_op jit(solution)/shard_map/ppermute | solution.py:524
  71.0 11.1 %collective-permute-start.10 = (bf16[160,256]{1,0:T(8,128)(2,1)S(1)}, bf16[160,256]{1,0:T(8,128)(2,1)S(1)}, u32[]{:S(2)}, u32[]{:S(2)}) collective-permute-start(bf16[160,256]{1,0:T(8,128)(2,1)S(1)} %get-tuple-element.49), channel_id=1, source_target_pairs={{0,32},{32,0},{64,96},{96,64},{128,160},{160,128},{192,224},{224,1... | collective-permute-start | bytes 245768 | tf_op jit(solution)/shard_map/ppermute | solution.py:524

commit v4 on v3

--- a/solution.py
+++ b/solution.py
@@ -12,7 +12,7 @@
 LANES = 128
 SUBS = 8
 GROUP = 8
-FORWARD_COST = pl.CostEstimate(flops=10**11, transcendentals=0, bytes_accessed=10**8)
+EARLY = pl.CostEstimate(flops=10**11, transcendentals=0, bytes_accessed=10**8)
 F32 = jnp.float32
 BF16 = jnp.bfloat16
 OVER_KEYS = (((0,), (0,)), ((), ()))
@@ -409,6 +409,12 @@
     dq_keep[...] = dqbuf[pl.ds(mine, rows), :]
 
 
+def far_body(dkv_keep, same2, cross2, total):
+    for slot in range(2):
+        total[0, slot] = dkv_keep[slot] + same2[slot].astype(F32)
+        total[1, slot] = cross2[slot].astype(F32)
+
+
 def gate_body(
     keep_rest,
     given,
@@ -417,6 +423,7 @@
     slots_in,
     incoming_all,
     params,
+    far_total,
     gate_keep,
     gate_give,
     res_keep,
@@ -478,31 +485,18 @@
         ).astype(BF16)
 
 
-def final_body(dq_keep,
-    dkv_keep,
-    swap_in,
-    same1,
-    cross1,
-    same2,
-    cross2,
-    gate_keep,
-    gate_in,
-    res_keep,
-    dq,
-    dk,
-    dv,
-    dgate,
-    dres,
+def final_body(
+    dq_keep, far_total, swap_in, same1, cross1, gate_keep, gate_in, res_keep, dq, dk, dv, dgate, dres
 ):
     rows, width = dq_keep.shape
     poles = res_keep.shape[0]
     own, other = halves(place()[0], width)
     for slot, out in ((0, dk), (1, dv)):
         out[:, pl.ds(own, width)] = (
-            dkv_keep[slot] + same1[slot].astype(F32) + same2[slot].astype(F32)
+            far_total[0, slot] + same1[slot].astype(F32)
         ).astype(BF16)
         out[:, pl.ds(other, width)] = (
-            swap_in[slot].astype(F32) + cross1[slot].astype(F32) + cross2[slot].astype(F32)
+            far_total[1, slot] + swap_in[slot].astype(F32) + cross1[slot].astype(F32)
         ).astype(BF16)
     dq[:, pl.ds(own, width)] = dq_keep[...]
     dq[:, pl.ds(other, width)] = swap_in[2]
@@ -588,7 +582,7 @@
         ],
         scratch=halo_buffers + [pltpu.VMEM((poles, width), F32), pltpu.VMEM((poles, width), F32)],
         near=tuple(range(10)),
-        cost=FORWARD_COST,
+        cost=EARLY,
         name="forward",
     )(*halo, delta, totals, params)
     tail_in = chip_exchange(tail_slots)
@@ -621,6 +615,9 @@
     back_same1 = chip_shift(out_same1, -1, False)
     back_cross1 = chip_shift(out_cross1, -1, True)
     swap_in = chip_shift(swap_out, 0, True)
+    (far_total,) = call(
+        far_body, [((2,) + pair, F32, True)], near=(0, 1, 2), cost=EARLY, name="far_sum"
+    )(dkv_keep, back_same2, back_cross2)
     gate_keep, gate_give, res_keep = call(
         gate_body,
         [
@@ -629,9 +626,9 @@
             ((poles, width), F32, True),
         ],
         scratch=[pltpu.VMEM(split, F32), pltpu.VMEM((chips, poles, width), F32)],
-        near=tuple(range(7)),
+        near=tuple(range(8)),
         name="gate",
-    )(keep_rest, given, attended, tail_totals, tail_in, incoming_all, params)
+    )(keep_rest, given, attended, tail_totals, tail_in, incoming_all, params, far_total)
     gate_in = chip_shift(gate_give, 0, True)
     full = (rows, channels)
     wide = (full, BF16, False)
@@ -639,20 +636,9 @@
         call(
             final_body,
             [wide, wide, wide, wide, ((poles, channels), F32, False)],
-            near=tuple(range(10)),
+            near=tuple(range(8)),
             name="final",
-        )(
-            dq_keep,
-            dkv_keep,
-            swap_in,
-            back_same1,
-            back_cross1,
-            back_same2,
-            back_cross2,
-            gate_keep,
-            gate_in,
-            res_keep,
-        )
+        )(dq_keep, far_total, swap_in, back_same1, back_cross1, gate_keep, gate_in, res_keep)
     )
 
 

time: 83.5 us -> 80.8 us (0.968)
  waiting for transfers between devices: 15.8 us -> 8.01 us
  starting transfers between devices: 55.6 us -> 58.9 us
  local copies, waits for them, and re-layouts: 0 us -> 1.55 us
    ppermute x11, waiting for transfers between devices: 12.4 us -> 4.64 us  [chip_shift(): return lax.ppermute(array, 'ctx', pairs)]
    ppermute x11, starting transfers between devices: 44.4 us -> 46.4 us  [chip_shift(): return lax.ppermute(array, 'ctx', pairs)]
    unnamed x0 -> x4, local copies, waits for them, and re-layouts: none -> 1.55 us
    all_to_all x2, starting transfers between devices: 11.2 us -> 12.5 us  [chip_exchange(): return lax.all_to_all(slots, 'ctx', 0, 0, axis_index_groups=groups)]
    pallas_call x6 -> x7, Pallas kernels: 10.8 us -> 10.9 us  [run(): pl.pallas_call(body, out_shape=[pltpu.VMEM(s, d) if local_out else jax.Sh...]
  transfers between devices with their start and end apart: 13 -> 13, of which waited for: 4 -> 3; matrix products, arithmetic and copies ran while one was open for 0% -> 0% of each run, Pallas kernels for 10% -> 7%
where the time goes in v4:
time: 80.8 us; the launch traced here: 80.2 us
  starting transfers between devices  58.9 us (73%)
  Pallas kernels  10.9 us (13%)
  waiting for transfers between devices  8.01 us (10%)
  local copies, waits for them, and re-layouts  1.55 us (2%)
  between operations  0.82 us (1%)
    ppermute x11, starting transfers between devices, chip_shift(): return lax.ppermute(array, 'ctx', pairs)  46.4 us
    all_to_all x2, starting transfers between devices, chip_exchange(): return lax.all_to_all(slots, 'ctx', 0, 0, axis_index_groups=groups)  12.5 us
    pallas_call x7, Pallas kernels, run(): pl.pallas_call(body, out_shape=[pltpu.VMEM(s, d) if local_out else jax.Sh...  10.9 us
    ppermute x11, waiting for transfers between devices, chip_shift(): return lax.ppermute(array, 'ctx', pairs)  4.64 us
    all_to_all x2, waiting for transfers between devices, chip_exchange(): return lax.all_to_all(slots, 'ctx', 0, 0, axis_index_groups=groups)  3.36 us
  transfers between devices with their start and end apart: 13, of which 3 were waited for; matrix products, arithmetic and copies ran while one was open for 0% of the time, Pallas kernels for 7%

profile of v4, /device:TPU:1, one launch (start us, length us, event | category | flops | bytes accessed | tf_op | source)
XLA Modules:
  0.0 80.2 jit_solution(9707763242186938149)
XLA Ops:
  0.6 1.3 %pack.1 = (bf16[2,128,256]{2,1,0:T(8,128)(2,1)S(1)}, bf16[2,128,256]{2,1,0:T(8,128)(2,1)S(1)}, bf16[3,128,256]{2,1,0:T(8,128)(2,1)S(1)}, bf16[5,128,256]{2,1,0:T(8,128)(2,1)S(1)}, f32[33,256]{1,0:T(8,128)S(1)}) custom-call(bf16[128,512]{1,0:T(8,128)(2,1)} %k.1, bf16[128,512]{1,0:T(8,128)(2,1)} %v.1, bf16[128,512]{1,0:T(8,128)(2,1)} %q.1, ...), custom_call_target="tpu_custom_call" | custom-call | tf_op jit(solution)/shard_map/pack/pallas_call | solution.py:31
  1.9 8.8 %collective-permute-start = (bf16[5,128,256]{2,1,0:T(8,128)(2,1)S(1)}, bf16[5,128,256]{2,1,0:T(8,128)(2,1)S(1)}, u32[]{:S(2)}, u32[]{:S(2)}) collective-permute-start(bf16[5,128,256]{2,1,0:T(8,128)(2,1)S(1)} %get-tuple-element.30), channel_id=1, source_target_pairs={{0,32},{32,0},{64,96},{96,64},{128,160},{160,128},{192,224},{224,1... | collective-permute-start | bytes 983048 | tf_op jit(solution)/shard_map/ppermute | solution.py:518
  10.7 1.9 %collective-permute-start.4 = (bf16[2,128,256]{2,1,0:T(8,128)(2,1)S(1)}, bf16[2,128,256]{2,1,0:T(8,128)(2,1)S(1)}, u32[]{:S(2)}, u32[]{:S(2)}) collective-permute-start(bf16[2,128,256]{2,1,0:T(8,128)(2,1)S(1)} %get-tuple-element.31), channel_id=1, source_target_pairs={{0,160},{32,128},{64,224},{96,192},{128,288},{160,256},{192,352},{... | collective-permute-start | bytes 393224 | tf_op jit(solution)/shard_map/ppermute | solution.py:518
  12.6 1.9 %collective-permute-start.2 = (bf16[2,128,256]{2,1,0:T(8,128)(2,1)S(1)}, bf16[2,128,256]{2,1,0:T(8,128)(2,1)S(1)}, u32[]{:S(2)}, u32[]{:S(2)}) collective-permute-start(bf16[2,128,256]{2,1,0:T(8,128)(2,1)S(1)} %get-tuple-element.31), channel_id=1, source_target_pairs={{0,96},{32,64},{64,160},{96,128},{128,224},{160,192},{192,288},{22... | collective-permute-start | bytes 393224 | tf_op jit(solution)/shard_map/ppermute | solution.py:518
  14.5 5.6 %collective-permute-start.3 = (bf16[2,128,256]{2,1,0:T(8,128)(2,1)S(1)}, bf16[2,128,256]{2,1,0:T(8,128)(2,1)S(1)}, u32[]{:S(2)}, u32[]{:S(2)}) collective-permute-start(bf16[2,128,256]{2,1,0:T(8,128)(2,1)S(1)} %get-tuple-element.29.keep_kv), channel_id=1, source_target_pairs={{0,128},{32,160},{64,192},{96,224},{128,256},{160,288},{192,320},{... | collective-permute-start | bytes 393224 | tf_op jit(solution)/shard_map/ppermute | solution.py:518
  20.2 3.5 %collective-permute-start.1 = (bf16[2,128,256]{2,1,0:T(8,128)(2,1)S(1)}, bf16[2,128,256]{2,1,0:T(8,128)(2,1)S(1)}, u32[]{:S(2)}, u32[]{:S(2)}) collective-permute-start(bf16[2,128,256]{2,1,0:T(8,128)(2,1)S(1)} %get-tuple-element.29.keep_kv), channel_id=1, source_target_pairs={{0,64},{32,96},{64,128},{96,160},{128,192},{160,224},{192,256},{22... | collective-permute-start | bytes 393224 | tf_op jit(solution)/shard_map/ppermute | solution.py:518
  23.7 0.0 collective-permute-done.given
  23.7 1.3 %head_states.1 = (f32[2,256,128]{2,1,0:T(8,128)S(1)}, f32[16,8,256]{2,1,0:T(8,128)S(1)}, bf16[8,16,256]{2,1,0:T(8,128)(2,1)}) custom-call(bf16[3,128,256]{2,1,0:T(8,128)(2,1)S(1)} %get-tuple-element.28.keep_rest, bf16[5,128,256]{2,1,0:T(8,128)(2,1)S(1)} %collective-permute-done.given, f32[33,256]{1,0:T(8,128)S(1)} %get-tuple-element.32.params), custom_call_target="tpu_custom_call" | custom-call | tf_op jit(solution)/shard_map/head_states/pallas_call | solution.py:31
  25.1 7.7 %all-to-all-start = ((bf16[8,16,256]{2,1,0:T(8,128)(2,1)}), bf16[8,16,256]{2,1,0:T(8,128)(2,1)S(1)}, u32[]{:S(2)}, u32[]{:S(2)}) async-start(bf16[8,16,256]{2,1,0:T(8,128)(2,1)} %get-tuple-element.36), calls=%async_computation | async-start | bytes 131072 | tf_op jit(solution)/shard_map/all_to_all | solution.py:524
  32.8 0.0 collective-permute-done.4.cross2
  32.8 0.0 collective-permute-done.2.cross1
  32.8 3.4 %collective-permute-done.3.same2 = bf16[2,128,256]{2,1,0:T(8,128)(2,1)S(1)} collective-permute-done((bf16[2,128,256]{2,1,0:T(8,128)(2,1)S(1)}, bf16[2,128,256]{2,1,0:T(8,128)(2,1)S(1)}, u32[]{:S(2)}, u32[]{:S(2)}) %collective-permute-start.3) | collective-permute-done | bytes 131104 | tf_op jit(solution)/shard_map/ppermute | solution.py:518
  36.2 0.0 collective-permute-done.1.same1
  36.2 3.0 %forward.1 = (f32[2,2,8,128]{3,2,1,0:T(8,128)S(1)}, f32[2,256,128]{2,1,0:T(8,128)S(1)}, f32[16,8,256]{2,1,0:T(8,128)S(1)}, bf16[8,32,256]{2,1,0:T(8,128)(2,1)}) custom-call(bf16[3,128,256]{2,1,0:T(8,128)(2,1)S(1)} %get-tuple-element.28.keep_rest, bf16[2,128,256]{2,1,0:T(8,128)(2,1)S(1)} %get-tuple-element.29.keep_kv, ...), custom_call_target="tpu_custom_call" | custom-call | flops 99999997952 | bytes 100000000 | tf_op jit(solution)/shard_map/forward/pallas_call | solution.py:31
  39.2 3.4 %all-to-all-done.slots_in = bf16[8,16,256]{2,1,0:T(8,128)(2,1)S(1)} async-done(((bf16[8,16,256]{2,1,0:T(8,128)(2,1)}), bf16[8,16,256]{2,1,0:T(8,128)(2,1)S(1)}, u32[]{:S(2)}, u32[]{:S(2)}) %all-to-all-start) | async-done | bytes 65568 | tf_op jit(solution)/shard_map/all_to_all | solution.py:524
  42.6 3.2 %backward.1 = (bf16[128,256]{1,0:T(8,128)(2,1)S(1)}, f32[2,128,256]{2,1,0:T(8,128)S(1)}, bf16[3,128,256]{2,1,0:T(8,128)(2,1)S(1)}, bf16[2,128,256]{2,1,0:T(8,128...) custom-call(bf16[3,128,256]{2,1,0:T(8,128)(2,1)S(1)} %get-tuple-elem, ...), custom_call_target="tpu_custom_call" | custom-call | tf_op jit(solution)/shard_map/backward/pallas_call | solution.py:31
  45.8 2.8 %collective-permute-start.5 = (bf16[2,128,256]{2,1,0:T(8,128)(2,1)S(1)}, bf16[2,128,256]{2,1,0:T(8,128)(2,1)S(1)}, u32[]{:S(2)}, u32[]{:S(2)}) collective-permute-start(bf16[2,128,256]{2,1,0:T(8,128)(2,1)S(1)} %get-tuple-element.39), channel_id=1, source_target_pairs={{0,384},{32,416},{64,448},{96,480},{128,0},{160,32},{192,64},{224,... | collective-permute-start | bytes 393224 | tf_op jit(solution)/shard_map/ppermute | solution.py:518
  48.6 5.4 %collective-permute-start.6 = (bf16[2,128,256]{2,1,0:T(8,128)(2,1)S(1)}, bf16[2,128,256]{2,1,0:T(8,128)(2,1)S(1)}, u32[]{:S(2)}, u32[]{:S(2)}) collective-permute-start(bf16[2,128,256]{2,1,0:T(8,128)(2,1)S(1)} %get-tuple-element.40), channel_id=1, source_target_pairs={{0,416},{32,384},{64,480},{96,448},{128,32},{160,0},{192,96},{224,... | collective-permute-start | bytes 393224 | tf_op jit(solution)/shard_map/ppermute | solution.py:518
  54.1 4.8 %all-to-all-start.1 = ((bf16[8,32,256]{2,1,0:T(8,128)(2,1)}), bf16[8,32,256]{2,1,0:T(8,128)(2,1)S(1)}, u32[]{:S(2)}, u32[]{:S(2)}) async-start(bf16[8,32,256]{2,1,0:T(8,128)(2,1)} %get-tuple-element.46), calls=%async_computation.1 | async-start | bytes 262144 | tf_op jit(solution)/shard_map/all_to_all | solution.py:524
  58.8 10.0 %collective-permute-start.8 = (bf16[2,128,256]{2,1,0:T(8,128)(2,1)S(1)}, bf16[2,128,256]{2,1,0:T(8,128)(2,1)S(1)}, u32[]{:S(2)}, u32[]{:S(2)}) collective-permute-start(bf16[2,128,256]{2,1,0:T(8,128)(2,1)S(1)} %get-tuple-element.42), channel_id=1, source_target_pairs={{0,448},{32,480},{64,0},{96,32},{128,64},{160,96},{192,128},{224,1... | collective-permute-start | bytes 393224 | tf_op jit(solution)/shard_map/ppermute | solution.py:518
  68.8 1.9 %collective-permute-start.9 = (bf16[2,128,256]{2,1,0:T(8,128)(2,1)S(1)}, bf16[2,128,256]{2,1,0:T(8,128)(2,1)S(1)}, u32[]{:S(2)}, u32[]{:S(2)}) collective-permute-start(bf16[2,128,256]{2,1,0:T(8,128)(2,1)S(1)} %get-tuple-element.43), channel_id=1, source_target_pairs={{0,480},{32,448},{64,32},{96,0},{128,96},{160,64},{192,160},{224,1... | collective-permute-start | bytes 393224 | tf_op jit(solution)/shard_map/ppermute | solution.py:518
  70.7 2.6 %collective-permute-start.7 = (bf16[3,128,256]{2,1,0:T(8,128)(2,1)S(1)}, bf16[3,128,256]{2,1,0:T(8,128)(2,1)S(1)}, u32[]{:S(2)}, u32[]{:S(2)}) collective-permute-start(bf16[3,128,256]{2,1,0:T(8,128)(2,1)S(1)} %get-tuple-element.41), channel_id=1, source_target_pairs={{0,32},{32,0},{64,96},{96,64},{128,160},{160,128},{192,224},{224,1... | collective-permute-start | bytes 589832 | tf_op jit(solution)/shard_map/ppermute | solution.py:518
  73.3 0.0 collective-permute-done.5.same2
  73.3 0.0 collective-permute-done.6.cross2
  73.3 0.0 copy-start
  73.3 0.6 copy-done
  74.0 0.9 %copy-done.1 = bf16[2,128,256]{2,1,0:T(8,128)(2,1)S(1)} copy-done((bf16[2,128,256]{2,1,0:T(8,128)(2,1)S(1)}, bf16[2,128,256]{2,1,0:T(8,128)(2,1)}, u32[]{:S(2)}) %copy-start.1) | copy-done | bytes 131096
  74.9 1.2 %gate.3 = (bf16[128,256]{1,0:T(8,128)(2,1)S(1)}, bf16[160,256]{1,0:T(8,128)(2,1)S(1)}, f32[16,256]{1,0:T(8,128)S(1)}) custom-call(bf16[3,128,256]{2,1,0:T(8,128)(2,1)S(1)} %get-tuple-element.28.keep_rest, bf16[5,128,256]{2,1,0:T(8,128)(2,1)S(1)} %collective-permute-done.given, f32[2,256,128]{2,1,0:T(8,128)S(1)} %get-tuple-element.44.attended, ...), custom_call_target="tpu_custom_call" | custom-call | tf_op jit(solution)/shard_map/gate/pallas_call | solution.py:31
  76.1 1.9 %collective-permute-start.10 = (bf16[160,256]{1,0:T(8,128)(2,1)S(1)}, bf16[160,256]{1,0:T(8,128)(2,1)S(1)}, u32[]{:S(2)}, u32[]{:S(2)}) collective-permute-start(bf16[160,256]{1,0:T(8,128)(2,1)S(1)} %get-tuple-element.49), channel_id=1, source_target_pairs={{0,32},{32,0},{64,96},{96,64},{128,160},{160,128},{192,224},{224,1... | collective-permute-start | bytes 245768 | tf_op jit(solution)/shard_map/ppermute | solution.py:518
  78.0 0.0 collective-permute-done.8.same1
  78.1 1.2 %collective-permute-done.10.gate_in = bf16[160,256]{1,0:T(8,128)(2,1)S(1)} collective-permute-done((bf16[160,256]{1,0:T(8,128)(2,1)S(1)}, bf16[160,256]{1,0:T(8,128)(2,1)S(1)}, u32[]{:S(2)}, u32[]{:S(2)}) %collective-permute-start.10) | collective-permute-done | bytes 81952 | tf_op jit(solution)/shard_map/ppermute | solution.py:518
  79.3 0.9 %final.1 = (bf16[128,512]{1,0:T(8,128)(2,1)}, bf16[128,512]{1,0:T(8,128)(2,1)}, bf16[128,512]{1,0:T(8,128)(2,1)}, bf16[128,512]{1,0:T(8,128)(2,1)}, f32[16,512]{1,0:T(8,128)}) custom-call(bf16[128,256]{1,0:T(8,128)(2,1)S(1)} %get-tuple-element.37.dq_keep, f32[2,2,128,256]{3,2,1,0:T(8,128)S(1)} %far_sum.1.far_total, ...), custom_call_target="tpu_custom_call" | custom-call | tf_op jit(solution)/shard_map/final/pallas_call | solution.py:31
  (5 shorter events, 0.0 us)
Async XLA Ops:
  1.9 21.8 %collective-permute-start = (bf16[5,128,256]{2,1,0:T(8,128)(2,1)S(1)}, bf16[5,128,256]{2,1,0:T(8,128)(2,1)S(1)}, u32[]{:S(2)}, u32[]{:S(2)}) collective-permute-start(bf16[5,128,256]{2,1,0:T(8,128)(2,1)S(1)} %get-tuple-element.30), channel_id=1, source_target_pairs={{0,32},{32,0},{64,96},{96,64},{128,160},{160,128},{192,224},{224,1... | collective-permute-start | bytes 983048 | tf_op jit(solution)/shard_map/ppermute | solution.py:518
  10.7 22.1 %collective-permute-start.4 = (bf16[2,128,256]{2,1,0:T(8,128)(2,1)S(1)}, bf16[2,128,256]{2,1,0:T(8,128)(2,1)S(1)}, u32[]{:S(2)}, u32[]{:S(2)}) collective-permute-start(bf16[2,128,256]{2,1,0:T(8,128)(2,1)S(1)} %get-tuple-element.31), channel_id=1, source_target_pairs={{0,160},{32,128},{64,224},{96,192},{128,288},{160,256},{192,352},{... | collective-permute-start | bytes 393224 | tf_op jit(solution)/shard_map/ppermute | solution.py:518
  12.6 20.2 %collective-permute-start.2 = (bf16[2,128,256]{2,1,0:T(8,128)(2,1)S(1)}, bf16[2,128,256]{2,1,0:T(8,128)(2,1)S(1)}, u32[]{:S(2)}, u32[]{:S(2)}) collective-permute-start(bf16[2,128,256]{2,1,0:T(8,128)(2,1)S(1)} %get-tuple-element.31), channel_id=1, source_target_pairs={{0,96},{32,64},{64,160},{96,128},{128,224},{160,192},{192,288},{22... | collective-permute-start | bytes 393224 | tf_op jit(solution)/shard_map/ppermute | solution.py:518
  14.5 21.7 %collective-permute-start.3 = (bf16[2,128,256]{2,1,0:T(8,128)(2,1)S(1)}, bf16[2,128,256]{2,1,0:T(8,128)(2,1)S(1)}, u32[]{:S(2)}, u32[]{:S(2)}) collective-permute-start(bf16[2,128,256]{2,1,0:T(8,128)(2,1)S(1)} %get-tuple-element.29.keep_kv), channel_id=1, source_target_pairs={{0,128},{32,160},{64,192},{96,224},{128,256},{160,288},{192,320},{... | collective-permute-start | bytes 393224 | tf_op jit(solution)/shard_map/ppermute | solution.py:518
  20.2 16.1 %collective-permute-start.1 = (bf16[2,128,256]{2,1,0:T(8,128)(2,1)S(1)}, bf16[2,128,256]{2,1,0:T(8,128)(2,1)S(1)}, u32[]{:S(2)}, u32[]{:S(2)}) collective-permute-start(bf16[2,128,256]{2,1,0:T(8,128)(2,1)S(1)} %get-tuple-element.29.keep_kv), channel_id=1, source_target_pairs={{0,64},{32,96},{64,128},{96,160},{128,192},{160,224},{192,256},{22... | collective-permute-start | bytes 393224 | tf_op jit(solution)/shard_map/ppermute | solution.py:518
  25.1 17.5 %all-to-all-start = ((bf16[8,16,256]{2,1,0:T(8,128)(2,1)}), bf16[8,16,256]{2,1,0:T(8,128)(2,1)S(1)}, u32[]{:S(2)}, u32[]{:S(2)}) async-start(bf16[8,16,256]{2,1,0:T(8,128)(2,1)} %get-tuple-element.36), calls=%async_computation | async-start | bytes 131072 | tf_op jit(solution)/shard_map/all_to_all | solution.py:524
  45.8 27.5 %collective-permute-start.5 = (bf16[2,128,256]{2,1,0:T(8,128)(2,1)S(1)}, bf16[2,128,256]{2,1,0:T(8,128)(2,1)S(1)}, u32[]{:S(2)}, u32[]{:S(2)}) collective-permute-start(bf16[2,128,256]{2,1,0:T(8,128)(2,1)S(1)} %get-tuple-element.39), channel_id=1, source_target_pairs={{0,384},{32,416},{64,448},{96,480},{128,0},{160,32},{192,64},{224,... | collective-permute-start | bytes 393224 | tf_op jit(solution)/shard_map/ppermute | solution.py:518
  48.6 24.7 %collective-permute-start.6 = (bf16[2,128,256]{2,1,0:T(8,128)(2,1)S(1)}, bf16[2,128,256]{2,1,0:T(8,128)(2,1)S(1)}, u32[]{:S(2)}, u32[]{:S(2)}) collective-permute-start(bf16[2,128,256]{2,1,0:T(8,128)(2,1)S(1)} %get-tuple-element.40), channel_id=1, source_target_pairs={{0,416},{32,384},{64,480},{96,448},{128,32},{160,0},{192,96},{224,... | collective-permute-start | bytes 393224 | tf_op jit(solution)/shard_map/ppermute | solution.py:518
  54.1 20.9 %all-to-all-start.1 = ((bf16[8,32,256]{2,1,0:T(8,128)(2,1)}), bf16[8,32,256]{2,1,0:T(8,128)(2,1)S(1)}, u32[]{:S(2)}, u32[]{:S(2)}) async-start(bf16[8,32,256]{2,1,0:T(8,128)(2,1)} %get-tuple-element.46), calls=%async_computation.1 | async-start | bytes 262144 | tf_op jit(solution)/shard_map/all_to_all | solution.py:524
  58.8 19.2 %collective-permute-start.8 = (bf16[2,128,256]{2,1,0:T(8,128)(2,1)S(1)}, bf16[2,128,256]{2,1,0:T(8,128)(2,1)S(1)}, u32[]{:S(2)}, u32[]{:S(2)}) collective-permute-start(bf16[2,128,256]{2,1,0:T(8,128)(2,1)S(1)} %get-tuple-element.42), channel_id=1, source_target_pairs={{0,448},{32,480},{64,0},{96,32},{128,64},{160,96},{192,128},{224,1... | collective-permute-start | bytes 393224 | tf_op jit(solution)/shard_map/ppermute | solution.py:518
  68.8 9.3 %collective-permute-start.9 = (bf16[2,128,256]{2,1,0:T(8,128)(2,1)S(1)}, bf16[2,128,256]{2,1,0:T(8,128)(2,1)S(1)}, u32[]{:S(2)}, u32[]{:S(2)}) collective-permute-start(bf16[2,128,256]{2,1,0:T(8,128)(2,1)S(1)} %get-tuple-element.43), channel_id=1, source_target_pairs={{0,480},{32,448},{64,32},{96,0},{128,96},{160,64},{192,160},{224,1... | collective-permute-start | bytes 393224 | tf_op jit(solution)/shard_map/ppermute | solution.py:518
  70.7 7.3 %collective-permute-start.7 = (bf16[3,128,256]{2,1,0:T(8,128)(2,1)S(1)}, bf16[3,128,256]{2,1,0:T(8,128)(2,1)S(1)}, u32[]{:S(2)}, u32[]{:S(2)}) collective-permute-start(bf16[3,128,256]{2,1,0:T(8,128)(2,1)S(1)} %get-tuple-element.41), channel_id=1, source_target_pairs={{0,32},{32,0},{64,96},{96,64},{128,160},{160,128},{192,224},{224,1... | collective-permute-start | bytes 589832 | tf_op jit(solution)/shard_map/ppermute | solution.py:518
  73.3 0.7 copy-start
  74.0 0.9 %copy-start.1 = (bf16[2,128,256]{2,1,0:T(8,128)(2,1)S(1)}, bf16[2,128,256]{2,1,0:T(8,128)(2,1)}, u32[]{:S(2)}) copy-start(bf16[2,128,256]{2,1,0:T(8,128)(2,1)} %copy-done) | copy-start | bytes 393220
  76.1 3.2 %collective-permute-start.10 = (bf16[160,256]{1,0:T(8,128)(2,1)S(1)}, bf16[160,256]{1,0:T(8,128)(2,1)S(1)}, u32[]{:S(2)}, u32[]{:S(2)}) collective-permute-start(bf16[160,256]{1,0:T(8,128)(2,1)S(1)} %get-tuple-element.49), channel_id=1, source_target_pairs={{0,32},{32,0},{64,96},{96,64},{128,160},{160,128},{192,224},{224,1... | collective-permute-start | bytes 245768 | tf_op jit(solution)/shard_map/ppermute | solution.py:518

commit v5 on v4

--- a/solution.py
+++ b/solution.py
@@ -184,7 +184,15 @@
     return jnp.sqrt(2.0 * tangent / (1.0 + tangent))
 
 
-def assemble(core, keep_rest, keep_kv, given, same1, cross1, same2, cross2, qbuf, kbuf, vbuf):
+def merge_body(keep_kv, given, chip_kv):
+    rows = keep_kv.shape[1]
+    core, chip = place()
+    for slot in range(2):
+        chip_kv[slot, pl.ds(pl.multiple_of(core * rows, rows), rows), :] = keep_kv[slot]
+        chip_kv[slot, pl.ds(pl.multiple_of((1 - core) * rows, rows), rows), :] = given[slot]
+
+
+def assemble(core, keep_rest, chip_kv, given, same1, cross1, far_kv, qbuf, kbuf, vbuf):
     rows = keep_rest.shape[1]
     tokens = 2 * rows
     mine = pl.multiple_of(core * rows, rows)
@@ -192,12 +200,10 @@
     qbuf[pl.ds(mine, rows), :] = keep_rest[0]
     qbuf[pl.ds(theirs, rows), :] = given[2]
     for slot, buf in ((0, kbuf), (1, vbuf)):
-        buf[pl.ds(mine, rows), :] = same2[slot]
-        buf[pl.ds(theirs, rows), :] = cross2[slot]
+        buf[0:tokens, :] = far_kv[slot]
         buf[pl.ds(mine + tokens, rows), :] = same1[slot]
         buf[pl.ds(theirs + tokens, rows), :] = cross1[slot]
-        buf[pl.ds(mine + 2 * tokens, rows), :] = keep_kv[slot]
-        buf[pl.ds(theirs + 2 * tokens, rows), :] = given[slot]
+        buf[2 * tokens : 3 * tokens, :] = chip_kv[slot]
 
 
 def allowed_pairs(rows):
@@ -209,12 +215,11 @@
 
 def forward_body(
     keep_rest,
-    keep_kv,
+    chip_kv,
     given,
     same1,
     cross1,
-    same2,
-    cross2,
+    far_kv,
     delta,
     totals,
     params,
@@ -235,7 +240,7 @@
     chips = slots.shape[0]
     core, chip = place()
     scale = 1.0 / math.sqrt(HEAD)
-    assemble(core, keep_rest, keep_kv, given, same1, cross1, same2, cross2, qbuf, kbuf, vbuf)
+    assemble(core, keep_rest, chip_kv, given, same1, cross1, far_kv, qbuf, kbuf, vbuf)
     span = (WIN + 1) * rows
     allowed = allowed_pairs(rows)
     for head in range(width // HEAD):
@@ -293,12 +298,11 @@
 
 def backward_body(
     keep_rest,
-    keep_kv,
+    chip_kv,
     given,
     same1,
     cross1,
-    same2,
-    cross2,
+    far_kv,
     stats,
     delta,
     totals,
@@ -330,7 +334,7 @@
     mine = pl.multiple_of(core * rows, rows)
     theirs = pl.multiple_of((1 - core) * rows, rows)
     scale = 1.0 / math.sqrt(HEAD)
-    assemble(core, keep_rest, keep_kv, given, same1, cross1, same2, cross2, qbuf, kbuf, vbuf)
+    assemble(core, keep_rest, chip_kv, given, same1, cross1, far_kv, qbuf, kbuf, vbuf)
 
     around(
         lambda n: slots_in[n].astype(F32),
@@ -410,9 +414,7 @@
 
 
 def far_body(dkv_keep, same2, cross2, total):
-    for slot in range(2):
-        total[0, slot] = dkv_keep[slot] + same2[slot].astype(F32)
-        total[1, slot] = cross2[slot].astype(F32)
+    total[...] = dkv_keep[...] + same2[...].astype(F32)
 
 
 def gate_body(
@@ -486,17 +488,17 @@
 
 
 def final_body(
-    dq_keep, far_total, swap_in, same1, cross1, gate_keep, gate_in, res_keep, dq, dk, dv, dgate, dres
+    dq_keep, far_total, swap_in, same1, cross1, cross2, gate_keep, gate_in, res_keep, dq, dk, dv, dgate, dres
 ):
     rows, width = dq_keep.shape
     poles = res_keep.shape[0]
     own, other = halves(place()[0], width)
     for slot, out in ((0, dk), (1, dv)):
         out[:, pl.ds(own, width)] = (
-            far_total[0, slot] + same1[slot].astype(F32)
+            far_total[slot] + same1[slot].astype(F32)
         ).astype(BF16)
         out[:, pl.ds(other, width)] = (
-            far_total[1, slot] + swap_in[slot].astype(F32) + cross1[slot].astype(F32)
+            swap_in[slot].astype(F32) + cross1[slot].astype(F32) + cross2[slot].astype(F32)
         ).astype(BF16)
     dq[:, pl.ds(own, width)] = dq_keep[...]
     dq[:, pl.ds(other, width)] = swap_in[2]
@@ -553,11 +555,13 @@
         far=tuple(range(8)),
         name="pack",
     )(key_rows, value_rows, queries, gate_values, cotangent, decay_rates, residues, skip)
-    same2 = chip_shift(keep_kv, 2, False)
-    cross2 = chip_shift(give_kv, 2, True)
+    given = chip_shift(give_all, 0, True)
+    (chip_kv,) = call(merge_body, [((2, tokens, width), BF16, True)], near=(0, 1), name="chip_kv")(
+        keep_kv, given
+    )
+    far_kv = chip_shift(chip_kv, 2, False)
     same1 = chip_shift(keep_kv, 1, False)
     cross1 = chip_shift(give_kv, 1, True)
-    given = chip_shift(give_all, 0, True)
     delta, totals, head_slots = call(
         head_body,
         [(split, F32, True), (states, F32, True), ((chips, poles, width), BF16, True)],
@@ -566,7 +570,7 @@
         name="head_states",
     )(keep_rest, given, params)
     head_in = chip_exchange(head_slots)
-    halo = (keep_rest, keep_kv, given, same1, cross1, same2, cross2)
+    halo = (keep_rest, chip_kv, given, same1, cross1, far_kv)
     halo_buffers = [
         pltpu.VMEM((tokens, width), BF16),
         pltpu.VMEM((span, width), BF16),
@@ -581,7 +585,7 @@
             ((chips, 2 * poles, width), BF16, True),
         ],
         scratch=halo_buffers + [pltpu.VMEM((poles, width), F32), pltpu.VMEM((poles, width), F32)],
-        near=tuple(range(10)),
+        near=tuple(range(9)),
         cost=EARLY,
         name="forward",
     )(*halo, delta, totals, params)
@@ -606,7 +610,7 @@
             pltpu.VMEM((span, width), F32),
             pltpu.VMEM((tokens, width), BF16),
         ],
-        near=tuple(range(12)),
+        near=tuple(range(11)),
         name="backward",
     )(*halo, stats, delta, totals, head_in, params)
     dq_keep, dkv_keep, swap_out, out_same1, out_cross1, out_same2, out_cross2, incoming_all = outs
@@ -616,7 +620,7 @@
     back_cross1 = chip_shift(out_cross1, -1, True)
     swap_in = chip_shift(swap_out, 0, True)
     (far_total,) = call(
-        far_body, [((2,) + pair, F32, True)], near=(0, 1, 2), cost=EARLY, name="far_sum"
+        far_body, [(pair, F32, True)], near=(0, 1, 2), cost=EARLY, name="far_sum"
     )(dkv_keep, back_same2, back_cross2)
     gate_keep, gate_give, res_keep = call(
         gate_body,
@@ -636,9 +640,19 @@
         call(
             final_body,
             [wide, wide, wide, wide, ((poles, channels), F32, False)],
-            near=tuple(range(8)),
+            near=tuple(range(9)),
             name="final",
-        )(dq_keep, far_total, swap_in, back_same1, back_cross1, gate_keep, gate_in, res_keep)
+        )(
+            dq_keep,
+            far_total,
+            swap_in,
+            back_same1,
+            back_cross1,
+            back_cross2,
+            gate_keep,
+            gate_in,
+            res_keep,
+        )
     )
 
 

time: 80.8 us -> 75.9 us (0.939)
  starting transfers between devices: 58.9 us -> 52.9 us
  waiting for transfers between devices: 8.01 us -> 10.8 us
  local copies, waits for them, and re-layouts: 1.55 us -> 0 us
    ppermute x11 -> x10, waiting for transfers between devices: 4.64 us -> 10.8 us  [chip_shift(): return lax.ppermute(array, 'ctx', pairs)]
    ppermute x11 -> x10, starting transfers between devices: 46.4 us -> 42.3 us  [chip_shift(): return lax.ppermute(array, 'ctx', pairs)]
    all_to_all x2, waiting for transfers between devices: 3.36 us -> 0.01 us  [chip_exchange(): return lax.all_to_all(slots, 'ctx', 0, 0, axis_index_groups=groups)]
    all_to_all x2, starting transfers between devices: 12.5 us -> 10.6 us  [chip_exchange(): return lax.all_to_all(slots, 'ctx', 0, 0, axis_index_groups=groups)]
    unnamed x4 -> x0, local copies, waits for them, and re-layouts: 1.55 us -> none
    pallas_call x7 -> x8, Pallas kernels: 10.9 us -> 10.9 us  [run(): pl.pallas_call(body, out_shape=[pltpu.VMEM(s, d) if local_out else jax.Sh...]
  transfers between devices with their start and end apart: 13 -> 12, of which waited for: 3 -> 5; matrix products, arithmetic and copies ran while one was open for 0% -> 0% of each run, Pallas kernels for 7% -> 7%
where the time goes in v5:
time: 75.9 us; the launch traced here: 75.4 us
  starting transfers between devices  52.9 us (70%)
  Pallas kernels  10.9 us (14%)
  waiting for transfers between devices  10.8 us (14%)
  between operations  0.8 us (1%)
    ppermute x10, starting transfers between devices, chip_shift(): return lax.ppermute(array, 'ctx', pairs)  42.3 us
    pallas_call x8, Pallas kernels, run(): pl.pallas_call(body, out_shape=[pltpu.VMEM(s, d) if local_out else jax.Sh...  10.9 us
    ppermute x10, waiting for transfers between devices, chip_shift(): return lax.ppermute(array, 'ctx', pairs)  10.8 us
    all_to_all x2, starting transfers between devices, chip_exchange(): return lax.all_to_all(slots, 'ctx', 0, 0, axis_index_groups=groups)  10.6 us
  transfers between devices with their start and end apart: 12, of which 5 were waited for; matrix products, arithmetic and copies ran while one was open for 0% of the time, Pallas kernels for 7%

profile of v5, /device:TPU:1, one launch (start us, length us, event | category | flops | bytes accessed | tf_op | source)
XLA Modules:
  0.0 75.4 jit_solution(14847321190026198340)
XLA Ops:
  0.6 1.3 %pack.1 = (bf16[2,128,256]{2,1,0:T(8,128)(2,1)S(1)}, bf16[2,128,256]{2,1,0:T(8,128)(2,1)S(1)}, bf16[3,128,256]{2,1,0:T(8,128)(2,1)S(1)}, bf16[5,128,256]{2,1,0:T(8,128)(2,1)S(1)}, f32[33,256]{1,0:T(8,128)S(1)}) custom-call(bf16[128,512]{1,0:T(8,128)(2,1)} %k.1, bf16[128,512]{1,0:T(8,128)(2,1)} %v.1, bf16[128,512]{1,0:T(8,128)(2,1)} %q.1, ...), custom_call_target="tpu_custom_call" | custom-call | tf_op jit(solution)/shard_map/pack/pallas_call | solution.py:31
  1.9 8.8 %collective-permute-start = (bf16[5,128,256]{2,1,0:T(8,128)(2,1)S(1)}, bf16[5,128,256]{2,1,0:T(8,128)(2,1)S(1)}, u32[]{:S(2)}, u32[]{:S(2)}) collective-permute-start(bf16[5,128,256]{2,1,0:T(8,128)(2,1)S(1)} %get-tuple-element.30), channel_id=1, source_target_pairs={{0,32},{32,0},{64,96},{96,64},{128,160},{160,128},{192,224},{224,1... | collective-permute-start | bytes 983048 | tf_op jit(solution)/shard_map/ppermute | solution.py:520
  10.7 1.2 %collective-permute-done.given = bf16[5,128,256]{2,1,0:T(8,128)(2,1)S(1)} collective-permute-done((bf16[5,128,256]{2,1,0:T(8,128)(2,1)S(1)}, bf16[5,128,256]{2,1,0:T(8,128)(2,1)S(1)}, u32[]{:S(2)}, u32[]{:S(2)}) %collective-permute-start) | collective-permute-done | bytes 327712 | tf_op jit(solution)/shard_map/ppermute | solution.py:520
  12.0 1.9 %collective-permute-start.3 = (bf16[2,256,256]{2,1,0:T(8,128)(2,1)S(1)}, bf16[2,256,256]{2,1,0:T(8,128)(2,1)S(1)}, u32[]{:S(2)}, u32[]{:S(2)}) collective-permute-start(bf16[2,256,256]{2,1,0:T(8,128)(2,1)S(1)} %chip_kv.1), channel_id=1, source_target_pairs={{0,128},{32,160},{64,192},{96,224},{128,256},{160,288},{192,320},{... | collective-permute-start | bytes 786440 | tf_op jit(solution)/shard_map/ppermute | solution.py:520
  13.9 1.9 %collective-permute-start.2 = (bf16[2,128,256]{2,1,0:T(8,128)(2,1)S(1)}, bf16[2,128,256]{2,1,0:T(8,128)(2,1)S(1)}, u32[]{:S(2)}, u32[]{:S(2)}) collective-permute-start(bf16[2,128,256]{2,1,0:T(8,128)(2,1)S(1)} %get-tuple-element.31), channel_id=1, source_target_pairs={{0,96},{32,64},{64,160},{96,128},{128,224},{160,192},{192,288},{22... | collective-permute-start | bytes 393224 | tf_op jit(solution)/shard_map/ppermute | solution.py:520
  15.8 4.5 %collective-permute-start.1 = (bf16[2,128,256]{2,1,0:T(8,128)(2,1)S(1)}, bf16[2,128,256]{2,1,0:T(8,128)(2,1)S(1)}, u32[]{:S(2)}, u32[]{:S(2)}) collective-permute-start(bf16[2,128,256]{2,1,0:T(8,128)(2,1)S(1)} %get-tuple-element.29.keep_kv), channel_id=1, source_target_pairs={{0,64},{32,96},{64,128},{96,160},{128,192},{160,224},{192,256},{22... | collective-permute-start | bytes 393224 | tf_op jit(solution)/shard_map/ppermute | solution.py:520
  20.4 1.3 %head_states.1 = (f32[2,256,128]{2,1,0:T(8,128)S(1)}, f32[16,8,256]{2,1,0:T(8,128)S(1)}, bf16[8,16,256]{2,1,0:T(8,128)(2,1)}) custom-call(bf16[3,128,256]{2,1,0:T(8,128)(2,1)S(1)} %get-tuple-element.28.keep_rest, bf16[5,128,256]{2,1,0:T(8,128)(2,1)S(1)} %collective-permute-done.given, f32[33,256]{1,0:T(8,128)S(1)} %get-tuple-element.32.params), custom_call_target="tpu_custom_call" | custom-call | tf_op jit(solution)/shard_map/head_states/pallas_call | solution.py:31
  21.7 7.3 %all-to-all-start = ((bf16[8,16,256]{2,1,0:T(8,128)(2,1)}), bf16[8,16,256]{2,1,0:T(8,128)(2,1)S(1)}, u32[]{:S(2)}, u32[]{:S(2)}) async-start(bf16[8,16,256]{2,1,0:T(8,128)(2,1)} %get-tuple-element.36), calls=%async_computation | async-start | bytes 131072 | tf_op jit(solution)/shard_map/all_to_all | solution.py:526
  29.0 0.5 collective-permute-done.2.cross1
  29.4 2.1 %collective-permute-done.1.same1 = bf16[2,128,256]{2,1,0:T(8,128)(2,1)S(1)} collective-permute-done((bf16[2,128,256]{2,1,0:T(8,128)(2,1)S(1)}, bf16[2,128,256]{2,1,0:T(8,128)(2,1)S(1)}, u32[]{:S(2)}, u32[]{:S(2)}) %collective-permute-start.1) | collective-permute-done | bytes 131104 | tf_op jit(solution)/shard_map/ppermute | solution.py:520
  31.5 6.0 %collective-permute-done.3.far_kv = bf16[2,256,256]{2,1,0:T(8,128)(2,1)S(1)} collective-permute-done((bf16[2,256,256]{2,1,0:T(8,128)(2,1)S(1)}, bf16[2,256,256]{2,1,0:T(8,128)(2,1)S(1)}, u32[]{:S(2)}, u32[]{:S(2)}) %collective-permute-start.3) | collective-permute-done | bytes 262176 | tf_op jit(solution)/shard_map/ppermute | solution.py:520
  37.5 3.0 %forward.1 = (f32[2,2,8,128]{3,2,1,0:T(8,128)S(1)}, f32[2,256,128]{2,1,0:T(8,128)S(1)}, f32[16,8,256]{2,1,0:T(8,128)S(1)}, bf16[8,32,256]{2,1,0:T(8,128)(2,1)}) custom-call(bf16[3,128,256]{2,1,0:T(8,128)(2,1)S(1)} %get-tuple-element.28.keep_rest, bf16[2,256,256]{2,1,0:T(8,128)(2,1)S(1)} %chip_kv.1, bf16[5,128,256]{2,1,0:T(8,128)(2,1)S(1)} %collective-permute-done.given, ...), custom_call_target="tpu_custom_call" | custom-call | flops 99999997952 | bytes 100000000 | tf_op jit(solution)/shard_map/forward/pallas_call | solution.py:31
  40.4 0.0 all-to-all-done.slots_in
  40.4 3.2 %backward.1 = (bf16[128,256]{1,0:T(8,128)(2,1)S(1)}, f32[2,128,256]{2,1,0:T(8,128)S(1)}, bf16[3,128,256]{2,1,0:T(8,128)(2,1)S(1)}, bf16[2,128,256]{2,1,0:T(8,128...) custom-call(bf16[3,128,256]{2,1,0:T(8,128)(2,1)S(1)} %get-tuple-elem, ...), custom_call_target="tpu_custom_call" | custom-call | tf_op jit(solution)/shard_map/backward/pallas_call | solution.py:31
  43.7 3.7 %collective-permute-start.4 = (bf16[2,128,256]{2,1,0:T(8,128)(2,1)S(1)}, bf16[2,128,256]{2,1,0:T(8,128)(2,1)S(1)}, u32[]{:S(2)}, u32[]{:S(2)}) collective-permute-start(bf16[2,128,256]{2,1,0:T(8,128)(2,1)S(1)} %get-tuple-element.39), channel_id=1, source_target_pairs={{0,384},{32,416},{64,448},{96,480},{128,0},{160,32},{192,64},{224,... | collective-permute-start | bytes 393224 | tf_op jit(solution)/shard_map/ppermute | solution.py:520
  47.4 4.9 %collective-permute-start.5 = (bf16[2,128,256]{2,1,0:T(8,128)(2,1)S(1)}, bf16[2,128,256]{2,1,0:T(8,128)(2,1)S(1)}, u32[]{:S(2)}, u32[]{:S(2)}) collective-permute-start(bf16[2,128,256]{2,1,0:T(8,128)(2,1)S(1)} %get-tuple-element.40), channel_id=1, source_target_pairs={{0,416},{32,384},{64,480},{96,448},{128,32},{160,0},{192,96},{224,... | collective-permute-start | bytes 393224 | tf_op jit(solution)/shard_map/ppermute | solution.py:520
  52.3 3.4 %all-to-all-start.1 = ((bf16[8,32,256]{2,1,0:T(8,128)(2,1)}), bf16[8,32,256]{2,1,0:T(8,128)(2,1)S(1)}, u32[]{:S(2)}, u32[]{:S(2)}) async-start(bf16[8,32,256]{2,1,0:T(8,128)(2,1)} %get-tuple-element.46), calls=%async_computation.1 | async-start | bytes 262144 | tf_op jit(solution)/shard_map/all_to_all | solution.py:526
  55.7 9.9 %collective-permute-start.7 = (bf16[2,128,256]{2,1,0:T(8,128)(2,1)S(1)}, bf16[2,128,256]{2,1,0:T(8,128)(2,1)S(1)}, u32[]{:S(2)}, u32[]{:S(2)}) collective-permute-start(bf16[2,128,256]{2,1,0:T(8,128)(2,1)S(1)} %get-tuple-element.42), channel_id=1, source_target_pairs={{0,448},{32,480},{64,0},{96,32},{128,64},{160,96},{192,128},{224,1... | collective-permute-start | bytes 393224 | tf_op jit(solution)/shard_map/ppermute | solution.py:520
  65.6 2.3 %collective-permute-start.8 = (bf16[2,128,256]{2,1,0:T(8,128)(2,1)S(1)}, bf16[2,128,256]{2,1,0:T(8,128)(2,1)S(1)}, u32[]{:S(2)}, u32[]{:S(2)}) collective-permute-start(bf16[2,128,256]{2,1,0:T(8,128)(2,1)S(1)} %get-tuple-element.43), channel_id=1, source_target_pairs={{0,480},{32,448},{64,32},{96,0},{128,96},{160,64},{192,160},{224,1... | collective-permute-start | bytes 393224 | tf_op jit(solution)/shard_map/ppermute | solution.py:520
  67.9 2.2 %collective-permute-start.6 = (bf16[3,128,256]{2,1,0:T(8,128)(2,1)S(1)}, bf16[3,128,256]{2,1,0:T(8,128)(2,1)S(1)}, u32[]{:S(2)}, u32[]{:S(2)}) collective-permute-start(bf16[3,128,256]{2,1,0:T(8,128)(2,1)S(1)} %get-tuple-element.41), channel_id=1, source_target_pairs={{0,32},{32,0},{64,96},{96,64},{128,160},{160,128},{192,224},{224,1... | collective-permute-start | bytes 589832 | tf_op jit(solution)/shard_map/ppermute | solution.py:520
  70.1 0.0 collective-permute-done.4.same2
  70.1 0.0 collective-permute-done.5.cross2
  70.1 0.0 all-to-all-done.1.slots_in
  70.2 1.2 %gate.3 = (bf16[128,256]{1,0:T(8,128)(2,1)S(1)}, bf16[160,256]{1,0:T(8,128)(2,1)S(1)}, f32[16,256]{1,0:T(8,128)S(1)}) custom-call(bf16[3,128,256]{2,1,0:T(8,128)(2,1)S(1)} %get-tuple-element.28.keep_rest, bf16[5,128,256]{2,1,0:T(8,128)(2,1)S(1)} %collective-permute-done.given, f32[2,256,128]{2,1,0:T(8,128)S(1)} %get-tuple-element.44.attended, ...), custom_call_target="tpu_custom_call" | custom-call | tf_op jit(solution)/shard_map/gate/pallas_call | solution.py:31
  71.3 2.1 %collective-permute-start.9 = (bf16[160,256]{1,0:T(8,128)(2,1)S(1)}, bf16[160,256]{1,0:T(8,128)(2,1)S(1)}, u32[]{:S(2)}, u32[]{:S(2)}) collective-permute-start(bf16[160,256]{1,0:T(8,128)(2,1)S(1)} %get-tuple-element.49), channel_id=1, source_target_pairs={{0,32},{32,0},{64,96},{96,64},{128,160},{160,128},{192,224},{224,1... | collective-permute-start | bytes 245768 | tf_op jit(solution)/shard_map/ppermute | solution.py:520
  73.5 0.0 collective-permute-done.7.same1
  73.5 0.0 collective-permute-done.8.cross1
  73.5 0.0 collective-permute-done.6.swap_in
  73.5 1.0 %collective-permute-done.9.gate_in = bf16[160,256]{1,0:T(8,128)(2,1)S(1)} collective-permute-done((bf16[160,256]{1,0:T(8,128)(2,1)S(1)}, bf16[160,256]{1,0:T(8,128)(2,1)S(1)}, u32[]{:S(2)}, u32[]{:S(2)}) %collective-permute-start.9) | collective-permute-done | bytes 81952 | tf_op jit(solution)/shard_map/ppermute | solution.py:520
  74.5 0.9 %final.1 = (bf16[128,512]{1,0:T(8,128)(2,1)}, bf16[128,512]{1,0:T(8,128)(2,1)}, bf16[128,512]{1,0:T(8,128)(2,1)}, bf16[128,512]{1,0:T(8,128)(2,1)}, f32[16,512]{1,0:T(8,128)}) custom-call(bf16[128,256]{1,0:T(8,128)(2,1)S(1)} %get-tuple-element.37.dq_keep, f32[2,128,256]{2,1,0:T(8,128)S(1)} %far_sum.1.far_total, ...), custom_call_target="tpu_custom_call" | custom-call | tf_op jit(solution)/shard_map/final/pallas_call | solution.py:31
  (2 shorter events, 0.1 us)
Async XLA Ops:
  1.9 10.0 %collective-permute-start = (bf16[5,128,256]{2,1,0:T(8,128)(2,1)S(1)}, bf16[5,128,256]{2,1,0:T(8,128)(2,1)S(1)}, u32[]{:S(2)}, u32[]{:S(2)}) collective-permute-start(bf16[5,128,256]{2,1,0:T(8,128)(2,1)S(1)} %get-tuple-element.30), channel_id=1, source_target_pairs={{0,32},{32,0},{64,96},{96,64},{128,160},{160,128},{192,224},{224,1... | collective-permute-start | bytes 983048 | tf_op jit(solution)/shard_map/ppermute | solution.py:520
  12.0 25.5 %collective-permute-start.3 = (bf16[2,256,256]{2,1,0:T(8,128)(2,1)S(1)}, bf16[2,256,256]{2,1,0:T(8,128)(2,1)S(1)}, u32[]{:S(2)}, u32[]{:S(2)}) collective-permute-start(bf16[2,256,256]{2,1,0:T(8,128)(2,1)S(1)} %chip_kv.1), channel_id=1, source_target_pairs={{0,128},{32,160},{64,192},{96,224},{128,256},{160,288},{192,320},{... | collective-permute-start | bytes 786440 | tf_op jit(solution)/shard_map/ppermute | solution.py:520
  13.9 15.5 %collective-permute-start.2 = (bf16[2,128,256]{2,1,0:T(8,128)(2,1)S(1)}, bf16[2,128,256]{2,1,0:T(8,128)(2,1)S(1)}, u32[]{:S(2)}, u32[]{:S(2)}) collective-permute-start(bf16[2,128,256]{2,1,0:T(8,128)(2,1)S(1)} %get-tuple-element.31), channel_id=1, source_target_pairs={{0,96},{32,64},{64,160},{96,128},{128,224},{160,192},{192,288},{22... | collective-permute-start | bytes 393224 | tf_op jit(solution)/shard_map/ppermute | solution.py:520
  15.8 15.7 %collective-permute-start.1 = (bf16[2,128,256]{2,1,0:T(8,128)(2,1)S(1)}, bf16[2,128,256]{2,1,0:T(8,128)(2,1)S(1)}, u32[]{:S(2)}, u32[]{:S(2)}) collective-permute-start(bf16[2,128,256]{2,1,0:T(8,128)(2,1)S(1)} %get-tuple-element.29.keep_kv), channel_id=1, source_target_pairs={{0,64},{32,96},{64,128},{96,160},{128,192},{160,224},{192,256},{22... | collective-permute-start | bytes 393224 | tf_op jit(solution)/shard_map/ppermute | solution.py:520
  21.7 18.7 %all-to-all-start = ((bf16[8,16,256]{2,1,0:T(8,128)(2,1)}), bf16[8,16,256]{2,1,0:T(8,128)(2,1)S(1)}, u32[]{:S(2)}, u32[]{:S(2)}) async-start(bf16[8,16,256]{2,1,0:T(8,128)(2,1)} %get-tuple-element.36), calls=%async_computation | async-start | bytes 131072 | tf_op jit(solution)/shard_map/all_to_all | solution.py:526
  43.7 26.4 %collective-permute-start.4 = (bf16[2,128,256]{2,1,0:T(8,128)(2,1)S(1)}, bf16[2,128,256]{2,1,0:T(8,128)(2,1)S(1)}, u32[]{:S(2)}, u32[]{:S(2)}) collective-permute-start(bf16[2,128,256]{2,1,0:T(8,128)(2,1)S(1)} %get-tuple-element.39), channel_id=1, source_target_pairs={{0,384},{32,416},{64,448},{96,480},{128,0},{160,32},{192,64},{224,... | collective-permute-start | bytes 393224 | tf_op jit(solution)/shard_map/ppermute | solution.py:520
  47.4 22.7 %collective-permute-start.5 = (bf16[2,128,256]{2,1,0:T(8,128)(2,1)S(1)}, bf16[2,128,256]{2,1,0:T(8,128)(2,1)S(1)}, u32[]{:S(2)}, u32[]{:S(2)}) collective-permute-start(bf16[2,128,256]{2,1,0:T(8,128)(2,1)S(1)} %get-tuple-element.40), channel_id=1, source_target_pairs={{0,416},{32,384},{64,480},{96,448},{128,32},{160,0},{192,96},{224,... | collective-permute-start | bytes 393224 | tf_op jit(solution)/shard_map/ppermute | solution.py:520
  52.3 17.9 %all-to-all-start.1 = ((bf16[8,32,256]{2,1,0:T(8,128)(2,1)}), bf16[8,32,256]{2,1,0:T(8,128)(2,1)S(1)}, u32[]{:S(2)}, u32[]{:S(2)}) async-start(bf16[8,32,256]{2,1,0:T(8,128)(2,1)} %get-tuple-element.46), calls=%async_computation.1 | async-start | bytes 262144 | tf_op jit(solution)/shard_map/all_to_all | solution.py:526
  55.7 17.8 %collective-permute-start.7 = (bf16[2,128,256]{2,1,0:T(8,128)(2,1)S(1)}, bf16[2,128,256]{2,1,0:T(8,128)(2,1)S(1)}, u32[]{:S(2)}, u32[]{:S(2)}) collective-permute-start(bf16[2,128,256]{2,1,0:T(8,128)(2,1)S(1)} %get-tuple-element.42), channel_id=1, source_target_pairs={{0,448},{32,480},{64,0},{96,32},{128,64},{160,96},{192,128},{224,1... | collective-permute-start | bytes 393224 | tf_op jit(solution)/shard_map/ppermute | solution.py:520
  65.6 7.9 %collective-permute-start.8 = (bf16[2,128,256]{2,1,0:T(8,128)(2,1)S(1)}, bf16[2,128,256]{2,1,0:T(8,128)(2,1)S(1)}, u32[]{:S(2)}, u32[]{:S(2)}) collective-permute-start(bf16[2,128,256]{2,1,0:T(8,128)(2,1)S(1)} %get-tuple-element.43), channel_id=1, source_target_pairs={{0,480},{32,448},{64,32},{96,0},{128,96},{160,64},{192,160},{224,1... | collective-permute-start | bytes 393224 | tf_op jit(solution)/shard_map/ppermute | solution.py:520
  67.9 5.6 %collective-permute-start.6 = (bf16[3,128,256]{2,1,0:T(8,128)(2,1)S(1)}, bf16[3,128,256]{2,1,0:T(8,128)(2,1)S(1)}, u32[]{:S(2)}, u32[]{:S(2)}) collective-permute-start(bf16[3,128,256]{2,1,0:T(8,128)(2,1)S(1)} %get-tuple-element.41), channel_id=1, source_target_pairs={{0,32},{32,0},{64,96},{96,64},{128,160},{160,128},{192,224},{224,1... | collective-permute-start | bytes 589832 | tf_op jit(solution)/shard_map/ppermute | solution.py:520
  71.3 3.2 %collective-permute-start.9 = (bf16[160,256]{1,0:T(8,128)(2,1)S(1)}, bf16[160,256]{1,0:T(8,128)(2,1)S(1)}, u32[]{:S(2)}, u32[]{:S(2)}) collective-permute-start(bf16[160,256]{1,0:T(8,128)(2,1)S(1)} %get-tuple-element.49), channel_id=1, source_target_pairs={{0,32},{32,0},{64,96},{96,64},{128,160},{160,128},{192,224},{224,1... | collective-permute-start | bytes 245768 | tf_op jit(solution)/shard_map/ppermute | solution.py:520

commit v6 on v5

--- a/solution.py
+++ b/solution.py
@@ -214,30 +214,10 @@
 
 
 def forward_body(
-    keep_rest,
-    chip_kv,
-    given,
-    same1,
-    cross1,
-    far_kv,
-    delta,
-    totals,
-    params,
-    stats,
-    attended,
-    tail_totals,
-    slots,
-    qbuf,
-    kbuf,
-    vbuf,
-    tail_ref,
-    part_ref,
+    keep_rest, chip_kv, given, same1, cross1, far_kv, stats, attended, qbuf, kbuf, vbuf
 ):
     rows, width = keep_rest.shape[1:]
-    poles = totals.shape[0]
-    tokens = delta.shape[1]
-    steps = tokens // SUBS
-    chips = slots.shape[0]
+    tokens = 2 * rows
     core, chip = place()
     scale = 1.0 / math.sqrt(HEAD)
     assemble(core, keep_rest, chip_kv, given, same1, cross1, far_kv, qbuf, kbuf, vbuf)
@@ -269,6 +249,12 @@
                 .astype(F32)
             )
 
+
+def tail_body(attended, delta, totals, params, tail_totals, slots, tail_ref, part_ref):
+    poles, _, width = totals.shape
+    steps = delta.shape[1] // SUBS
+    chips = slots.shape[0]
+
     def tail_group(first_pole, lane_group, first_lane):
         rate = params[pl.ds(first_pole, GROUP), pl.ds(first_lane, LANES)]
         pole_at = pl.ds(first_pole, GROUP)
@@ -308,13 +294,11 @@
     totals,
     slots_in,
     params,
-    dq_keep,
-    dkv_keep,
-    swap_out,
+    dq,
+    dkv_chip,
+    out_far,
     out_same1,
     out_cross1,
-    out_same2,
-    out_cross2,
     incoming_all,
     qbuf,
     kbuf,
@@ -323,7 +307,6 @@
     adj32,
     dk_acc,
     dv_acc,
-    dqbuf,
 ):
     tokens, width = qbuf.shape
     rows = tokens // 2
@@ -385,7 +368,7 @@
             weight = lax.dot_general(value, adjoint, OVER_HEAD, preferred_element_type=F32)
             inner = jnp.sum(probability * weight, axis=0, keepdims=True)
             score_adjoint = (probability * (weight - inner) * scale).astype(BF16)
-            dqbuf[at_rows, at_head] = lax.dot_general(
+            dq[at_rows, at_head] = lax.dot_general(
                 score_adjoint, key, OVER_KEYS, preferred_element_type=F32
             ).astype(BF16)
             dk = jnp.dot(score_adjoint, query, preferred_element_type=F32)
@@ -403,18 +386,26 @@
                 dv_acc[last, at_head] = dv[edge:]
 
     for slot, acc in ((0, dk_acc), (1, dv_acc)):
-        out_same2[slot] = acc[pl.ds(mine, rows), :].astype(BF16)
-        out_cross2[slot] = acc[pl.ds(theirs, rows), :].astype(BF16)
+        out_far[slot] = acc[0:tokens, :].astype(BF16)
         out_same1[slot] = acc[pl.ds(mine + tokens, rows), :].astype(BF16)
         out_cross1[slot] = acc[pl.ds(theirs + tokens, rows), :].astype(BF16)
-        dkv_keep[slot] = acc[pl.ds(mine + 2 * tokens, rows), :]
-        swap_out[slot] = acc[pl.ds(theirs + 2 * tokens, rows), :].astype(BF16)
-    swap_out[2] = dqbuf[pl.ds(theirs, rows), :]
-    dq_keep[...] = dqbuf[pl.ds(mine, rows), :]
-
-
-def far_body(dkv_keep, same2, cross2, total):
-    total[...] = dkv_keep[...] + same2[...].astype(F32)
+        dkv_chip[slot] = acc[2 * tokens : 3 * tokens, :]
+
+
+def far_body(dkv_chip, far, dq, own_total, give):
+    rows = own_total.shape[1]
+    core, chip = place()
+    mine = pl.ds(pl.multiple_of(core * rows, rows), rows)
+    theirs = pl.ds(pl.multiple_of((1 - core) * rows, rows), rows)
+    for slot in range(2):
+        own_total[slot] = dkv_chip[slot, mine, :] + far[slot, mine, :].astype(F32)
+        give[slot] = (dkv_chip[slot, theirs, :] + far[slot, theirs, :].astype(F32)).astype(BF16)
+    give[2] = dq[theirs, :]
+
+
+def near_body(own_total, same1, cross1, own, other):
+    own[...] = (own_total[...] + same1[...].astype(F32)).astype(BF16)
+    other[...] = cross1[...].astype(F32)
 
 
 def gate_body(
@@ -425,7 +416,7 @@
     slots_in,
     incoming_all,
     params,
-    far_total,
+    partner,
     gate_keep,
     gate_give,
     res_keep,
@@ -454,6 +445,9 @@
     high = total.astype(BF16)
     gate_give[rows : rows + poles, :] = high
     gate_give[rows + poles : rows + 2 * poles, :] = (total - high.astype(F32)).astype(BF16)
+    first = rows + 2 * poles
+    for slot in range(3):
+        gate_give[first + slot * rows : first + (slot + 1) * rows, :] = partner[slot]
     for lane_group in range(width // LANES):
         gain = params[2 * poles : 2 * poles + 1, lane_group * LANES : (lane_group + 1) * LANES]
         mix32[lane_group] = gain * attended[lane_group]
@@ -487,21 +481,19 @@
         ).astype(BF16)
 
 
-def final_body(
-    dq_keep, far_total, swap_in, same1, cross1, cross2, gate_keep, gate_in, res_keep, dq, dk, dv, dgate, dres
-):
-    rows, width = dq_keep.shape
+def final_body(all_dq, own_part, other_part, gate_keep, gate_in, res_keep, dq, dk, dv, dgate, dres):
+    rows, width = gate_keep.shape
     poles = res_keep.shape[0]
-    own, other = halves(place()[0], width)
+    core, chip = place()
+    own, other = halves(core, width)
+    first = rows + 2 * poles
     for slot, out in ((0, dk), (1, dv)):
-        out[:, pl.ds(own, width)] = (
-            far_total[slot] + same1[slot].astype(F32)
+        out[:, pl.ds(own, width)] = own_part[slot]
+        out[:, pl.ds(other, width)] = (
+            gate_in[first + slot * rows : first + (slot + 1) * rows, :].astype(F32) + other_part[slot]
         ).astype(BF16)
-        out[:, pl.ds(other, width)] = (
-            swap_in[slot].astype(F32) + cross1[slot].astype(F32) + cross2[slot].astype(F32)
-        ).astype(BF16)
-    dq[:, pl.ds(own, width)] = dq_keep[...]
-    dq[:, pl.ds(other, width)] = swap_in[2]
+    dq[:, pl.ds(own, width)] = all_dq[pl.ds(pl.multiple_of(core * rows, rows), rows), :]
+    dq[:, pl.ds(other, width)] = gate_in[first + 2 * rows : first + 3 * rows, :]
     dgate[:, pl.ds(own, width)] = gate_keep[...]
     dgate[:, pl.ds(other, width)] = gate_in[0:rows, :]
     dres[:, pl.ds(own, width)] = res_keep[...]
@@ -576,28 +568,28 @@
         pltpu.VMEM((span, width), BF16),
         pltpu.VMEM((span, width), BF16),
     ]
-    stats, attended, tail_totals, tail_slots = call(
+    stats, attended = call(
         forward_body,
-        [
-            ((groups, 2, SUBS, rows), F32, True),
-            (split, F32, True),
-            (states, F32, True),
-            ((chips, 2 * poles, width), BF16, True),
-        ],
-        scratch=halo_buffers + [pltpu.VMEM((poles, width), F32), pltpu.VMEM((poles, width), F32)],
-        near=tuple(range(9)),
+        [((groups, 2, SUBS, rows), F32, True), (split, F32, True)],
+        scratch=halo_buffers,
+        near=tuple(range(6)),
         cost=EARLY,
         name="forward",
-    )(*halo, delta, totals, params)
+    )(*halo)
+    tail_totals, tail_slots = call(
+        tail_body,
+        [(states, F32, True), ((chips, 2 * poles, width), BF16, True)],
+        scratch=[pltpu.VMEM((poles, width), F32), pltpu.VMEM((poles, width), F32)],
+        near=(0, 1, 2, 3),
+        name="tail",
+    )(attended, delta, totals, params)
     tail_in = chip_exchange(tail_slots)
-    outs = call(
+    dq, dkv_chip, out_far, out_same1, out_cross1, incoming_all = call(
         backward_body,
         [
-            ((rows, width), BF16, True),
-            (pair, F32, True),
-            ((3, rows, width), BF16, True),
-            (pair, BF16, True),
-            (pair, BF16, True),
+            ((tokens, width), BF16, True),
+            ((2, tokens, width), F32, True),
+            ((2, tokens, width), BF16, True),
             (pair, BF16, True),
             (pair, BF16, True),
             ((chips, poles, width), F32, True),
@@ -608,31 +600,38 @@
             pltpu.VMEM(split, F32),
             pltpu.VMEM((span, width), F32),
             pltpu.VMEM((span, width), F32),
-            pltpu.VMEM((tokens, width), BF16),
         ],
         near=tuple(range(11)),
         name="backward",
     )(*halo, stats, delta, totals, head_in, params)
-    dq_keep, dkv_keep, swap_out, out_same1, out_cross1, out_same2, out_cross2, incoming_all = outs
-    back_same2 = chip_shift(out_same2, -2, False)
-    back_cross2 = chip_shift(out_cross2, -2, True)
+    back_far = chip_shift(out_far, -2, False)
     back_same1 = chip_shift(out_same1, -1, False)
     back_cross1 = chip_shift(out_cross1, -1, True)
-    swap_in = chip_shift(swap_out, 0, True)
-    (far_total,) = call(
-        far_body, [(pair, F32, True)], near=(0, 1, 2), cost=EARLY, name="far_sum"
-    )(dkv_keep, back_same2, back_cross2)
+    own_total, partner = call(
+        far_body,
+        [(pair, F32, True), ((3, rows, width), BF16, True)],
+        near=(0, 1, 2),
+        cost=EARLY,
+        name="far_sum",
+    )(dkv_chip, back_far, dq)
+    own_part, other_part = call(
+        near_body,
+        [(pair, BF16, True), (pair, F32, True)],
+        near=(0, 1, 2),
+        cost=EARLY,
+        name="near_sum",
+    )(own_total, back_same1, back_cross1)
     gate_keep, gate_give, res_keep = call(
         gate_body,
         [
             ((rows, width), BF16, True),
-            ((rows + 2 * poles, width), BF16, True),
+            ((4 * rows + 2 * poles, width), BF16, True),
             ((poles, width), F32, True),
         ],
         scratch=[pltpu.VMEM(split, F32), pltpu.VMEM((chips, poles, width), F32)],
         near=tuple(range(8)),
         name="gate",
-    )(keep_rest, given, attended, tail_totals, tail_in, incoming_all, params, far_total)
+    )(keep_rest, given, attended, tail_totals, tail_in, incoming_all, params, partner)
     gate_in = chip_shift(gate_give, 0, True)
     full = (rows, channels)
     wide = (full, BF16, False)
@@ -640,19 +639,9 @@
         call(
             final_body,
             [wide, wide, wide, wide, ((poles, channels), F32, False)],
-            near=tuple(range(9)),
+            near=tuple(range(6)),
             name="final",
-        )(
-            dq_keep,
-            far_total,
-            swap_in,
-            back_same1,
-            back_cross1,
-            back_cross2,
-            gate_keep,
-            gate_in,
-            res_keep,
-        )
+        )(dq, own_part, other_part, gate_keep, gate_in, res_keep)
     )
 
 

time: 75.9 us -> 77.6 us (1.022)
  waiting for transfers between devices: 10.8 us -> 23.4 us
  starting transfers between devices: 52.9 us -> 42.1 us
    all_to_all x2, waiting for transfers between devices: 0.01 us -> 12.8 us  [chip_exchange(): return lax.all_to_all(slots, 'ctx', 0, 0, axis_index_groups=groups)]
    ppermute x10 -> x8, starting transfers between devices: 42.3 us -> 31 us  [chip_shift(): return lax.ppermute(array, 'ctx', pairs)]
    ppermute x10 -> x8, waiting for transfers between devices: 10.8 us -> 10.6 us  [chip_shift(): return lax.ppermute(array, 'ctx', pairs)]
    pallas_call x8 -> x10, Pallas kernels: 10.9 us -> 10.8 us  [run(): pl.pallas_call(body, out_shape=[pltpu.VMEM(s, d) if local_out else jax.Sh...]
  transfers between devices with their start and end apart: 12 -> 10, of which waited for: 5 -> 6; matrix products, arithmetic and copies ran while one was open for 0% -> 0% of each run, Pallas kernels for 7% -> 7%
where the time goes in v6:
time: 77.6 us; the launch traced here: 77.1 us
  starting transfers between devices  42.1 us (54%)
  waiting for transfers between devices  23.4 us (30%)
  Pallas kernels  10.8 us (14%)
    ppermute x8, starting transfers between devices, chip_shift(): return lax.ppermute(array, 'ctx', pairs)  31 us
    all_to_all x2, waiting for transfers between devices, chip_exchange(): return lax.all_to_all(slots, 'ctx', 0, 0, axis_index_groups=groups)  12.8 us
    all_to_all x2, starting transfers between devices, chip_exchange(): return lax.all_to_all(slots, 'ctx', 0, 0, axis_index_groups=groups)  11.1 us
    pallas_call x10, Pallas kernels, run(): pl.pallas_call(body, out_shape=[pltpu.VMEM(s, d) if local_out else jax.Sh...  10.8 us
    ppermute x8, waiting for transfers between devices, chip_shift(): return lax.ppermute(array, 'ctx', pairs)  10.6 us
  transfers between devices with their start and end apart: 10, of which 6 were waited for; matrix products, arithmetic and copies ran while one was open for 0% of the time, Pallas kernels for 7%

profile of v6, /device:TPU:1, one launch (start us, length us, event | category | flops | bytes accessed | tf_op | source)
XLA Modules:
  0.0 77.1 jit_solution(16019676348377596443)
XLA Ops:
  0.6 1.3 %pack.1 = (bf16[2,128,256]{2,1,0:T(8,128)(2,1)S(1)}, bf16[2,128,256]{2,1,0:T(8,128)(2,1)S(1)}, bf16[3,128,256]{2,1,0:T(8,128)(2,1)S(1)}, bf16[5,128,256]{2,1,0:T(8,128)(2,1)S(1)}, f32[33,256]{1,0:T(8,128)S(1)}) custom-call(bf16[128,512]{1,0:T(8,128)(2,1)} %k.1, bf16[128,512]{1,0:T(8,128)(2,1)} %v.1, bf16[128,512]{1,0:T(8,128)(2,1)} %q.1, ...), custom_call_target="tpu_custom_call" | custom-call | tf_op jit(solution)/shard_map/pack/pallas_call | solution.py:31
  1.9 8.8 %collective-permute-start = (bf16[5,128,256]{2,1,0:T(8,128)(2,1)S(1)}, bf16[5,128,256]{2,1,0:T(8,128)(2,1)S(1)}, u32[]{:S(2)}, u32[]{:S(2)}) collective-permute-start(bf16[5,128,256]{2,1,0:T(8,128)(2,1)S(1)} %get-tuple-element.32), channel_id=1, source_target_pairs={{0,32},{32,0},{64,96},{96,64},{128,160},{160,128},{192,224},{224,1... | collective-permute-start | bytes 983048 | tf_op jit(solution)/shard_map/ppermute | solution.py:512
  10.7 1.2 %collective-permute-done.given = bf16[5,128,256]{2,1,0:T(8,128)(2,1)S(1)} collective-permute-done((bf16[5,128,256]{2,1,0:T(8,128)(2,1)S(1)}, bf16[5,128,256]{2,1,0:T(8,128)(2,1)S(1)}, u32[]{:S(2)}, u32[]{:S(2)}) %collective-permute-start) | collective-permute-done | bytes 327712 | tf_op jit(solution)/shard_map/ppermute | solution.py:512
  12.0 1.9 %collective-permute-start.3 = (bf16[2,256,256]{2,1,0:T(8,128)(2,1)S(1)}, bf16[2,256,256]{2,1,0:T(8,128)(2,1)S(1)}, u32[]{:S(2)}, u32[]{:S(2)}) collective-permute-start(bf16[2,256,256]{2,1,0:T(8,128)(2,1)S(1)} %chip_kv.1), channel_id=1, source_target_pairs={{0,128},{32,160},{64,192},{96,224},{128,256},{160,288},{192,320},{... | collective-permute-start | bytes 786440 | tf_op jit(solution)/shard_map/ppermute | solution.py:512
  13.9 1.9 %collective-permute-start.1 = (bf16[2,128,256]{2,1,0:T(8,128)(2,1)S(1)}, bf16[2,128,256]{2,1,0:T(8,128)(2,1)S(1)}, u32[]{:S(2)}, u32[]{:S(2)}) collective-permute-start(bf16[2,128,256]{2,1,0:T(8,128)(2,1)S(1)} %get-tuple-element.31.keep_kv), channel_id=1, source_target_pairs={{0,64},{32,96},{64,128},{96,160},{128,192},{160,224},{192,256},{22... | collective-permute-start | bytes 393224 | tf_op jit(solution)/shard_map/ppermute | solution.py:512
  15.8 4.8 %collective-permute-start.2 = (bf16[2,128,256]{2,1,0:T(8,128)(2,1)S(1)}, bf16[2,128,256]{2,1,0:T(8,128)(2,1)S(1)}, u32[]{:S(2)}, u32[]{:S(2)}) collective-permute-start(bf16[2,128,256]{2,1,0:T(8,128)(2,1)S(1)} %get-tuple-element.33), channel_id=1, source_target_pairs={{0,96},{32,64},{64,160},{96,128},{128,224},{160,192},{192,288},{22... | collective-permute-start | bytes 393224 | tf_op jit(solution)/shard_map/ppermute | solution.py:512
  20.6 1.3 %head_states.1 = (f32[2,256,128]{2,1,0:T(8,128)S(1)}, f32[16,8,256]{2,1,0:T(8,128)S(1)}, bf16[8,16,256]{2,1,0:T(8,128)(2,1)}) custom-call(bf16[3,128,256]{2,1,0:T(8,128)(2,1)S(1)} %get-tuple-element.30.keep_rest, bf16[5,128,256]{2,1,0:T(8,128)(2,1)S(1)} %collective-permute-done.given, f32[33,256]{1,0:T(8,128)S(1)} %get-tuple-element.35.params), custom_call_target="tpu_custom_call" | custom-call | tf_op jit(solution)/shard_map/head_states/pallas_call | solution.py:31
  22.0 7.3 %all-to-all-start = ((bf16[8,16,256]{2,1,0:T(8,128)(2,1)}), bf16[8,16,256]{2,1,0:T(8,128)(2,1)S(1)}, u32[]{:S(2)}, u32[]{:S(2)}) async-start(bf16[8,16,256]{2,1,0:T(8,128)(2,1)} %get-tuple-element.38), calls=%async_computation | async-start | bytes 131072 | tf_op jit(solution)/shard_map/all_to_all | solution.py:518
  29.2 0.0 collective-permute-done.1.same1
  29.2 2.5 %collective-permute-done.2.cross1 = bf16[2,128,256]{2,1,0:T(8,128)(2,1)S(1)} collective-permute-done((bf16[2,128,256]{2,1,0:T(8,128)(2,1)S(1)}, bf16[2,128,256]{2,1,0:T(8,128)(2,1)S(1)}, u32[]{:S(2)}, u32[]{:S(2)}) %collective-permute-start.2) | collective-permute-done | bytes 131104 | tf_op jit(solution)/shard_map/ppermute | solution.py:512
  31.7 5.7 %collective-permute-done.3.far_kv = bf16[2,256,256]{2,1,0:T(8,128)(2,1)S(1)} collective-permute-done((bf16[2,256,256]{2,1,0:T(8,128)(2,1)S(1)}, bf16[2,256,256]{2,1,0:T(8,128)(2,1)S(1)}, u32[]{:S(2)}, u32[]{:S(2)}) %collective-permute-start.3) | collective-permute-done | bytes 262176 | tf_op jit(solution)/shard_map/ppermute | solution.py:512
  37.5 1.0 %forward.1 = (f32[2,2,8,128]{3,2,1,0:T(8,128)S(1)}, f32[2,256,128]{2,1,0:T(8,128)S(1)}) custom-call(bf16[3,128,256]{2,1,0:T(8,128)(2,1)S(1)} %get-tuple-element.30.keep_rest, bf16[2,256,256]{2,1,0:T(8,128)(2,1)S(1)} %chip_kv.1, bf16[5,128,256]{2,1,0:T(8,128)(2,1)S(1)} %collective-permute-done.given, bf16[2,128,256]{2,1,0:T(8,128)(2,1)S(1)} %collective-permute-done.1.same1, ...), custom_call_target="tpu_custom_call" | custom-call | flops 99999997952 | bytes 100000000 | tf_op jit(solution)/shard_map/forward/pallas_call | solution.py:31
  38.5 1.8 %all-to-all-done.slots_in = bf16[8,16,256]{2,1,0:T(8,128)(2,1)S(1)} async-done(((bf16[8,16,256]{2,1,0:T(8,128)(2,1)}), bf16[8,16,256]{2,1,0:T(8,128)(2,1)S(1)}, u32[]{:S(2)}, u32[]{:S(2)}) %all-to-all-start) | async-done | bytes 65568 | tf_op jit(solution)/shard_map/all_to_all | solution.py:518
  40.3 3.1 %backward.1 = (bf16[256,256]{1,0:T(8,128)(2,1)S(1)}, f32[2,256,256]{2,1,0:T(8,128)S(1)}, bf16[2,256,256]{2,1,0:T(8,128)(2,1)S(1)}, bf16[2,128,256]{2,1,0:T(8,128...) custom-call(bf16[3,128,256]{2,1,0:T(8,128)(2,1)S(1)} %get-tuple-element.30.keep_rest, ...), custom_call_target="tpu_custom_call" | custom-call | tf_op jit(solution)/shard_map/backward/pallas_call | solution.py:31
  43.4 3.0 %collective-permute-start.4 = (bf16[2,256,256]{2,1,0:T(8,128)(2,1)S(1)}, bf16[2,256,256]{2,1,0:T(8,128)(2,1)S(1)}, u32[]{:S(2)}, u32[]{:S(2)}) collective-permute-start(bf16[2,256,256]{2,1,0:T(8,128)(2,1)S(1)} %get-tuple-element.41), channel_id=1, source_target_pairs={{0,384},{32,416},{64,448},{96,480},{128,0},{160,32},{192,64},{224,... | collective-permute-start | bytes 786440 | tf_op jit(solution)/shard_map/ppermute | solution.py:512
  46.5 3.3 %collective-permute-start.5 = (bf16[2,128,256]{2,1,0:T(8,128)(2,1)S(1)}, bf16[2,128,256]{2,1,0:T(8,128)(2,1)S(1)}, u32[]{:S(2)}, u32[]{:S(2)}) collective-permute-start(bf16[2,128,256]{2,1,0:T(8,128)(2,1)S(1)} %get-tuple-element.43), channel_id=1, source_target_pairs={{0,448},{32,480},{64,0},{96,32},{128,64},{160,96},{192,128},{224,1... | collective-permute-start | bytes 393224 | tf_op jit(solution)/shard_map/ppermute | solution.py:512
  49.8 3.6 %collective-permute-start.6 = (bf16[2,128,256]{2,1,0:T(8,128)(2,1)S(1)}, bf16[2,128,256]{2,1,0:T(8,128)(2,1)S(1)}, u32[]{:S(2)}, u32[]{:S(2)}) collective-permute-start(bf16[2,128,256]{2,1,0:T(8,128)(2,1)S(1)} %get-tuple-element.44), channel_id=1, source_target_pairs={{0,480},{32,448},{64,32},{96,0},{128,96},{160,64},{192,160},{224,1... | collective-permute-start | bytes 393224 | tf_op jit(solution)/shard_map/ppermute | solution.py:512
  53.5 2.0 %tail.1 = (f32[16,8,256]{2,1,0:T(8,128)S(1)}, bf16[8,32,256]{2,1,0:T(8,128)(2,1)}) custom-call(f32[2,256,128]{2,1,0:T(8,128)S(1)} %get-tuple-element.47.attended, f32[2,256,128]{2,1,0:T(8,128)S(1)} %get-tuple-element.36.delta, f32[16,8,256]{2,1,0:T(8,128)S(1)} %get-tuple-element.37.totals, f32[33,256]{1,0:T(8,128)S(1)} %get-tuple-element.35.params), custom_call_target="tpu_custom_call" | custom-call | tf_op jit(solution)/shard_map/tail/pallas_call | solution.py:31
  55.4 3.8 %all-to-all-start.1 = ((bf16[8,32,256]{2,1,0:T(8,128)(2,1)}), bf16[8,32,256]{2,1,0:T(8,128)(2,1)S(1)}, u32[]{:S(2)}, u32[]{:S(2)}) async-start(bf16[8,32,256]{2,1,0:T(8,128)(2,1)} %get-tuple-element.49), calls=%async_computation.1 | async-start | bytes 262144 | tf_op jit(solution)/shard_map/all_to_all | solution.py:518
  59.3 0.0 collective-permute-done.4.far
  59.3 0.1 far_sum.1
  59.3 11.0 %all-to-all-done.1.slots_in = bf16[8,32,256]{2,1,0:T(8,128)(2,1)S(1)} async-done(((bf16[8,32,256]{2,1,0:T(8,128)(2,1)}), bf16[8,32,256]{2,1,0:T(8,128)(2,1)S(1)}, u32[]{:S(2)}, u32[]{:S(2)}) %all-to-all-start.1) | async-done | bytes 131104 | tf_op jit(solution)/shard_map/all_to_all | solution.py:518
  70.4 1.2 %gate.3 = (bf16[128,256]{1,0:T(8,128)(2,1)S(1)}, bf16[544,256]{1,0:T(8,128)(2,1)S(1)}, f32[16,256]{1,0:T(8,128)S(1)}) custom-call(bf16[3,128,256]{2,1,0:T(8,128)(2,1)S(1)} %get-tuple-element.30.keep_rest, bf16[5,128,256]{2,1,0:T(8,128)(2,1)S(1)} %collective-permute-done.given, f32[2,256,128]{2,1,0:T(8,128)S(1)} %get-tuple-element.47.attended, ...), custom_call_target="tpu_custom_call" | custom-call | tf_op jit(solution)/shard_map/gate/pallas_call | solution.py:31
  71.5 3.6 %collective-permute-start.7 = (bf16[544,256]{1,0:T(8,128)(2,1)S(1)}, bf16[544,256]{1,0:T(8,128)(2,1)S(1)}, u32[]{:S(2)}, u32[]{:S(2)}) collective-permute-start(bf16[544,256]{1,0:T(8,128)(2,1)S(1)} %get-tuple-element.53), channel_id=1, source_target_pairs={{0,32},{32,0},{64,96},{96,64},{128,160},{160,128},{192,224},{224,1... | collective-permute-start | bytes 835592 | tf_op jit(solution)/shard_map/ppermute | solution.py:512
  75.1 0.0 collective-permute-done.5.same1
  75.1 0.0 collective-permute-done.6.cross1
  75.2 1.1 %collective-permute-done.7.gate_in = bf16[544,256]{1,0:T(8,128)(2,1)S(1)} collective-permute-done((bf16[544,256]{1,0:T(8,128)(2,1)S(1)}, bf16[544,256]{1,0:T(8,128)(2,1)S(1)}, u32[]{:S(2)}, u32[]{:S(2)}) %collective-permute-start.7) | collective-permute-done | bytes 278560 | tf_op jit(solution)/shard_map/ppermute | solution.py:512
  76.3 0.8 %final.1 = (bf16[128,512]{1,0:T(8,128)(2,1)}, bf16[128,512]{1,0:T(8,128)(2,1)}, bf16[128,512]{1,0:T(8,128)(2,1)}, bf16[128,512]{1,0:T(8,128)(2,1)}, f32[16,512]{1,0:T(8,128)}) custom-call(bf16[256,256]{1,0:T(8,128)(2,1)S(1)} %get-tuple-element.39.dq.all_dq, bf16[2,128,256]{2,1,0:T(8,128)(2,1)S(1)} %get-tuple-element.45.own_part, ...), custom_call_target="tpu_custom_call" | custom-call | tf_op jit(solution)/shard_map/final/pallas_call | solution.py:31
  (2 shorter events, 0.1 us)
Async XLA Ops:
  1.9 10.0 %collective-permute-start = (bf16[5,128,256]{2,1,0:T(8,128)(2,1)S(1)}, bf16[5,128,256]{2,1,0:T(8,128)(2,1)S(1)}, u32[]{:S(2)}, u32[]{:S(2)}) collective-permute-start(bf16[5,128,256]{2,1,0:T(8,128)(2,1)S(1)} %get-tuple-element.32), channel_id=1, source_target_pairs={{0,32},{32,0},{64,96},{96,64},{128,160},{160,128},{192,224},{224,1... | collective-permute-start | bytes 983048 | tf_op jit(solution)/shard_map/ppermute | solution.py:512
  12.0 25.5 %collective-permute-start.3 = (bf16[2,256,256]{2,1,0:T(8,128)(2,1)S(1)}, bf16[2,256,256]{2,1,0:T(8,128)(2,1)S(1)}, u32[]{:S(2)}, u32[]{:S(2)}) collective-permute-start(bf16[2,256,256]{2,1,0:T(8,128)(2,1)S(1)} %chip_kv.1), channel_id=1, source_target_pairs={{0,128},{32,160},{64,192},{96,224},{128,256},{160,288},{192,320},{... | collective-permute-start | bytes 786440 | tf_op jit(solution)/shard_map/ppermute | solution.py:512
  13.9 15.4 %collective-permute-start.1 = (bf16[2,128,256]{2,1,0:T(8,128)(2,1)S(1)}, bf16[2,128,256]{2,1,0:T(8,128)(2,1)S(1)}, u32[]{:S(2)}, u32[]{:S(2)}) collective-permute-start(bf16[2,128,256]{2,1,0:T(8,128)(2,1)S(1)} %get-tuple-element.31.keep_kv), channel_id=1, source_target_pairs={{0,64},{32,96},{64,128},{96,160},{128,192},{160,224},{192,256},{22... | collective-permute-start | bytes 393224 | tf_op jit(solution)/shard_map/ppermute | solution.py:512
  15.8 15.9 %collective-permute-start.2 = (bf16[2,128,256]{2,1,0:T(8,128)(2,1)S(1)}, bf16[2,128,256]{2,1,0:T(8,128)(2,1)S(1)}, u32[]{:S(2)}, u32[]{:S(2)}) collective-permute-start(bf16[2,128,256]{2,1,0:T(8,128)(2,1)S(1)} %get-tuple-element.33), channel_id=1, source_target_pairs={{0,96},{32,64},{64,160},{96,128},{128,224},{160,192},{192,288},{22... | collective-permute-start | bytes 393224 | tf_op jit(solution)/shard_map/ppermute | solution.py:512
  22.0 18.3 %all-to-all-start = ((bf16[8,16,256]{2,1,0:T(8,128)(2,1)}), bf16[8,16,256]{2,1,0:T(8,128)(2,1)S(1)}, u32[]{:S(2)}, u32[]{:S(2)}) async-start(bf16[8,16,256]{2,1,0:T(8,128)(2,1)} %get-tuple-element.38), calls=%async_computation | async-start | bytes 131072 | tf_op jit(solution)/shard_map/all_to_all | solution.py:518
  43.4 15.8 %collective-permute-start.4 = (bf16[2,256,256]{2,1,0:T(8,128)(2,1)S(1)}, bf16[2,256,256]{2,1,0:T(8,128)(2,1)S(1)}, u32[]{:S(2)}, u32[]{:S(2)}) collective-permute-start(bf16[2,256,256]{2,1,0:T(8,128)(2,1)S(1)} %get-tuple-element.41), channel_id=1, source_target_pairs={{0,384},{32,416},{64,448},{96,480},{128,0},{160,32},{192,64},{224,... | collective-permute-start | bytes 786440 | tf_op jit(solution)/shard_map/ppermute | solution.py:512
  46.5 28.6 %collective-permute-start.5 = (bf16[2,128,256]{2,1,0:T(8,128)(2,1)S(1)}, bf16[2,128,256]{2,1,0:T(8,128)(2,1)S(1)}, u32[]{:S(2)}, u32[]{:S(2)}) collective-permute-start(bf16[2,128,256]{2,1,0:T(8,128)(2,1)S(1)} %get-tuple-element.43), channel_id=1, source_target_pairs={{0,448},{32,480},{64,0},{96,32},{128,64},{160,96},{192,128},{224,1... | collective-permute-start | bytes 393224 | tf_op jit(solution)/shard_map/ppermute | solution.py:512
  49.8 25.3 %collective-permute-start.6 = (bf16[2,128,256]{2,1,0:T(8,128)(2,1)S(1)}, bf16[2,128,256]{2,1,0:T(8,128)(2,1)S(1)}, u32[]{:S(2)}, u32[]{:S(2)}) collective-permute-start(bf16[2,128,256]{2,1,0:T(8,128)(2,1)S(1)} %get-tuple-element.44), channel_id=1, source_target_pairs={{0,480},{32,448},{64,32},{96,0},{128,96},{160,64},{192,160},{224,1... | collective-permute-start | bytes 393224 | tf_op jit(solution)/shard_map/ppermute | solution.py:512
  55.4 14.9 %all-to-all-start.1 = ((bf16[8,32,256]{2,1,0:T(8,128)(2,1)}), bf16[8,32,256]{2,1,0:T(8,128)(2,1)S(1)}, u32[]{:S(2)}, u32[]{:S(2)}) async-start(bf16[8,32,256]{2,1,0:T(8,128)(2,1)} %get-tuple-element.49), calls=%async_computation.1 | async-start | bytes 262144 | tf_op jit(solution)/shard_map/all_to_all | solution.py:518
  71.5 4.7 %collective-permute-start.7 = (bf16[544,256]{1,0:T(8,128)(2,1)S(1)}, bf16[544,256]{1,0:T(8,128)(2,1)S(1)}, u32[]{:S(2)}, u32[]{:S(2)}) collective-permute-start(bf16[544,256]{1,0:T(8,128)(2,1)S(1)} %get-tuple-element.53), channel_id=1, source_target_pairs={{0,32},{32,0},{64,96},{96,64},{128,160},{160,128},{192,224},{224,1... | collective-permute-start | bytes 835592 | tf_op jit(solution)/shard_map/ppermute | solution.py:512

commit v7 on v6

--- a/solution.py
+++ b/solution.py
@@ -290,6 +290,7 @@
     cross1,
     far_kv,
     stats,
+    tail_totals,
     delta,
     totals,
     slots_in,
@@ -601,9 +602,9 @@
             pltpu.VMEM((span, width), F32),
             pltpu.VMEM((span, width), F32),
         ],
-        near=tuple(range(11)),
+        near=tuple(range(12)),
         name="backward",
-    )(*halo, stats, delta, totals, head_in, params)
+    )(*halo, stats, tail_totals, delta, totals, head_in, params)
     back_far = chip_shift(out_far, -2, False)
     back_same1 = chip_shift(out_same1, -1, False)
     back_cross1 = chip_shift(out_cross1, -1, True)

time: 77.6 us -> 75 us (0.966)
  the two profiles are of different devices: /device:TPU:1 before, /device:TPU:501 now
where the time goes in v7:
time: 75 us; the launch traced here: 74.5 us
  starting transfers between devices  47.1 us (63%)
  waiting for transfers between devices  15.8 us (21%)
  Pallas kernels  10.8 us (14%)
  between operations  0.78 us (1%)
    ppermute x8, starting transfers between devices, chip_shift(): return lax.ppermute(array, 'ctx', pairs)  27 us
    all_to_all x2, starting transfers between devices, chip_exchange(): return lax.all_to_all(slots, 'ctx', 0, 0, axis_index_groups=groups)  20.1 us
    pallas_call x10, Pallas kernels, run(): pl.pallas_call(body, out_shape=[pltpu.VMEM(s, d) if local_out else jax.Sh...  10.8 us
    all_to_all x2, waiting for transfers between devices, chip_exchange(): return lax.all_to_all(slots, 'ctx', 0, 0, axis_index_groups=groups)  9.77 us
    ppermute x8, waiting for transfers between devices, chip_shift(): return lax.ppermute(array, 'ctx', pairs)  6.04 us
  transfers between devices with their start and end apart: 10, of which 5 were waited for; matrix products, arithmetic and copies ran while one was open for 0% of the time, Pallas kernels for 7%

profile of v7, /device:TPU:501, one launch (start us, length us, event | category | flops | bytes accessed | tf_op | source)
XLA Modules:
  0.0 74.5 jit_solution(16112213733454855264)
XLA Ops:
  0.6 1.3 %pack.1 = (bf16[2,128,256]{2,1,0:T(8,128)(2,1)S(1)}, bf16[2,128,256]{2,1,0:T(8,128)(2,1)S(1)}, bf16[3,128,256]{2,1,0:T(8,128)(2,1)S(1)}, bf16[5,128,256]{2,1,0:T(8,128)(2,1)S(1)}, f32[33,256]{1,0:T(8,128)S(1)}) custom-call(bf16[128,512]{1,0:T(8,128)(2,1)} %k.1, bf16[128,512]{1,0:T(8,128)(2,1)} %v.1, bf16[128,512]{1,0:T(8,128)(2,1)} %q.1, ...), custom_call_target="tpu_custom_call" | custom-call | tf_op jit(solution)/shard_map/pack/pallas_call | solution.py:31
  1.9 2.6 %collective-permute-start = (bf16[5,128,256]{2,1,0:T(8,128)(2,1)S(1)}, bf16[5,128,256]{2,1,0:T(8,128)(2,1)S(1)}, u32[]{:S(2)}, u32[]{:S(2)}) collective-permute-start(bf16[5,128,256]{2,1,0:T(8,128)(2,1)S(1)} %get-tuple-element.32), channel_id=1, source_target_pairs={{0,32},{32,0},{64,96},{96,64},{128,160},{160,128},{192,224},{224,1... | collective-permute-start | bytes 983048 | tf_op jit(solution)/shard_map/ppermute | solution.py:513
  4.5 1.2 %collective-permute-done.given = bf16[5,128,256]{2,1,0:T(8,128)(2,1)S(1)} collective-permute-done((bf16[5,128,256]{2,1,0:T(8,128)(2,1)S(1)}, bf16[5,128,256]{2,1,0:T(8,128)(2,1)S(1)}, u32[]{:S(2)}, u32[]{:S(2)}) %collective-permute-start) | collective-permute-done | bytes 327712 | tf_op jit(solution)/shard_map/ppermute | solution.py:513
  5.8 6.1 %collective-permute-start.3 = (bf16[2,256,256]{2,1,0:T(8,128)(2,1)S(1)}, bf16[2,256,256]{2,1,0:T(8,128)(2,1)S(1)}, u32[]{:S(2)}, u32[]{:S(2)}) collective-permute-start(bf16[2,256,256]{2,1,0:T(8,128)(2,1)S(1)} %chip_kv.1), channel_id=1, source_target_pairs={{0,128},{32,160},{64,192},{96,224},{128,256},{160,288},{192,320},{... | collective-permute-start | bytes 786440 | tf_op jit(solution)/shard_map/ppermute | solution.py:513
  11.8 4.1 %collective-permute-start.2 = (bf16[2,128,256]{2,1,0:T(8,128)(2,1)S(1)}, bf16[2,128,256]{2,1,0:T(8,128)(2,1)S(1)}, u32[]{:S(2)}, u32[]{:S(2)}) collective-permute-start(bf16[2,128,256]{2,1,0:T(8,128)(2,1)S(1)} %get-tuple-element.33), channel_id=1, source_target_pairs={{0,96},{32,64},{64,160},{96,128},{128,224},{160,192},{192,288},{22... | collective-permute-start | bytes 393224 | tf_op jit(solution)/shard_map/ppermute | solution.py:513
  15.9 2.6 %collective-permute-start.1 = (bf16[2,128,256]{2,1,0:T(8,128)(2,1)S(1)}, bf16[2,128,256]{2,1,0:T(8,128)(2,1)S(1)}, u32[]{:S(2)}, u32[]{:S(2)}) collective-permute-start(bf16[2,128,256]{2,1,0:T(8,128)(2,1)S(1)} %get-tuple-element.31.keep_kv), channel_id=1, source_target_pairs={{0,64},{32,96},{64,128},{96,160},{128,192},{160,224},{192,256},{22... | collective-permute-start | bytes 393224 | tf_op jit(solution)/shard_map/ppermute | solution.py:513
  18.6 1.3 %head_states.1 = (f32[2,256,128]{2,1,0:T(8,128)S(1)}, f32[16,8,256]{2,1,0:T(8,128)S(1)}, bf16[8,16,256]{2,1,0:T(8,128)(2,1)}) custom-call(bf16[3,128,256]{2,1,0:T(8,128)(2,1)S(1)} %get-tuple-element.30.keep_rest, bf16[5,128,256]{2,1,0:T(8,128)(2,1)S(1)} %collective-permute-done.given, f32[33,256]{1,0:T(8,128)S(1)} %get-tuple-element.36.params), custom_call_target="tpu_custom_call" | custom-call | tf_op jit(solution)/shard_map/head_states/pallas_call | solution.py:31
  19.9 9.3 %all-to-all-start = ((bf16[8,16,256]{2,1,0:T(8,128)(2,1)}), bf16[8,16,256]{2,1,0:T(8,128)(2,1)S(1)}, u32[]{:S(2)}, u32[]{:S(2)}) async-start(bf16[8,16,256]{2,1,0:T(8,128)(2,1)} %get-tuple-element.40), calls=%async_computation | async-start | bytes 131072 | tf_op jit(solution)/shard_map/all_to_all | solution.py:519
  29.3 0.0 collective-permute-done.2.cross1
  29.3 0.0 collective-permute-done.1.same1
  29.3 0.0 collective-permute-done.3.far_kv
  29.3 1.0 %forward.1 = (f32[2,2,8,128]{3,2,1,0:T(8,128)S(1)}, f32[2,256,128]{2,1,0:T(8,128)S(1)}) custom-call(bf16[3,128,256]{2,1,0:T(8,128)(2,1)S(1)} %get-tuple-element.30.keep_rest, bf16[2,256,256]{2,1,0:T(8,128)(2,1)S(1)} %chip_kv.1, bf16[5,128,256]{2,1,0:T(8,128)(2,1)S(1)} %collective-permute-done.given, bf16[2,128,256]{2,1,0:T(8,128)(2,1)S(1)} %collective-permute-done.1.same1, ...), custom_call_target="tpu_custom_call" | custom-call | flops 99999997952 | bytes 100000000 | tf_op jit(solution)/shard_map/forward/pallas_call | solution.py:31
  30.3 2.0 %tail.1 = (f32[16,8,256]{2,1,0:T(8,128)S(1)}, bf16[8,32,256]{2,1,0:T(8,128)(2,1)}) custom-call(f32[2,256,128]{2,1,0:T(8,128)S(1)} %get-tuple-element.35.attended, f32[2,256,128]{2,1,0:T(8,128)S(1)} %get-tuple-element.37.delta, f32[16,8,256]{2,1,0:T(8,128)S(1)} %get-tuple-element.38.totals, f32[33,256]{1,0:T(8,128)S(1)} %get-tuple-element.36.params), custom_call_target="tpu_custom_call" | custom-call | tf_op jit(solution)/shard_map/tail/pallas_call | solution.py:31
  32.3 1.1 %all-to-all-done.slots_in = bf16[8,16,256]{2,1,0:T(8,128)(2,1)S(1)} async-done(((bf16[8,16,256]{2,1,0:T(8,128)(2,1)}), bf16[8,16,256]{2,1,0:T(8,128)(2,1)S(1)}, u32[]{:S(2)}, u32[]{:S(2)}) %all-to-all-start) | async-done | bytes 65568 | tf_op jit(solution)/shard_map/all_to_all | solution.py:519
  33.3 3.1 %backward.1 = (bf16[256,256]{1,0:T(8,128)(2,1)S(1)}, f32[2,256,256]{2,1,0:T(8,128)S(1)}, bf16[2,256,256]{2,1,0:T(8,128)(2,1)S(1)}, bf16[2,128,256]{2,1,0:T(8,128...) custom-call(bf16[3,128,256]{2,1,0:T(8,128)(2,1)S(1)} %get-tuple-element.30.keep_rest, ...), custom_call_target="tpu_custom_call" | custom-call | tf_op jit(solution)/shard_map/backward/pallas_call | solution.py:31
  36.5 1.9 %collective-permute-start.4 = (bf16[2,256,256]{2,1,0:T(8,128)(2,1)S(1)}, bf16[2,256,256]{2,1,0:T(8,128)(2,1)S(1)}, u32[]{:S(2)}, u32[]{:S(2)}) collective-permute-start(bf16[2,256,256]{2,1,0:T(8,128)(2,1)S(1)} %get-tuple-element.43), channel_id=1, source_target_pairs={{0,384},{32,416},{64,448},{96,480},{128,0},{160,32},{192,64},{224,... | collective-permute-start | bytes 786440 | tf_op jit(solution)/shard_map/ppermute | solution.py:513
  38.4 10.7 %all-to-all-start.1 = ((bf16[8,32,256]{2,1,0:T(8,128)(2,1)}), bf16[8,32,256]{2,1,0:T(8,128)(2,1)S(1)}, u32[]{:S(2)}, u32[]{:S(2)}) async-start(bf16[8,32,256]{2,1,0:T(8,128)(2,1)} %get-tuple-element.49), calls=%async_computation.1 | async-start | bytes 262144 | tf_op jit(solution)/shard_map/all_to_all | solution.py:519
  49.1 2.2 %collective-permute-start.5 = (bf16[2,128,256]{2,1,0:T(8,128)(2,1)S(1)}, bf16[2,128,256]{2,1,0:T(8,128)(2,1)S(1)}, u32[]{:S(2)}, u32[]{:S(2)}) collective-permute-start(bf16[2,128,256]{2,1,0:T(8,128)(2,1)S(1)} %get-tuple-element.45), channel_id=1, source_target_pairs={{0,448},{32,480},{64,0},{96,32},{128,64},{160,96},{192,128},{224,1... | collective-permute-start | bytes 393224 | tf_op jit(solution)/shard_map/ppermute | solution.py:513
  51.3 4.7 %collective-permute-start.6 = (bf16[2,128,256]{2,1,0:T(8,128)(2,1)S(1)}, bf16[2,128,256]{2,1,0:T(8,128)(2,1)S(1)}, u32[]{:S(2)}, u32[]{:S(2)}) collective-permute-start(bf16[2,128,256]{2,1,0:T(8,128)(2,1)S(1)} %get-tuple-element.46), channel_id=1, source_target_pairs={{0,480},{32,448},{64,32},{96,0},{128,96},{160,64},{192,160},{224,1... | collective-permute-start | bytes 393224 | tf_op jit(solution)/shard_map/ppermute | solution.py:513
  56.1 3.7 %collective-permute-done.4.far = bf16[2,256,256]{2,1,0:T(8,128)(2,1)S(1)} collective-permute-done((bf16[2,256,256]{2,1,0:T(8,128)(2,1)S(1)}, bf16[2,256,256]{2,1,0:T(8,128)(2,1)S(1)}, u32[]{:S(2)}, u32[]{:S(2)}) %collective-permute-start.4) | collective-permute-done | bytes 262176 | tf_op jit(solution)/shard_map/ppermute | solution.py:513
  59.8 8.7 %all-to-all-done.1.slots_in = bf16[8,32,256]{2,1,0:T(8,128)(2,1)S(1)} async-done(((bf16[8,32,256]{2,1,0:T(8,128)(2,1)}), bf16[8,32,256]{2,1,0:T(8,128)(2,1)S(1)}, u32[]{:S(2)}, u32[]{:S(2)}) %all-to-all-start.1) | async-done | bytes 131104 | tf_op jit(solution)/shard_map/all_to_all | solution.py:519
  68.5 1.2 %gate.3 = (bf16[128,256]{1,0:T(8,128)(2,1)S(1)}, bf16[544,256]{1,0:T(8,128)(2,1)S(1)}, f32[16,256]{1,0:T(8,128)S(1)}) custom-call(bf16[3,128,256]{2,1,0:T(8,128)(2,1)S(1)} %get-tuple-element.30.keep_rest, bf16[5,128,256]{2,1,0:T(8,128)(2,1)S(1)} %collective-permute-done.given, f32[2,256,128]{2,1,0:T(8,128)S(1)} %get-tuple-element.35.attended, ...), custom_call_target="tpu_custom_call" | custom-call | tf_op jit(solution)/shard_map/gate/pallas_call | solution.py:31
  69.7 2.8 %collective-permute-start.7 = (bf16[544,256]{1,0:T(8,128)(2,1)S(1)}, bf16[544,256]{1,0:T(8,128)(2,1)S(1)}, u32[]{:S(2)}, u32[]{:S(2)}) collective-permute-start(bf16[544,256]{1,0:T(8,128)(2,1)S(1)} %get-tuple-element.53), channel_id=1, source_target_pairs={{0,32},{32,0},{64,96},{96,64},{128,160},{160,128},{192,224},{224,1... | collective-permute-start | bytes 835592 | tf_op jit(solution)/shard_map/ppermute | solution.py:513
  72.5 0.0 collective-permute-done.5.same1
  72.5 0.0 collective-permute-done.6.cross1
  72.5 1.1 %collective-permute-done.7.gate_in = bf16[544,256]{1,0:T(8,128)(2,1)S(1)} collective-permute-done((bf16[544,256]{1,0:T(8,128)(2,1)S(1)}, bf16[544,256]{1,0:T(8,128)(2,1)S(1)}, u32[]{:S(2)}, u32[]{:S(2)}) %collective-permute-start.7) | collective-permute-done | bytes 278560 | tf_op jit(solution)/shard_map/ppermute | solution.py:513
  73.6 0.8 %final.1 = (bf16[128,512]{1,0:T(8,128)(2,1)}, bf16[128,512]{1,0:T(8,128)(2,1)}, bf16[128,512]{1,0:T(8,128)(2,1)}, bf16[128,512]{1,0:T(8,128)(2,1)}, f32[16,512]{1,0:T(8,128)}) custom-call(bf16[256,256]{1,0:T(8,128)(2,1)S(1)} %get-tuple-element.41.dq.all_dq, bf16[2,128,256]{2,1,0:T(8,128)(2,1)S(1)} %get-tuple-element.47.own_part, ...), custom_call_target="tpu_custom_call" | custom-call | tf_op jit(solution)/shard_map/final/pallas_call | solution.py:31
  (3 shorter events, 0.1 us)
Async XLA Ops:
  1.9 3.8 %collective-permute-start = (bf16[5,128,256]{2,1,0:T(8,128)(2,1)S(1)}, bf16[5,128,256]{2,1,0:T(8,128)(2,1)S(1)}, u32[]{:S(2)}, u32[]{:S(2)}) collective-permute-start(bf16[5,128,256]{2,1,0:T(8,128)(2,1)S(1)} %get-tuple-element.32), channel_id=1, source_target_pairs={{0,32},{32,0},{64,96},{96,64},{128,160},{160,128},{192,224},{224,1... | collective-permute-start | bytes 983048 | tf_op jit(solution)/shard_map/ppermute | solution.py:513
  5.8 23.5 %collective-permute-start.3 = (bf16[2,256,256]{2,1,0:T(8,128)(2,1)S(1)}, bf16[2,256,256]{2,1,0:T(8,128)(2,1)S(1)}, u32[]{:S(2)}, u32[]{:S(2)}) collective-permute-start(bf16[2,256,256]{2,1,0:T(8,128)(2,1)S(1)} %chip_kv.1), channel_id=1, source_target_pairs={{0,128},{32,160},{64,192},{96,224},{128,256},{160,288},{192,320},{... | collective-permute-start | bytes 786440 | tf_op jit(solution)/shard_map/ppermute | solution.py:513
  11.8 17.4 %collective-permute-start.2 = (bf16[2,128,256]{2,1,0:T(8,128)(2,1)S(1)}, bf16[2,128,256]{2,1,0:T(8,128)(2,1)S(1)}, u32[]{:S(2)}, u32[]{:S(2)}) collective-permute-start(bf16[2,128,256]{2,1,0:T(8,128)(2,1)S(1)} %get-tuple-element.33), channel_id=1, source_target_pairs={{0,96},{32,64},{64,160},{96,128},{128,224},{160,192},{192,288},{22... | collective-permute-start | bytes 393224 | tf_op jit(solution)/shard_map/ppermute | solution.py:513
  15.9 13.4 %collective-permute-start.1 = (bf16[2,128,256]{2,1,0:T(8,128)(2,1)S(1)}, bf16[2,128,256]{2,1,0:T(8,128)(2,1)S(1)}, u32[]{:S(2)}, u32[]{:S(2)}) collective-permute-start(bf16[2,128,256]{2,1,0:T(8,128)(2,1)S(1)} %get-tuple-element.31.keep_kv), channel_id=1, source_target_pairs={{0,64},{32,96},{64,128},{96,160},{128,192},{160,224},{192,256},{22... | collective-permute-start | bytes 393224 | tf_op jit(solution)/shard_map/ppermute | solution.py:513
  19.9 13.4 %all-to-all-start = ((bf16[8,16,256]{2,1,0:T(8,128)(2,1)}), bf16[8,16,256]{2,1,0:T(8,128)(2,1)S(1)}, u32[]{:S(2)}, u32[]{:S(2)}) async-start(bf16[8,16,256]{2,1,0:T(8,128)(2,1)} %get-tuple-element.40), calls=%async_computation | async-start | bytes 131072 | tf_op jit(solution)/shard_map/all_to_all | solution.py:519
  36.5 23.3 %collective-permute-start.4 = (bf16[2,256,256]{2,1,0:T(8,128)(2,1)S(1)}, bf16[2,256,256]{2,1,0:T(8,128)(2,1)S(1)}, u32[]{:S(2)}, u32[]{:S(2)}) collective-permute-start(bf16[2,256,256]{2,1,0:T(8,128)(2,1)S(1)} %get-tuple-element.43), channel_id=1, source_target_pairs={{0,384},{32,416},{64,448},{96,480},{128,0},{160,32},{192,64},{224,... | collective-permute-start | bytes 786440 | tf_op jit(solution)/shard_map/ppermute | solution.py:513
  38.4 30.1 %all-to-all-start.1 = ((bf16[8,32,256]{2,1,0:T(8,128)(2,1)}), bf16[8,32,256]{2,1,0:T(8,128)(2,1)S(1)}, u32[]{:S(2)}, u32[]{:S(2)}) async-start(bf16[8,32,256]{2,1,0:T(8,128)(2,1)} %get-tuple-element.49), calls=%async_computation.1 | async-start | bytes 262144 | tf_op jit(solution)/shard_map/all_to_all | solution.py:519
  49.1 23.3 %collective-permute-start.5 = (bf16[2,128,256]{2,1,0:T(8,128)(2,1)S(1)}, bf16[2,128,256]{2,1,0:T(8,128)(2,1)S(1)}, u32[]{:S(2)}, u32[]{:S(2)}) collective-permute-start(bf16[2,128,256]{2,1,0:T(8,128)(2,1)S(1)} %get-tuple-element.45), channel_id=1, source_target_pairs={{0,448},{32,480},{64,0},{96,32},{128,64},{160,96},{192,128},{224,1... | collective-permute-start | bytes 393224 | tf_op jit(solution)/shard_map/ppermute | solution.py:513
  51.3 21.2 %collective-permute-start.6 = (bf16[2,128,256]{2,1,0:T(8,128)(2,1)S(1)}, bf16[2,128,256]{2,1,0:T(8,128)(2,1)S(1)}, u32[]{:S(2)}, u32[]{:S(2)}) collective-permute-start(bf16[2,128,256]{2,1,0:T(8,128)(2,1)S(1)} %get-tuple-element.46), channel_id=1, source_target_pairs={{0,480},{32,448},{64,32},{96,0},{128,96},{160,64},{192,160},{224,1... | collective-permute-start | bytes 393224 | tf_op jit(solution)/shard_map/ppermute | solution.py:513
  69.7 3.9 %collective-permute-start.7 = (bf16[544,256]{1,0:T(8,128)(2,1)S(1)}, bf16[544,256]{1,0:T(8,128)(2,1)S(1)}, u32[]{:S(2)}, u32[]{:S(2)}) collective-permute-start(bf16[544,256]{1,0:T(8,128)(2,1)S(1)} %get-tuple-element.53), channel_id=1, source_target_pairs={{0,32},{32,0},{64,96},{96,64},{128,160},{160,128},{192,224},{224,1... | collective-permute-start | bytes 835592 | tf_op jit(solution)/shard_map/ppermute | solution.py:513

commit v8 on v7

--- a/solution.py
+++ b/solution.py
@@ -56,7 +56,7 @@
 
 
 def pack_body(
-    k, v, q, gate, cot, rates, residues, skip, keep_kv, give_kv, keep_rest, give_all, params, buf, small, sems
+    k, v, q, gate, cot, rates, residues, skip, keep_kv, keep_rest, give_all, params, buf, small, sems
 ):
     width = k.shape[1] // 2
     poles = rates.shape[0]
@@ -73,11 +73,9 @@
         copy.start()
     for n in range(len(arrays)):
         copies[n].wait()
-        give = buf[n, :, pl.ds(other, width)]
         keep = buf[n, :, pl.ds(own, width)]
-        give_all[n] = give
+        give_all[n] = buf[n, :, pl.ds(other, width)]
         if n < 2:
-            give_kv[n] = give
             keep_kv[n] = keep
         else:
             keep_rest[n - 2] = keep
@@ -192,7 +190,7 @@
         chip_kv[slot, pl.ds(pl.multiple_of((1 - core) * rows, rows), rows), :] = given[slot]
 
 
-def assemble(core, keep_rest, chip_kv, given, same1, cross1, far_kv, qbuf, kbuf, vbuf):
+def assemble(core, keep_rest, chip_kv, given, near_kv, far_kv, qbuf, kbuf, vbuf):
     rows = keep_rest.shape[1]
     tokens = 2 * rows
     mine = pl.multiple_of(core * rows, rows)
@@ -201,8 +199,7 @@
     qbuf[pl.ds(theirs, rows), :] = given[2]
     for slot, buf in ((0, kbuf), (1, vbuf)):
         buf[0:tokens, :] = far_kv[slot]
-        buf[pl.ds(mine + tokens, rows), :] = same1[slot]
-        buf[pl.ds(theirs + tokens, rows), :] = cross1[slot]
+        buf[tokens : 2 * tokens, :] = near_kv[slot]
         buf[2 * tokens : 3 * tokens, :] = chip_kv[slot]
 
 
@@ -214,13 +211,13 @@
 
 
 def forward_body(
-    keep_rest, chip_kv, given, same1, cross1, far_kv, stats, attended, qbuf, kbuf, vbuf
+    keep_rest, chip_kv, given, near_kv, far_kv, stats, attended, qbuf, kbuf, vbuf
 ):
     rows, width = keep_rest.shape[1:]
     tokens = 2 * rows
     core, chip = place()
     scale = 1.0 / math.sqrt(HEAD)
-    assemble(core, keep_rest, chip_kv, given, same1, cross1, far_kv, qbuf, kbuf, vbuf)
+    assemble(core, keep_rest, chip_kv, given, near_kv, far_kv, qbuf, kbuf, vbuf)
     span = (WIN + 1) * rows
     allowed = allowed_pairs(rows)
     for head in range(width // HEAD):
@@ -286,8 +283,7 @@
     keep_rest,
     chip_kv,
     given,
-    same1,
-    cross1,
+    near_kv,
     far_kv,
     stats,
     tail_totals,
@@ -318,7 +314,7 @@
     mine = pl.multiple_of(core * rows, rows)
     theirs = pl.multiple_of((1 - core) * rows, rows)
     scale = 1.0 / math.sqrt(HEAD)
-    assemble(core, keep_rest, chip_kv, given, same1, cross1, far_kv, qbuf, kbuf, vbuf)
+    assemble(core, keep_rest, chip_kv, given, near_kv, far_kv, qbuf, kbuf, vbuf)
 
     around(
         lambda n: slots_in[n].astype(F32),
@@ -531,10 +527,9 @@
     split = (groups, tokens, LANES)
     states = (poles, SUBS, width)
     span = (WIN + 2) * rows
-    keep_kv, give_kv, keep_rest, give_all, params = call(
+    keep_kv, keep_rest, give_all, params = call(
         pack_body,
         [
-            (pair, BF16, True),
             (pair, BF16, True),
             ((3, rows, width), BF16, True),
             ((5, rows, width), BF16, True),
@@ -553,8 +548,7 @@
         keep_kv, given
     )
     far_kv = chip_shift(chip_kv, 2, False)
-    same1 = chip_shift(keep_kv, 1, False)
-    cross1 = chip_shift(give_kv, 1, True)
+    near_kv = chip_shift(chip_kv, 1, False)
     delta, totals, head_slots = call(
         head_body,
         [(split, F32, True), (states, F32, True), ((chips, poles, width), BF16, True)],
@@ -563,7 +557,7 @@
         name="head_states",
     )(keep_rest, given, params)
     head_in = chip_exchange(head_slots)
-    halo = (keep_rest, chip_kv, given, same1, cross1, far_kv)
+    halo = (keep_rest, chip_kv, given, near_kv, far_kv)
     halo_buffers = [
         pltpu.VMEM((tokens, width), BF16),
         pltpu.VMEM((span, width), BF16),
@@ -573,7 +567,7 @@
         forward_body,
         [((groups, 2, SUBS, rows), F32, True), (split, F32, True)],
         scratch=halo_buffers,
-        near=tuple(range(6)),
+        near=tuple(range(5)),
         cost=EARLY,
         name="forward",
     )(*halo)
@@ -602,7 +596,7 @@
             pltpu.VMEM((span, width), F32),
             pltpu.VMEM((span, width), F32),
         ],
-        near=tuple(range(12)),
+        near=tuple(range(11)),
         name="backward",
     )(*halo, stats, tail_totals, delta, totals, head_in, params)
     back_far = chip_shift(out_far, -2, False)

time: 75 us -> 74.1 us (0.988)
  the two profiles are of different devices: /device:TPU:501 before, /device:TPU:97 now
where the time goes in v8:
time: 74.1 us; the launch traced here: 73.7 us
  starting transfers between devices  39.5 us (53%)
  waiting for transfers between devices  22.5 us (30%)
  Pallas kernels  10.8 us (15%)
  between operations  0.77 us (1%)
    ppermute x7, starting transfers between devices, chip_shift(): return lax.ppermute(array, 'ctx', pairs)  24.8 us
    all_to_all x2, starting transfers between devices, chip_exchange(): return lax.all_to_all(slots, 'ctx', 0, 0, axis_index_groups=groups)  14.7 us
    all_to_all x2, waiting for transfers between devices, chip_exchange(): return lax.all_to_all(slots, 'ctx', 0, 0, axis_index_groups=groups)  13.8 us
    pallas_call x10, Pallas kernels, run(): pl.pallas_call(body, out_shape=[pltpu.VMEM(s, d) if local_out else jax.Sh...  10.8 us
    ppermute x7, waiting for transfers between devices, chip_shift(): return lax.ppermute(array, 'ctx', pairs)  8.76 us
  transfers between devices with their start and end apart: 9, of which 5 were waited for; matrix products, arithmetic and copies ran while one was open for 0% of the time, Pallas kernels for 8%

profile of v8, /device:TPU:97, one launch (start us, length us, event | category | flops | bytes accessed | tf_op | source)
XLA Modules:
  0.0 73.7 jit_solution(14789051330539545298)
XLA Ops:
  0.6 1.3 %pack.1 = (bf16[2,128,256]{2,1,0:T(8,128)(2,1)S(1)}, bf16[3,128,256]{2,1,0:T(8,128)(2,1)S(1)}, bf16[5,128,256]{2,1,0:T(8,128)(2,1)S(1)}, f32[33,256]{1,0:T(8,128)S(1)}) custom-call(bf16[128,512]{1,0:T(8,128)(2,1)} %k.1, bf16[128,512]{1,0:T(8,128)(2,1)} %v.1, bf16[128,512]{1,0:T(8,128)(2,1)} %q.1, bf16[128,512]{1,0:T(8,128)(2,1)} %gate.2, ...), custom_call_target="tpu_custom_call" | custom-call | tf_op jit(solution)/shard_map/pack/pallas_call | solution.py:31
  1.9 2.6 %collective-permute-start = (bf16[5,128,256]{2,1,0:T(8,128)(2,1)S(1)}, bf16[5,128,256]{2,1,0:T(8,128)(2,1)S(1)}, u32[]{:S(2)}, u32[]{:S(2)}) collective-permute-start(bf16[5,128,256]{2,1,0:T(8,128)(2,1)S(1)} %get-tuple-element.31), channel_id=1, source_target_pairs={{0,32},{32,0},{64,96},{96,64},{128,160},{160,128},{192,224},{224,1... | collective-permute-start | bytes 983048 | tf_op jit(solution)/shard_map/ppermute | solution.py:509
  4.5 1.2 %collective-permute-done.given = bf16[5,128,256]{2,1,0:T(8,128)(2,1)S(1)} collective-permute-done((bf16[5,128,256]{2,1,0:T(8,128)(2,1)S(1)}, bf16[5,128,256]{2,1,0:T(8,128)(2,1)S(1)}, u32[]{:S(2)}, u32[]{:S(2)}) %collective-permute-start) | collective-permute-done | bytes 327712 | tf_op jit(solution)/shard_map/ppermute | solution.py:509
  5.8 6.1 %collective-permute-start.2 = (bf16[2,256,256]{2,1,0:T(8,128)(2,1)S(1)}, bf16[2,256,256]{2,1,0:T(8,128)(2,1)S(1)}, u32[]{:S(2)}, u32[]{:S(2)}) collective-permute-start(bf16[2,256,256]{2,1,0:T(8,128)(2,1)S(1)} %chip_kv.1), channel_id=1, source_target_pairs={{0,128},{32,160},{64,192},{96,224},{128,256},{160,288},{192,320},{... | collective-permute-start | bytes 786440 | tf_op jit(solution)/shard_map/ppermute | solution.py:509
  11.9 3.5 %collective-permute-start.1 = (bf16[2,256,256]{2,1,0:T(8,128)(2,1)S(1)}, bf16[2,256,256]{2,1,0:T(8,128)(2,1)S(1)}, u32[]{:S(2)}, u32[]{:S(2)}) collective-permute-start(bf16[2,256,256]{2,1,0:T(8,128)(2,1)S(1)} %chip_kv.1), channel_id=1, source_target_pairs={{0,64},{32,96},{64,128},{96,160},{128,192},{160,224},{192,256},{22... | collective-permute-start | bytes 786440 | tf_op jit(solution)/shard_map/ppermute | solution.py:509
  15.4 1.3 %head_states.1 = (f32[2,256,128]{2,1,0:T(8,128)S(1)}, f32[16,8,256]{2,1,0:T(8,128)S(1)}, bf16[8,16,256]{2,1,0:T(8,128)(2,1)}) custom-call(bf16[3,128,256]{2,1,0:T(8,128)(2,1)S(1)} %get-tuple-element.29.keep_rest, bf16[5,128,256]{2,1,0:T(8,128)(2,1)S(1)} %collective-permute-done.given, f32[33,256]{1,0:T(8,128)S(1)} %get-tuple-element.34.params), custom_call_target="tpu_custom_call" | custom-call | tf_op jit(solution)/shard_map/head_states/pallas_call | solution.py:31
  16.8 7.8 %all-to-all-start = ((bf16[8,16,256]{2,1,0:T(8,128)(2,1)}), bf16[8,16,256]{2,1,0:T(8,128)(2,1)S(1)}, u32[]{:S(2)}, u32[]{:S(2)}) async-start(bf16[8,16,256]{2,1,0:T(8,128)(2,1)} %get-tuple-element.38), calls=%async_computation | async-start | bytes 131072 | tf_op jit(solution)/shard_map/all_to_all | solution.py:515
  24.6 0.0 collective-permute-done.2.far_kv
  24.6 6.4 %collective-permute-done.1.near_kv = bf16[2,256,256]{2,1,0:T(8,128)(2,1)S(1)} collective-permute-done((bf16[2,256,256]{2,1,0:T(8,128)(2,1)S(1)}, bf16[2,256,256]{2,1,0:T(8,128)(2,1)S(1)}, u32[]{:S(2)}, u32[]{:S(2)}) %collective-permute-start.1) | collective-permute-done | bytes 262176 | tf_op jit(solution)/shard_map/ppermute | solution.py:509
  31.0 1.0 %forward.1 = (f32[2,2,8,128]{3,2,1,0:T(8,128)S(1)}, f32[2,256,128]{2,1,0:T(8,128)S(1)}) custom-call(bf16[3,128,256]{2,1,0:T(8,128)(2,1)S(1)} %get-tuple-element.29.keep_rest, bf16[2,256,256]{2,1,0:T(8,128)(2,1)S(1)} %chip_kv.1, bf16[5,128,256]{2,1,0:T(8,128)(2,1)S(1)} %collective-permute-done.given, bf16[2,256,256]{2,1,0:T(8,128)(2,1)S(1)} %collective-permute-done.1.near_kv, ...), custom_call_target="tpu_custom_call" | custom-call | flops 99999997952 | bytes 100000000 | tf_op jit(solution)/shard_map/forward/pallas_call | solution.py:31
  32.0 2.0 %tail.1 = (f32[16,8,256]{2,1,0:T(8,128)S(1)}, bf16[8,32,256]{2,1,0:T(8,128)(2,1)}) custom-call(f32[2,256,128]{2,1,0:T(8,128)S(1)} %get-tuple-element.33.attended, f32[2,256,128]{2,1,0:T(8,128)S(1)} %get-tuple-element.35.delta, f32[16,8,256]{2,1,0:T(8,128)S(1)} %get-tuple-element.36.totals, f32[33,256]{1,0:T(8,128)S(1)} %get-tuple-element.34.params), custom_call_target="tpu_custom_call" | custom-call | tf_op jit(solution)/shard_map/tail/pallas_call | solution.py:31
  34.0 0.7 all-to-all-done.slots_in
  34.7 3.1 %backward.1 = (bf16[256,256]{1,0:T(8,128)(2,1)S(1)}, f32[2,256,256]{2,1,0:T(8,128)S(1)}, bf16[2,256,256]{2,1,0:T(8,128)(2,1)S(1)}, bf16[2,128,256]{2,1,0:T(8,128...) custom-call(bf16[3,128,256]{2,1,0:T(8,128)(2,1)S(1)} %get-tuple-element.29.keep_rest, ...), custom_call_target="tpu_custom_call" | custom-call | tf_op jit(solution)/shard_map/backward/pallas_call | solution.py:31
  37.8 4.2 %collective-permute-start.3 = (bf16[2,256,256]{2,1,0:T(8,128)(2,1)S(1)}, bf16[2,256,256]{2,1,0:T(8,128)(2,1)S(1)}, u32[]{:S(2)}, u32[]{:S(2)}) collective-permute-start(bf16[2,256,256]{2,1,0:T(8,128)(2,1)S(1)} %get-tuple-element.41), channel_id=1, source_target_pairs={{0,384},{32,416},{64,448},{96,480},{128,0},{160,32},{192,64},{224,... | collective-permute-start | bytes 786440 | tf_op jit(solution)/shard_map/ppermute | solution.py:509
  42.0 6.9 %all-to-all-start.1 = ((bf16[8,32,256]{2,1,0:T(8,128)(2,1)}), bf16[8,32,256]{2,1,0:T(8,128)(2,1)S(1)}, u32[]{:S(2)}, u32[]{:S(2)}) async-start(bf16[8,32,256]{2,1,0:T(8,128)(2,1)} %get-tuple-element.47), calls=%async_computation.1 | async-start | bytes 262144 | tf_op jit(solution)/shard_map/all_to_all | solution.py:515
  48.9 2.2 %collective-permute-start.4 = (bf16[2,128,256]{2,1,0:T(8,128)(2,1)S(1)}, bf16[2,128,256]{2,1,0:T(8,128)(2,1)S(1)}, u32[]{:S(2)}, u32[]{:S(2)}) collective-permute-start(bf16[2,128,256]{2,1,0:T(8,128)(2,1)S(1)} %get-tuple-element.43), channel_id=1, source_target_pairs={{0,448},{32,480},{64,0},{96,32},{128,64},{160,96},{192,128},{224,1... | collective-permute-start | bytes 393224 | tf_op jit(solution)/shard_map/ppermute | solution.py:509
  51.1 3.8 %collective-permute-start.5 = (bf16[2,128,256]{2,1,0:T(8,128)(2,1)S(1)}, bf16[2,128,256]{2,1,0:T(8,128)(2,1)S(1)}, u32[]{:S(2)}, u32[]{:S(2)}) collective-permute-start(bf16[2,128,256]{2,1,0:T(8,128)(2,1)S(1)} %get-tuple-element.44), channel_id=1, source_target_pairs={{0,480},{32,448},{64,32},{96,0},{128,96},{160,64},{192,160},{224,1... | collective-permute-start | bytes 393224 | tf_op jit(solution)/shard_map/ppermute | solution.py:509
  54.9 0.0 collective-permute-done.3.far
  54.9 0.1 far_sum.1
  55.0 13.0 %all-to-all-done.1.slots_in = bf16[8,32,256]{2,1,0:T(8,128)(2,1)S(1)} async-done(((bf16[8,32,256]{2,1,0:T(8,128)(2,1)}), bf16[8,32,256]{2,1,0:T(8,128)(2,1)S(1)}, u32[]{:S(2)}, u32[]{:S(2)}) %all-to-all-start.1) | async-done | bytes 131104 | tf_op jit(solution)/shard_map/all_to_all | solution.py:515
  68.0 1.2 %gate.3 = (bf16[128,256]{1,0:T(8,128)(2,1)S(1)}, bf16[544,256]{1,0:T(8,128)(2,1)S(1)}, f32[16,256]{1,0:T(8,128)S(1)}) custom-call(bf16[3,128,256]{2,1,0:T(8,128)(2,1)S(1)} %get-tuple-element.29.keep_rest, bf16[5,128,256]{2,1,0:T(8,128)(2,1)S(1)} %collective-permute-done.given, f32[2,256,128]{2,1,0:T(8,128)S(1)} %get-tuple-element.33.attended, ...), custom_call_target="tpu_custom_call" | custom-call | tf_op jit(solution)/shard_map/gate/pallas_call | solution.py:31
  69.1 2.5 %collective-permute-start.6 = (bf16[544,256]{1,0:T(8,128)(2,1)S(1)}, bf16[544,256]{1,0:T(8,128)(2,1)S(1)}, u32[]{:S(2)}, u32[]{:S(2)}) collective-permute-start(bf16[544,256]{1,0:T(8,128)(2,1)S(1)} %get-tuple-element.51), channel_id=1, source_target_pairs={{0,32},{32,0},{64,96},{96,64},{128,160},{160,128},{192,224},{224,1... | collective-permute-start | bytes 835592 | tf_op jit(solution)/shard_map/ppermute | solution.py:509
  71.7 0.0 collective-permute-done.4.same1
  71.7 0.0 collective-permute-done.5.cross1
  71.7 1.1 %collective-permute-done.6.gate_in = bf16[544,256]{1,0:T(8,128)(2,1)S(1)} collective-permute-done((bf16[544,256]{1,0:T(8,128)(2,1)S(1)}, bf16[544,256]{1,0:T(8,128)(2,1)S(1)}, u32[]{:S(2)}, u32[]{:S(2)}) %collective-permute-start.6) | collective-permute-done | bytes 278560 | tf_op jit(solution)/shard_map/ppermute | solution.py:509
  72.8 0.8 %final.1 = (bf16[128,512]{1,0:T(8,128)(2,1)}, bf16[128,512]{1,0:T(8,128)(2,1)}, bf16[128,512]{1,0:T(8,128)(2,1)}, bf16[128,512]{1,0:T(8,128)(2,1)}, f32[16,512]{1,0:T(8,128)}) custom-call(bf16[256,256]{1,0:T(8,128)(2,1)S(1)} %get-tuple-element.39.dq.all_dq, bf16[2,128,256]{2,1,0:T(8,128)(2,1)S(1)} %get-tuple-element.45.own_part, ...), custom_call_target="tpu_custom_call" | custom-call | tf_op jit(solution)/shard_map/final/pallas_call | solution.py:31
  (2 shorter events, 0.1 us)
Async XLA Ops:
  1.9 3.8 %collective-permute-start = (bf16[5,128,256]{2,1,0:T(8,128)(2,1)S(1)}, bf16[5,128,256]{2,1,0:T(8,128)(2,1)S(1)}, u32[]{:S(2)}, u32[]{:S(2)}) collective-permute-start(bf16[5,128,256]{2,1,0:T(8,128)(2,1)S(1)} %get-tuple-element.31), channel_id=1, source_target_pairs={{0,32},{32,0},{64,96},{96,64},{128,160},{160,128},{192,224},{224,1... | collective-permute-start | bytes 983048 | tf_op jit(solution)/shard_map/ppermute | solution.py:509
  5.8 18.8 %collective-permute-start.2 = (bf16[2,256,256]{2,1,0:T(8,128)(2,1)S(1)}, bf16[2,256,256]{2,1,0:T(8,128)(2,1)S(1)}, u32[]{:S(2)}, u32[]{:S(2)}) collective-permute-start(bf16[2,256,256]{2,1,0:T(8,128)(2,1)S(1)} %chip_kv.1), channel_id=1, source_target_pairs={{0,128},{32,160},{64,192},{96,224},{128,256},{160,288},{192,320},{... | collective-permute-start | bytes 786440 | tf_op jit(solution)/shard_map/ppermute | solution.py:509
  11.9 19.1 %collective-permute-start.1 = (bf16[2,256,256]{2,1,0:T(8,128)(2,1)S(1)}, bf16[2,256,256]{2,1,0:T(8,128)(2,1)S(1)}, u32[]{:S(2)}, u32[]{:S(2)}) collective-permute-start(bf16[2,256,256]{2,1,0:T(8,128)(2,1)S(1)} %chip_kv.1), channel_id=1, source_target_pairs={{0,64},{32,96},{64,128},{96,160},{128,192},{160,224},{192,256},{22... | collective-permute-start | bytes 786440 | tf_op jit(solution)/shard_map/ppermute | solution.py:509
  16.8 17.9 %all-to-all-start = ((bf16[8,16,256]{2,1,0:T(8,128)(2,1)}), bf16[8,16,256]{2,1,0:T(8,128)(2,1)S(1)}, u32[]{:S(2)}, u32[]{:S(2)}) async-start(bf16[8,16,256]{2,1,0:T(8,128)(2,1)} %get-tuple-element.38), calls=%async_computation | async-start | bytes 131072 | tf_op jit(solution)/shard_map/all_to_all | solution.py:515
  37.8 17.0 %collective-permute-start.3 = (bf16[2,256,256]{2,1,0:T(8,128)(2,1)S(1)}, bf16[2,256,256]{2,1,0:T(8,128)(2,1)S(1)}, u32[]{:S(2)}, u32[]{:S(2)}) collective-permute-start(bf16[2,256,256]{2,1,0:T(8,128)(2,1)S(1)} %get-tuple-element.41), channel_id=1, source_target_pairs={{0,384},{32,416},{64,448},{96,480},{128,0},{160,32},{192,64},{224,... | collective-permute-start | bytes 786440 | tf_op jit(solution)/shard_map/ppermute | solution.py:509
  42.0 26.0 %all-to-all-start.1 = ((bf16[8,32,256]{2,1,0:T(8,128)(2,1)}), bf16[8,32,256]{2,1,0:T(8,128)(2,1)S(1)}, u32[]{:S(2)}, u32[]{:S(2)}) async-start(bf16[8,32,256]{2,1,0:T(8,128)(2,1)} %get-tuple-element.47), calls=%async_computation.1 | async-start | bytes 262144 | tf_op jit(solution)/shard_map/all_to_all | solution.py:515
  48.9 22.7 %collective-permute-start.4 = (bf16[2,128,256]{2,1,0:T(8,128)(2,1)S(1)}, bf16[2,128,256]{2,1,0:T(8,128)(2,1)S(1)}, u32[]{:S(2)}, u32[]{:S(2)}) collective-permute-start(bf16[2,128,256]{2,1,0:T(8,128)(2,1)S(1)} %get-tuple-element.43), channel_id=1, source_target_pairs={{0,448},{32,480},{64,0},{96,32},{128,64},{160,96},{192,128},{224,1... | collective-permute-start | bytes 393224 | tf_op jit(solution)/shard_map/ppermute | solution.py:509
  51.1 20.5 %collective-permute-start.5 = (bf16[2,128,256]{2,1,0:T(8,128)(2,1)S(1)}, bf16[2,128,256]{2,1,0:T(8,128)(2,1)S(1)}, u32[]{:S(2)}, u32[]{:S(2)}) collective-permute-start(bf16[2,128,256]{2,1,0:T(8,128)(2,1)S(1)} %get-tuple-element.44), channel_id=1, source_target_pairs={{0,480},{32,448},{64,32},{96,0},{128,96},{160,64},{192,160},{224,1... | collective-permute-start | bytes 393224 | tf_op jit(solution)/shard_map/ppermute | solution.py:509
  69.1 3.7 %collective-permute-start.6 = (bf16[544,256]{1,0:T(8,128)(2,1)S(1)}, bf16[544,256]{1,0:T(8,128)(2,1)S(1)}, u32[]{:S(2)}, u32[]{:S(2)}) collective-permute-start(bf16[544,256]{1,0:T(8,128)(2,1)S(1)} %get-tuple-element.51), channel_id=1, source_target_pairs={{0,32},{32,0},{64,96},{96,64},{128,160},{160,128},{192,224},{224,1... | collective-permute-start | bytes 835592 | tf_op jit(solution)/shard_map/ppermute | solution.py:509

commit v9 on v8

--- a/solution.py
+++ b/solution.py
@@ -294,8 +294,7 @@
     dq,
     dkv_chip,
     out_far,
-    out_same1,
-    out_cross1,
+    out_near,
     incoming_all,
     qbuf,
     kbuf,
@@ -384,25 +383,21 @@
 
     for slot, acc in ((0, dk_acc), (1, dv_acc)):
         out_far[slot] = acc[0:tokens, :].astype(BF16)
-        out_same1[slot] = acc[pl.ds(mine + tokens, rows), :].astype(BF16)
-        out_cross1[slot] = acc[pl.ds(theirs + tokens, rows), :].astype(BF16)
+        out_near[slot] = acc[tokens : 2 * tokens, :].astype(BF16)
         dkv_chip[slot] = acc[2 * tokens : 3 * tokens, :]
 
 
-def far_body(dkv_chip, far, dq, own_total, give):
-    rows = own_total.shape[1]
+def sum_body(dkv_chip, far, near, dq, own_part, give):
+    rows = own_part.shape[1]
     core, chip = place()
     mine = pl.ds(pl.multiple_of(core * rows, rows), rows)
     theirs = pl.ds(pl.multiple_of((1 - core) * rows, rows), rows)
-    for slot in range(2):
-        own_total[slot] = dkv_chip[slot, mine, :] + far[slot, mine, :].astype(F32)
-        give[slot] = (dkv_chip[slot, theirs, :] + far[slot, theirs, :].astype(F32)).astype(BF16)
+    for at, out in ((mine, own_part), (theirs, give)):
+        for slot in range(2):
+            out[slot] = (
+                dkv_chip[slot, at, :] + near[slot, at, :].astype(F32) + far[slot, at, :].astype(F32)
+            ).astype(BF16)
     give[2] = dq[theirs, :]
-
-
-def near_body(own_total, same1, cross1, own, other):
-    own[...] = (own_total[...] + same1[...].astype(F32)).astype(BF16)
-    other[...] = cross1[...].astype(F32)
 
 
 def gate_body(
@@ -478,7 +473,7 @@
         ).astype(BF16)
 
 
-def final_body(all_dq, own_part, other_part, gate_keep, gate_in, res_keep, dq, dk, dv, dgate, dres):
+def final_body(all_dq, own_part, gate_keep, gate_in, res_keep, dq, dk, dv, dgate, dres):
     rows, width = gate_keep.shape
     poles = res_keep.shape[0]
     core, chip = place()
@@ -486,9 +481,7 @@
     first = rows + 2 * poles
     for slot, out in ((0, dk), (1, dv)):
         out[:, pl.ds(own, width)] = own_part[slot]
-        out[:, pl.ds(other, width)] = (
-            gate_in[first + slot * rows : first + (slot + 1) * rows, :].astype(F32) + other_part[slot]
-        ).astype(BF16)
+        out[:, pl.ds(other, width)] = gate_in[first + slot * rows : first + (slot + 1) * rows, :]
     dq[:, pl.ds(own, width)] = all_dq[pl.ds(pl.multiple_of(core * rows, rows), rows), :]
     dq[:, pl.ds(other, width)] = gate_in[first + 2 * rows : first + 3 * rows, :]
     dgate[:, pl.ds(own, width)] = gate_keep[...]
@@ -579,14 +572,13 @@
         name="tail",
     )(attended, delta, totals, params)
     tail_in = chip_exchange(tail_slots)
-    dq, dkv_chip, out_far, out_same1, out_cross1, incoming_all = call(
+    dq, dkv_chip, out_far, out_near, incoming_all = call(
         backward_body,
         [
             ((tokens, width), BF16, True),
             ((2, tokens, width), F32, True),
             ((2, tokens, width), BF16, True),
-            (pair, BF16, True),
-            (pair, BF16, True),
+            ((2, tokens, width), BF16, True),
             ((chips, poles, width), F32, True),
         ],
         scratch=halo_buffers
@@ -600,22 +592,14 @@
         name="backward",
     )(*halo, stats, tail_totals, delta, totals, head_in, params)
     back_far = chip_shift(out_far, -2, False)
-    back_same1 = chip_shift(out_same1, -1, False)
-    back_cross1 = chip_shift(out_cross1, -1, True)
-    own_total, partner = call(
-        far_body,
-        [(pair, F32, True), ((3, rows, width), BF16, True)],
-        near=(0, 1, 2),
+    back_near = chip_shift(out_near, -1, False)
+    own_part, partner = call(
+        sum_body,
+        [(pair, BF16, True), ((3, rows, width), BF16, True)],
+        near=(0, 1, 2, 3),
         cost=EARLY,
-        name="far_sum",
-    )(dkv_chip, back_far, dq)
-    own_part, other_part = call(
-        near_body,
-        [(pair, BF16, True), (pair, F32, True)],
-        near=(0, 1, 2),
-        cost=EARLY,
-        name="near_sum",
-    )(own_total, back_same1, back_cross1)
+        name="block_sums",
+    )(dkv_chip, back_far, back_near, dq)
     gate_keep, gate_give, res_keep = call(
         gate_body,
         [
@@ -634,9 +618,9 @@
         call(
             final_body,
             [wide, wide, wide, wide, ((poles, channels), F32, False)],
-            near=tuple(range(6)),
+            near=tuple(range(5)),
             name="final",
-        )(dq, own_part, other_part, gate_keep, gate_in, res_keep)
+        )(dq, own_part, gate_keep, gate_in, res_keep)
     )
 
 

time: 74.1 us -> 77.8 us (1.050)
  the two profiles are of different devices: /device:TPU:97 before, /device:TPU:1 now
where the time goes in v9:
time: 77.8 us; the launch traced here: 77.3 us
  starting transfers between devices  33.6 us (43%)
  waiting for transfers between devices  32.3 us (42%)
  Pallas kernels  10.7 us (14%)
    ppermute x6, waiting for transfers between devices, chip_shift(): return lax.ppermute(array, 'ctx', pairs)  22.4 us
    ppermute x6, starting transfers between devices, chip_shift(): return lax.ppermute(array, 'ctx', pairs)  20.2 us
    all_to_all x2, starting transfers between devices, chip_exchange(): return lax.all_to_all(slots, 'ctx', 0, 0, axis_index_groups=groups)  13.4 us
    pallas_call x9, Pallas kernels, run(): pl.pallas_call(body, out_shape=[pltpu.VMEM(s, d) if local_out else jax.Sh...  10.7 us
    all_to_all x2, waiting for transfers between devices, chip_exchange(): return lax.all_to_all(slots, 'ctx', 0, 0, axis_index_groups=groups)  9.85 us
  transfers between devices with their start and end apart: 8, of which 6 were waited for; matrix products, arithmetic and copies ran while one was open for 0% of the time, Pallas kernels for 6%

profile of v9, /device:TPU:1, one launch (start us, length us, event | category | flops | bytes accessed | tf_op | source)
XLA Modules:
  0.0 77.3 jit_solution(10366420076106073002)
XLA Ops:
  0.6 1.3 %pack.1 = (bf16[2,128,256]{2,1,0:T(8,128)(2,1)S(1)}, bf16[3,128,256]{2,1,0:T(8,128)(2,1)S(1)}, bf16[5,128,256]{2,1,0:T(8,128)(2,1)S(1)}, f32[33,256]{1,0:T(8,128)S(1)}) custom-call(bf16[128,512]{1,0:T(8,128)(2,1)} %k.1, bf16[128,512]{1,0:T(8,128)(2,1)} %v.1, bf16[128,512]{1,0:T(8,128)(2,1)} %q.1, bf16[128,512]{1,0:T(8,128)(2,1)} %gate.2, ...), custom_call_target="tpu_custom_call" | custom-call | tf_op jit(solution)/shard_map/pack/pallas_call | solution.py:31
  1.9 8.8 %collective-permute-start = (bf16[5,128,256]{2,1,0:T(8,128)(2,1)S(1)}, bf16[5,128,256]{2,1,0:T(8,128)(2,1)S(1)}, u32[]{:S(2)}, u32[]{:S(2)}) collective-permute-start(bf16[5,128,256]{2,1,0:T(8,128)(2,1)S(1)} %get-tuple-element.28), channel_id=1, source_target_pairs={{0,32},{32,0},{64,96},{96,64},{128,160},{160,128},{192,224},{224,1... | collective-permute-start | bytes 983048 | tf_op jit(solution)/shard_map/ppermute | solution.py:502
  10.7 1.2 %collective-permute-done.given = bf16[5,128,256]{2,1,0:T(8,128)(2,1)S(1)} collective-permute-done((bf16[5,128,256]{2,1,0:T(8,128)(2,1)S(1)}, bf16[5,128,256]{2,1,0:T(8,128)(2,1)S(1)}, u32[]{:S(2)}, u32[]{:S(2)}) %collective-permute-start) | collective-permute-done | bytes 327712 | tf_op jit(solution)/shard_map/ppermute | solution.py:502
  12.0 1.9 %collective-permute-start.2 = (bf16[2,256,256]{2,1,0:T(8,128)(2,1)S(1)}, bf16[2,256,256]{2,1,0:T(8,128)(2,1)S(1)}, u32[]{:S(2)}, u32[]{:S(2)}) collective-permute-start(bf16[2,256,256]{2,1,0:T(8,128)(2,1)S(1)} %chip_kv.1), channel_id=1, source_target_pairs={{0,128},{32,160},{64,192},{96,224},{128,256},{160,288},{192,320},{... | collective-permute-start | bytes 786440 | tf_op jit(solution)/shard_map/ppermute | solution.py:502
  13.9 1.9 %collective-permute-start.1 = (bf16[2,256,256]{2,1,0:T(8,128)(2,1)S(1)}, bf16[2,256,256]{2,1,0:T(8,128)(2,1)S(1)}, u32[]{:S(2)}, u32[]{:S(2)}) collective-permute-start(bf16[2,256,256]{2,1,0:T(8,128)(2,1)S(1)} %chip_kv.1), channel_id=1, source_target_pairs={{0,64},{32,96},{64,128},{96,160},{128,192},{160,224},{192,256},{22... | collective-permute-start | bytes 786440 | tf_op jit(solution)/shard_map/ppermute | solution.py:502
  15.8 1.3 %head_states.1 = (f32[2,256,128]{2,1,0:T(8,128)S(1)}, f32[16,8,256]{2,1,0:T(8,128)S(1)}, bf16[8,16,256]{2,1,0:T(8,128)(2,1)}) custom-call(bf16[3,128,256]{2,1,0:T(8,128)(2,1)S(1)} %get-tuple-element.26.keep_rest, bf16[5,128,256]{2,1,0:T(8,128)(2,1)S(1)} %collective-permute-done.given, f32[33,256]{1,0:T(8,128)S(1)} %get-tuple-element.31.params), custom_call_target="tpu_custom_call" | custom-call | tf_op jit(solution)/shard_map/head_states/pallas_call | solution.py:31
  17.2 9.3 %all-to-all-start = ((bf16[8,16,256]{2,1,0:T(8,128)(2,1)}), bf16[8,16,256]{2,1,0:T(8,128)(2,1)S(1)}, u32[]{:S(2)}, u32[]{:S(2)}) async-start(bf16[8,16,256]{2,1,0:T(8,128)(2,1)} %get-tuple-element.35), calls=%async_computation | async-start | bytes 131072 | tf_op jit(solution)/shard_map/all_to_all | solution.py:508
  26.5 12.1 %collective-permute-done.2.far_kv = bf16[2,256,256]{2,1,0:T(8,128)(2,1)S(1)} collective-permute-done((bf16[2,256,256]{2,1,0:T(8,128)(2,1)S(1)}, bf16[2,256,256]{2,1,0:T(8,128)(2,1)S(1)}, u32[]{:S(2)}, u32[]{:S(2)}) %collective-permute-start.2) | collective-permute-done | bytes 262176 | tf_op jit(solution)/shard_map/ppermute | solution.py:502
  38.6 0.0 collective-permute-done.1.near_kv
  38.6 1.0 %forward.1 = (f32[2,2,8,128]{3,2,1,0:T(8,128)S(1)}, f32[2,256,128]{2,1,0:T(8,128)S(1)}) custom-call(bf16[3,128,256]{2,1,0:T(8,128)(2,1)S(1)} %get-tuple-element.26.keep_rest, bf16[2,256,256]{2,1,0:T(8,128)(2,1)S(1)} %chip_kv.1, bf16[5,128,256]{2,1,0:T(8,128)(2,1)S(1)} %collective-permute-done.given, bf16[2,256,256]{2,1,0:T(8,128)(2,1)S(1)} %collective-permute-done.1.near_kv, ...), custom_call_target="tpu_custom_call" | custom-call | flops 99999997952 | bytes 100000000 | tf_op jit(solution)/shard_map/forward/pallas_call | solution.py:31
  39.6 2.0 %tail.1 = (f32[16,8,256]{2,1,0:T(8,128)S(1)}, bf16[8,32,256]{2,1,0:T(8,128)(2,1)}) custom-call(f32[2,256,128]{2,1,0:T(8,128)S(1)} %get-tuple-element.30.attended, f32[2,256,128]{2,1,0:T(8,128)S(1)} %get-tuple-element.32.delta, f32[16,8,256]{2,1,0:T(8,128)S(1)} %get-tuple-element.33.totals, f32[33,256]{1,0:T(8,128)S(1)} %get-tuple-element.31.params), custom_call_target="tpu_custom_call" | custom-call | tf_op jit(solution)/shard_map/tail/pallas_call | solution.py:31
  41.5 0.0 all-to-all-done.slots_in
  41.5 3.1 %backward.1 = (bf16[256,256]{1,0:T(8,128)(2,1)S(1)}, f32[2,256,256]{2,1,0:T(8,128)S(1)}, bf16[2,256,256]{2,1,0:T(8,128)(2,1)S(1)}, bf16[2,256,256]{2,1,0:T(8,128)(2,1)S(1)}, f32[8,16,256]{2,1,0:T(8,128)S(1)}) custom-call(bf16[3,128,256]{2,1,0:T(8,128)(2,1)S(1)} %get-tuple-element.26.keep_rest, bf16[2,256,256]{2,1,0:T(8,128)(2,1)S(1)} %chip_kv.1, ...), custom_call_target="tpu_custom_call" | custom-call | tf_op jit(solution)/shard_map/backward/pallas_call | solution.py:31
  44.6 2.9 %collective-permute-start.3 = (bf16[2,256,256]{2,1,0:T(8,128)(2,1)S(1)}, bf16[2,256,256]{2,1,0:T(8,128)(2,1)S(1)}, u32[]{:S(2)}, u32[]{:S(2)}) collective-permute-start(bf16[2,256,256]{2,1,0:T(8,128)(2,1)S(1)} %get-tuple-element.38), channel_id=1, source_target_pairs={{0,384},{32,416},{64,448},{96,480},{128,0},{160,32},{192,64},{224,... | collective-permute-start | bytes 786440 | tf_op jit(solution)/shard_map/ppermute | solution.py:502
  47.5 2.3 %collective-permute-start.4 = (bf16[2,256,256]{2,1,0:T(8,128)(2,1)S(1)}, bf16[2,256,256]{2,1,0:T(8,128)(2,1)S(1)}, u32[]{:S(2)}, u32[]{:S(2)}) collective-permute-start(bf16[2,256,256]{2,1,0:T(8,128)(2,1)S(1)} %get-tuple-element.39), channel_id=1, source_target_pairs={{0,448},{32,480},{64,0},{96,32},{128,64},{160,96},{192,128},{224,1... | collective-permute-start | bytes 786440 | tf_op jit(solution)/shard_map/ppermute | solution.py:502
  49.8 4.1 %all-to-all-start.1 = ((bf16[8,32,256]{2,1,0:T(8,128)(2,1)}), bf16[8,32,256]{2,1,0:T(8,128)(2,1)S(1)}, u32[]{:S(2)}, u32[]{:S(2)}) async-start(bf16[8,32,256]{2,1,0:T(8,128)(2,1)} %get-tuple-element.41), calls=%async_computation.1 | async-start | bytes 262144 | tf_op jit(solution)/shard_map/all_to_all | solution.py:508
  53.9 5.4 %collective-permute-done.3.far = bf16[2,256,256]{2,1,0:T(8,128)(2,1)S(1)} collective-permute-done((bf16[2,256,256]{2,1,0:T(8,128)(2,1)S(1)}, bf16[2,256,256]{2,1,0:T(8,128)(2,1)S(1)}, u32[]{:S(2)}, u32[]{:S(2)}) %collective-permute-start.3) | collective-permute-done | bytes 262176 | tf_op jit(solution)/shard_map/ppermute | solution.py:502
  59.3 2.5 %collective-permute-done.4.near = bf16[2,256,256]{2,1,0:T(8,128)(2,1)S(1)} collective-permute-done((bf16[2,256,256]{2,1,0:T(8,128)(2,1)S(1)}, bf16[2,256,256]{2,1,0:T(8,128)(2,1)S(1)}, u32[]{:S(2)}, u32[]{:S(2)}) %collective-permute-start.4) | collective-permute-done | bytes 262176 | tf_op jit(solution)/shard_map/ppermute | solution.py:502
  61.8 0.1 block_sums.1
  61.9 9.8 %all-to-all-done.1.slots_in = bf16[8,32,256]{2,1,0:T(8,128)(2,1)S(1)} async-done(((bf16[8,32,256]{2,1,0:T(8,128)(2,1)}), bf16[8,32,256]{2,1,0:T(8,128)(2,1)S(1)}, u32[]{:S(2)}, u32[]{:S(2)}) %all-to-all-start.1) | async-done | bytes 131104 | tf_op jit(solution)/shard_map/all_to_all | solution.py:508
  71.8 1.2 %gate.3 = (bf16[128,256]{1,0:T(8,128)(2,1)S(1)}, bf16[544,256]{1,0:T(8,128)(2,1)S(1)}, f32[16,256]{1,0:T(8,128)S(1)}) custom-call(bf16[3,128,256]{2,1,0:T(8,128)(2,1)S(1)} %get-tuple-element.26.keep_rest, bf16[5,128,256]{2,1,0:T(8,128)(2,1)S(1)} %collective-permute-done.given, f32[2,256,128]{2,1,0:T(8,128)S(1)} %get-tuple-element.30.attended, ...), custom_call_target="tpu_custom_call" | custom-call | tf_op jit(solution)/shard_map/gate/pallas_call | solution.py:31
  72.9 2.4 %collective-permute-start.5 = (bf16[544,256]{1,0:T(8,128)(2,1)S(1)}, bf16[544,256]{1,0:T(8,128)(2,1)S(1)}, u32[]{:S(2)}, u32[]{:S(2)}) collective-permute-start(bf16[544,256]{1,0:T(8,128)(2,1)S(1)} %get-tuple-element.45), channel_id=1, source_target_pairs={{0,32},{32,0},{64,96},{96,64},{128,160},{160,128},{192,224},{224,1... | collective-permute-start | bytes 835592 | tf_op jit(solution)/shard_map/ppermute | solution.py:502
  75.3 1.2 %collective-permute-done.5.gate_in = bf16[544,256]{1,0:T(8,128)(2,1)S(1)} collective-permute-done((bf16[544,256]{1,0:T(8,128)(2,1)S(1)}, bf16[544,256]{1,0:T(8,128)(2,1)S(1)}, u32[]{:S(2)}, u32[]{:S(2)}) %collective-permute-start.5) | collective-permute-done | bytes 278560 | tf_op jit(solution)/shard_map/ppermute | solution.py:502
  76.5 0.8 %final.1 = (bf16[128,512]{1,0:T(8,128)(2,1)}, bf16[128,512]{1,0:T(8,128)(2,1)}, bf16[128,512]{1,0:T(8,128)(2,1)}, bf16[128,512]{1,0:T(8,128)(2,1)}, f32[16,512]{1,0:T(8,128)}) custom-call(bf16[256,256]{1,0:T(8,128)(2,1)S(1)} %get-tuple-element.36.dq.all_dq, bf16[2,128,256]{2,1,0:T(8,128)(2,1)S(1)} %get-tuple-element.40.own_part, ...), custom_call_target="tpu_custom_call" | custom-call | tf_op jit(solution)/shard_map/final/pallas_call | solution.py:31
  (1 shorter events, 0.0 us)
Async XLA Ops:
  1.9 10.0 %collective-permute-start = (bf16[5,128,256]{2,1,0:T(8,128)(2,1)S(1)}, bf16[5,128,256]{2,1,0:T(8,128)(2,1)S(1)}, u32[]{:S(2)}, u32[]{:S(2)}) collective-permute-start(bf16[5,128,256]{2,1,0:T(8,128)(2,1)S(1)} %get-tuple-element.28), channel_id=1, source_target_pairs={{0,32},{32,0},{64,96},{96,64},{128,160},{160,128},{192,224},{224,1... | collective-permute-start | bytes 983048 | tf_op jit(solution)/shard_map/ppermute | solution.py:502
  12.0 26.6 %collective-permute-start.2 = (bf16[2,256,256]{2,1,0:T(8,128)(2,1)S(1)}, bf16[2,256,256]{2,1,0:T(8,128)(2,1)S(1)}, u32[]{:S(2)}, u32[]{:S(2)}) collective-permute-start(bf16[2,256,256]{2,1,0:T(8,128)(2,1)S(1)} %chip_kv.1), channel_id=1, source_target_pairs={{0,128},{32,160},{64,192},{96,224},{128,256},{160,288},{192,320},{... | collective-permute-start | bytes 786440 | tf_op jit(solution)/shard_map/ppermute | solution.py:502
  13.9 24.7 %collective-permute-start.1 = (bf16[2,256,256]{2,1,0:T(8,128)(2,1)S(1)}, bf16[2,256,256]{2,1,0:T(8,128)(2,1)S(1)}, u32[]{:S(2)}, u32[]{:S(2)}) collective-permute-start(bf16[2,256,256]{2,1,0:T(8,128)(2,1)S(1)} %chip_kv.1), channel_id=1, source_target_pairs={{0,64},{32,96},{64,128},{96,160},{128,192},{160,224},{192,256},{22... | collective-permute-start | bytes 786440 | tf_op jit(solution)/shard_map/ppermute | solution.py:502
  17.2 24.4 %all-to-all-start = ((bf16[8,16,256]{2,1,0:T(8,128)(2,1)}), bf16[8,16,256]{2,1,0:T(8,128)(2,1)S(1)}, u32[]{:S(2)}, u32[]{:S(2)}) async-start(bf16[8,16,256]{2,1,0:T(8,128)(2,1)} %get-tuple-element.35), calls=%async_computation | async-start | bytes 131072 | tf_op jit(solution)/shard_map/all_to_all | solution.py:508
  44.6 14.7 %collective-permute-start.3 = (bf16[2,256,256]{2,1,0:T(8,128)(2,1)S(1)}, bf16[2,256,256]{2,1,0:T(8,128)(2,1)S(1)}, u32[]{:S(2)}, u32[]{:S(2)}) collective-permute-start(bf16[2,256,256]{2,1,0:T(8,128)(2,1)S(1)} %get-tuple-element.38), channel_id=1, source_target_pairs={{0,384},{32,416},{64,448},{96,480},{128,0},{160,32},{192,64},{224,... | collective-permute-start | bytes 786440 | tf_op jit(solution)/shard_map/ppermute | solution.py:502
  47.5 14.3 %collective-permute-start.4 = (bf16[2,256,256]{2,1,0:T(8,128)(2,1)S(1)}, bf16[2,256,256]{2,1,0:T(8,128)(2,1)S(1)}, u32[]{:S(2)}, u32[]{:S(2)}) collective-permute-start(bf16[2,256,256]{2,1,0:T(8,128)(2,1)S(1)} %get-tuple-element.39), channel_id=1, source_target_pairs={{0,448},{32,480},{64,0},{96,32},{128,64},{160,96},{192,128},{224,1... | collective-permute-start | bytes 786440 | tf_op jit(solution)/shard_map/ppermute | solution.py:502
  49.8 22.0 %all-to-all-start.1 = ((bf16[8,32,256]{2,1,0:T(8,128)(2,1)}), bf16[8,32,256]{2,1,0:T(8,128)(2,1)S(1)}, u32[]{:S(2)}, u32[]{:S(2)}) async-start(bf16[8,32,256]{2,1,0:T(8,128)(2,1)} %get-tuple-element.41), calls=%async_computation.1 | async-start | bytes 262144 | tf_op jit(solution)/shard_map/all_to_all | solution.py:508
  72.9 3.6 %collective-permute-start.5 = (bf16[544,256]{1,0:T(8,128)(2,1)S(1)}, bf16[544,256]{1,0:T(8,128)(2,1)S(1)}, u32[]{:S(2)}, u32[]{:S(2)}) collective-permute-start(bf16[544,256]{1,0:T(8,128)(2,1)S(1)} %get-tuple-element.45), channel_id=1, source_target_pairs={{0,32},{32,0},{64,96},{96,64},{128,160},{160,128},{192,224},{224,1... | collective-permute-start | bytes 835592 | tf_op jit(solution)/shard_map/ppermute | solution.py:502

commit v10 on v8

--- a/solution.py
+++ b/solution.py
@@ -400,16 +400,36 @@
     give[2] = dq[theirs, :]
 
 
-def near_body(own_total, same1, cross1, own, other):
-    own[...] = (own_total[...] + same1[...].astype(F32)).astype(BF16)
-    other[...] = cross1[...].astype(F32)
+def local_mix_body(attended, tail_totals, params, partner, mix):
+    poles, _, width = tail_totals.shape
+    steps = attended.shape[1] // SUBS
+    for lane_group in range(width // LANES):
+        gain = params[2 * poles : 2 * poles + 1, lane_group * LANES : (lane_group + 1) * LANES]
+        mix[lane_group] = gain * attended[lane_group]
+
+    def group(first_pole, lane_group, first_lane):
+        rate = params[pl.ds(first_pole, GROUP), pl.ds(first_lane, LANES)]
+        lam = rows3(jnp.exp(-rate))
+        mixing = rows3(
+            params[pl.ds(poles + first_pole, GROUP), pl.ds(first_lane, LANES)] * pole_weights(rate)
+        )
+        state = entering_earlier(
+            tail_totals[pl.ds(first_pole, GROUP), :, pl.ds(first_lane, LANES)],
+            jnp.zeros((GROUP, LANES), F32),
+            rows3(jnp.exp(-rate * steps)),
+        )
+        for j in range(steps):
+            at = pl.ds(j, SUBS, stride=steps)
+            state = lam * state + attended[lane_group, at, :][None]
+            mix[lane_group, at, :] = mix[lane_group, at, :] + jnp.sum(mixing * state, axis=0)
+
+    each_group(poles, width, group)
 
 
 def gate_body(
     keep_rest,
     given,
-    attended,
-    tail_totals,
+    local_mix,
     slots_in,
     incoming_all,
     params,
@@ -422,16 +442,38 @@
 ):
     core, chip = place()
     rows, width = keep_rest.shape[1:]
-    poles = tail_totals.shape[0]
-    tokens = attended.shape[1]
+    chips, poles, _ = incoming_all.shape
+    tokens = local_mix.shape[1]
     steps = tokens // SUBS
-    chips = slots_in.shape[0]
     mine = pl.multiple_of(core * rows, rows)
     theirs = pl.multiple_of((1 - core) * rows, rows)
     rate = params[0:poles, :]
     around(
         lambda n: slots_in[n, 0:poles, :].astype(F32), rate, tokens, list(range(chips)), arriving_ref
     )
+    mix32[...] = local_mix[...]
+
+    def group(first_pole, lane_group, first_lane):
+        rate = params[pl.ds(first_pole, GROUP), pl.ds(first_lane, LANES)]
+        lam = rows3(jnp.exp(-rate))
+        mixing = params[pl.ds(poles + first_pole, GROUP), pl.ds(first_lane, LANES)] * pole_weights(rate)
+        arriving = arriving_ref[chip, pl.ds(first_pole, GROUP), pl.ds(first_lane, LANES)]
+        blocks = block_ids((GROUP, SUBS, LANES)).astype(F32)
+        value = rows3(mixing * arriving) * jnp.exp(-rows3(rate) * (blocks * steps))
+        for j in range(steps):
+            at = pl.ds(j, SUBS, stride=steps)
+            value = lam * value
+            mix32[lane_group, at, :] = mix32[lane_group, at, :] + jnp.sum(value, axis=0)
+
+    each_group(poles, width, group)
+    for lane_group in range(width // LANES):
+        lanes = slice(lane_group * LANES, (lane_group + 1) * LANES)
+        gate_keep[:, lanes] = (
+            keep_rest[2, :, lanes].astype(F32) * mix32[lane_group, pl.ds(mine, rows), :]
+        ).astype(BF16)
+        gate_give[0:rows, lanes] = (
+            given[4, :, lanes].astype(F32) * mix32[lane_group, pl.ds(theirs, rows), :]
+        ).astype(BF16)
     parts = slots_in[0, poles : 2 * poles, :].astype(F32)
     crossed = slots_in[0, 0:poles, :].astype(F32) * incoming_all[0]
     for n in range(1, chips):
@@ -442,55 +484,28 @@
     high = total.astype(BF16)
     gate_give[rows : rows + poles, :] = high
     gate_give[rows + poles : rows + 2 * poles, :] = (total - high.astype(F32)).astype(BF16)
-    first = rows + 2 * poles
-    for slot in range(3):
-        gate_give[first + slot * rows : first + (slot + 1) * rows, :] = partner[slot]
-    for lane_group in range(width // LANES):
-        gain = params[2 * poles : 2 * poles + 1, lane_group * LANES : (lane_group + 1) * LANES]
-        mix32[lane_group] = gain * attended[lane_group]
-
-    def group(first_pole, lane_group, first_lane):
-        rate = params[pl.ds(first_pole, GROUP), pl.ds(first_lane, LANES)]
-        lam = rows3(jnp.exp(-rate))
-        mixing = rows3(
-            params[pl.ds(poles + first_pole, GROUP), pl.ds(first_lane, LANES)] * pole_weights(rate)
-        )
-        lane_at = pl.ds(first_lane, LANES)
-        pole_at = pl.ds(first_pole, GROUP)
-        state = entering_earlier(
-            tail_totals[pole_at, :, lane_at],
-            arriving_ref[chip, pole_at, lane_at],
-            rows3(jnp.exp(-rate * steps)),
-        )
-        for j in range(steps):
-            at = pl.ds(j, SUBS, stride=steps)
-            state = lam * state + attended[lane_group, at, :][None]
-            mix32[lane_group, at, :] = mix32[lane_group, at, :] + jnp.sum(mixing * state, axis=0)
-
-    each_group(poles, width, group)
-    for lane_group in range(width // LANES):
-        lanes = slice(lane_group * LANES, (lane_group + 1) * LANES)
-        gate_keep[:, lanes] = (
-            keep_rest[2, :, lanes].astype(F32) * mix32[lane_group, pl.ds(mine, rows), :]
-        ).astype(BF16)
-        gate_give[0:rows, lanes] = (
-            given[4, :, lanes].astype(F32) * mix32[lane_group, pl.ds(theirs, rows), :]
-        ).astype(BF16)
-
-
-def final_body(all_dq, own_part, other_part, gate_keep, gate_in, res_keep, dq, dk, dv, dgate, dres):
+
+
+def near_body(own_total, same1, cross1, own, other):
+    own[...] = (own_total[...] + same1[...].astype(F32)).astype(BF16)
+    other[...] = cross1[...].astype(F32)
+
+
+def block_body(all_dq, own_part, other_part, swapped, dq, dk, dv):
+    _, rows, width = own_part.shape
+    core, chip = place()
+    own, other = halves(core, width)
+    for slot, out in ((0, dk), (1, dv)):
+        out[:, pl.ds(own, width)] = own_part[slot]
+        out[:, pl.ds(other, width)] = (swapped[slot].astype(F32) + other_part[slot]).astype(BF16)
+    dq[:, pl.ds(own, width)] = all_dq[pl.ds(pl.multiple_of(core * rows, rows), rows), :]
+    dq[:, pl.ds(other, width)] = swapped[2]
+
+
+def final_body(gate_keep, gate_in, res_keep, dgate, dres):
     rows, width = gate_keep.shape
     poles = res_keep.shape[0]
-    core, chip = place()
-    own, other = halves(core, width)
-    first = rows + 2 * poles
-    for slot, out in ((0, dk), (1, dv)):
-        out[:, pl.ds(own, width)] = own_part[slot]
-        out[:, pl.ds(other, width)] = (
-            gate_in[first + slot * rows : first + (slot + 1) * rows, :].astype(F32) + other_part[slot]
-        ).astype(BF16)
-    dq[:, pl.ds(own, width)] = all_dq[pl.ds(pl.multiple_of(core * rows, rows), rows), :]
-    dq[:, pl.ds(other, width)] = gate_in[first + 2 * rows : first + 3 * rows, :]
+    own, other = halves(place()[0], width)
     dgate[:, pl.ds(own, width)] = gate_keep[...]
     dgate[:, pl.ds(other, width)] = gate_in[0:rows, :]
     dres[:, pl.ds(own, width)] = res_keep[...]
@@ -609,6 +624,23 @@
         cost=EARLY,
         name="far_sum",
     )(dkv_chip, back_far, dq)
+    (local_mix,) = call(local_mix_body, [(split, F32, True)], near=(0, 1, 2, 3), name="local_mix")(
+        attended, tail_totals, params, partner
+    )
+    gate_keep, gate_give, res_keep = call(
+        gate_body,
+        [
+            ((rows, width), BF16, True),
+            ((rows + 2 * poles, width), BF16, True),
+            ((poles, width), F32, True),
+        ],
+        scratch=[pltpu.VMEM(split, F32), pltpu.VMEM((chips, poles, width), F32)],
+        near=tuple(range(7)),
+        name="gate",
+    )(keep_rest, given, local_mix, tail_in, incoming_all, params, partner)
+    swapped = chip_shift(partner, 0, True)
+    gate_in = chip_shift(gate_give, 0, True)
+    wide = ((rows, channels), BF16, False)
     own_part, other_part = call(
         near_body,
         [(pair, BF16, True), (pair, F32, True)],
@@ -616,28 +648,13 @@
         cost=EARLY,
         name="near_sum",
     )(own_total, back_same1, back_cross1)
-    gate_keep, gate_give, res_keep = call(
-        gate_body,
-        [
-            ((rows, width), BF16, True),
-            ((4 * rows + 2 * poles, width), BF16, True),
-            ((poles, width), F32, True),
-        ],
-        scratch=[pltpu.VMEM(split, F32), pltpu.VMEM((chips, poles, width), F32)],
-        near=tuple(range(8)),
-        name="gate",
-    )(keep_rest, given, attended, tail_totals, tail_in, incoming_all, params, partner)
-    gate_in = chip_shift(gate_give, 0, True)
-    full = (rows, channels)
-    wide = (full, BF16, False)
-    return tuple(
-        call(
-            final_body,
-            [wide, wide, wide, wide, ((poles, channels), F32, False)],
-            near=tuple(range(6)),
-            name="final",
-        )(dq, own_part, other_part, gate_keep, gate_in, res_keep)
+    dq, dk, dv = call(block_body, [wide, wide, wide], near=tuple(range(4)), name="blocks")(
+        dq, own_part, other_part, swapped
     )
+    dgate, dres = call(
+        final_body, [wide, ((poles, channels), F32, False)], near=(0, 1, 2), name="final"
+    )(gate_keep, gate_in, res_keep)
+    return dq, dk, dv, dgate, dres
 
 
 def solution(mesh):

time: 74.1 us -> 73.4 us (level)
  the two profiles are of different devices: /device:TPU:97 before, /device:TPU:1 now
where the time goes in v10:
time: 73.4 us; the launch traced here: 72.5 us
  starting transfers between devices  46.2 us (63%)
  waiting for transfers between devices  13.4 us (18%)
  Pallas kernels  12.2 us (17%)
  between operations  0.8 us (1%)
    ppermute x8, starting transfers between devices, chip_shift(): return lax.ppermute(array, 'ctx', pairs)  33.4 us
    ppermute x8, waiting for transfers between devices, chip_shift(): return lax.ppermute(array, 'ctx', pairs)  13.4 us
    all_to_all x2, starting transfers between devices, chip_exchange(): return lax.all_to_all(slots, 'ctx', 0, 0, axis_index_groups=groups)  12.7 us
    pallas_call x12, Pallas kernels, run(): pl.pallas_call(body, out_shape=[pltpu.VMEM(s, d) if local_out else jax.Sh...  12.2 us
  transfers between devices with their start and end apart: 10, of which 2 were waited for; matrix products, arithmetic and copies ran while one was open for 0% of the time, Pallas kernels for 10%

profile of v10, /device:TPU:1, one launch (start us, length us, event | category | flops | bytes accessed | tf_op | source)
XLA Modules:
  0.0 72.5 jit_solution(10508685668213740618)
XLA Ops:
  0.6 1.3 %pack.1 = (bf16[2,128,256]{2,1,0:T(8,128)(2,1)S(1)}, bf16[3,128,256]{2,1,0:T(8,128)(2,1)S(1)}, bf16[5,128,256]{2,1,0:T(8,128)(2,1)S(1)}, f32[33,256]{1,0:T(8,128)S(1)}) custom-call(bf16[128,512]{1,0:T(8,128)(2,1)} %k.1, bf16[128,512]{1,0:T(8,128)(2,1)} %v.1, bf16[128,512]{1,0:T(8,128)(2,1)} %q.1, bf16[128,512]{1,0:T(8,128)(2,1)} %gate.2, ...), custom_call_target="tpu_custom_call" | custom-call | tf_op jit(solution)/shard_map/pack/pallas_call | solution.py:31
  1.9 8.8 %collective-permute-start = (bf16[5,128,256]{2,1,0:T(8,128)(2,1)S(1)}, bf16[5,128,256]{2,1,0:T(8,128)(2,1)S(1)}, u32[]{:S(2)}, u32[]{:S(2)}) collective-permute-start(bf16[5,128,256]{2,1,0:T(8,128)(2,1)S(1)} %get-tuple-element.36), channel_id=1, source_target_pairs={{0,32},{32,0},{64,96},{96,64},{128,160},{160,128},{192,224},{224,1... | collective-permute-start | bytes 983048 | tf_op jit(solution)/shard_map/ppermute | solution.py:524
  10.7 1.2 %collective-permute-done.given = bf16[5,128,256]{2,1,0:T(8,128)(2,1)S(1)} collective-permute-done((bf16[5,128,256]{2,1,0:T(8,128)(2,1)S(1)}, bf16[5,128,256]{2,1,0:T(8,128)(2,1)S(1)}, u32[]{:S(2)}, u32[]{:S(2)}) %collective-permute-start) | collective-permute-done | bytes 327712 | tf_op jit(solution)/shard_map/ppermute | solution.py:524
  12.0 1.9 %collective-permute-start.2 = (bf16[2,256,256]{2,1,0:T(8,128)(2,1)S(1)}, bf16[2,256,256]{2,1,0:T(8,128)(2,1)S(1)}, u32[]{:S(2)}, u32[]{:S(2)}) collective-permute-start(bf16[2,256,256]{2,1,0:T(8,128)(2,1)S(1)} %chip_kv.1), channel_id=1, source_target_pairs={{0,128},{32,160},{64,192},{96,224},{128,256},{160,288},{192,320},{... | collective-permute-start | bytes 786440 | tf_op jit(solution)/shard_map/ppermute | solution.py:524
  13.9 1.9 %collective-permute-start.1 = (bf16[2,256,256]{2,1,0:T(8,128)(2,1)S(1)}, bf16[2,256,256]{2,1,0:T(8,128)(2,1)S(1)}, u32[]{:S(2)}, u32[]{:S(2)}) collective-permute-start(bf16[2,256,256]{2,1,0:T(8,128)(2,1)S(1)} %chip_kv.1), channel_id=1, source_target_pairs={{0,64},{32,96},{64,128},{96,160},{128,192},{160,224},{192,256},{22... | collective-permute-start | bytes 786440 | tf_op jit(solution)/shard_map/ppermute | solution.py:524
  15.8 1.3 %head_states.1 = (f32[2,256,128]{2,1,0:T(8,128)S(1)}, f32[16,8,256]{2,1,0:T(8,128)S(1)}, bf16[8,16,256]{2,1,0:T(8,128)(2,1)}) custom-call(bf16[3,128,256]{2,1,0:T(8,128)(2,1)S(1)} %get-tuple-element.34.keep_rest, bf16[5,128,256]{2,1,0:T(8,128)(2,1)S(1)} %collective-permute-done.given, f32[33,256]{1,0:T(8,128)S(1)} %get-tuple-element.39.params), custom_call_target="tpu_custom_call" | custom-call | tf_op jit(solution)/shard_map/head_states/pallas_call | solution.py:31
  17.2 9.3 %all-to-all-start = ((bf16[8,16,256]{2,1,0:T(8,128)(2,1)}), bf16[8,16,256]{2,1,0:T(8,128)(2,1)S(1)}, u32[]{:S(2)}, u32[]{:S(2)}) async-start(bf16[8,16,256]{2,1,0:T(8,128)(2,1)} %get-tuple-element.43), calls=%async_computation | async-start | bytes 131072 | tf_op jit(solution)/shard_map/all_to_all | solution.py:530
  26.5 12.1 %collective-permute-done.2.far_kv = bf16[2,256,256]{2,1,0:T(8,128)(2,1)S(1)} collective-permute-done((bf16[2,256,256]{2,1,0:T(8,128)(2,1)S(1)}, bf16[2,256,256]{2,1,0:T(8,128)(2,1)S(1)}, u32[]{:S(2)}, u32[]{:S(2)}) %collective-permute-start.2) | collective-permute-done | bytes 262176 | tf_op jit(solution)/shard_map/ppermute | solution.py:524
  38.6 0.0 collective-permute-done.1.near_kv
  38.6 1.0 %forward.1 = (f32[2,2,8,128]{3,2,1,0:T(8,128)S(1)}, f32[2,256,128]{2,1,0:T(8,128)S(1)}) custom-call(bf16[3,128,256]{2,1,0:T(8,128)(2,1)S(1)} %get-tuple-element.34.keep_rest, bf16[2,256,256]{2,1,0:T(8,128)(2,1)S(1)} %chip_kv.1, bf16[5,128,256]{2,1,0:T(8,128)(2,1)S(1)} %collective-permute-done.given, bf16[2,256,256]{2,1,0:T(8,128)(2,1)S(1)} %collective-permute-done.1.near_kv, ...), custom_call_target="tpu_custom_call" | custom-call | flops 99999997952 | bytes 100000000 | tf_op jit(solution)/shard_map/forward/pallas_call | solution.py:31
  39.6 2.0 %tail.1 = (f32[16,8,256]{2,1,0:T(8,128)S(1)}, bf16[8,32,256]{2,1,0:T(8,128)(2,1)}) custom-call(f32[2,256,128]{2,1,0:T(8,128)S(1)} %get-tuple-element.38.attended, f32[2,256,128]{2,1,0:T(8,128)S(1)} %get-tuple-element.40.delta, f32[16,8,256]{2,1,0:T(8,128)S(1)} %get-tuple-element.41.totals, f32[33,256]{1,0:T(8,128)S(1)} %get-tuple-element.39.params), custom_call_target="tpu_custom_call" | custom-call | tf_op jit(solution)/shard_map/tail/pallas_call | solution.py:31
  41.5 0.0 all-to-all-done.slots_in
  41.5 3.1 %backward.1 = (bf16[256,256]{1,0:T(8,128)(2,1)S(1)}, f32[2,256,256]{2,1,0:T(8,128)S(1)}, bf16[2,256,256]{2,1,0:T(8,128)(2,1)S(1)}, bf16[2,128,256]{2,1,0:T(8,128...) custom-call(bf16[3,128,256]{2,1,0:T(8,128)(2,1)S(1)} %get-tuple-element.34.keep_rest, ...), custom_call_target="tpu_custom_call" | custom-call | tf_op jit(solution)/shard_map/backward/pallas_call | solution.py:31
  44.7 2.9 %collective-permute-start.3 = (bf16[2,256,256]{2,1,0:T(8,128)(2,1)S(1)}, bf16[2,256,256]{2,1,0:T(8,128)(2,1)S(1)}, u32[]{:S(2)}, u32[]{:S(2)}) collective-permute-start(bf16[2,256,256]{2,1,0:T(8,128)(2,1)S(1)} %get-tuple-element.46), channel_id=1, source_target_pairs={{0,384},{32,416},{64,448},{96,480},{128,0},{160,32},{192,64},{224,... | collective-permute-start | bytes 786440 | tf_op jit(solution)/shard_map/ppermute | solution.py:524
  47.5 3.4 %all-to-all-start.1 = ((bf16[8,32,256]{2,1,0:T(8,128)(2,1)}), bf16[8,32,256]{2,1,0:T(8,128)(2,1)S(1)}, u32[]{:S(2)}, u32[]{:S(2)}) async-start(bf16[8,32,256]{2,1,0:T(8,128)(2,1)} %get-tuple-element.56), calls=%async_computation.1 | async-start | bytes 262144 | tf_op jit(solution)/shard_map/all_to_all | solution.py:530
  50.9 9.9 %collective-permute-start.4 = (bf16[2,128,256]{2,1,0:T(8,128)(2,1)S(1)}, bf16[2,128,256]{2,1,0:T(8,128)(2,1)S(1)}, u32[]{:S(2)}, u32[]{:S(2)}) collective-permute-start(bf16[2,128,256]{2,1,0:T(8,128)(2,1)S(1)} %get-tuple-element.48), channel_id=1, source_target_pairs={{0,448},{32,480},{64,0},{96,32},{128,64},{160,96},{192,128},{224,1... | collective-permute-start | bytes 393224 | tf_op jit(solution)/shard_map/ppermute | solution.py:524
  60.8 3.7 %collective-permute-start.5 = (bf16[2,128,256]{2,1,0:T(8,128)(2,1)S(1)}, bf16[2,128,256]{2,1,0:T(8,128)(2,1)S(1)}, u32[]{:S(2)}, u32[]{:S(2)}) collective-permute-start(bf16[2,128,256]{2,1,0:T(8,128)(2,1)S(1)} %get-tuple-element.49), channel_id=1, source_target_pairs={{0,480},{32,448},{64,32},{96,0},{128,96},{160,64},{192,160},{224,1... | collective-permute-start | bytes 393224 | tf_op jit(solution)/shard_map/ppermute | solution.py:524
  64.6 0.0 collective-permute-done.3.far
  64.6 0.1 far_sum.1
  64.7 1.1 %local_mix.1 = f32[2,256,128]{2,1,0:T(8,128)S(1)} custom-call(f32[2,256,128]{2,1,0:T(8,128)S(1)} %get-tuple-element.38.attended, f32[16,8,256]{2,1,0:T(8,128)S(1)} %get-tuple-element.42.tail_totals, f32[33,256]{1,0:T(8,128)S(1)} %get-tuple-element.39.params, bf16[3,128,256]{2,1,0:T(8,128)(2,1)S(1)} %get-tuple-element.52.partner), custom_call_target="tpu_custom_call" | custom-call | tf_op jit(solution)/shard_map/local_mix/pallas_call | solution.py:31
  65.7 1.9 %collective-permute-start.6 = (bf16[3,128,256]{2,1,0:T(8,128)(2,1)S(1)}, bf16[3,128,256]{2,1,0:T(8,128)(2,1)S(1)}, u32[]{:S(2)}, u32[]{:S(2)}) collective-permute-start(bf16[3,128,256]{2,1,0:T(8,128)(2,1)S(1)} %get-tuple-element.52.partner), channel_id=1, source_target_pairs={{0,32},{32,0},{64,96},{96,64},{128,160},{160,128},{192,224},{224,1... | collective-permute-start | bytes 589832 | tf_op jit(solution)/shard_map/ppermute | solution.py:524
  67.7 0.0 all-to-all-done.1.slots_in
  67.7 0.8 %gate.3 = (bf16[128,256]{1,0:T(8,128)(2,1)S(1)}, bf16[160,256]{1,0:T(8,128)(2,1)S(1)}, f32[16,256]{1,0:T(8,128)S(1)}) custom-call(bf16[3,128,256]{2,1,0:T(8,128)(2,1)S(1)} %get-tuple-element.34.keep_rest, bf16[5,128,256]{2,1,0:T(8,128)(2,1)S(1)} %collective-permute-done.given, f32[2,256,128]{2,1,0:T(8,128)S(1)} %local_mix.1, ...), custom_call_target="tpu_custom_call" | custom-call | tf_op jit(solution)/shard_map/gate/pallas_call | solution.py:31
  68.5 2.4 %collective-permute-start.7 = (bf16[160,256]{1,0:T(8,128)(2,1)S(1)}, bf16[160,256]{1,0:T(8,128)(2,1)S(1)}, u32[]{:S(2)}, u32[]{:S(2)}) collective-permute-start(bf16[160,256]{1,0:T(8,128)(2,1)S(1)} %get-tuple-element.59), channel_id=1, source_target_pairs={{0,32},{32,0},{64,96},{96,64},{128,160},{160,128},{192,224},{224,1... | collective-permute-start | bytes 245768 | tf_op jit(solution)/shard_map/ppermute | solution.py:524
  70.9 0.0 collective-permute-done.4.same1
  70.9 0.0 collective-permute-done.5.cross1
  71.0 0.0 collective-permute-done.6.swapped
  71.0 0.8 %blocks.1 = (bf16[128,512]{1,0:T(8,128)(2,1)}, bf16[128,512]{1,0:T(8,128)(2,1)}, bf16[128,512]{1,0:T(8,128)(2,1)}) custom-call(bf16[256,256]{1,0:T(8,128)(2,1)S(1)} %get-tuple-element.44.dq.all_dq, bf16[2,128,256]{2,1,0:T(8,128)(2,1)S(1)} %get-tuple-element.50.own_part, f32[2,128,256]{2,1,0:T(8,128)S(1)} %get-tuple-element.51.other_part, ...), custom_call_target="tpu_custom_call" | custom-call | tf_op jit(solution)/shard_map/blocks/pallas_call | solution.py:31
  71.8 0.0 collective-permute-done.7.gate_in
  71.8 0.7 final.1
  (2 shorter events, 0.1 us)
Async XLA Ops:
  1.9 10.0 %collective-permute-start = (bf16[5,128,256]{2,1,0:T(8,128)(2,1)S(1)}, bf16[5,128,256]{2,1,0:T(8,128)(2,1)S(1)}, u32[]{:S(2)}, u32[]{:S(2)}) collective-permute-start(bf16[5,128,256]{2,1,0:T(8,128)(2,1)S(1)} %get-tuple-element.36), channel_id=1, source_target_pairs={{0,32},{32,0},{64,96},{96,64},{128,160},{160,128},{192,224},{224,1... | collective-permute-start | bytes 983048 | tf_op jit(solution)/shard_map/ppermute | solution.py:524
  12.0 26.6 %collective-permute-start.2 = (bf16[2,256,256]{2,1,0:T(8,128)(2,1)S(1)}, bf16[2,256,256]{2,1,0:T(8,128)(2,1)S(1)}, u32[]{:S(2)}, u32[]{:S(2)}) collective-permute-start(bf16[2,256,256]{2,1,0:T(8,128)(2,1)S(1)} %chip_kv.1), channel_id=1, source_target_pairs={{0,128},{32,160},{64,192},{96,224},{128,256},{160,288},{192,320},{... | collective-permute-start | bytes 786440 | tf_op jit(solution)/shard_map/ppermute | solution.py:524
  13.9 24.7 %collective-permute-start.1 = (bf16[2,256,256]{2,1,0:T(8,128)(2,1)S(1)}, bf16[2,256,256]{2,1,0:T(8,128)(2,1)S(1)}, u32[]{:S(2)}, u32[]{:S(2)}) collective-permute-start(bf16[2,256,256]{2,1,0:T(8,128)(2,1)S(1)} %chip_kv.1), channel_id=1, source_target_pairs={{0,64},{32,96},{64,128},{96,160},{128,192},{160,224},{192,256},{22... | collective-permute-start | bytes 786440 | tf_op jit(solution)/shard_map/ppermute | solution.py:524
  17.2 24.4 %all-to-all-start = ((bf16[8,16,256]{2,1,0:T(8,128)(2,1)}), bf16[8,16,256]{2,1,0:T(8,128)(2,1)S(1)}, u32[]{:S(2)}, u32[]{:S(2)}) async-start(bf16[8,16,256]{2,1,0:T(8,128)(2,1)} %get-tuple-element.43), calls=%async_computation | async-start | bytes 131072 | tf_op jit(solution)/shard_map/all_to_all | solution.py:530
  44.7 19.9 %collective-permute-start.3 = (bf16[2,256,256]{2,1,0:T(8,128)(2,1)S(1)}, bf16[2,256,256]{2,1,0:T(8,128)(2,1)S(1)}, u32[]{:S(2)}, u32[]{:S(2)}) collective-permute-start(bf16[2,256,256]{2,1,0:T(8,128)(2,1)S(1)} %get-tuple-element.46), channel_id=1, source_target_pairs={{0,384},{32,416},{64,448},{96,480},{128,0},{160,32},{192,64},{224,... | collective-permute-start | bytes 786440 | tf_op jit(solution)/shard_map/ppermute | solution.py:524
  47.5 20.1 %all-to-all-start.1 = ((bf16[8,32,256]{2,1,0:T(8,128)(2,1)}), bf16[8,32,256]{2,1,0:T(8,128)(2,1)S(1)}, u32[]{:S(2)}, u32[]{:S(2)}) async-start(bf16[8,32,256]{2,1,0:T(8,128)(2,1)} %get-tuple-element.56), calls=%async_computation.1 | async-start | bytes 262144 | tf_op jit(solution)/shard_map/all_to_all | solution.py:530
  50.9 20.0 %collective-permute-start.4 = (bf16[2,128,256]{2,1,0:T(8,128)(2,1)S(1)}, bf16[2,128,256]{2,1,0:T(8,128)(2,1)S(1)}, u32[]{:S(2)}, u32[]{:S(2)}) collective-permute-start(bf16[2,128,256]{2,1,0:T(8,128)(2,1)S(1)} %get-tuple-element.48), channel_id=1, source_target_pairs={{0,448},{32,480},{64,0},{96,32},{128,64},{160,96},{192,128},{224,1... | collective-permute-start | bytes 393224 | tf_op jit(solution)/shard_map/ppermute | solution.py:524
  60.8 10.1 %collective-permute-start.5 = (bf16[2,128,256]{2,1,0:T(8,128)(2,1)S(1)}, bf16[2,128,256]{2,1,0:T(8,128)(2,1)S(1)}, u32[]{:S(2)}, u32[]{:S(2)}) collective-permute-start(bf16[2,128,256]{2,1,0:T(8,128)(2,1)S(1)} %get-tuple-element.49), channel_id=1, source_target_pairs={{0,480},{32,448},{64,32},{96,0},{128,96},{160,64},{192,160},{224,1... | collective-permute-start | bytes 393224 | tf_op jit(solution)/shard_map/ppermute | solution.py:524
  65.7 5.2 %collective-permute-start.6 = (bf16[3,128,256]{2,1,0:T(8,128)(2,1)S(1)}, bf16[3,128,256]{2,1,0:T(8,128)(2,1)S(1)}, u32[]{:S(2)}, u32[]{:S(2)}) collective-permute-start(bf16[3,128,256]{2,1,0:T(8,128)(2,1)S(1)} %get-tuple-element.52.partner), channel_id=1, source_target_pairs={{0,32},{32,0},{64,96},{96,64},{128,160},{160,128},{192,224},{224,1... | collective-permute-start | bytes 589832 | tf_op jit(solution)/shard_map/ppermute | solution.py:524
  68.5 3.3 %collective-permute-start.7 = (bf16[160,256]{1,0:T(8,128)(2,1)S(1)}, bf16[160,256]{1,0:T(8,128)(2,1)S(1)}, u32[]{:S(2)}, u32[]{:S(2)}) collective-permute-start(bf16[160,256]{1,0:T(8,128)(2,1)S(1)} %get-tuple-element.59), channel_id=1, source_target_pairs={{0,32},{32,0},{64,96},{96,64},{128,160},{160,128},{192,224},{224,1... | collective-permute-start | bytes 245768 | tf_op jit(solution)/shard_map/ppermute | solution.py:524

commit v11 on v10

--- a/solution.py
+++ b/solution.py
@@ -203,11 +203,13 @@
         buf[2 * tokens : 3 * tokens, :] = chip_kv[slot]
 
 
-def allowed_pairs(rows):
-    span = (WIN + 1) * rows
-    key_ids = lax.broadcasted_iota(jnp.int32, (span, rows), 0)
-    row_ids = lax.broadcasted_iota(jnp.int32, (span, rows), 1)
-    return (key_ids > row_ids) & (key_ids <= row_ids + WIN * rows)
+def masked(scores):
+    rows = scores.shape[1]
+    key_ids = lax.broadcasted_iota(jnp.int32, (rows, rows), 0)
+    row_ids = lax.broadcasted_iota(jnp.int32, (rows, rows), 1)
+    oldest = jnp.where(key_ids > row_ids, scores[:rows], -jnp.inf)
+    newest = jnp.where(key_ids <= row_ids, scores[WIN * rows :], -jnp.inf)
+    return jnp.concatenate([oldest, scores[rows : WIN * rows], newest], axis=0)
 
 
 def forward_body(
@@ -219,7 +221,6 @@
     scale = 1.0 / math.sqrt(HEAD)
     assemble(core, keep_rest, chip_kv, given, near_kv, far_kv, qbuf, kbuf, vbuf)
     span = (WIN + 1) * rows
-    allowed = allowed_pairs(rows)
     for head in range(width // HEAD):
         at_head = slice(head * HEAD, (head + 1) * HEAD)
         for block in range(tokens // rows):
@@ -231,7 +232,7 @@
                 )
                 * scale
             )
-            scores = jnp.where(allowed, scores, -jnp.inf)
+            scores = masked(scores)
             top = jnp.max(scores, axis=0, keepdims=True)
             raised = jnp.exp(scores - top)
             share = 1.0 / jnp.sum(raised, axis=0, keepdims=True)
@@ -348,7 +349,6 @@
     adj16[...] = adj32[...].astype(BF16)
 
     span = (WIN + 1) * rows
-    allowed = allowed_pairs(rows)
     for head in range(width // HEAD):
         at_head = slice(head * HEAD, (head + 1) * HEAD)
         for block in range(tokens // rows):
@@ -359,7 +359,7 @@
             value = vbuf[at_keys, at_head]
             adjoint = adj16[head, at_rows, :]
             scores = lax.dot_general(key, query, OVER_HEAD, preferred_element_type=F32) * scale
-            scores = jnp.where(allowed, scores, -jnp.inf)
+            scores = masked(scores)
             probability = jnp.exp(scores - stats[head, block, 0:1, :]) * stats[head, block, 1:2, :]
             rounded = probability.astype(BF16)
             weight = lax.dot_general(value, adjoint, OVER_HEAD, preferred_element_type=F32)

time: 73.4 us -> 73.4 us (level)
  no operation moved by 1% of the time
where the time goes in v11:
time: 73.4 us; the launch traced here: 72.5 us
  starting transfers between devices  46.2 us (63%)
  waiting for transfers between devices  13.4 us (18%)
  Pallas kernels  12.2 us (17%)
  between operations  0.8 us (1%)
    ppermute x8, starting transfers between devices, chip_shift(): return lax.ppermute(array, 'ctx', pairs)  33.4 us
    ppermute x8, waiting for transfers between devices, chip_shift(): return lax.ppermute(array, 'ctx', pairs)  13.4 us
    all_to_all x2, starting transfers between devices, chip_exchange(): return lax.all_to_all(slots, 'ctx', 0, 0, axis_index_groups=groups)  12.7 us
    pallas_call x12, Pallas kernels, run(): pl.pallas_call(body, out_shape=[pltpu.VMEM(s, d) if local_out else jax.Sh...  12.2 us
  transfers between devices with their start and end apart: 10, of which 2 were waited for; matrix products, arithmetic and copies ran while one was open for 0% of the time, Pallas kernels for 10%

profile of v11, /device:TPU:1, one launch (start us, length us, event | category | flops | bytes accessed | tf_op | source)
XLA Modules:
  0.0 72.5 jit_solution(14984916590808366087)
XLA Ops:
  0.6 1.3 %pack.1 = (bf16[2,128,256]{2,1,0:T(8,128)(2,1)S(1)}, bf16[3,128,256]{2,1,0:T(8,128)(2,1)S(1)}, bf16[5,128,256]{2,1,0:T(8,128)(2,1)S(1)}, f32[33,256]{1,0:T(8,128)S(1)}) custom-call(bf16[128,512]{1,0:T(8,128)(2,1)} %k.1, bf16[128,512]{1,0:T(8,128)(2,1)} %v.1, bf16[128,512]{1,0:T(8,128)(2,1)} %q.1, bf16[128,512]{1,0:T(8,128)(2,1)} %gate.2, ...), custom_call_target="tpu_custom_call" | custom-call | tf_op jit(solution)/shard_map/pack/pallas_call | solution.py:31
  1.9 8.8 %collective-permute-start = (bf16[5,128,256]{2,1,0:T(8,128)(2,1)S(1)}, bf16[5,128,256]{2,1,0:T(8,128)(2,1)S(1)}, u32[]{:S(2)}, u32[]{:S(2)}) collective-permute-start(bf16[5,128,256]{2,1,0:T(8,128)(2,1)S(1)} %get-tuple-element.36), channel_id=1, source_target_pairs={{0,32},{32,0},{64,96},{96,64},{128,160},{160,128},{192,224},{224,1... | collective-permute-start | bytes 983048 | tf_op jit(solution)/shard_map/ppermute | solution.py:524
  10.7 1.2 %collective-permute-done.given = bf16[5,128,256]{2,1,0:T(8,128)(2,1)S(1)} collective-permute-done((bf16[5,128,256]{2,1,0:T(8,128)(2,1)S(1)}, bf16[5,128,256]{2,1,0:T(8,128)(2,1)S(1)}, u32[]{:S(2)}, u32[]{:S(2)}) %collective-permute-start) | collective-permute-done | bytes 327712 | tf_op jit(solution)/shard_map/ppermute | solution.py:524
  12.0 1.9 %collective-permute-start.2 = (bf16[2,256,256]{2,1,0:T(8,128)(2,1)S(1)}, bf16[2,256,256]{2,1,0:T(8,128)(2,1)S(1)}, u32[]{:S(2)}, u32[]{:S(2)}) collective-permute-start(bf16[2,256,256]{2,1,0:T(8,128)(2,1)S(1)} %chip_kv.1), channel_id=1, source_target_pairs={{0,128},{32,160},{64,192},{96,224},{128,256},{160,288},{192,320},{... | collective-permute-start | bytes 786440 | tf_op jit(solution)/shard_map/ppermute | solution.py:524
  13.9 1.9 %collective-permute-start.1 = (bf16[2,256,256]{2,1,0:T(8,128)(2,1)S(1)}, bf16[2,256,256]{2,1,0:T(8,128)(2,1)S(1)}, u32[]{:S(2)}, u32[]{:S(2)}) collective-permute-start(bf16[2,256,256]{2,1,0:T(8,128)(2,1)S(1)} %chip_kv.1), channel_id=1, source_target_pairs={{0,64},{32,96},{64,128},{96,160},{128,192},{160,224},{192,256},{22... | collective-permute-start | bytes 786440 | tf_op jit(solution)/shard_map/ppermute | solution.py:524
  15.8 1.3 %head_states.1 = (f32[2,256,128]{2,1,0:T(8,128)S(1)}, f32[16,8,256]{2,1,0:T(8,128)S(1)}, bf16[8,16,256]{2,1,0:T(8,128)(2,1)}) custom-call(bf16[3,128,256]{2,1,0:T(8,128)(2,1)S(1)} %get-tuple-element.34.keep_rest, bf16[5,128,256]{2,1,0:T(8,128)(2,1)S(1)} %collective-permute-done.given, f32[33,256]{1,0:T(8,128)S(1)} %get-tuple-element.39.params), custom_call_target="tpu_custom_call" | custom-call | tf_op jit(solution)/shard_map/head_states/pallas_call | solution.py:31
  17.2 9.3 %all-to-all-start = ((bf16[8,16,256]{2,1,0:T(8,128)(2,1)}), bf16[8,16,256]{2,1,0:T(8,128)(2,1)S(1)}, u32[]{:S(2)}, u32[]{:S(2)}) async-start(bf16[8,16,256]{2,1,0:T(8,128)(2,1)} %get-tuple-element.43), calls=%async_computation | async-start | bytes 131072 | tf_op jit(solution)/shard_map/all_to_all | solution.py:530
  26.5 12.1 %collective-permute-done.2.far_kv = bf16[2,256,256]{2,1,0:T(8,128)(2,1)S(1)} collective-permute-done((bf16[2,256,256]{2,1,0:T(8,128)(2,1)S(1)}, bf16[2,256,256]{2,1,0:T(8,128)(2,1)S(1)}, u32[]{:S(2)}, u32[]{:S(2)}) %collective-permute-start.2) | collective-permute-done | bytes 262176 | tf_op jit(solution)/shard_map/ppermute | solution.py:524
  38.6 0.0 collective-permute-done.1.near_kv
  38.6 1.0 %forward.1 = (f32[2,2,8,128]{3,2,1,0:T(8,128)S(1)}, f32[2,256,128]{2,1,0:T(8,128)S(1)}) custom-call(bf16[3,128,256]{2,1,0:T(8,128)(2,1)S(1)} %get-tuple-element.34.keep_rest, bf16[2,256,256]{2,1,0:T(8,128)(2,1)S(1)} %chip_kv.1, bf16[5,128,256]{2,1,0:T(8,128)(2,1)S(1)} %collective-permute-done.given, bf16[2,256,256]{2,1,0:T(8,128)(2,1)S(1)} %collective-permute-done.1.near_kv, ...), custom_call_target="tpu_custom_call" | custom-call | flops 99999997952 | bytes 100000000 | tf_op jit(solution)/shard_map/forward/pallas_call | solution.py:31
  39.6 2.0 %tail.1 = (f32[16,8,256]{2,1,0:T(8,128)S(1)}, bf16[8,32,256]{2,1,0:T(8,128)(2,1)}) custom-call(f32[2,256,128]{2,1,0:T(8,128)S(1)} %get-tuple-element.38.attended, f32[2,256,128]{2,1,0:T(8,128)S(1)} %get-tuple-element.40.delta, f32[16,8,256]{2,1,0:T(8,128)S(1)} %get-tuple-element.41.totals, f32[33,256]{1,0:T(8,128)S(1)} %get-tuple-element.39.params), custom_call_target="tpu_custom_call" | custom-call | tf_op jit(solution)/shard_map/tail/pallas_call | solution.py:31
  41.5 0.0 all-to-all-done.slots_in
  41.5 3.1 %backward.1 = (bf16[256,256]{1,0:T(8,128)(2,1)S(1)}, f32[2,256,256]{2,1,0:T(8,128)S(1)}, bf16[2,256,256]{2,1,0:T(8,128)(2,1)S(1)}, bf16[2,128,256]{2,1,0:T(8,128...) custom-call(bf16[3,128,256]{2,1,0:T(8,128)(2,1)S(1)} %get-tuple-element.34.keep_rest, ...), custom_call_target="tpu_custom_call" | custom-call | tf_op jit(solution)/shard_map/backward/pallas_call | solution.py:31
  44.7 2.9 %collective-permute-start.3 = (bf16[2,256,256]{2,1,0:T(8,128)(2,1)S(1)}, bf16[2,256,256]{2,1,0:T(8,128)(2,1)S(1)}, u32[]{:S(2)}, u32[]{:S(2)}) collective-permute-start(bf16[2,256,256]{2,1,0:T(8,128)(2,1)S(1)} %get-tuple-element.46), channel_id=1, source_target_pairs={{0,384},{32,416},{64,448},{96,480},{128,0},{160,32},{192,64},{224,... | collective-permute-start | bytes 786440 | tf_op jit(solution)/shard_map/ppermute | solution.py:524
  47.5 3.4 %all-to-all-start.1 = ((bf16[8,32,256]{2,1,0:T(8,128)(2,1)}), bf16[8,32,256]{2,1,0:T(8,128)(2,1)S(1)}, u32[]{:S(2)}, u32[]{:S(2)}) async-start(bf16[8,32,256]{2,1,0:T(8,128)(2,1)} %get-tuple-element.56), calls=%async_computation.1 | async-start | bytes 262144 | tf_op jit(solution)/shard_map/all_to_all | solution.py:530
  50.9 9.9 %collective-permute-start.4 = (bf16[2,128,256]{2,1,0:T(8,128)(2,1)S(1)}, bf16[2,128,256]{2,1,0:T(8,128)(2,1)S(1)}, u32[]{:S(2)}, u32[]{:S(2)}) collective-permute-start(bf16[2,128,256]{2,1,0:T(8,128)(2,1)S(1)} %get-tuple-element.48), channel_id=1, source_target_pairs={{0,448},{32,480},{64,0},{96,32},{128,64},{160,96},{192,128},{224,1... | collective-permute-start | bytes 393224 | tf_op jit(solution)/shard_map/ppermute | solution.py:524
  60.8 3.7 %collective-permute-start.5 = (bf16[2,128,256]{2,1,0:T(8,128)(2,1)S(1)}, bf16[2,128,256]{2,1,0:T(8,128)(2,1)S(1)}, u32[]{:S(2)}, u32[]{:S(2)}) collective-permute-start(bf16[2,128,256]{2,1,0:T(8,128)(2,1)S(1)} %get-tuple-element.49), channel_id=1, source_target_pairs={{0,480},{32,448},{64,32},{96,0},{128,96},{160,64},{192,160},{224,1... | collective-permute-start | bytes 393224 | tf_op jit(solution)/shard_map/ppermute | solution.py:524
  64.6 0.0 collective-permute-done.3.far
  64.6 0.1 far_sum.1
  64.7 1.1 %local_mix.1 = f32[2,256,128]{2,1,0:T(8,128)S(1)} custom-call(f32[2,256,128]{2,1,0:T(8,128)S(1)} %get-tuple-element.38.attended, f32[16,8,256]{2,1,0:T(8,128)S(1)} %get-tuple-element.42.tail_totals, f32[33,256]{1,0:T(8,128)S(1)} %get-tuple-element.39.params, bf16[3,128,256]{2,1,0:T(8,128)(2,1)S(1)} %get-tuple-element.52.partner), custom_call_target="tpu_custom_call" | custom-call | tf_op jit(solution)/shard_map/local_mix/pallas_call | solution.py:31
  65.7 1.9 %collective-permute-start.6 = (bf16[3,128,256]{2,1,0:T(8,128)(2,1)S(1)}, bf16[3,128,256]{2,1,0:T(8,128)(2,1)S(1)}, u32[]{:S(2)}, u32[]{:S(2)}) collective-permute-start(bf16[3,128,256]{2,1,0:T(8,128)(2,1)S(1)} %get-tuple-element.52.partner), channel_id=1, source_target_pairs={{0,32},{32,0},{64,96},{96,64},{128,160},{160,128},{192,224},{224,1... | collective-permute-start | bytes 589832 | tf_op jit(solution)/shard_map/ppermute | solution.py:524
  67.7 0.0 all-to-all-done.1.slots_in
  67.7 0.8 %gate.3 = (bf16[128,256]{1,0:T(8,128)(2,1)S(1)}, bf16[160,256]{1,0:T(8,128)(2,1)S(1)}, f32[16,256]{1,0:T(8,128)S(1)}) custom-call(bf16[3,128,256]{2,1,0:T(8,128)(2,1)S(1)} %get-tuple-element.34.keep_rest, bf16[5,128,256]{2,1,0:T(8,128)(2,1)S(1)} %collective-permute-done.given, f32[2,256,128]{2,1,0:T(8,128)S(1)} %local_mix.1, ...), custom_call_target="tpu_custom_call" | custom-call | tf_op jit(solution)/shard_map/gate/pallas_call | solution.py:31
  68.5 2.4 %collective-permute-start.7 = (bf16[160,256]{1,0:T(8,128)(2,1)S(1)}, bf16[160,256]{1,0:T(8,128)(2,1)S(1)}, u32[]{:S(2)}, u32[]{:S(2)}) collective-permute-start(bf16[160,256]{1,0:T(8,128)(2,1)S(1)} %get-tuple-element.59), channel_id=1, source_target_pairs={{0,32},{32,0},{64,96},{96,64},{128,160},{160,128},{192,224},{224,1... | collective-permute-start | bytes 245768 | tf_op jit(solution)/shard_map/ppermute | solution.py:524
  70.9 0.0 collective-permute-done.4.same1
  70.9 0.0 collective-permute-done.5.cross1
  71.0 0.0 collective-permute-done.6.swapped
  71.0 0.8 %blocks.1 = (bf16[128,512]{1,0:T(8,128)(2,1)}, bf16[128,512]{1,0:T(8,128)(2,1)}, bf16[128,512]{1,0:T(8,128)(2,1)}) custom-call(bf16[256,256]{1,0:T(8,128)(2,1)S(1)} %get-tuple-element.44.dq.all_dq, bf16[2,128,256]{2,1,0:T(8,128)(2,1)S(1)} %get-tuple-element.50.own_part, f32[2,128,256]{2,1,0:T(8,128)S(1)} %get-tuple-element.51.other_part, ...), custom_call_target="tpu_custom_call" | custom-call | tf_op jit(solution)/shard_map/blocks/pallas_call | solution.py:31
  71.8 0.0 collective-permute-done.7.gate_in
  71.8 0.7 final.1
  (2 shorter events, 0.1 us)
Async XLA Ops:
  1.9 10.0 %collective-permute-start = (bf16[5,128,256]{2,1,0:T(8,128)(2,1)S(1)}, bf16[5,128,256]{2,1,0:T(8,128)(2,1)S(1)}, u32[]{:S(2)}, u32[]{:S(2)}) collective-permute-start(bf16[5,128,256]{2,1,0:T(8,128)(2,1)S(1)} %get-tuple-element.36), channel_id=1, source_target_pairs={{0,32},{32,0},{64,96},{96,64},{128,160},{160,128},{192,224},{224,1... | collective-permute-start | bytes 983048 | tf_op jit(solution)/shard_map/ppermute | solution.py:524
  12.0 26.6 %collective-permute-start.2 = (bf16[2,256,256]{2,1,0:T(8,128)(2,1)S(1)}, bf16[2,256,256]{2,1,0:T(8,128)(2,1)S(1)}, u32[]{:S(2)}, u32[]{:S(2)}) collective-permute-start(bf16[2,256,256]{2,1,0:T(8,128)(2,1)S(1)} %chip_kv.1), channel_id=1, source_target_pairs={{0,128},{32,160},{64,192},{96,224},{128,256},{160,288},{192,320},{... | collective-permute-start | bytes 786440 | tf_op jit(solution)/shard_map/ppermute | solution.py:524
  13.9 24.7 %collective-permute-start.1 = (bf16[2,256,256]{2,1,0:T(8,128)(2,1)S(1)}, bf16[2,256,256]{2,1,0:T(8,128)(2,1)S(1)}, u32[]{:S(2)}, u32[]{:S(2)}) collective-permute-start(bf16[2,256,256]{2,1,0:T(8,128)(2,1)S(1)} %chip_kv.1), channel_id=1, source_target_pairs={{0,64},{32,96},{64,128},{96,160},{128,192},{160,224},{192,256},{22... | collective-permute-start | bytes 786440 | tf_op jit(solution)/shard_map/ppermute | solution.py:524
  17.2 24.4 %all-to-all-start = ((bf16[8,16,256]{2,1,0:T(8,128)(2,1)}), bf16[8,16,256]{2,1,0:T(8,128)(2,1)S(1)}, u32[]{:S(2)}, u32[]{:S(2)}) async-start(bf16[8,16,256]{2,1,0:T(8,128)(2,1)} %get-tuple-element.43), calls=%async_computation | async-start | bytes 131072 | tf_op jit(solution)/shard_map/all_to_all | solution.py:530
  44.7 19.9 %collective-permute-start.3 = (bf16[2,256,256]{2,1,0:T(8,128)(2,1)S(1)}, bf16[2,256,256]{2,1,0:T(8,128)(2,1)S(1)}, u32[]{:S(2)}, u32[]{:S(2)}) collective-permute-start(bf16[2,256,256]{2,1,0:T(8,128)(2,1)S(1)} %get-tuple-element.46), channel_id=1, source_target_pairs={{0,384},{32,416},{64,448},{96,480},{128,0},{160,32},{192,64},{224,... | collective-permute-start | bytes 786440 | tf_op jit(solution)/shard_map/ppermute | solution.py:524
  47.5 20.1 %all-to-all-start.1 = ((bf16[8,32,256]{2,1,0:T(8,128)(2,1)}), bf16[8,32,256]{2,1,0:T(8,128)(2,1)S(1)}, u32[]{:S(2)}, u32[]{:S(2)}) async-start(bf16[8,32,256]{2,1,0:T(8,128)(2,1)} %get-tuple-element.56), calls=%async_computation.1 | async-start | bytes 262144 | tf_op jit(solution)/shard_map/all_to_all | solution.py:530
  50.9 20.0 %collective-permute-start.4 = (bf16[2,128,256]{2,1,0:T(8,128)(2,1)S(1)}, bf16[2,128,256]{2,1,0:T(8,128)(2,1)S(1)}, u32[]{:S(2)}, u32[]{:S(2)}) collective-permute-start(bf16[2,128,256]{2,1,0:T(8,128)(2,1)S(1)} %get-tuple-element.48), channel_id=1, source_target_pairs={{0,448},{32,480},{64,0},{96,32},{128,64},{160,96},{192,128},{224,1... | collective-permute-start | bytes 393224 | tf_op jit(solution)/shard_map/ppermute | solution.py:524
  60.8 10.1 %collective-permute-start.5 = (bf16[2,128,256]{2,1,0:T(8,128)(2,1)S(1)}, bf16[2,128,256]{2,1,0:T(8,128)(2,1)S(1)}, u32[]{:S(2)}, u32[]{:S(2)}) collective-permute-start(bf16[2,128,256]{2,1,0:T(8,128)(2,1)S(1)} %get-tuple-element.49), channel_id=1, source_target_pairs={{0,480},{32,448},{64,32},{96,0},{128,96},{160,64},{192,160},{224,1... | collective-permute-start | bytes 393224 | tf_op jit(solution)/shard_map/ppermute | solution.py:524
  65.7 5.2 %collective-permute-start.6 = (bf16[3,128,256]{2,1,0:T(8,128)(2,1)S(1)}, bf16[3,128,256]{2,1,0:T(8,128)(2,1)S(1)}, u32[]{:S(2)}, u32[]{:S(2)}) collective-permute-start(bf16[3,128,256]{2,1,0:T(8,128)(2,1)S(1)} %get-tuple-element.52.partner), channel_id=1, source_target_pairs={{0,32},{32,0},{64,96},{96,64},{128,160},{160,128},{192,224},{224,1... | collective-permute-start | bytes 589832 | tf_op jit(solution)/shard_map/ppermute | solution.py:524
  68.5 3.3 %collective-permute-start.7 = (bf16[160,256]{1,0:T(8,128)(2,1)S(1)}, bf16[160,256]{1,0:T(8,128)(2,1)S(1)}, u32[]{:S(2)}, u32[]{:S(2)}) collective-permute-start(bf16[160,256]{1,0:T(8,128)(2,1)S(1)} %get-tuple-element.59), channel_id=1, source_target_pairs={{0,32},{32,0},{64,96},{96,64},{128,160},{160,128},{192,224},{224,1... | collective-permute-start | bytes 245768 | tf_op jit(solution)/shard_map/ppermute | solution.py:524
